TPU v7x, 32 devices: a whole 2x2x4 slice. The times are simulated.
32 devices in a mesh: narrow: 8 (over y, x, core), wide: 4 (over z).
Axes of the slice: x: 2, y: 2, z: 4, core: 2. Of those that a mesh axis runs over, the one named last changes fastest.
Arguments:
- block_input: bfloat16 [8192, 2048], P(('narrow', 'wide')), may hold values from -6 to 6
- cotangent: bfloat16 [8192, 2048], P(('narrow', 'wide')), may hold values from -6 to 6
- query_weight: bfloat16 [2048, 1536], P('narrow'), may hold values from -0.125 to 0.125
- key_weight: bfloat16 [2048, 384], P('narrow'), may hold values from -0.125 to 0.125
- value_weight: bfloat16 [2048, 384], P('narrow'), may hold values from -0.125 to 0.125
- project_weight: bfloat16 [1536, 2048], P(None, 'narrow'), may hold values from -0.625 to 0.625
- prenorm_gain: bfloat16 [2048], P('narrow'), may hold values from 0.5 to 1.5
- midnorm_gain: bfloat16 [2048], P('narrow'), may hold values from 0.5 to 1.5
- gate_weight: bfloat16 [2048, 4608], P(None, 'wide'), may hold values from -0.125 to 0.125
- up_weight: bfloat16 [2048, 4608], P(None, 'wide'), may hold values from -0.125 to 0.125
- down_weight: bfloat16 [4608, 2048], P('wide'), may hold values from -0.125 to 0.125
- doc_lengths: int32 [32, 4], P(('narrow', 'wide')), may hold values from 1 to 128, 256 in all within a row
- tile_counts: int32 [4], replicated, may hold values from 1 to 9, as said below
Outputs:
- block_output: bfloat16 [8192, 2048], P(('narrow', 'wide'))
- input_grad: bfloat16 [8192, 2048], P(('narrow', 'wide'))
- query_grad: float32 [2048, 1536], P('narrow')
- key_grad: float32 [2048, 384], P('narrow')
- value_grad: float32 [2048, 384], P('narrow')
- project_grad: float32 [1536, 2048], P(None, 'narrow')
- prenorm_grad: float32 [2048], P('narrow')
- midnorm_grad: float32 [2048], P('narrow')
- gate_grad: float32 [2048, 4608], P(None, 'wide')
- up_grad: float32 [2048, 4608], P(None, 'wide')
- down_grad: float32 [4608, 2048], P('wide')
Inputs may be any that keep to these rules, and one draw needn't show every extreme that they name: `doc_lengths`: each row's 4 lengths sum to 256, and the longest of every row has 128 tokens. `tile_counts`: the counts sum to 34, and one index of wide holds 9.
All inputs are finite; a program needn't handle non-finite values.
Results may differ from a plain program's by a relative error of at most 0.02.
Values may be sent and summed in bfloat16 or wider, within the bound.
A program may use at most 192 MiB of HBM per device.

v0:
```python
import jax
import jax.numpy as jnp
from jax import lax
from jax.sharding import PartitionSpec as P

HEADS = 24
KV_HEADS = 6
HEAD_DIM = 64
TILE = 128


EPSILON = 1e-06


def rms_scale(rows, gain):
    factor = lax.rsqrt(jnp.mean(rows * rows, axis=-1, keepdims=True) + EPSILON)
    return rows * factor * gain


def contract_rows(left, right):
    return lax.dot_general(
        left, right, (((0,), (0,)), ((), ())), preferred_element_type=jnp.float32
    )


def contract_cols(left, right):
    return lax.dot_general(
        left, right, (((1,), (1,)), ((), ())), preferred_element_type=jnp.float32
    )


def per_device(
    block_input,
    cotangent,
    query_weight,
    key_weight,
    value_weight,
    project_weight,
    prenorm_gain,
    midnorm_gain,
    gate_weight,
    up_weight,
    down_weight,
    doc_lengths,
    tile_counts,
):
    query_full, key_full, value_full, project_full, prenorm_full, midnorm_full = (
        lax.all_gather(query_weight, "narrow", axis=0, tiled=True),
        lax.all_gather(key_weight, "narrow", axis=0, tiled=True),
        lax.all_gather(value_weight, "narrow", axis=0, tiled=True),
        lax.all_gather(project_weight, "narrow", axis=1, tiled=True),
        lax.all_gather(prenorm_gain, "narrow", axis=0, tiled=True),
        lax.all_gather(midnorm_gain, "narrow", axis=0, tiled=True),
    )
    tokens_here = block_input.shape[0]
    group = HEADS // KV_HEADS
    scale = HEAD_DIM ** (-0.5)
    first_gain = prenorm_full.astype(jnp.float32)
    second_gain = midnorm_full.astype(jnp.float32)
    inputs_f = block_input.astype(jnp.float32)
    normed = rms_scale(inputs_f, first_gain).astype(jnp.bfloat16)
    query_rows = (
        jnp.dot(normed, query_full, preferred_element_type=jnp.float32)
        .astype(jnp.bfloat16)
        .reshape(tokens_here, KV_HEADS, group, HEAD_DIM)
    )
    key_rows = (
        jnp.dot(normed, key_full, preferred_element_type=jnp.float32)
        .astype(jnp.bfloat16)
        .reshape(tokens_here, KV_HEADS, HEAD_DIM)
    )
    value_rows = (
        jnp.dot(normed, value_full, preferred_element_type=jnp.float32)
        .astype(jnp.bfloat16)
        .reshape(tokens_here, KV_HEADS, HEAD_DIM)
    )
    ends = jnp.cumsum(doc_lengths[0])
    position = jnp.arange(tokens_here, dtype=jnp.int32)
    segment = jnp.sum((position[:, None] >= ends[None, :]).astype(jnp.int32), axis=1)
    allowed = (segment[:, None] == segment[None, :]) & (position[None, :] <= position[:, None])
    scores = (
        jnp.einsum("qcgd,kcd->cgqk", query_rows, key_rows, preferred_element_type=jnp.float32)
        * scale
    )
    masked = jnp.where(allowed, scores, -1e30)
    peak = jnp.max(masked, axis=-1, keepdims=True)
    expo = jnp.exp(masked - peak)
    total = jnp.sum(expo, axis=-1, keepdims=True)
    probs_low = (expo / total).astype(jnp.bfloat16)
    logsum = peak + jnp.log(total)
    attended = (
        jnp.einsum("cgqk,kcd->qcgd", probs_low, value_rows, preferred_element_type=jnp.float32)
        .astype(jnp.bfloat16)
        .reshape(tokens_here, HEADS * HEAD_DIM)
    )
    branch = jnp.dot(attended, project_full, preferred_element_type=jnp.float32)
    middle = inputs_f + branch
    mixed_in = rms_scale(middle, second_gain).astype(jnp.bfloat16)
    gathered = lax.all_gather(mixed_in, "wide", axis=0, tiled=True)
    width = gate_weight.shape[1]
    wide_index = lax.axis_index("wide")
    my_count = jnp.sum(
        jnp.where(jnp.arange(tile_counts.shape[0], dtype=jnp.int32) == wide_index, tile_counts, 0)
    )
    live = (jnp.arange(width, dtype=jnp.int32) // TILE < my_count).astype(jnp.float32)
    gate_pre = jnp.dot(gathered, gate_weight, preferred_element_type=jnp.float32)
    up_pre = jnp.dot(gathered, up_weight, preferred_element_type=jnp.float32)
    hidden = (jax.nn.silu(gate_pre) * up_pre * live).astype(jnp.bfloat16)
    partial_rows = jnp.dot(hidden, down_weight, preferred_element_type=jnp.float32)
    feed = lax.psum_scatter(
        partial_rows.astype(jnp.bfloat16), "wide", scatter_dimension=0, tiled=True
    ).astype(jnp.float32)
    block_output = (middle + feed).astype(jnp.bfloat16)
    out_grad = cotangent.astype(jnp.float32)
    grad_rows = lax.all_gather(cotangent, "wide", axis=0, tiled=True)
    kept_inputs = lax.all_gather(mixed_in, "wide", axis=0, tiled=True)
    gate_again = jnp.dot(kept_inputs, gate_weight, preferred_element_type=jnp.float32)
    up_again = jnp.dot(kept_inputs, up_weight, preferred_element_type=jnp.float32)
    hidden_again = (jax.nn.silu(gate_again) * up_again * live).astype(jnp.bfloat16)
    hidden_back = contract_cols(grad_rows, down_weight)
    sigma = jax.nn.sigmoid(gate_again)
    gate_back = (hidden_back * up_again * live * sigma * (1.0 + gate_again * (1.0 - sigma))).astype(
        jnp.bfloat16
    )
    up_back = (hidden_back * gate_again * sigma * live).astype(jnp.bfloat16)
    down_part = contract_rows(hidden_again, grad_rows)
    gate_part = contract_rows(kept_inputs, gate_back)
    up_part = contract_rows(kept_inputs, up_back)
    mixed_terms = contract_cols(gate_back, gate_weight) + contract_cols(up_back, up_weight)
    mixed_back = lax.psum_scatter(mixed_terms, "wide", scatter_dimension=0, tiled=True)
    unused_second, second_backward = jax.vjp(rms_scale, middle, second_gain)
    middle_norm_back, second_gain_part = second_backward(mixed_back)
    middle_back = out_grad + middle_norm_back
    branch_back = middle_back.astype(jnp.bfloat16)
    project_part = contract_rows(attended, branch_back)
    attended_back = (
        contract_cols(branch_back, project_full)
        .astype(jnp.bfloat16)
        .reshape(tokens_here, KV_HEADS, group, HEAD_DIM)
    )
    scores_again = (
        jnp.einsum("qcgd,kcd->cgqk", query_rows, key_rows, preferred_element_type=jnp.float32)
        * scale
    )
    probs_again = jnp.where(allowed, jnp.exp(scores_again - logsum), 0.0)
    probs_again_low = probs_again.astype(jnp.bfloat16)
    value_back = (
        jnp.einsum(
            "cgqk,qcgd->kcd", probs_again_low, attended_back, preferred_element_type=jnp.float32
        )
        .astype(jnp.bfloat16)
        .reshape(tokens_here, KV_HEADS * HEAD_DIM)
    )
    probs_back = jnp.einsum(
        "qcgd,kcd->cgqk", attended_back, value_rows, preferred_element_type=jnp.float32
    )
    scores_back = (
        probs_again * (probs_back - jnp.sum(probs_again * probs_back, axis=-1, keepdims=True))
    ).astype(jnp.bfloat16)
    query_back = (
        (
            jnp.einsum("cgqk,kcd->qcgd", scores_back, key_rows, preferred_element_type=jnp.float32)
            * scale
        )
        .astype(jnp.bfloat16)
        .reshape(tokens_here, HEADS * HEAD_DIM)
    )
    key_back = (
        (
            jnp.einsum(
                "cgqk,qcgd->kcd", scores_back, query_rows, preferred_element_type=jnp.float32
            )
            * scale
        )
        .astype(jnp.bfloat16)
        .reshape(tokens_here, KV_HEADS * HEAD_DIM)
    )
    query_part = contract_rows(normed, query_back)
    key_part = contract_rows(normed, key_back)
    value_part = contract_rows(normed, value_back)
    normed_back = (
        contract_cols(query_back, query_full)
        + contract_cols(key_back, key_full)
        + contract_cols(value_back, value_full)
    )
    unused_first, first_backward = jax.vjp(rms_scale, inputs_f, first_gain)
    input_norm_back, first_gain_part = first_backward(normed_back)
    input_grad = (middle_back + input_norm_back).astype(jnp.bfloat16)
    layer_terms = (
        query_part,
        key_part,
        value_part,
        project_part,
        first_gain_part,
        second_gain_part,
    )
    shares = (
        lax.psum_scatter(
            layer_terms[0].astype(jnp.bfloat16), "narrow", scatter_dimension=0, tiled=True
        ).astype(jnp.float32),
        lax.psum_scatter(
            layer_terms[1].astype(jnp.bfloat16), "narrow", scatter_dimension=0, tiled=True
        ).astype(jnp.float32),
        lax.psum_scatter(
            layer_terms[2].astype(jnp.bfloat16), "narrow", scatter_dimension=0, tiled=True
        ).astype(jnp.float32),
        lax.psum_scatter(
            layer_terms[3].astype(jnp.bfloat16), "narrow", scatter_dimension=1, tiled=True
        ).astype(jnp.float32),
        lax.psum_scatter(
            layer_terms[4].astype(jnp.bfloat16), "narrow", scatter_dimension=0, tiled=True
        ).astype(jnp.float32),
        lax.psum_scatter(
            layer_terms[5].astype(jnp.bfloat16), "narrow", scatter_dimension=0, tiled=True
        ).astype(jnp.float32),
    )
    totals = (
        lax.psum(shares[0].astype(jnp.bfloat16), "wide").astype(jnp.float32),
        lax.psum(shares[1].astype(jnp.bfloat16), "wide").astype(jnp.float32),
        lax.psum(shares[2].astype(jnp.bfloat16), "wide").astype(jnp.float32),
        lax.psum(shares[3].astype(jnp.bfloat16), "wide").astype(jnp.float32),
        lax.psum(shares[4].astype(jnp.bfloat16), "wide").astype(jnp.float32),
        lax.psum(shares[5].astype(jnp.bfloat16), "wide").astype(jnp.float32),
    )
    gate_total, up_total, down_total = (
        lax.psum(gate_part.astype(jnp.bfloat16), "narrow").astype(jnp.float32),
        lax.psum(up_part.astype(jnp.bfloat16), "narrow").astype(jnp.float32),
        lax.psum(down_part.astype(jnp.bfloat16), "narrow").astype(jnp.float32),
    )
    return (
        block_output,
        input_grad,
        totals[0],
        totals[1],
        totals[2],
        totals[3],
        totals[4],
        totals[5],
        gate_total,
        up_total,
        down_total,
    )


def solution(mesh):
    placed = (
        P(("narrow", "wide"), None),
        P(("narrow", "wide"), None),
        P("narrow", None),
        P("narrow", None),
        P("narrow", None),
        P(None, "narrow"),
        P("narrow"),
        P("narrow"),
        P(None, "wide"),
        P(None, "wide"),
        P("wide", None),
        P(("narrow", "wide"), None),
        P(),
    )
    return jax.shard_map(
        per_device,
        mesh=mesh,
        in_specs=placed,
        out_specs=(
            P(("narrow", "wide"), None),
            P(("narrow", "wide"), None),
            P("narrow", None),
            P("narrow", None),
            P("narrow", None),
            P(None, "narrow"),
            P("narrow"),
            P("narrow"),
            P(None, "wide"),
            P(None, "wide"),
            P("wide", None),
        ),
        check_vma=False,
    )
```

profile of v0, /device:TPU:0, one launch (start us, length us, event | category | flops | bytes accessed | tf_op | source)
XLA Modules:
  0.0 1093.1 jit_solution(2750439035582643579)
XLA Ops:
  10.7 10.4 all-gather
  21.8 8.9 all-gather.1
  30.7 0.8 reduce-window.8
  31.6 1.5 fusion.19
  33.2 5.0 all-gather.9.cloned.1.call-done
  38.2 2.2 convolution_convert_fusion.11
  40.5 25.2 %all-gather.11.cloned.1.call-done = bf16[2048,384]{1,0:T(8,128)(2,1)} async-done(((bf16[256,384]{1,0:T(8,128)(2,1)}), bf16[2048,384]{1,0:T(8,128)(2,1)}) %all-gather.11.cloned.1.call-update) | async-done | bytes 1572880 | tf_op jit(solution)/shard_map/all_gather | solution.py:49
  65.7 2.2 convolution_convert_fusion.10
  68.0 45.0 %all-gather.13.cloned.1.call-done = bf16[2048,1536]{1,0:T(8,128)(2,1)} async-done(((bf16[256,1536]{1,0:T(8,128)(2,1)}), bf16[2048,1536]{1,0:T(8,128)(2,1)}) %all-gather.13.cloned.1.call-update) | async-done | bytes 6291472 | tf_op jit(solution)/shard_map/all_gather | solution.py:48
  113.0 4.6 convolution_convert_fusion.9
  117.9 1.1 fusion.5
  119.0 1.3 fusion.6
  120.4 1.3 copy-done
  121.7 2.7 fusion.21
  124.4 36.9 %all-gather.15.cloned.1.call-done = bf16[1536,2048]{1,0:T(8,128)(2,1)} async-done(((bf16[1536,256]{1,0:T(8,128)(2,1)}), bf16[1536,2048]{1,0:T(8,128)(2,1)}) %all-gather.15.cloned.1.call-update) | async-done | bytes 6291472 | tf_op jit(solution)/shard_map/all_gather | solution.py:51
  161.3 5.0 multiply_reduce_fusion.2
  166.3 1.2 multiply_convert_fusion.3
  169.9 78.5 %all-gather.17.cloned.1.call-done = bf16[1024,2048]{1,0:T(8,128)(2,1)} async-done(((bf16[256,2048]{1,0:T(8,128)(2,1)}), bf16[1024,2048]{1,0:T(8,128)(2,1)}) %all-gather.17.cloned.1.call-update) | async-done | bytes 4194320 | tf_op jit(solution)/shard_map/all_gather | solution.py:99
  248.4 10.3 fusion.51
  258.7 9.5 fusion.52
  268.3 60.9 %all-gather.19.cloned.1.call-done = bf16[1024,2048]{1,0:T(8,128)(2,1)} async-done(((bf16[256,2048]{1,0:T(8,128)(2,1)}), bf16[1024,2048]{1,0:T(8,128)(2,1)}) %all-gather.19.cloned.1.call-update) | async-done | bytes 4194320 | tf_op jit(solution)/shard_map/all_gather | solution.py:115
  329.1 13.9 %multiply_convert_fusion = (bf16[1024,1152]{1,0:T(8,128)(2,1)S(1)}, bf16[1024,1152]{1,0:T(8,128)(2,1)S(1)}, bf16[1024,1152]{1,0:T(8,128)(2,1)}) fusion(f32[1024,1152]{1,0:T(8,128)} %fusion.51, f32[1152]{0:T(1024)S(1)} %fusion.37, f32[1024,1152]{1,0:T(8,128)} %fusion.52, bf16[1024,2048]{1,0:T(8,128)(2,1)} %all-gather.19.cloned.1.call-done, ...), kind=kOutput, calls=%fused_computation.18 | convolution fusion | flops 4854251520 | bytes 25432576 | tf_op jit(solution)/shard_map/dot_general | solution.py:27
  343.0 9.2 fusion.53
  352.2 10.2 convolution_add_fusion
  362.7 9.5 convolution_convert_fusion.5
  372.2 9.7 convolution_convert_fusion.2
  382.0 7.3 convolution_convert_fusion.1
  389.4 6.8 convolution_convert_fusion
  396.5 109.2 %reduce-scatter.9.cloned.1.call-done = f32[256,2048]{1,0:T(8,128)} async-done(((f32[1024,2048]{1,0:T(8,128)}), f32[256,2048]{1,0:T(8,128)}) %reduce-scatter.9.cloned.1.call-update) | async-done | bytes 2097168 | tf_op jit(solution)/shard_map/reduce_scatter | solution.py:130
  505.7 2.7 multiply_reduce_fusion
  508.4 77.0 %reduce-scatter.7.cloned.1.call-done = bf16[256,2048]{1,0:T(8,128)(2,1)} async-done(((bf16[1024,2048]{1,0:T(8,128)(2,1)}), bf16[256,2048]{1,0:T(8,128)(2,1)}) %reduce-scatter.7.cloned.1.call-update) | async-done | bytes 1048592 | tf_op jit(solution)/shard_map/reduce_scatter | solution.py:110
  585.4 3.8 fusion.16
  589.2 1.3 copy-done.3
  590.5 4.7 convolution_convert_fusion.8
  595.6 6.4 fusion
  601.9 2.7 fusion.2
  604.7 1.7 copy-done.2
  606.4 1.1 fusion.26
  608.1 2.0 convolution_convert_fusion.7
  610.2 4.2 fusion.27
  614.4 2.0 convolution_convert_fusion.6
  616.7 2.6 multiply_convert_fusion.4
  619.3 0.9 copy-done.8
  620.2 4.6 convolution_convert_fusion.4
  624.8 1.8 copy-done.4
  626.6 5.5 convolution_convert_fusion.3
  634.0 145.7 %all-reduce.9.cloned.1.call-done = (bf16[2048,1152]{1,0:T(8,128)(2,1)}, bf16[2048,1152]{1,0:T(8,128)(2,1)}, bf16[1152,2048]{1,0:T(8,128)(2,1)}) async-done(((bf16[2048,1152]{1,0:T(8,128)(2,1)}, bf16[2048,1152]{1,0:T(8,128)(2,1)}, bf16[1152,2048]{1,0:T(8,128)(2,1)}), (bf16[2048,1152]{1,0:T(8,128)(2,1)}, bf16[2048,1152]{1,0:T(8,128)(2,1)}, bf16[1152,2048]{1,0:T(8,128)(2,1)})) %all-reduce.9.cloned.1.call-update) | async-done | bytes 14155792 | tf_op jit(solution)/shard_map/psum | solution.py:226
  779.7 7.3 convert_element_type.208
  787.1 4.3 convert_element_type.210
  791.4 4.9 convert_element_type.212
  796.4 25.6 %reduce-scatter.13.cloned.1.call-done = bf16[256,384]{1,0:T(8,128)(2,1)} async-done(((bf16[2048,384]{1,0:T(8,128)(2,1)}), bf16[256,384]{1,0:T(8,128)(2,1)}) %reduce-scatter.13.cloned.1.call-update) | async-done | bytes 196624 | tf_op jit(solution)/shard_map/reduce_scatter | solution.py:201
  821.9 42.3 %reduce-scatter.15.cloned.1.call-done = bf16[256,384]{1,0:T(8,128)(2,1)} async-done(((bf16[2048,384]{1,0:T(8,128)(2,1)}), bf16[256,384]{1,0:T(8,128)(2,1)}) %reduce-scatter.15.cloned.1.call-update) | async-done | bytes 196624 | tf_op jit(solution)/shard_map/reduce_scatter | solution.py:204
  864.2 65.0 %reduce-scatter.11.cloned.1.call-done = bf16[256,1536]{1,0:T(8,128)(2,1)} async-done(((bf16[2048,1536]{1,0:T(8,128)(2,1)}), bf16[256,1536]{1,0:T(8,128)(2,1)}) %reduce-scatter.11.cloned.1.call-update) | async-done | bytes 786448 | tf_op jit(solution)/shard_map/reduce_scatter | solution.py:198
  929.2 65.0 %reduce-scatter.17.cloned.1.call-done = bf16[1536,256]{1,0:T(8,128)(2,1)} async-done(((bf16[1536,2048]{1,0:T(8,128)(2,1)}), bf16[1536,256]{1,0:T(8,128)(2,1)}) %reduce-scatter.17.cloned.1.call-update) | async-done | bytes 786448 | tf_op jit(solution)/shard_map/reduce_scatter | solution.py:207
  994.3 5.0 fusion.54
  1000.7 2.4 fusion.15
  1003.1 13.6 %all-reduce.2 = (bf16[2048]{0:T(1024)(128)(2,1)S(1)}, bf16[2048]{0:T(1024)(128)(2,1)S(1)}) all-reduce(bf16[2048]{0:T(1024)(128)(2,1)S(1)} %get-tuple-element.13, bf16[2048]{0:T(1024)(128)(2,1)S(1)} %copy-done.22), channel_id=8, replica_groups=mesh['narrow'=8,'wide'=4] {'narrow'}, use_global_device_ids=true, to_apply=%region_21.22.clone | all-reduce | flops 4096 | bytes 16384
  1016.9 12.3 %all-reduce.4 = (bf16[256]{0:T(256)(128)(2,1)S(1)}, bf16[256]{0:T(256)(128)(2,1)S(1)}) all-reduce(bf16[256]{0:T(256)(128)(2,1)S(1)} %dynamic-slice.1, bf16[256]{0:T(256)(128)(2,1)S(1)} %dynamic-slice.3), channel_id=1, replica_groups=mesh['narrow'=8,'wide'=4] {'wide'}, use_global_device_ids=true, to_apply=%region_22.23 | all-reduce | flops 512 | bytes 2048 | tf_op jit(solution)/shard_map/psum | solution.py:222
  1030.3 3.2 fusion.18
  1033.5 45.4 %all-reduce.11.cloned.1.call-done = (bf16[256,1536]{1,0:T(8,128)(2,1)}, bf16[256,384]{1,0:T(8,128)(2,1)}, bf16[256,384]{1,0:T(8,128)(2,1)}, bf16[1536,256]{1,0:T(8,128)(2,1)}) async-done(((bf16[256,1536]{1,0:T(8,128)(2,1)}, bf16[256,384]{1,0:T(8,128)(2,1)}, bf16[256,384]{1,0:T(8,128)(2,1)}, bf16[1536,256]{1,0:T(8,128)(2,1)}), (bf16[256,1536]{1,0:T(8,128)(2,1)}, bf16[256,384]{1,0:T(8,128)(2,1)}, ...) | async-done | bytes 1966096 | tf_op jit(solution)/shard_map/psum | solution.py:218
  1079.0 2.5 convert_element_type.196
  1081.5 1.7 convert_element_type.198
  1083.2 1.7 convert_element_type.200
  1084.9 1.3 convert_element_type.202
  (124 shorter events, 13.2 us)
Async XLA Ops:
  7.2 31.0 %copy-start.1 = (bf16[256,2048]{1,0:T(8,128)(2,1)S(1)}, bf16[256,2048]{1,0:T(8,128)(2,1)}, u32[]{:S(2)}) copy-start(bf16[256,2048]{1,0:T(8,128)(2,1)} %param.13) | copy-start | bytes 3145732
  7.2 31.0 %all-gather.9.cloned.1.call-start = ((), (), s32[]{:S(2)}) async-start(), calls=%async_computation.6 | async-start | bytes 1769472 | tf_op jit(solution)/shard_map/all_gather | solution.py:50
  7.9 57.8 %all-gather.11.cloned.1.call-start = ((), (), s32[]{:S(2)}) async-start(), calls=%async_computation.7 | async-start | bytes 1769472 | tf_op jit(solution)/shard_map/all_gather | solution.py:49
  8.7 104.3 %all-gather.13.cloned.1.call-start = ((), (), s32[]{:S(2)}) async-start(), calls=%async_computation.8 | async-start | bytes 7077888 | tf_op jit(solution)/shard_map/all_gather | solution.py:48
  9.4 151.9 %all-gather.15.cloned.1.call-start = ((), (), s32[]{:S(2)}) async-start(), calls=%async_computation.9 | async-start | bytes 7077888 | tf_op jit(solution)/shard_map/all_gather | solution.py:51
  10.0 238.5 %all-gather.17.cloned.1.call-start = ((), (), s32[]{:S(2)}) async-start(), calls=%async_computation.10 | async-start | bytes 5242880 | tf_op jit(solution)/shard_map/all_gather | solution.py:99
  33.1 34.8 %copy-start.23 = (f32[256]{0:T(256)}, f32[256]{0:T(256)S(1)}, u32[]{:S(2)}) copy-start(f32[256]{0:T(256)S(1)} %fusion.19) | copy-start | bytes 3076
  40.5 79.8 %copy-start.16 = (bf16[256,384]{0,1:T(8,128)(2,1)}, bf16[256,384]{0,1:T(8,128)(2,1)S(1)}, u32[]{:S(2)}) copy-start(bf16[256,384]{0,1:T(8,128)(2,1)S(1)} %copy.52) | copy-start | bytes 589828
  117.9 1.1 copy-start.5
  119.0 2.7 copy-start
  166.3 2.4 copy-start.28
  167.6 161.6 %all-gather.19.cloned.1.call-start = ((), (), s32[]{:S(2)}) async-start(), calls=%async_computation.12 | async-start | bytes 5242880 | tf_op jit(solution)/shard_map/all_gather | solution.py:115
  168.1 337.6 %reduce-scatter.9.cloned.1.call-start = ((), (), s32[]{:S(2)}) async-start(), calls=%async_computation.13 | async-start | bytes 10485760 | tf_op jit(solution)/shard_map/reduce_scatter | solution.py:130
  248.4 10.3 copy-start.25
  343.0 9.2 copy-start.33
  343.0 9.2 copy-start.31
  362.4 223.0 %reduce-scatter.7.cloned.1.call-start = ((), (), s32[]{:S(2)}) async-start(), calls=%async_computation.11 | async-start | bytes 5242880 | tf_op jit(solution)/shard_map/reduce_scatter | solution.py:110
  372.2 407.5 %all-reduce.9.cloned.1.call-start = ((), (), s32[]{:S(2)}) async-start(), calls=%async_computation.18 | async-start | bytes 28311552 | tf_op jit(solution)/shard_map/psum | solution.py:226
  372.2 9.8 copy-start.26
  372.2 9.8 copy-start.32
  382.0 7.4 copy-start.27
  382.0 7.4 copy-start.30
  396.2 425.7 %reduce-scatter.13.cloned.1.call-start = ((), (), s32[]{:S(2)}) async-start(), calls=%async_computation.15 | async-start | bytes 1769472 | tf_op jit(solution)/shard_map/reduce_scatter | solution.py:201
  396.5 199.1 %copy-start.18 = (f32[3,8,256]{2,1,0:T(8,128)}, f32[3,8,256]{2,1,0:T(8,128)S(1)}, u32[]{:S(2)}) copy-start(f32[3,8,256]{2,1,0:T(8,128)S(1)} %log_add_fusion) | copy-start | bytes 73732
  589.2 1.3 copy-start.3
  590.5 5.0 copy-start.17
  595.5 6.4 copy-start.9
  595.5 6.4 slice-start
  595.5 6.4 slice-start.1
  601.9 4.4 copy-start.6
  604.7 1.7 copy-start.2
  607.4 0.7 copy-start.13
  607.4 2.7 copy-start.10
  607.5 2.7 copy-start.19
  610.1 254.1 %reduce-scatter.15.cloned.1.call-start = ((), (), s32[]{:S(2)}) async-start(), calls=%async_computation.16 | async-start | bytes 1769472 | tf_op jit(solution)/shard_map/reduce_scatter | solution.py:204
  614.4 4.9 copy-start.20
  616.4 312.8 %reduce-scatter.11.cloned.1.call-start = ((), (), s32[]{:S(2)}) async-start(), calls=%async_computation.14 | async-start | bytes 7077888 | tf_op jit(solution)/shard_map/reduce_scatter | solution.py:198
  619.3 0.9 copy-start.8
  624.8 1.8 copy-start.4
  624.8 369.4 %reduce-scatter.17.cloned.1.call-start = ((), (), s32[]{:S(2)}) async-start(), calls=%async_computation.17 | async-start | bytes 7077888 | tf_op jit(solution)/shard_map/reduce_scatter | solution.py:207
  632.1 0.7 copy-start.29
  632.2 446.8 %all-reduce.11.cloned.1.call-start = ((), (), s32[]{:S(2)}) async-start(), calls=%async_computation.19 | async-start | bytes 3932160 | tf_op jit(solution)/shard_map/psum | solution.py:218
  779.7 7.3 copy-start.7
  779.7 11.7 %slice-start.2 = ((s8[4718592]{0:T(1024)(128)(4,1)}), s8[4194304]{0:T(1024)(128)(4,1)S(1)}, s32[]{:S(2)}) async-start(s8[4718592]{0:T(1024)(128)(4,1)} %bitcast.132), calls=%async_computation.22 | async-start | bytes 8388608
  787.1 4.4 slice-start.3
  994.2 5.0 copy-start.12
  994.2 5.0 copy-start.14
  999.3 1.4 copy-start.11
  999.3 1.4 copy-start.21
  1000.7 2.5 copy-start.22
  1000.7 29.6 %copy-start.24 = (f32[256]{0:T(256)S(1)}, f32[256]{0:T(256)}, u32[]{:S(2)}) copy-start(f32[256]{0:T(256)} %copy-done.23) | copy-start | bytes 3076
  1079.0 5.9 copy-start.15
Sparse Core Ops, SparseCore 0:
  9.9 28.2 all-gather.8
  40.1 25.5 all-gather.10
  67.6 45.3 all-gather.12
  114.7 46.5 all-gather.14
  167.7 80.7 all-gather.16
  249.9 79.2 all-gather.18
  362.6 143.0 reduce-scatter.8
  508.0 77.3 reduce-scatter.6
  590.0 189.6 all-reduce.8
  783.4 38.4 reduce-scatter.12
  825.8 38.3 reduce-scatter.14
  867.4 61.7 reduce-scatter.10
  932.6 61.5 reduce-scatter.16
  996.7 82.2 all-reduce.10
where the time goes:
time: 1100 us; the launch traced here: 1090 us
  waiting for transfers between devices  830 us (75%)
  matrix products  145 us (13%)
  blocking collectives  45.2 us (4%)
  other arithmetic  43.8 us (4%)
  between operations  15.5 us (1%)
  local copies, waits for them, and re-layouts  11.9 us (1%)
    psum x1, waiting for transfers between devices, per_device(): lax.psum(gate_part.astype(jnp.bfloat16), 'narrow').astype(jnp.float32)  146 us
    reduce_scatter x1, waiting for transfers between devices, per_device(): lax.psum_scatter(mixed_terms, 'wide', scatter_dimension=0, tiled=True)  109 us
    all_gather x1, waiting for transfers between devices, per_device(): gathered = lax.all_gather(mixed_in, 'wide', axis=0, tiled=True)  78.5 us
    reduce_scatter x1, waiting for transfers between devices, per_device(): lax.psum_scatter(partial_rows.astype(jnp.bfloat16), 'wide', scatter_dimen...  77 us
    reduce_scatter x1, waiting for transfers between devices, per_device(): lax.psum_scatter(layer_terms[0].astype(jnp.bfloat16), 'narrow', scatter_d...  65 us
    reduce_scatter x1, waiting for transfers between devices, per_device(): lax.psum_scatter(layer_terms[3].astype(jnp.bfloat16), 'narrow', scatter_d...  65 us
    all_gather x1, waiting for transfers between devices, per_device(): grad_rows = lax.all_gather(cotangent, 'wide', axis=0, tiled=True)  60.9 us
    dot_general x7, matrix products, contract_cols(): lax.dot_general(left, right, (((1,), (1,)), ((), ())), preferred_element_...  46.1 us
  transfers between devices with their start and end apart: 14, of which 14 were waited for; matrix products, arithmetic and copies ran while one was open for 13% of the time, Pallas kernels for 0%

commit v1 on v0

v1 whole, which is shorter than its diff:
```python
import functools

import jax
import jax.numpy as jnp
from jax import lax
from jax.experimental import pallas as pl
from jax.experimental.pallas import tpu as pltpu
from jax.sharding import PartitionSpec as P

HEADS = 24
KV_HEADS = 6
HEAD_DIM = 64
TILE = 128


EPSILON = 1e-06

BF = jnp.bfloat16
F32 = jnp.float32


def rms_scale(rows, gain):
    factor = lax.rsqrt(jnp.mean(rows * rows, axis=-1, keepdims=True) + EPSILON)
    return rows * factor * gain


def contract_rows(left, right):
    return lax.dot_general(
        left, right, (((0,), (0,)), ((), ())), preferred_element_type=jnp.float32
    )


def contract_cols(left, right):
    return lax.dot_general(
        left, right, (((1,), (1,)), ((), ())), preferred_element_type=jnp.float32
    )


def flip(n, bit):
    return n + bit - 2 * bit * lax.rem(n // bit, 2)


def at(n, w):
    return {"narrow": n, "wide": w}


def send(src, dst, ssem, rsem, n, w):
    return pltpu.make_async_remote_copy(
        src_ref=src,
        dst_ref=dst,
        send_sem=ssem,
        recv_sem=rsem,
        device_id=at(n, w),
        device_id_type=pl.DeviceIdType.MESH,
    )


def greet(narrow_peers, n, w, line):
    barrier = pltpu.get_barrier_semaphore()
    for peer in narrow_peers:
        pl.semaphore_signal(
            barrier, inc=1, device_id=at(peer, w), device_id_type=pl.DeviceIdType.MESH
        )
    if not line:
        pl.semaphore_wait(barrier, len(narrow_peers))
    if line:
        pl.semaphore_signal(
            barrier, inc=1, device_id=at(n, flip(w, 2)), device_id_type=pl.DeviceIdType.MESH
        )

        @pl.when(w > 0)
        def _():
            pl.semaphore_signal(
                barrier, inc=1, device_id=at(n, w - 1), device_id_type=pl.DeviceIdType.MESH
            )

        @pl.when(w < 3)
        def _():
            pl.semaphore_signal(
                barrier, inc=1, device_id=at(n, w + 1), device_id_type=pl.DeviceIdType.MESH
            )

        @pl.when((w == 0) | (w == 3))
        def _():
            pl.semaphore_wait(barrier, len(narrow_peers) + 2)

        @pl.when((w == 1) | (w == 2))
        def _():
            pl.semaphore_wait(barrier, len(narrow_peers) + 3)


class LineGather:
    KINDS = 4

    def __init__(self, n, w, own, whole, ssem, rsem, chunks):
        self.n, self.w, self.own, self.whole = n, w, own, whole
        self.ssem, self.rsem, self.chunks = ssem, rsem, chunks
        self.rows = own.shape[0] // chunks

    def part(self, shard, i):
        return self.whole.at[shard, pl.ds(i * self.rows, self.rows), :]

    def mine(self, i):
        return self.own.at[pl.ds(i * self.rows, self.rows), :]

    def copy(self, kind, i, src, shard, w):
        k = kind * self.chunks + i
        return send(src, self.part(shard, i), self.ssem.at[k], self.rsem.at[k], self.n, w)

    def far(self, i):
        return self.copy(0, i, self.mine(i), self.w, flip(self.w, 2))

    def left(self, i):
        return self.copy(1, i, self.mine(i), self.w, jnp.maximum(self.w - 1, 0))

    def right(self, i):
        return self.copy(2, i, self.mine(i), self.w, jnp.minimum(self.w + 1, 3))

    def onward(self, i):
        shard = flip(self.w, 2)
        return self.copy(3, i, self.part(shard, i), shard, 3 * (self.w // 2))

    def middle(self):
        return (self.w == 1) | (self.w == 2)

    def start(self):
        for i in range(self.chunks):
            self.far(i).start()

        @pl.when(self.w > 0)
        def _():
            for i in range(self.chunks):
                self.left(i).start()

        @pl.when(self.w < 3)
        def _():
            for i in range(self.chunks):
                self.right(i).start()

    def forward(self, i):
        self.far(i).wait_recv()

        @pl.when(self.middle())
        def _():
            self.onward(i).start()

    def finish(self):
        for i in range(self.chunks):
            self.far(i).wait_send()

        @pl.when(self.w > 0)
        def _():
            for i in range(self.chunks):
                self.left(i).wait_send()
                self.right(i).wait_recv()

        @pl.when(self.w < 3)
        def _():
            for i in range(self.chunks):
                self.right(i).wait_send()
                self.left(i).wait_recv()

        @pl.when(self.middle())
        def _():
            for i in range(self.chunks):
                self.onward(i).wait_send()

        @pl.when((self.w == 0) | (self.w == 3))
        def _():
            for i in range(self.chunks):
                self.onward(i).wait_recv()


def first_kernel(
    q_ref,
    k_ref,
    v_ref,
    p_ref,
    g_ref,
    c_ref,
    qkv_full,
    p_full,
    g_full,
    c_full,
    q_buf,
    k_buf,
    v_buf,
    p_buf,
    g_buf,
    c_buf,
    in_sem,
    out_sem,
    ssem,
    rsem,
    gs_sem,
    gr_sem,
    zs_sem,
    zr_sem,
):
    n, w = lax.axis_index("narrow"), lax.axis_index("wide")
    x, y, c, d = flip(n, 2), flip(n, 4), flip(n, 1), flip(flip(n, 2), 4)
    others = [lax.rem(n + i, 8) for i in range(1, 8)]
    rows = q_ref.shape[0]
    half = rows // 2
    depth = p_ref.shape[0]
    qc, kc = q_ref.shape[1], k_ref.shape[1]
    cols = ((0, qc), (qc, kc), (qc + kc, kc))

    locals_in = []
    for i, (src, dst) in enumerate(
        ((q_ref, q_buf), (k_ref, k_buf), (v_ref, v_buf), (p_ref, p_buf), (g_ref, g_buf), (c_ref, c_buf))
    ):
        cp = pltpu.make_async_copy(src, dst, in_sem.at[i])
        cp.start()
        locals_in.append(cp)

    greet(others, n, w, True)

    def region(t, block, h):
        if t == 3:
            r = pl.ds(0, depth) if h == 2 else pl.ds(h * (depth // 2), depth // 2)
            return p_full.at[r, pl.ds(pl.multiple_of(block * rows, rows), rows)]
        r = pl.ds(block * rows, rows) if h == 2 else pl.ds(block * rows + h * half, half)
        return qkv_full.at[r, pl.ds(cols[t][0], cols[t][1])]

    def own(t, h):
        ref = (q_ref, k_ref, v_ref, p_ref)[t]
        if h == 2:
            return ref
        size = ref.shape[0] // 2
        return ref.at[pl.ds(h * size, size), :]

    def msg(t, kind, src, block, h, peer):
        k = t * 10 + kind
        return send(src, region(t, block, h), ssem.at[k], rsem.at[k], peer, w)

    def to_x(t, h):
        return msg(t, h, own(t, h), n, h, x)

    def to_y(t, h):
        return msg(t, 2 + h, own(t, h), n, h, y)

    def on_x(t):
        return msg(t, 4, region(t, y, 0), y, 0, x)

    def on_y(t):
        return msg(t, 5, region(t, x, 1), x, 1, y)

    def to_c(t, which):
        block = (n, x, y, d)[which]
        src = own(t, 2) if which == 0 else region(t, block, 2)
        return msg(t, 6 + which, src, block, 2, c)

    line = LineGather(n, w, c_ref, c_full, zs_sem, zr_sem, 4)
    for t in range(4):
        to_x(t, 1).start()
        to_y(t, 0).start()
        to_x(t, 0).start()
        to_y(t, 1).start()
        if t == 0:
            line.start()
    for t in range(4):
        to_c(t, 0).start()
    for i, peer in enumerate(others):
        send(g_ref, g_full.at[n], gs_sem.at[i], gr_sem.at[i], peer, w).start()

    outs = (
        (q_buf, region(0, n, 2)),
        (k_buf, region(1, n, 2)),
        (v_buf, region(2, n, 2)),
        (p_buf, region(3, n, 2)),
        (g_buf, g_full.at[n]),
        (c_buf, c_full.at[w]),
    )
    locals_out = []
    for i, (src, dst) in enumerate(outs):
        locals_in[i].wait()
        cp = pltpu.make_async_copy(src, dst, out_sem.at[i])
        cp.start()
        locals_out.append(cp)

    def relay(t):
        to_y(t, 0).wait_recv()
        on_x(t).start()
        to_x(t, 1).wait_recv()
        on_y(t).start()
        to_x(t, 0).wait_recv()
        to_c(t, 1).start()
        to_y(t, 1).wait_recv()
        to_c(t, 2).start()

    def corner(t):
        on_x(t).wait_recv()
        on_y(t).wait_recv()
        to_c(t, 3).start()

    line.forward(0)
    relay(0)
    line.forward(1)
    relay(1)
    relay(2)
    line.forward(2)
    relay(3)
    line.forward(3)
    for t in range(4):
        corner(t)
    for t in range(4):
        for h in range(2):
            to_x(t, h).wait_send()
            to_y(t, h).wait_send()
        on_x(t).wait_send()
        on_y(t).wait_send()
        for which in range(4):
            to_c(t, which).wait()
    for i, peer in enumerate(others):
        send(g_ref, g_full.at[n], gs_sem.at[i], gr_sem.at[i], peer, w).wait()
    line.finish()
    for cp in locals_out:
        cp.wait()


def gather_first(query, key, value, project, gains, cotangent):
    rows = query.shape[0]
    width = query.shape[1] + 2 * key.shape[1]
    spec = pl.BlockSpec(memory_space=pl.ANY)
    return pl.pallas_call(
        first_kernel,
        name="gather_first",
        out_shape=(
            jax.ShapeDtypeStruct((8 * rows, width), BF),
            jax.ShapeDtypeStruct((project.shape[0], 8 * rows), BF),
            jax.ShapeDtypeStruct((8,) + gains.shape, gains.dtype),
            jax.ShapeDtypeStruct((4,) + cotangent.shape, BF),
        ),
        in_specs=[spec] * 6,
        out_specs=[spec] * 4,
        scratch_shapes=[
            pltpu.VMEM(query.shape, BF),
            pltpu.VMEM(key.shape, BF),
            pltpu.VMEM(value.shape, BF),
            pltpu.VMEM(project.shape, BF),
            pltpu.VMEM(gains.shape, gains.dtype),
            pltpu.VMEM(cotangent.shape, BF),
            pltpu.SemaphoreType.DMA((6,)),
            pltpu.SemaphoreType.DMA((6,)),
            pltpu.SemaphoreType.DMA((40,)),
            pltpu.SemaphoreType.DMA((40,)),
            pltpu.SemaphoreType.DMA((7,)),
            pltpu.SemaphoreType.DMA((7,)),
            pltpu.SemaphoreType.DMA((16,)),
            pltpu.SemaphoreType.DMA((16,)),
        ],
        compiler_params=pltpu.CompilerParams(collective_id=1, has_side_effects=True),
    )(query, key, value, project, gains, cotangent)


def line_gather_kernel(x_ref, whole, buf, in_sem, out_sem, ssem, rsem):
    n, w = lax.axis_index("narrow"), lax.axis_index("wide")
    cp = pltpu.make_async_copy(x_ref, buf, in_sem)
    cp.start()
    greet([], n, w, True)
    line = LineGather(n, w, x_ref, whole, ssem, rsem, 4)
    line.start()
    cp.wait()
    cp = pltpu.make_async_copy(buf, whole.at[w], out_sem)
    cp.start()
    for i in range(4):
        line.forward(i)
    line.finish()
    cp.wait()


def line_gather(rows):
    spec = pl.BlockSpec(memory_space=pl.ANY)
    return pl.pallas_call(
        line_gather_kernel,
        name="line_gather",
        out_shape=jax.ShapeDtypeStruct((4,) + rows.shape, BF),
        in_specs=[spec],
        out_specs=spec,
        scratch_shapes=[
            pltpu.VMEM(rows.shape, BF),
            pltpu.SemaphoreType.DMA,
            pltpu.SemaphoreType.DMA,
            pltpu.SemaphoreType.DMA((16,)),
            pltpu.SemaphoreType.DMA((16,)),
        ],
        compiler_params=pltpu.CompilerParams(collective_id=2, has_side_effects=True),
    )(rows)


class LineScatter:
    def __init__(self, n, w, terms, bufs, ssem, rsem, chunks):
        self.n, self.w, self.terms = n, w, terms
        self.from_left, self.from_right, self.from_far, self.relayed, self.total = bufs
        self.ssem, self.rsem, self.chunks = ssem, rsem, chunks
        self.rows = terms.shape[1] // chunks

    def cut(self, ref, i):
        return ref.at[pl.ds(i * self.rows, self.rows), :]

    def term(self, d, i):
        return self.terms.at[d, pl.ds(i * self.rows, self.rows), :]

    def copy(self, kind, i, src, dst, w):
        k = kind * self.chunks + i
        return send(src, self.cut(dst, i), self.ssem.at[k], self.rsem.at[k], self.n, w)

    def relay(self, i):
        end = 3 - 3 * (self.w // 2)
        return self.copy(0, i, self.term(end, i), self.relayed, 1 + self.w // 3)

    def far(self, i):
        d = flip(self.w, 2)
        return self.copy(1, i, self.term(d, i), self.from_far, d)

    def far_sum(self, i):
        return self.copy(1, i, self.cut(self.total, i), self.from_far, flip(self.w, 2))

    def left(self, i):
        d = jnp.maximum(self.w - 1, 0)
        return self.copy(2, i, self.term(d, i), self.from_right, d)

    def right(self, i):
        d = jnp.minimum(self.w + 1, 3)
        return self.copy(3, i, self.term(d, i), self.from_left, d)

    def middle(self):
        return (self.w == 1) | (self.w == 2)

    def end(self):
        return (self.w == 0) | (self.w == 3)

    def start(self):
        @pl.when(self.end())
        def _():
            for i in range(self.chunks):
                self.relay(i).start()
            for i in range(self.chunks):
                self.far(i).start()

        @pl.when(self.w > 0)
        def _():
            for i in range(self.chunks):
                self.left(i).start()

        @pl.when(self.w < 3)
        def _():
            for i in range(self.chunks):
                self.right(i).start()

    def pass_on(self, i, mine):
        @pl.when(self.middle())
        def _():
            self.relay(i).wait_recv()
            rows = pl.ds(i * self.rows, self.rows)
            self.total[rows, :] = (
                mine[rows, :].astype(F32) + self.relayed[rows, :].astype(F32)
            ).astype(BF)
            self.far_sum(i).start()

    def finish(self, i, mine, out):
        rows = pl.ds(i * self.rows, self.rows)
        self.far(i).wait_recv()

        @pl.when(self.w > 0)
        def _():
            self.right(i).wait_recv()

        @pl.when(self.w < 3)
        def _():
            self.left(i).wait_recv()

        @pl.when(self.w == 0)
        def _():
            out[rows, :] = (
                mine[rows, :].astype(F32)
                + self.from_far[rows, :].astype(F32)
                + self.from_right[rows, :].astype(F32)
            ).astype(out.dtype)

        @pl.when(self.w == 3)
        def _():
            out[rows, :] = (
                mine[rows, :].astype(F32)
                + self.from_far[rows, :].astype(F32)
                + self.from_left[rows, :].astype(F32)
            ).astype(out.dtype)

        @pl.when(self.middle())
        def _():
            out[rows, :] = (
                mine[rows, :].astype(F32)
                + self.from_far[rows, :].astype(F32)
                + self.from_left[rows, :].astype(F32)
                + self.from_right[rows, :].astype(F32)
            ).astype(out.dtype)

    def drain(self):
        for i in range(self.chunks):
            self.far(i).wait_send()

        @pl.when(self.end())
        def _():
            for i in range(self.chunks):
                self.relay(i).wait_send()

        @pl.when(self.w > 0)
        def _():
            for i in range(self.chunks):
                self.left(i).wait_send()

        @pl.when(self.w < 3)
        def _():
            for i in range(self.chunks):
                self.right(i).wait_send()


def line_scatter_kernel(terms, out, mine, away, fl, fr, ff, rl, tot, in_sem, ssem, rsem):
    n, w = lax.axis_index("narrow"), lax.axis_index("wide")
    cps = [
        pltpu.make_async_copy(terms.at[w], mine, in_sem.at[0]),
        pltpu.make_async_copy(terms.at[flip(w, 2)], away, in_sem.at[1]),
    ]
    for cp in cps:
        cp.start()
    greet([], n, w, True)
    line = LineScatter(n, w, terms, (fl, fr, ff, rl, tot), ssem, rsem, 4)
    line.start()
    for cp in cps:
        cp.wait()
    for i in range(4):
        line.pass_on(i, away)
    for i in range(4):
        line.finish(i, mine, out)
    line.drain()


def line_scatter(terms):
    shape = terms.shape[1:]
    return pl.pallas_call(
        line_scatter_kernel,
        name="line_scatter",
        out_shape=jax.ShapeDtypeStruct(shape, F32),
        in_specs=[pl.BlockSpec(memory_space=pl.ANY)],
        out_specs=pl.BlockSpec(memory_space=pltpu.VMEM),
        scratch_shapes=[pltpu.VMEM(shape, BF)] * 7
        + [
            pltpu.SemaphoreType.DMA((2,)),
            pltpu.SemaphoreType.DMA((16,)),
            pltpu.SemaphoreType.DMA((16,)),
        ],
        compiler_params=pltpu.CompilerParams(collective_id=3, has_side_effects=True),
    )(terms)


def per_device(
    fast,
    block_input,
    cotangent,
    query_weight,
    key_weight,
    value_weight,
    project_weight,
    prenorm_gain,
    midnorm_gain,
    gate_weight,
    up_weight,
    down_weight,
    doc_lengths,
    tile_counts,
):
    tokens_here, model = block_input.shape
    if fast:
        gains = jnp.stack([prenorm_gain, midnorm_gain]).astype(F32).reshape(1, -1)
        qkv_full, project_full, gains_full, grad_rows = gather_first(
            query_weight, key_weight, value_weight, project_weight, gains, cotangent
        )
        grad_rows = grad_rows.reshape(-1, model)
        gains_full = gains_full.reshape(8, 2, -1)
        first_gain = gains_full[:, 0].reshape(-1)
        second_gain = gains_full[:, 1].reshape(-1)
    else:
        qkv_full = jnp.concatenate(
            [
                lax.all_gather(query_weight, "narrow", axis=0, tiled=True),
                lax.all_gather(key_weight, "narrow", axis=0, tiled=True),
                lax.all_gather(value_weight, "narrow", axis=0, tiled=True),
            ],
            axis=1,
        )
        project_full = lax.all_gather(project_weight, "narrow", axis=1, tiled=True)
        first_gain = lax.all_gather(prenorm_gain, "narrow", axis=0, tiled=True).astype(F32)
        second_gain = lax.all_gather(midnorm_gain, "narrow", axis=0, tiled=True).astype(F32)
        grad_rows = lax.all_gather(cotangent, "wide", axis=0, tiled=True)
    group = HEADS // KV_HEADS
    scale = HEAD_DIM ** (-0.5)
    q_cols, k_cols = HEADS * HEAD_DIM, KV_HEADS * HEAD_DIM
    inputs_f = block_input.astype(jnp.float32)
    normed = rms_scale(inputs_f, first_gain).astype(jnp.bfloat16)
    qkv = jnp.dot(normed, qkv_full, preferred_element_type=jnp.float32).astype(jnp.bfloat16)
    query_rows = qkv[:, :q_cols].reshape(tokens_here, KV_HEADS, group, HEAD_DIM)
    key_rows = qkv[:, q_cols : q_cols + k_cols].reshape(tokens_here, KV_HEADS, HEAD_DIM)
    value_rows = qkv[:, q_cols + k_cols :].reshape(tokens_here, KV_HEADS, HEAD_DIM)
    ends = jnp.cumsum(doc_lengths[0])
    position = jnp.arange(tokens_here, dtype=jnp.int32)
    segment = jnp.sum((position[:, None] >= ends[None, :]).astype(jnp.int32), axis=1)
    allowed = (segment[:, None] == segment[None, :]) & (position[None, :] <= position[:, None])
    scores = (
        jnp.einsum("qcgd,kcd->cgqk", query_rows, key_rows, preferred_element_type=jnp.float32)
        * scale
    )
    masked = jnp.where(allowed, scores, -1e30)
    peak = jnp.max(masked, axis=-1, keepdims=True)
    expo = jnp.exp(masked - peak)
    total = jnp.sum(expo, axis=-1, keepdims=True)
    probs_low = (expo / total).astype(jnp.bfloat16)
    logsum = peak + jnp.log(total)
    attended = (
        jnp.einsum("cgqk,kcd->qcgd", probs_low, value_rows, preferred_element_type=jnp.float32)
        .astype(jnp.bfloat16)
        .reshape(tokens_here, HEADS * HEAD_DIM)
    )
    branch = jnp.dot(attended, project_full, preferred_element_type=jnp.float32)
    middle = inputs_f + branch
    mixed_in = rms_scale(middle, second_gain).astype(jnp.bfloat16)
    if fast:
        gathered = line_gather(mixed_in).reshape(-1, model)
    else:
        gathered = lax.all_gather(mixed_in, "wide", axis=0, tiled=True)
    width = gate_weight.shape[1]
    wide_index = lax.axis_index("wide")
    my_count = jnp.sum(
        jnp.where(jnp.arange(tile_counts.shape[0], dtype=jnp.int32) == wide_index, tile_counts, 0)
    )
    live = (jnp.arange(width, dtype=jnp.int32) // TILE < my_count).astype(jnp.float32)
    gate_pre = jnp.dot(gathered, gate_weight, preferred_element_type=jnp.float32)
    up_pre = jnp.dot(gathered, up_weight, preferred_element_type=jnp.float32)
    hidden_back = contract_cols(grad_rows, down_weight)
    sigma = jax.nn.sigmoid(gate_pre)
    hidden = (gate_pre * sigma * up_pre * live).astype(jnp.bfloat16)
    gate_back = (hidden_back * up_pre * live * sigma * (1.0 + gate_pre * (1.0 - sigma))).astype(
        jnp.bfloat16
    )
    up_back = (hidden_back * gate_pre * sigma * live).astype(jnp.bfloat16)
    mixed_terms = (
        contract_cols(gate_back, gate_weight) + contract_cols(up_back, up_weight)
    ).astype(jnp.bfloat16)
    if fast:
        mixed_back = line_scatter(mixed_terms.reshape(4, tokens_here, model))
    else:
        mixed_back = lax.psum_scatter(
            mixed_terms, "wide", scatter_dimension=0, tiled=True
        ).astype(F32)
    partial_rows = jnp.dot(hidden, down_weight, preferred_element_type=jnp.float32)
    feed = lax.psum_scatter(
        partial_rows.astype(jnp.bfloat16), "wide", scatter_dimension=0, tiled=True
    ).astype(jnp.float32)
    block_output = (middle + feed).astype(jnp.bfloat16)
    out_grad = cotangent.astype(jnp.float32)
    down_part = contract_rows(hidden, grad_rows)
    gate_part = contract_rows(gathered, gate_back)
    up_part = contract_rows(gathered, up_back)
    unused_second, second_backward = jax.vjp(rms_scale, middle, second_gain)
    middle_norm_back, second_gain_part = second_backward(mixed_back)
    middle_back = out_grad + middle_norm_back
    branch_back = middle_back.astype(jnp.bfloat16)
    project_part = contract_rows(attended, branch_back)
    attended_back = (
        contract_cols(branch_back, project_full)
        .astype(jnp.bfloat16)
        .reshape(tokens_here, KV_HEADS, group, HEAD_DIM)
    )
    scores_again = (
        jnp.einsum("qcgd,kcd->cgqk", query_rows, key_rows, preferred_element_type=jnp.float32)
        * scale
    )
    probs_again = jnp.where(allowed, jnp.exp(scores_again - logsum), 0.0)
    probs_again_low = probs_again.astype(jnp.bfloat16)
    value_back = (
        jnp.einsum(
            "cgqk,qcgd->kcd", probs_again_low, attended_back, preferred_element_type=jnp.float32
        )
        .astype(jnp.bfloat16)
        .reshape(tokens_here, KV_HEADS * HEAD_DIM)
    )
    probs_back = jnp.einsum(
        "qcgd,kcd->cgqk", attended_back, value_rows, preferred_element_type=jnp.float32
    )
    scores_back = (
        probs_again * (probs_back - jnp.sum(probs_again * probs_back, axis=-1, keepdims=True))
    ).astype(jnp.bfloat16)
    query_back = (
        (
            jnp.einsum("cgqk,kcd->qcgd", scores_back, key_rows, preferred_element_type=jnp.float32)
            * scale
        )
        .astype(jnp.bfloat16)
        .reshape(tokens_here, HEADS * HEAD_DIM)
    )
    key_back = (
        (
            jnp.einsum(
                "cgqk,qcgd->kcd", scores_back, query_rows, preferred_element_type=jnp.float32
            )
            * scale
        )
        .astype(jnp.bfloat16)
        .reshape(tokens_here, KV_HEADS * HEAD_DIM)
    )
    qkv_back = jnp.concatenate([query_back, key_back, value_back], axis=1)
    qkv_part = contract_rows(normed, qkv_back)
    normed_back = contract_cols(qkv_back, qkv_full)
    unused_first, first_backward = jax.vjp(rms_scale, inputs_f, first_gain)
    input_norm_back, first_gain_part = first_backward(normed_back)
    input_grad = (middle_back + input_norm_back).astype(jnp.bfloat16)

    def owned(part, axis):
        share = lax.psum_scatter(
            part.astype(jnp.bfloat16), "narrow", scatter_dimension=axis, tiled=True
        )
        return lax.psum(share, "wide").astype(jnp.float32)

    qkv_total = owned(qkv_part, 0)
    project_total = owned(project_part, 1)
    first_total = owned(first_gain_part, 0)
    second_total = owned(second_gain_part, 0)
    gate_total, up_total, down_total = (
        lax.psum(gate_part.astype(jnp.bfloat16), "narrow").astype(jnp.float32),
        lax.psum(up_part.astype(jnp.bfloat16), "narrow").astype(jnp.float32),
        lax.psum(down_part.astype(jnp.bfloat16), "narrow").astype(jnp.float32),
    )
    return (
        block_output,
        input_grad,
        qkv_total[:, :q_cols],
        qkv_total[:, q_cols : q_cols + k_cols],
        qkv_total[:, q_cols + k_cols :],
        project_total,
        first_total,
        second_total,
        gate_total,
        up_total,
        down_total,
    )


def solution(mesh):
    fast = mesh.shape["narrow"] == 8 and mesh.shape["wide"] == 4
    placed = (
        P(("narrow", "wide"), None),
        P(("narrow", "wide"), None),
        P("narrow", None),
        P("narrow", None),
        P("narrow", None),
        P(None, "narrow"),
        P("narrow"),
        P("narrow"),
        P(None, "wide"),
        P(None, "wide"),
        P("wide", None),
        P(("narrow", "wide"), None),
        P(),
    )
    return jax.shard_map(
        functools.partial(per_device, fast),
        mesh=mesh,
        in_specs=placed,
        out_specs=(
            P(("narrow", "wide"), None),
            P(("narrow", "wide"), None),
            P("narrow", None),
            P("narrow", None),
            P("narrow", None),
            P(None, "narrow"),
            P("narrow"),
            P("narrow"),
            P(None, "wide"),
            P(None, "wide"),
            P("wide", None),
        ),
        check_vma=False,
    )
```

time: 1100 us -> 815 us (0.74)
  waiting for transfers between devices: 830 us -> 316 us
  Pallas kernels: 0 us -> 273 us
  matrix products: 145 us -> 121 us
  blocking collectives: 45.2 us -> 25.1 us
    pallas_call x0 -> x3, Pallas kernels: none -> 273 us  [the longest x1 126 us: line_scatter(): pl.pallas_call(line_scatter_kernel, name='line_scatter', out_shape=jax.Sh...]
    all_gather x6 -> x0, waiting for transfers between devices: 251 us -> none  [the longest x1 78.5 us: per_device(): gathered = lax.all_gather(mixed_in, 'wide', axis=0, tiled=True)]
    reduce_scatter x5 -> x2, waiting for transfers between devices: 307 us -> 90.8 us  [owned(): lax.psum_scatter(part.astype(jnp.bfloat16), 'narrow', scatter_dimension=a...]
    reduce_scatter x1, waiting for transfers between devices: 77 us -> 0.01 us  [per_device(): lax.psum_scatter(partial_rows.astype(jnp.bfloat16), 'wide', scatter_dimen...]
    psum x1, waiting for transfers between devices: 146 us -> 192 us  [per_device(): lax.psum(gate_part.astype(jnp.bfloat16), 'narrow').astype(jnp.float32)]
    all_gather x2 -> x0, blocking collectives: 19.3 us -> none  [the longest x1 10.4 us: per_device(): lax.all_gather(prenorm_gain, 'narrow', axis=0, tiled=True)]
    psum x1, waiting for transfers between devices: 45.4 us -> 32.7 us  [owned(): return lax.psum(share, 'wide').astype(jnp.float32)]
    dot_general x7 -> x5, matrix products: 46.1 us -> 39.2 us  [contract_cols(): lax.dot_general(left, right, (((1,), (1,)), ((), ())), preferred_element_...]
  transfers between devices with their start and end apart: 14 -> 5, of which waited for: 14 -> 4; matrix products, arithmetic and copies ran while one was open for 13% -> 12% of each run, Pallas kernels for 0% -> 16%
where the time goes in v1:
time: 815 us; the launch traced here: 807 us
  waiting for transfers between devices  316 us (39%)
  Pallas kernels  273 us (33%)
  matrix products  121 us (15%)
  other arithmetic  39.2 us (5%)
  blocking collectives  25.1 us (3%)
  local copies, waits for them, and re-layouts  16.2 us (2%)
  between operations  15.3 us (2%)
    psum x1, waiting for transfers between devices, per_device(): lax.psum(gate_part.astype(jnp.bfloat16), 'narrow').astype(jnp.float32)  192 us
    pallas_call x1, Pallas kernels, line_scatter(): pl.pallas_call(line_scatter_kernel, name='line_scatter', out_shape=jax.Sh...  126 us
    reduce_scatter x2, waiting for transfers between devices, owned(): lax.psum_scatter(part.astype(jnp.bfloat16), 'narrow', scatter_dimension=a...  90.8 us
    pallas_call x1, Pallas kernels, gather_first(): pl.pallas_call(first_kernel, name='gather_first', out_shape=(jax.ShapeDty...  75.5 us
    pallas_call x1, Pallas kernels, line_gather(): pl.pallas_call(line_gather_kernel, name='line_gather', out_shape=jax.Shap...  71.5 us
    dot_general x5, matrix products, contract_cols(): lax.dot_general(left, right, (((1,), (1,)), ((), ())), preferred_element_...  39.2 us
    dot_general x5, matrix products, contract_rows(): lax.dot_general(left, right, (((0,), (0,)), ((), ())), preferred_element_...  33.8 us
    psum x1, waiting for transfers between devices, owned(): return lax.psum(share, 'wide').astype(jnp.float32)  32.7 us
  transfers between devices with their start and end apart: 5, of which 4 were waited for; matrix products, arithmetic and copies ran while one was open for 12% of the time, Pallas kernels for 16%

profile of v1, /device:TPU:0, one launch (start us, length us, event | category | flops | bytes accessed | tf_op | source)
XLA Modules:
  0.0 806.9 jit_solution(14511083768213101121)
XLA Ops:
  7.2 0.7 stack.10
  7.9 0.7 stack.9
  8.6 0.6 copy.68
  9.1 75.5 %gather_first.1 = (bf16[2048,2304]{1,0:T(8,128)(2,1)}, bf16[1536,2048]{1,0:T(8,128)(2,1)}, f32[8,1,512]{2,1,0:T(1,128)}, bf16[4,256,2048]{2,1,0:T(8,128)(2,1)}) custom-call(bf16[256,1536]{1,0:T(8,128)(2,1)} %q_ref.1, bf16[256,384]{1,0:T(8,128)(2,1)} %k_ref.1, bf16[256,384]{1,0:T(8,128)(2,1)} %v_ref.1, bf16[1536,256]{1,0:T(8,128)(2,1)} %p_ref.1, ...), custom_call_target="tpu_custom_call" | custom-call | tf_op jit(solution)/shard_map/gather_first/pallas_call | solution.py:326
  84.6 0.8 reduce
  85.4 1.5 fusion.19
  87.0 6.7 convolution_convert_fusion.5
  94.5 0.3 copy.54
  94.8 1.1 fusion.5
  95.8 1.3 fusion.6
  97.2 1.8 fusion.21
  99.0 1.6 slice-done.2
  100.6 0.3 copy-done.1
  100.9 0.7 slice-done.3
  101.6 1.9 multiply_reduce_fusion.2
  103.5 1.2 multiply_convert_fusion.3.x_ref
  104.7 71.5 %line_gather.1 = bf16[4,256,2048]{2,1,0:T(8,128)(2,1)} custom-call(bf16[256,2048]{1,0:T(8,128)(2,1)} %multiply_convert_fusion.3.x_ref), custom_call_target="tpu_custom_call" | custom-call | tf_op jit(solution)/shard_map/line_gather/pallas_call | solution.py:375
  176.3 0.6 fusion.43
  176.9 0.6 fusion.40
  177.6 10.3 %fusion.53 = f32[1024,1152]{1,0:T(8,128)} fusion(bf16[1024,2048]{1,0:T(8,128)(2,1)} %bitcast.133, bf16[2048,1152]{1,0:T(8,128)(2,1)} %param.21), kind=kOutput, calls=%fused_computation.94 | convolution fusion | flops 4831838208 | bytes 13631488 | tf_op jit(solution)/shard_map/dot_general | solution.py:637
  187.9 9.7 %fusion.54 = f32[1024,1152]{1,0:T(8,128)} fusion(bf16[1024,2048]{1,0:T(8,128)(2,1)S(1)} %bitcast.135, bf16[2048,1152]{1,0:T(8,128)(2,1)} %param.22), kind=kOutput, calls=%fused_computation.95 | convolution fusion | flops 4831838208 | bytes 13631488 | tf_op jit(solution)/shard_map/dot_general | solution.py:638
  197.6 11.6 %multiply_convert_fusion = (bf16[1024,1152]{1,0:T(8,128)(2,1)}, bf16[1024,1152]{1,0:T(8,128)(2,1)}, bf16[1024,1152]{1,0:T(8,128)(2,1)S(1)}) fusion(f32[1024,1152]{1,0:T(8,128)} %fusion.53, f32[1152]{0:T(1024)S(1)} %fusion.40, f32[1024,1152]{1,0:T(8,128)} %fusion.54, bf16[1024,2048]{1,0:T(8,128)(2,1)S(1)} %bitcast.167, bf16[1152,2048]{1,0:T(8,128)(2,1)S(1)} %bitcast.166), kind=kOutput, calls=%fused_computation.19 | convolution fusion | flops 4854251520 | bytes 25432576 | tf_op jit(solution)/shard_map/dot_general | solution.py:34
  209.2 1.4 copy-done.30
  210.6 7.1 convolution_convert_fusion.6
  217.7 0.6 reduce-scatter.8.cloned.1.call-start
  218.3 8.4 %fusion.55 = f32[1024,2048]{1,0:T(8,128)S(1)} fusion(bf16[1024,1152]{1,0:T(8,128)(2,1)} %get-tuple-element.33, bf16[2048,1152]{1,0:T(8,128)(2,1)} %param.21), kind=kOutput, calls=%fused_computation.96 | convolution fusion | flops 4831838208 | bytes 15466496 | tf_op jit(solution)/shard_map/dot_general | solution.py:34
  226.7 9.5 %add_convert_fusion = bf16[1024,2048]{1,0:T(8,128)(2,1)} fusion(f32[1024,2048]{1,0:T(8,128)S(1)} %fusion.55, bf16[1024,1152]{1,0:T(8,128)(2,1)S(1)} %copy-done.32, bf16[2048,1152]{1,0:T(8,128)(2,1)} %param.22), kind=kOutput, calls=%fused_computation.1 | convolution fusion | flops 4836032512 | bytes 19660800 | tf_op jit(solution)/shard_map/dot_general | solution.py:34
  236.2 125.6 %line_scatter.1 = f32[256,2048]{1,0:T(8,128)} custom-call(bf16[4,256,2048]{2,1,0:T(8,128)(2,1)} %bitcast.137), custom_call_target="tpu_custom_call" | custom-call | tf_op jit(solution)/shard_map/line_scatter/pallas_call | solution.py:541
  361.8 2.7 multiply_reduce_fusion
  364.6 3.9 fusion.16
  368.5 1.3 copy-done.2
  369.8 4.5 convolution_convert_fusion.4
  374.3 0.2 reduce-scatter.6.cloned.1.call-start
  374.6 1.3 copy-done.3
  375.9 5.5 convolution_convert_fusion.7
  381.4 1.5 copy.56
  383.0 6.7 fusion
  389.7 2.7 fusion.2
  392.4 1.1 fusion.26
  393.5 0.7 multiply_convert_fusion.4
  394.2 1.2 fusion.27
  395.5 5.4 convolution_convert_fusion
  400.9 0.3 all-reduce.9.cloned.1.call-start
  401.2 9.7 %convolution_convert_fusion.3 = bf16[2048,1152]{1,0:T(8,128)(2,1)} fusion(bf16[1024,2048]{1,0:T(8,128)(2,1)} %bitcast.134, bf16[1024,1152]{1,0:T(8,128)(2,1)} %get-tuple-element.33), kind=kOutput, calls=%fused_computation.4 | convolution fusion | flops 4834197504 | bytes 11272192 | tf_op jit(solution)/shard_map/dot_general | solution.py:28
  411.0 7.3 convolution_convert_fusion.2
  418.3 6.8 convolution_convert_fusion.1
  425.1 0.3 all-reduce.11.cloned.1.call-start
  425.4 9.9 %reduce-scatter.8.cloned.1.call-done = bf16[1536,256]{1,0:T(8,128)(2,1)} async-done(((bf16[1536,2048]{1,0:T(8,128)(2,1)}), bf16[1536,256]{1,0:T(8,128)(2,1)}) %reduce-scatter.8.cloned.1.call-update) | async-done | bytes 786448 | tf_op jit(solution)/shard_map/reduce_scatter | solution.py:719
  435.3 80.9 %reduce-scatter.6.cloned.1.call-done = bf16[256,2304]{1,0:T(8,128)(2,1)} async-done(((bf16[2048,2304]{1,0:T(8,128)(2,1)}), bf16[256,2304]{1,0:T(8,128)(2,1)}) %reduce-scatter.6.cloned.1.call-update) | async-done | bytes 1179664 | tf_op jit(solution)/shard_map/reduce_scatter | solution.py:719
  516.3 0.6 dynamic-slice
  517.5 192.4 %all-reduce.9.cloned.1.call-done = (bf16[2048,1152]{1,0:T(8,128)(2,1)}, bf16[2048,1152]{1,0:T(8,128)(2,1)}, bf16[1152,2048]{1,0:T(8,128)(2,1)}) async-done(((bf16[2048,1152]{1,0:T(8,128)(2,1)}, bf16[2048,1152]{1,0:T(8,128)(2,1)}, bf16[1152,2048]{1,0:T(8,128)(2,1)}), (bf16[2048,1152]{1,0:T(8,128)(2,1)}, bf16[2048,1152]{1,0:T(8,128)(2,1)}, bf16[1152,2048]{1,0:T(8,128)(2,1)})) %all-reduce.9.cloned.1.call-update) | async-done | bytes 14155792 | tf_op jit(solution)/shard_map/psum | solution.py:729
  709.9 7.7 convert_element_type.182
  717.5 5.1 convert_element_type.184
  722.7 4.9 convert_element_type.186
  727.7 4.3 fusion.15
  732.0 13.5 %all-reduce.2 = (bf16[2048]{0:T(1024)(128)(2,1)S(1)}, bf16[2048]{0:T(1024)(128)(2,1)S(1)}) all-reduce(bf16[2048]{0:T(1024)(128)(2,1)S(1)} %get-tuple-element.21, bf16[2048]{0:T(1024)(128)(2,1)S(1)} %copy-done.22), channel_id=5, replica_groups=mesh['narrow'=8,'wide'=4] {'narrow'}, use_global_device_ids=true, to_apply=%region_16.17.clone | all-reduce | flops 4096 | bytes 16384
  745.6 11.7 %all-reduce.4 = (bf16[256]{0:T(256)(128)(2,1)S(1)}, bf16[256]{0:T(256)(128)(2,1)S(1)}) all-reduce(bf16[256]{0:T(256)(128)(2,1)S(1)} %dynamic-slice.1, bf16[256]{0:T(256)(128)(2,1)S(1)} %dynamic-slice.3), channel_id=1, replica_groups=mesh['narrow'=8,'wide'=4] {'wide'}, use_global_device_ids=true, to_apply=%region_17.18 | all-reduce | flops 512 | bytes 2048 | tf_op jit(solution)/shard_map/psum | solution.py:722
  757.3 0.6 convert_element_type.178
  757.9 0.6 convert_element_type.180
  758.4 3.3 fusion.18
  761.7 32.7 %all-reduce.11.cloned.1.call-done = (bf16[256,2304]{1,0:T(8,128)(2,1)}, bf16[1536,256]{1,0:T(8,128)(2,1)}) async-done(((bf16[256,2304]{1,0:T(8,128)(2,1)}, bf16[1536,256]{1,0:T(8,128)(2,1)}), (bf16[256,2304]{1,0:T(8,128)(2,1)}, bf16[1536,256]{1,0:T(8,128)(2,1)})) %all-reduce.11.cloned.1.call-update) | async-done | bytes 1966096 | tf_op jit(solution)/shard_map/psum | solution.py:722
  794.4 2.5 slice.37
  796.9 1.9 fusion.50
  798.9 1.3 convert_element_type.176
  (113 shorter events, 1.4 us)
Async XLA Ops:
  7.2 357.4 %reduce-scatter.4.cloned.1.call-start = ((), (), s32[]{:S(2)}) async-start(), calls=%async_computation.3 | async-start | bytes 5242880 | tf_op jit(solution)/shard_map/reduce_scatter | solution.py:656
  86.9 6.7 copy-start.23
  87.0 7.0 copy-start.27
  93.9 3.3 copy-start.19
  94.7 2.5 copy-start.7
  95.8 3.2 copy-start
  95.8 4.7 slice-start.2
  97.2 3.7 copy-start.1
  97.2 4.3 slice-start.3
  99.0 4.5 copy-start.5
  103.5 72.8 %copy-start.28 = (s32[4]{0:T(128)S(1)}, s32[4]{0:T(128)}, u32[]{:S(2)}) copy-start(s32[4]{0:T(128)} %param.25) | copy-start | bytes 52
  177.6 10.3 %copy-start.10 = (bf16[4,256,2048]{2,1,0:T(8,128)(2,1)S(1)}, bf16[4,256,2048]{2,1,0:T(8,128)(2,1)}, u32[]{:S(2)}) copy-start(bf16[4,256,2048]{2,1,0:T(8,128)(2,1)} %line_gather.1) | copy-start | bytes 12582916
  177.6 20.0 %slice-start.9 = ((s8[4718592]{0:T(1024)(128)(4,1)}), s8[4194304]{0:T(1024)(128)(4,1)S(1)}, s32[]{:S(2)}) async-start(s8[4718592]{0:T(1024)(128)(4,1)} %bitcast.165), calls=%async_computation.17 | async-start | bytes 8388608
  187.9 9.7 %slice-start.10 = ((s8[4718592]{0:T(1024)(128)(4,1)}), s8[524288]{0:T(1024)(128)(4,1)S(1)}, s32[]{:S(2)}) async-start(s8[4718592]{0:T(1024)(128)(4,1)} %bitcast.165), calls=%async_computation.18 | async-start | bytes 1048576
  187.9 9.7 %copy-start.25 = (bf16[4,256,2048]{2,1,0:T(8,128)(2,1)S(1)}, bf16[4,256,2048]{2,1,0:T(8,128)(2,1)}, u32[]{:S(2)}) copy-start(bf16[4,256,2048]{2,1,0:T(8,128)(2,1)} %get-tuple-element.18) | copy-start | bytes 12582916
  209.2 1.4 copy-start.30
  217.7 217.6 %reduce-scatter.8.cloned.1.call-start = ((), (), s32[]{:S(2)}) async-start(), calls=%async_computation.5 | async-start | bytes 7077888 | tf_op jit(solution)/shard_map/reduce_scatter | solution.py:719
  218.3 8.4 %copy-start.32 = (bf16[1024,1152]{1,0:T(8,128)(2,1)S(1)}, bf16[1024,1152]{1,0:T(8,128)(2,1)}, u32[]{:S(2)}) copy-start(bf16[1024,1152]{1,0:T(8,128)(2,1)} %get-tuple-element.32) | copy-start | bytes 7077892
  364.6 5.2 copy-start.6
  368.5 1.3 copy-start.2
  374.3 1.6 copy-start.3
  374.3 141.9 %reduce-scatter.6.cloned.1.call-start = ((), (), s32[]{:S(2)}) async-start(), calls=%async_computation.4 | async-start | bytes 10616832 | tf_op jit(solution)/shard_map/reduce_scatter | solution.py:719
  375.9 7.1 copy-start.20
  382.9 6.7 copy-start.12
  382.9 6.7 slice-start
  383.0 6.7 slice-start.1
  389.6 2.8 copy-start.8
  392.4 1.8 copy-start.13
  392.4 1.8 copy-start.21
  393.5 2.0 copy-start.16
  394.2 1.3 copy-start.14
  400.9 309.0 %all-reduce.9.cloned.1.call-start = ((), (), s32[]{:S(2)}) async-start(), calls=%async_computation.6 | async-start | bytes 28311552 | tf_op jit(solution)/shard_map/psum | solution.py:729
  401.2 9.8 %copy-start.11 = (bf16[4,256,2048]{2,1,0:T(8,128)(2,1)S(1)}, bf16[4,256,2048]{2,1,0:T(8,128)(2,1)}, u32[]{:S(2)}) copy-start(bf16[4,256,2048]{2,1,0:T(8,128)(2,1)} %line_gather.1) | copy-start | bytes 12582916
  401.2 9.8 %copy-start.33 = (bf16[1024,1152]{1,0:T(8,128)(2,1)S(1)}, bf16[1024,1152]{1,0:T(8,128)(2,1)}, u32[]{:S(2)}) copy-start(bf16[1024,1152]{1,0:T(8,128)(2,1)} %get-tuple-element.32) | copy-start | bytes 7077892
  411.0 7.4 copy-start.26
  411.0 7.4 copy-start.31
  425.1 91.2 %copy-start.29 = (u32[32]{0:T(128)S(1)}, u32[32]{0:T(128)}, u32[]{:S(2)}) copy-start(u32[32]{0:T(128)} %constant.51) | copy-start | bytes 388
  425.1 369.3 %all-reduce.11.cloned.1.call-start = ((), (), s32[]{:S(2)}) async-start(), calls=%async_computation.7 | async-start | bytes 3932160 | tf_op jit(solution)/shard_map/psum | solution.py:722
  709.9 7.7 copy-start.9
  709.9 12.8 %slice-start.4 = ((s8[4718592]{0:T(1024)(128)(4,1)}), s8[4194304]{0:T(1024)(128)(4,1)S(1)}, s32[]{:S(2)}) async-start(s8[4718592]{0:T(1024)(128)(4,1)} %bitcast.131), calls=%async_computation.12 | async-start | bytes 8388608
  717.5 5.1 slice-start.5
  717.5 10.1 %slice-start.6 = ((s8[9437184]{0:T(1024)(128)(4,1)}), s8[1048576]{0:T(1024)(128)(4,1)S(1)}, s32[]{:S(2)}) async-start(s8[9437184]{0:T(1024)(128)(4,1)} %bitcast.163), calls=%async_computation.14 | async-start | bytes 2097152
  717.5 10.1 %slice-start.7 = ((s8[9437184]{0:T(1024)(128)(4,1)}), s8[4194304]{0:T(1024)(128)(4,1)S(1)}, s32[]{:S(2)}) async-start(s8[9437184]{0:T(1024)(128)(4,1)} %bitcast.163), calls=%async_computation.15 | async-start | bytes 8388608
  722.7 5.0 copy-start.15
  722.7 5.0 copy-start.17
  722.7 5.0 slice-start.8
  727.7 4.3 copy-start.22
  727.7 30.8 %copy-start.24 = (f32[256]{0:T(256)S(1)}, f32[256]{0:T(256)}, u32[]{:S(2)}) copy-start(f32[256]{0:T(256)} %copy-done.23) | copy-start | bytes 3076
  727.7 30.8 %copy-start.4 = (f32[256,2048]{1,0:T(8,128)S(1)}, f32[256,2048]{1,0:T(8,128)}, u32[]{:S(2)}) copy-start(f32[256,2048]{1,0:T(8,128)} %copy-done.2) | copy-start | bytes 6291460
  794.4 4.5 copy-start.18
Sparse Core Ops, SparseCore 0:
  217.8 125.8 reduce-scatter.3
  374.5 60.7 reduce-scatter.7
  439.4 76.8 reduce-scatter.5
  520.7 189.1 all-reduce.8
  712.2 82.1 all-reduce.10

commit v2 on v1

--- a/solution.py
+++ b/solution.py
@@ -554,6 +554,395 @@
     )(terms)
 
 
+class Reduce:
+    def __init__(self, me, part, cols, x_first, bufs, sems, k):
+        self.n, self.w, self.y, self.x, self.core = me
+        self.part, self.cols, self.x_first = part, pl.ds(*cols), x_first
+        self.sum, self.pair, self.one, self.two = bufs
+        self.sems, self.k = sems, k
+        self.rows = part.shape[3]
+        self.near = flip(self.n, 2) if x_first else flip(self.n, 4)
+        self.next = flip(self.n, 4) if x_first else flip(self.n, 2)
+
+    def load(self):
+        return pltpu.make_async_copy(
+            self.part.at[:, :, self.core, :, self.cols], self.sum, self.sems[0].at[self.k]
+        )
+
+    def swap(self):
+        return send(
+            self.part.at[:, :, 1 - self.core, :, self.cols],
+            self.pair,
+            self.sems[1].at[self.k],
+            self.sems[2].at[self.k],
+            flip(self.n, 1),
+            self.w,
+        )
+
+    def block(self, first, second):
+        return (second, first) if self.x_first else (first, second)
+
+    def axes(self):
+        return (self.x, self.y) if self.x_first else (self.y, self.x)
+
+    def stage(self, s):
+        a, b = self.axes()
+        if s == 1:
+            src = self.sum.at[:, 1 - a] if self.x_first else self.sum.at[1 - a]
+            dst, peer = self.one, self.near
+        else:
+            src = self.sum.at[self.block(a, 1 - b)]
+            dst, peer = self.two, self.next
+        k = 2 * self.k + s - 1
+        return send(src, dst, self.sems[3].at[k], self.sems[4].at[k], peer, self.w)
+
+    def add(self, block, other):
+        step = 64 if self.rows % 64 == 0 else 48
+
+        @pl.loop(0, self.rows // step)
+        def _(i):
+            r = pl.ds(pl.multiple_of(i * step, step), step)
+            self.sum[block[0], block[1], r, :] = (
+                self.sum[block[0], block[1], r, :] + other[r, :]
+            )
+
+    def after_swap(self):
+        a, b = self.axes()
+        self.swap().wait_recv()
+        self.load().wait()
+        for first in (1 - a, a):
+            for second in (1 - b, b):
+                block = self.block(first, second)
+                self.add(block, self.pair.at[block])
+
+    def after_one(self):
+        a, b = self.axes()
+        self.stage(1).wait()
+        self.add(self.block(a, 1 - b), self.one.at[1 - b])
+        self.stage(2).start()
+        self.add(self.block(a, b), self.one.at[b])
+
+    def after_two(self):
+        a, b = self.axes()
+        self.stage(2).wait()
+        self.add(self.block(a, b), self.two)
+
+    def result(self):
+        return self.sum.at[self.y, self.x]
+
+
+class Spread:
+    def __init__(self, item, full, sems, k):
+        self.item, self.full, self.sems, self.k = item, full, sems, k
+        n = item.n
+        self.blocks = (n, flip(n, 2), flip(n, 4), flip(flip(n, 2), 4))
+
+    def region(self, block):
+        return self.full.at[block, :, self.item.cols]
+
+    def copy(self, kind, src, block, peer):
+        k = 7 * self.k + kind
+        return send(
+            src, self.region(block), self.sems[0].at[k], self.sems[1].at[k], peer, self.item.w
+        )
+
+    def own(self, kind):
+        n = self.item.n
+        return self.copy(kind, self.item.result(), n, (flip(n, 2), flip(n, 4), flip(n, 1))[kind])
+
+    def corner(self):
+        n, b = self.item.n, self.blocks
+        if self.item.x_first:
+            return self.copy(3, self.region(b[2]), b[2], flip(n, 2))
+        return self.copy(3, self.region(b[1]), b[1], flip(n, 4))
+
+    def to_core(self, which):
+        block = self.blocks[which]
+        return self.copy(3 + which, self.region(block), block, flip(self.item.n, 1))
+
+    def keep(self):
+        return pltpu.make_async_copy(
+            self.item.result(), self.region(self.item.n), self.sems[2].at[self.k]
+        )
+
+    def start(self):
+        order = (1, 0, 2) if self.item.x_first else (0, 1, 2)
+        for kind in order:
+            self.own(kind).start()
+        self.keep().start()
+
+    def relay(self):
+        first, second = (1, 0) if self.item.x_first else (0, 1)
+        self.own(first).wait_recv()
+        self.corner().start()
+        self.to_core(1 + first).start()
+        self.own(second).wait_recv()
+        self.to_core(1 + second).start()
+
+    def last(self):
+        self.corner().wait_recv()
+        self.to_core(3).start()
+
+    def finish(self):
+        for kind in range(2):
+            self.own(kind).wait_send()
+        self.own(2).wait()
+        self.corner().wait_send()
+        for which in range(1, 4):
+            self.to_core(which).wait()
+        self.keep().wait()
+
+
+class Rows:
+    def __init__(self, ref):
+        self.ref = ref
+        self.shape = (4, ref.shape[0] // 4, ref.shape[1])
+
+    @property
+    def at(self):
+        return self
+
+    def __getitem__(self, index):
+        d, r, _ = index
+        return self.ref.at[pl.ds(d * self.shape[1] + r.start, r.size), :]
+
+
+def last_kernel(items, n_attn, *refs):
+    refs = list(refs)
+
+    def take(count):
+        out = refs[:count]
+        del refs[:count]
+        return out
+
+    parts = take(5)
+    feed_terms, gain_parts = take(2)
+    outs = take(n_attn)
+    full = take(3)
+    feed_out, gain_out = take(2)
+    bufs = [take(4) for _ in items]
+    line_bufs = [take(6) for _ in range(n_attn)]
+    feed_bufs = take(7)
+    gain_in, gain_sum, gain_line = take(3)
+    load_sem, swap_s, swap_r, st_s, st_r = take(5)
+    sp_s, sp_r, sp_l = take(3)
+    lr_s, lr_r, lg_s, lg_r, lg_l = take(5)
+    fd_s, fd_r, fd_l = take(3)
+    gn_s, gn_r, gz_s, gz_r = take(4)
+
+    n, w = lax.axis_index("narrow"), lax.axis_index("wide")
+    me = (n, w, n // 4, lax.rem(n // 2, 2), lax.rem(n, 2))
+    red = [
+        Reduce(me, parts[p], cols, xf, bufs[k], (load_sem, swap_s, swap_r, st_s, st_r), k)
+        for k, (p, cols, xf) in enumerate(items)
+    ]
+    attn, ffn = red[:n_attn], red[n_attn:]
+    spread = [
+        Spread(item, full[items[n_attn + k][0] - 2], (sp_s, sp_r, sp_l), k)
+        for k, item in enumerate(ffn)
+    ]
+    for item in red:
+        item.load().start()
+    mine, away = feed_bufs[0], feed_bufs[1]
+    feed_loads = [
+        pltpu.make_async_copy(feed_terms.at[w], mine, fd_l.at[0]),
+        pltpu.make_async_copy(feed_terms.at[flip(w, 2)], away, fd_l.at[1]),
+    ]
+    for cp in feed_loads:
+        cp.start()
+
+    barrier = pltpu.get_barrier_semaphore()
+    narrow_peers = [lax.rem(n + i, 8) for i in range(1, 8)]
+    wide_peers = [lax.rem(w + i, 4) for i in range(1, 4)]
+    for peer in narrow_peers:
+        pl.semaphore_signal(
+            barrier, inc=1, device_id=at(peer, w), device_id_type=pl.DeviceIdType.MESH
+        )
+    for peer in wide_peers:
+        pl.semaphore_signal(
+            barrier, inc=1, device_id=at(n, peer), device_id_type=pl.DeviceIdType.MESH
+        )
+    pl.semaphore_wait(barrier, 10)
+
+    for item in red:
+        item.swap().start()
+    feed = LineScatter(n, w, feed_terms, feed_bufs[2:], fd_s, fd_r, 4)
+    feed.start()
+
+    def gain_narrow(i):
+        peer = narrow_peers[i]
+        return send(gain_parts.at[peer], gain_in.at[i], gn_s.at[i], gn_r.at[i], peer, w)
+
+    def gain_wide(i):
+        return send(gain_sum, gain_line.at[i], gz_s.at[i], gz_r.at[i], n, wide_peers[i])
+
+    for i in range(7):
+        gain_narrow(i).start()
+
+    for item in attn:
+        item.after_swap()
+        item.stage(1).start()
+    for cp in feed_loads:
+        cp.wait()
+    feed.pass_on(0, away)
+    for item in ffn[:2]:
+        item.after_swap()
+    feed.pass_on(1, away)
+    for item in attn[:2]:
+        item.after_one()
+    for item in ffn[:2]:
+        item.stage(1).start()
+    feed.pass_on(2, away)
+    for item in ffn[2:]:
+        item.after_swap()
+    feed.pass_on(3, away)
+    for item in attn[2:]:
+        item.after_one()
+    for item in ffn[2:]:
+        item.stage(1).start()
+
+    for i in range(7):
+        gain_narrow(i).wait()
+    total = gain_parts[n]
+    for i in range(7):
+        total = total + gain_in[i]
+    gain_sum[...] = total
+    for i in range(3):
+        gain_wide(i).start()
+
+    scatters, gathers = [], []
+    for k, item in enumerate(attn):
+        own = line_bufs[k][5]
+        scatters.append(
+            LineScatter(n, w, Rows(item.result()), line_bufs[k][:5], lr_s.at[k], lr_r.at[k], 1)
+        )
+        gathers.append(LineGather(n, w, own, outs[k], lg_s.at[k], lg_r.at[k], 1))
+
+    def quarter(item, d):
+        return item.result().at[pl.ds(d * (item.rows // 4), item.rows // 4), :]
+
+    def line_pass(k):
+        scatters[k].pass_on(0, quarter(attn[k], flip(w, 2)))
+
+    def keep(k):
+        return pltpu.make_async_copy(line_bufs[k][5], outs[k].at[w], lg_l.at[k])
+
+    def line_turn(k):
+        scatters[k].finish(0, quarter(attn[k], w), line_bufs[k][5])
+        gathers[k].start()
+        keep(k).start()
+
+    for k in (0, 1):
+        attn[k].after_two()
+        scatters[k].start()
+    for i in range(4):
+        feed.finish(i, mine, feed_out)
+    for k in (2, 3):
+        attn[k].after_two()
+        scatters[k].start()
+    for k in (0, 1):
+        line_pass(k)
+    for item in ffn[:2]:
+        item.after_one()
+    for k in (2, 3):
+        line_pass(k)
+    for k in (0, 1):
+        line_turn(k)
+    for item in ffn[2:]:
+        item.after_one()
+    for k in (2, 3):
+        line_turn(k)
+    for k in (0, 1):
+        gathers[k].forward(0)
+    for k in (0, 1):
+        ffn[k].after_two()
+        spread[k].start()
+    for k in (2, 3):
+        gathers[k].forward(0)
+    for k in (2, 3):
+        ffn[k].after_two()
+        spread[k].start()
+    for i in range(3):
+        gain_wide(i).wait()
+    gain_out[...] = ((gain_sum[...] + gain_line[0]) + (gain_line[1] + gain_line[2]))
+    for s in spread:
+        s.relay()
+    for s in spread:
+        s.last()
+    for s in spread:
+        s.finish()
+    for item in red:
+        item.swap().wait_send()
+    for k in range(n_attn):
+        scatters[k].drain()
+        gathers[k].finish()
+        keep(k).wait()
+    feed.drain()
+
+
+def reduce_last(qkv_part, project_part, gate_part, up_part, down_part, feed_terms, gain_parts):
+    whole = [qkv_part, project_part, gate_part, up_part, down_part]
+    parts = [p.reshape(2, 2, 2, p.shape[0] // 8, p.shape[1]) for p in whole]
+    items = []
+    for p, xf in ((0, True), (0, False), (1, True), (1, False)):
+        half = parts[p].shape[4] // 2
+        items.append((p, (0 if xf else half, half), xf))
+    n_attn = len(items)
+    items.append((2, (0, gate_part.shape[1]), True))
+    items.append((3, (0, up_part.shape[1]), False))
+    half = down_part.shape[1] // 2
+    items.append((4, (0, half), True))
+    items.append((4, (half, half), False))
+    scratch = []
+    for p, (_, cols), _ in items:
+        rows = parts[p].shape[3]
+        scratch += [
+            pltpu.VMEM((2, 2, rows, cols), BF),
+            pltpu.VMEM((2, 2, rows, cols), BF),
+            pltpu.VMEM((2, rows, cols), BF),
+            pltpu.VMEM((rows, cols), BF),
+        ]
+    outs = []
+    for p, (_, cols), _ in items[:n_attn]:
+        quarter = (parts[p].shape[3] // 4, cols)
+        scratch += [pltpu.VMEM(quarter, BF)] * 6
+        outs.append(jax.ShapeDtypeStruct((4,) + quarter, BF))
+    for part in parts[2:]:
+        outs.append(jax.ShapeDtypeStruct((8,) + part.shape[3:], BF))
+    outs.append(jax.ShapeDtypeStruct(feed_terms.shape[1:], F32))
+    outs.append(jax.ShapeDtypeStruct(gain_parts.shape[1:], F32))
+    scratch += [pltpu.VMEM(feed_terms.shape[1:], BF)] * 7
+    scratch += [
+        pltpu.VMEM((7,) + gain_parts.shape[1:], F32),
+        pltpu.VMEM(gain_parts.shape[1:], F32),
+        pltpu.VMEM((3,) + gain_parts.shape[1:], F32),
+    ]
+    dma = pltpu.SemaphoreType.DMA
+    k, f = len(items), len(items) - n_attn
+    scratch += [dma((k,)), dma((k,)), dma((k,)), dma((2 * k,)), dma((2 * k,))]
+    scratch += [dma((7 * f,)), dma((7 * f,)), dma((f,))]
+    scratch += [dma((n_attn, 4))] * 4 + [dma((n_attn,))]
+    scratch += [dma((16,)), dma((16,)), dma((2,))]
+    scratch += [dma((7,)), dma((7,)), dma((3,)), dma((3,))]
+    hbm, vmem = pl.BlockSpec(memory_space=pl.ANY), pl.BlockSpec(memory_space=pltpu.VMEM)
+    out = pl.pallas_call(
+        functools.partial(last_kernel, items, n_attn),
+        name="reduce_last",
+        out_shape=tuple(outs),
+        in_specs=[hbm] * 6 + [vmem],
+        out_specs=[hbm] * (n_attn + 3) + [vmem] * 2,
+        scratch_shapes=scratch,
+        compiler_params=pltpu.CompilerParams(
+            collective_id=4, has_side_effects=True, vmem_limit_bytes=64 * 1024 * 1024 - 65536
+        ),
+    )(*parts, feed_terms, gain_parts)
+    rows = parts[0].shape[3]
+    qkv = jnp.concatenate([out[0].reshape(rows, -1), out[1].reshape(rows, -1)], axis=1)
+    project = jnp.concatenate([out[2].reshape(rows, -1), out[3].reshape(rows, -1)], axis=1)
+    ffn = [o.reshape(-1, o.shape[2]) for o in out[n_attn : n_attn + 3]]
+    return qkv, project, ffn, out[n_attn + 3], out[n_attn + 4]
+
+
 def per_device(
     fast,
     block_input,
@@ -653,10 +1042,6 @@
             mixed_terms, "wide", scatter_dimension=0, tiled=True
         ).astype(F32)
     partial_rows = jnp.dot(hidden, down_weight, preferred_element_type=jnp.float32)
-    feed = lax.psum_scatter(
-        partial_rows.astype(jnp.bfloat16), "wide", scatter_dimension=0, tiled=True
-    ).astype(jnp.float32)
-    block_output = (middle + feed).astype(jnp.bfloat16)
     out_grad = cotangent.astype(jnp.float32)
     down_part = contract_rows(hidden, grad_rows)
     gate_part = contract_rows(gathered, gate_back)
@@ -665,7 +1050,7 @@
     middle_norm_back, second_gain_part = second_backward(mixed_back)
     middle_back = out_grad + middle_norm_back
     branch_back = middle_back.astype(jnp.bfloat16)
-    project_part = contract_rows(attended, branch_back)
+    project_part = contract_rows(branch_back, attended)
     attended_back = (
         contract_cols(branch_back, project_full)
         .astype(jnp.bfloat16)
@@ -715,21 +1100,43 @@
     input_norm_back, first_gain_part = first_backward(normed_back)
     input_grad = (middle_back + input_norm_back).astype(jnp.bfloat16)
 
-    def owned(part, axis):
-        share = lax.psum_scatter(
-            part.astype(jnp.bfloat16), "narrow", scatter_dimension=axis, tiled=True
-        )
-        return lax.psum(share, "wide").astype(jnp.float32)
-
-    qkv_total = owned(qkv_part, 0)
-    project_total = owned(project_part, 1)
-    first_total = owned(first_gain_part, 0)
-    second_total = owned(second_gain_part, 0)
-    gate_total, up_total, down_total = (
-        lax.psum(gate_part.astype(jnp.bfloat16), "narrow").astype(jnp.float32),
-        lax.psum(up_part.astype(jnp.bfloat16), "narrow").astype(jnp.float32),
-        lax.psum(down_part.astype(jnp.bfloat16), "narrow").astype(jnp.float32),
-    )
+    if fast:
+        gain_parts = jnp.stack(
+            [first_gain_part.reshape(8, -1), second_gain_part.reshape(8, -1)], axis=1
+        ).reshape(8, 1, -1)
+        qkv_total, project_total, ffn_totals, feed, gain_total = reduce_last(
+            qkv_part.astype(BF),
+            project_part.astype(BF),
+            gate_part.astype(BF),
+            up_part.astype(BF),
+            down_part.astype(BF),
+            partial_rows.astype(BF).reshape(4, tokens_here, model),
+            gain_parts,
+        )
+        gain_total = gain_total.reshape(2, -1)
+        first_total, second_total = gain_total[0], gain_total[1]
+        qkv_total = qkv_total.astype(F32)
+        project_total = project_total.T.astype(F32)
+        gate_total, up_total, down_total = [t.astype(F32) for t in ffn_totals]
+    else:
+
+        def owned(part):
+            share = lax.psum_scatter(part.astype(BF), "narrow", scatter_dimension=0, tiled=True)
+            return lax.psum(share, "wide").astype(F32)
+
+        qkv_total = owned(qkv_part)
+        project_total = owned(project_part).T
+        first_total = owned(first_gain_part)
+        second_total = owned(second_gain_part)
+        gate_total, up_total, down_total = (
+            lax.psum(gate_part.astype(BF), "narrow").astype(F32),
+            lax.psum(up_part.astype(BF), "narrow").astype(F32),
+            lax.psum(down_part.astype(BF), "narrow").astype(F32),
+        )
+        feed = lax.psum_scatter(
+            partial_rows.astype(BF), "wide", scatter_dimension=0, tiled=True
+        ).astype(F32)
+    block_output = (middle + feed).astype(BF)
     return (
         block_output,
         input_grad,

time: 815 us -> 606 us (0.74)
  waiting for transfers between devices: 316 us -> 0 us
  Pallas kernels: 273 us -> 427 us
  blocking collectives: 25.1 us -> 0 us
  between operations: 15.3 us -> 1.48 us
    psum x2 -> x0, waiting for transfers between devices: 225 us -> none  [the longest x1 192 us: per_device(): lax.psum(gate_part.astype(jnp.bfloat16), 'narrow').astype(jnp.float32)]
    pallas_call x0 -> x1, Pallas kernels: none -> 207 us  [reduce_last(): pl.pallas_call(functools.partial(last_kernel, items, n_attn), name='reduc...]
    reduce_scatter x3 -> x0, waiting for transfers between devices: 90.8 us -> none  [the longest x2 90.8 us: owned(): lax.psum_scatter(part.astype(jnp.bfloat16), 'narrow', scatter_dimension=a...]
    pallas_call x1, Pallas kernels: 126 us -> 72.9 us  [line_scatter(): pl.pallas_call(line_scatter_kernel, name='line_scatter', out_shape=jax.Sh...]
    unnamed x1 -> x0, blocking collectives: 13.5 us -> none
    psum x1 -> x0, blocking collectives: 11.7 us -> none  [owned(): return lax.psum(share, 'wide').astype(jnp.float32)]
    convert_element_type x6 -> x4, other arithmetic: 20.1 us -> 20.6 us  [the longest x2 19.1 us: per_device(): gate_total, up_total, down_total = [t.astype(F32) for t in ffn_totals]]
  transfers between devices with their start and end apart: 5 -> 0, of which waited for: 4 -> 0; matrix products, arithmetic and copies ran while one was open for 12% -> 0% of each run, Pallas kernels for 16% -> 0%
where the time goes in v2:
time: 606 us; the launch traced here: 599 us
  Pallas kernels  427 us (70%)
  matrix products  120 us (20%)
  other arithmetic  39.7 us (7%)
  local copies, waits for them, and re-layouts  10.7 us (2%)
    pallas_call x1, Pallas kernels, reduce_last(): pl.pallas_call(functools.partial(last_kernel, items, n_attn), name='reduc...  207 us
    pallas_call x1, Pallas kernels, gather_first(): pl.pallas_call(first_kernel, name='gather_first', out_shape=(jax.ShapeDty...  75.5 us
    pallas_call x1, Pallas kernels, line_scatter(): pl.pallas_call(line_scatter_kernel, name='line_scatter', out_shape=jax.Sh...  72.9 us
    pallas_call x1, Pallas kernels, line_gather(): pl.pallas_call(line_gather_kernel, name='line_gather', out_shape=jax.Shap...  71.4 us
    dot_general x5, matrix products, contract_cols(): lax.dot_general(left, right, (((1,), (1,)), ((), ())), preferred_element_...  36.1 us
    dot_general x5, matrix products, contract_rows(): lax.dot_general(left, right, (((0,), (0,)), ((), ())), preferred_element_...  31.9 us
    convert_element_type x2, other arithmetic, per_device(): gate_total, up_total, down_total = [t.astype(F32) for t in ffn_totals]  19.1 us

profile of v2, /device:TPU:0, one launch (start us, length us, event | category | flops | bytes accessed | tf_op | source)
XLA Modules:
  0.0 598.9 jit_solution(6342457705982537446)
XLA Ops:
  0.6 0.7 stack.13
  1.3 0.7 stack.12
  2.0 0.6 copy.66
  2.6 75.5 %gather_first.1 = (bf16[2048,2304]{1,0:T(8,128)(2,1)}, bf16[1536,2048]{1,0:T(8,128)(2,1)}, f32[8,1,512]{2,1,0:T(1,128)}, bf16[4,256,2048]{2,1,0:T(8,128)(2,1)}) custom-call(bf16[256,1536]{1,0:T(8,128)(2,1)} %q_ref.1, bf16[256,384]{1,0:T(8,128)(2,1)} %k_ref.1, bf16[256,384]{1,0:T(8,128)(2,1)} %v_ref.1, bf16[1536,256]{1,0:T(8,128)(2,1)} %p_ref.1, ...), custom_call_target="tpu_custom_call" | custom-call | tf_op jit(solution)/shard_map/gather_first/pallas_call | solution.py:326
  78.0 0.8 reduce
  78.9 1.5 fusion.19
  80.4 6.7 %convolution_convert_fusion.5 = bf16[256,2304]{1,0:T(8,128)(2,1)S(1)} fusion(bf16[2048,2304]{1,0:T(8,128)(2,1)} %get-tuple-element.25, bf16[256,2048]{1,0:T(8,128)(2,1)} %param.13, f32[2048]{0:T(1024)S(1)} %bitcast.186, f32[256]{0:T(256)S(1)} %fusion.41), kind=kOutput, calls=%fused_computation.31 | convolution fusion | flops 2418606080 | bytes 11674624 | tf_op jit(solution)/shard_map/dot_general | solution.py:990
  87.1 0.8 copy.48
  88.0 0.2 reduce-window.8
  88.1 0.1 convert_reduce_fusion
  88.2 0.1 fusion.35
  88.3 0.1 copy.49
  88.5 0.1 slice.45
  88.5 0.3 copy.50
  88.8 1.1 fusion.5
  89.9 1.3 fusion.6
  91.3 1.8 fusion.21
  93.1 0.0 copy-done
  93.1 1.6 slice-done.2
  94.8 0.3 copy-done.4
  95.0 0.7 slice-done.3
  95.7 1.9 multiply_reduce_fusion.2
  97.7 1.4 multiply_convert_fusion.3.x_ref
  99.1 71.4 %line_gather.1 = bf16[4,256,2048]{2,1,0:T(8,128)(2,1)} custom-call(bf16[256,2048]{1,0:T(8,128)(2,1)} %multiply_convert_fusion.3.x_ref), custom_call_target="tpu_custom_call" | custom-call | tf_op jit(solution)/shard_map/line_gather/pallas_call | solution.py:375
  170.5 10.1 %fusion.54 = f32[1024,1152]{1,0:T(8,128)} fusion(bf16[1024,2048]{1,0:T(8,128)(2,1)} %bitcast.160, bf16[2048,1152]{1,0:T(8,128)(2,1)} %param.21), kind=kOutput, calls=%fused_computation.103 | convolution fusion | flops 4831838208 | bytes 13631488 | tf_op jit(solution)/shard_map/dot_general | solution.py:1026
  180.7 0.6 fusion.43
  181.3 0.6 fusion.40
  182.0 9.0 %fusion.53 = f32[1024,1152]{1,0:T(8,128)S(1)} fusion(bf16[1024,2048]{1,0:T(8,128)(2,1)} %bitcast.207, bf16[1152,2048]{1,0:T(8,128)(2,1)} %param.23), kind=kOutput, calls=%fused_computation.102 | convolution fusion | flops 4831838208 | bytes 13631488 | tf_op jit(solution)/shard_map/dot_general | solution.py:34
  191.0 0.0 slice-start.5
  191.0 11.6 %multiply_convert_fusion = (bf16[1024,1152]{1,0:T(8,128)(2,1)}, bf16[1024,1152]{1,0:T(8,128)(2,1)}, bf16[1024,1152]{1,0:T(8,128)(2,1)}) fusion(f32[1024,1152]{1,0:T(8,128)S(1)} %copy-done.25, f32[1152]{0:T(1024)S(1)} %fusion.40, f32[1024,1152]{1,0:T(8,128)S(1)} %fusion.53, bf16[1024,2048]{1,0:T(8,128)(2,1)S(1)} %bitcast.161, bf16[2048,1152]{1,0:T(8,128)(2,1)} %param.22), kind=kOutput, calls=%fused_computation.22 | convolution fusion | flops 4854251520 | bytes 25432576 | tf_op jit(solution)/shard_map/dot_general | solution.py:1027
  202.7 7.4 %fusion.55 = f32[1024,2048]{1,0:T(8,128)S(1)} fusion(bf16[1024,1152]{1,0:T(8,128)(2,1)} %get-tuple-element.42, bf16[2048,1152]{1,0:T(8,128)(2,1)S(1)} %bitcast.202), kind=kOutput, calls=%fused_computation.104 | convolution fusion | flops 4831838208 | bytes 15466496 | tf_op jit(solution)/shard_map/dot_general | solution.py:34
  210.1 7.2 %add_convert_fusion = bf16[1024,2048]{1,0:T(8,128)(2,1)} fusion(f32[1024,2048]{1,0:T(8,128)S(1)} %fusion.55, bf16[1024,1152]{1,0:T(8,128)(2,1)S(1)} %copy-done.27, bf16[2048,1152]{1,0:T(8,128)(2,1)S(1)} %bitcast.204), kind=kOutput, calls=%fused_computation.1 | convolution fusion | flops 4836032512 | bytes 19660800 | tf_op jit(solution)/shard_map/dot_general | solution.py:34
  217.3 72.9 %line_scatter.1 = f32[256,2048]{1,0:T(8,128)} custom-call(bf16[4,256,2048]{2,1,0:T(8,128)(2,1)} %bitcast.164), custom_call_target="tpu_custom_call" | custom-call | tf_op jit(solution)/shard_map/line_scatter/pallas_call | solution.py:541
  290.3 2.3 multiply_reduce_fusion
  292.6 0.2 copy-done.11
  292.7 0.6 fusion.16
  293.4 1.3 copy-done.2
  294.7 4.7 convolution_convert_fusion.7
  299.3 0.3 copy.52
  299.6 4.1 fusion.27
  303.8 4.9 fusion
  308.7 1.9 fusion.2
  310.6 2.2 fusion.26
  312.8 0.7 multiply_convert_fusion.4
  313.5 7.9 %fusion.20 = (f32[256]{0:T(256)S(1)}, f32[2048]{0:T(1024)S(1)}, f32[256,2048]{1,0:T(8,128)}) fusion(bf16[256,2048]{1,0:T(8,128)(2,1)S(1)} %copy-done.4, f32[2048]{0:T(1024)S(1)} %bitcast.187, f32[256]{0:T(256)S(1)} %fusion.41, bf16[2048,2304]{1,0:T(8,128)(2,1)} %get-tuple-element.25, bf16[256,384]{0,1:T(8,128)(2,1)S(1)} %bitcast.190, ...), kind=kOutput, calls=%fused_computation.48 | convolution fusion | flops 2423125760 | bytes 13780992 | tf_op jit(solution)/shard_map/dot_general | solution.py:34
  321.4 0.6 multiply_multiply_fusion
  321.9 5.6 convolution_convert_fusion
  327.6 4.6 convolution_convert_fusion.4
  332.1 7.5 %convolution_convert_fusion.3 = bf16[2048,1152]{1,0:T(8,128)(2,1)} fusion(bf16[1024,2048]{1,0:T(8,128)(2,1)S(1)} %bitcast.162, bf16[1024,1152]{1,0:T(8,128)(2,1)S(1)} %copy-done.26), kind=kOutput, calls=%fused_computation.4 | convolution fusion | flops 4834197504 | bytes 11272192 | tf_op jit(solution)/shard_map/dot_general | solution.py:28
  339.6 7.5 %convolution_convert_fusion.2 = bf16[2048,1152]{1,0:T(8,128)(2,1)} fusion(bf16[1024,2048]{1,0:T(8,128)(2,1)S(1)} %bitcast.163, bf16[1024,1152]{1,0:T(8,128)(2,1)S(1)} %copy-done.28), kind=kOutput, calls=%fused_computation.3 | convolution fusion | flops 4834197504 | bytes 11272192 | tf_op jit(solution)/shard_map/dot_general | solution.py:28
  347.1 6.9 %convolution_convert_fusion.1 = bf16[1152,2048]{1,0:T(8,128)(2,1)} fusion(bf16[1024,1152]{1,0:T(8,128)(2,1)S(1)} %copy-done.24, bf16[1024,2048]{1,0:T(8,128)(2,1)S(1)} %bitcast.208), kind=kOutput, calls=%fused_computation.2 | convolution fusion | flops 4834197504 | bytes 11272192 | tf_op jit(solution)/shard_map/dot_general | solution.py:28
  353.9 7.4 %convolution_convert_fusion.6 = bf16[1024,2048]{1,0:T(8,128)(2,1)} fusion(bf16[1024,1152]{1,0:T(8,128)(2,1)S(1)} %copy-done.24, bf16[1152,2048]{1,0:T(8,128)(2,1)S(1)} %bitcast.206), kind=kOutput, calls=%fused_computation.32 | convolution fusion | flops 4833935360 | bytes 11272192 | tf_op jit(solution)/shard_map/dot_general | solution.py:1044
  361.4 0.6 reshape.232.refs_6_
  362.0 206.7 %reduce_last.1 = (bf16[4,64,1152]{2,1,0:T(8,128)(2,1)}, bf16[4,64,1152]{2,1,0:T(8,128)(2,1)}, bf16[4,64,768]{2,1,0:T(8,128)(2,1)}, bf16[4,64,768]{2,1,0:T(8,128)...) custom-call(bf16[2,2,2,256,2304]{4,3,2,1,0:T(8,128)(2,1)} %bitcast.1, ...), custom_call_target="tpu_custom_call" | custom-call | tf_op jit(solution)/shard_map/reduce_last/pallas_call | solution.py:928
  568.7 6.1 %fusion.18 = (bf16[256,2048]{1,0:T(8,128)(2,1)}, bf16[256,2048]{1,0:T(8,128)(2,1)}) fusion(f32[256,2048]{1,0:T(8,128)} %copy-done.2, bf16[256,2048]{1,0:T(8,128)(2,1)} %param.13, f32[256,2048]{1,0:T(8,128)} %get-tuple-element.58, f32[256]{0:T(256)} %multiply_multiply_fusion, f32[2048]{0:T(1024)} %bitcast.189, f32[256]{0:T(256)} %copy-done.19, ...), kind=kLoop, calls=%fused_computation.46 | loop fusion | flops 5242880 | bytes 11544576 | tf_op jit(solution)/shard_map/convert_element_type | solution.py:1101
  574.9 0.2 maximum_convert_fusion
  575.1 1.3 slice.47
  576.4 0.9 maximum_convert_fusion.1
  577.3 0.2 copy.57
  577.5 0.2 copy.56
  577.7 1.3 convert_bitcast_fusion
  578.9 0.6 fusion.52
  579.5 11.8 %bitcast_convert_fusion.1 = (f32[2048,1152]{1,0:T(8,128)}, f32[2048,1152]{1,0:T(8,128)}) fusion(bf16[8,256,1152]{2,1,0:T(8,128)(2,1)} %get-tuple-element.35, bf16[8,256,1152]{2,1,0:T(8,128)(2,1)} %get-tuple-element.34), kind=kLoop, calls=%fused_computation.20 | loop fusion | flops 4718592 | bytes 28311552 | tf_op jit(solution)/shard_map/convert_element_type | solution.py:1120
  591.3 7.3 %bitcast_convert_fusion = f32[1152,2048]{1,0:T(8,128)} fusion(bf16[8,144,2048]{2,1,0:T(8,128)(2,1)} %get-tuple-element.36), kind=kLoop, calls=%fused_computation.19 | loop fusion | flops 2359296 | bytes 14155776 | tf_op jit(solution)/shard_map/convert_element_type | solution.py:1120
  (85 shorter events, 0.3 us)
Async XLA Ops:
  78.8 243.1 %copy-start.18 = (f32[8,1,256]{2,1,0:T(1,128)}, f32[8,1,256]{2,1,0:T(1,128)S(1)}, u32[]{:S(2)}) copy-start(f32[8,1,256]{2,1,0:T(1,128)S(1)} %get-tuple-element.49) | copy-start | bytes 24580
  80.4 241.6 %copy-start.19 = (f32[256]{0:T(256)}, f32[256]{0:T(256)S(1)}, u32[]{:S(2)}) copy-start(f32[256]{0:T(256)S(1)} %fusion.41) | copy-start | bytes 3076
  80.4 7.6 %copy-start.22 = (s32[1,4]{1,0:T(1,128)S(1)}, s32[1,4]{1,0:T(1,128)}, u32[]{:S(2)}) copy-start(s32[1,4]{1,0:T(1,128)} %param.24) | copy-start | bytes 52
  88.8 2.5 copy-start.6
  89.9 3.2 copy-start
  89.9 1.4 copy-start.14
  89.9 4.8 slice-start.2
  91.3 3.8 copy-start.4
  91.3 4.4 slice-start.3
  93.1 4.6 copy-start.7
  97.7 194.9 %copy-start.1 = (f32[256,2048]{1,0:T(8,128)}, f32[256,2048]{1,0:T(8,128)S(1)}, u32[]{:S(2)}) copy-start(f32[256,2048]{1,0:T(8,128)S(1)} %get-tuple-element.55) | copy-start | bytes 6291460
  170.5 10.2 %copy-start.23 = (s32[4]{0:T(128)S(1)}, s32[4]{0:T(128)}, u32[]{:S(2)}) copy-start(s32[4]{0:T(128)} %param.25) | copy-start | bytes 52
  182.0 9.0 %copy-start.9 = (bf16[4,256,2048]{2,1,0:T(8,128)(2,1)S(1)}, bf16[4,256,2048]{2,1,0:T(8,128)(2,1)}, u32[]{:S(2)}) copy-start(bf16[4,256,2048]{2,1,0:T(8,128)(2,1)} %line_gather.1) | copy-start | bytes 12582916
  182.0 9.0 %copy-start.25 = (f32[1024,1152]{1,0:T(8,128)S(1)}, f32[1024,1152]{1,0:T(8,128)}, u32[]{:S(2)}) copy-start(f32[1024,1152]{1,0:T(8,128)} %fusion.54) | copy-start | bytes 14155780
  182.0 20.7 %slice-start.4 = ((s8[4718592]{0:T(1024)(128)(4,1)}), s8[4194304]{0:T(1024)(128)(4,1)S(1)}, s32[]{:S(2)}) async-start(s8[4718592]{0:T(1024)(128)(4,1)} %bitcast.201), calls=%async_computation.4 | async-start | bytes 8388608
  182.0 28.1 %slice-start.6 = ((s8[4718592]{0:T(1024)(128)(4,1)}), s8[4194304]{0:T(1024)(128)(4,1)S(1)}, s32[]{:S(2)}) async-start(s8[4718592]{0:T(1024)(128)(4,1)} %bitcast.203), calls=%async_computation.6 | async-start | bytes 8388608
  191.0 11.7 %slice-start.5 = ((s8[4718592]{0:T(1024)(128)(4,1)}), s8[524288]{0:T(1024)(128)(4,1)S(1)}, s32[]{:S(2)}) async-start(s8[4718592]{0:T(1024)(128)(4,1)} %bitcast.201), calls=%async_computation.5 | async-start | bytes 1048576
  191.0 19.1 %slice-start.7 = ((s8[4718592]{0:T(1024)(128)(4,1)}), s8[524288]{0:T(1024)(128)(4,1)S(1)}, s32[]{:S(2)}) async-start(s8[4718592]{0:T(1024)(128)(4,1)} %bitcast.203), calls=%async_computation.7 | async-start | bytes 1048576
  202.7 7.5 %copy-start.27 = (bf16[1024,1152]{1,0:T(8,128)(2,1)S(1)}, bf16[1024,1152]{1,0:T(8,128)(2,1)}, u32[]{:S(2)}) copy-start(bf16[1024,1152]{1,0:T(8,128)(2,1)} %get-tuple-element.43) | copy-start | bytes 7077892
  290.2 2.3 copy-start.5
  290.3 2.5 copy-start.11
  293.4 1.3 copy-start.2
  299.6 4.1 copy-start.15
  303.7 4.9 slice-start
  303.7 4.9 slice-start.1
  321.9 5.6 copy-start.3
  321.9 5.6 copy-start.8
  327.5 4.6 copy-start.10
  327.5 4.6 copy-start.26
  332.1 7.5 %copy-start.28 = (bf16[1024,1152]{1,0:T(8,128)(2,1)S(1)}, bf16[1024,1152]{1,0:T(8,128)(2,1)}, u32[]{:S(2)}) copy-start(bf16[1024,1152]{1,0:T(8,128)(2,1)} %get-tuple-element.43) | copy-start | bytes 7077892
  332.1 21.8 %slice-start.8 = ((s8[4718592]{0:T(1024)(128)(4,1)}), s8[4194304]{0:T(1024)(128)(4,1)S(1)}, s32[]{:S(2)}) async-start(s8[4718592]{0:T(1024)(128)(4,1)} %bitcast.205), calls=%async_computation.8 | async-start | bytes 8388608
  339.6 7.5 %copy-start.21 = (bf16[4,256,2048]{2,1,0:T(8,128)(2,1)S(1)}, bf16[4,256,2048]{2,1,0:T(8,128)(2,1)}, u32[]{:S(2)}) copy-start(bf16[4,256,2048]{2,1,0:T(8,128)(2,1)} %get-tuple-element.27) | copy-start | bytes 12582916
  339.6 7.5 %copy-start.24 = (bf16[1024,1152]{1,0:T(8,128)(2,1)S(1)}, bf16[1024,1152]{1,0:T(8,128)(2,1)}, u32[]{:S(2)}) copy-start(bf16[1024,1152]{1,0:T(8,128)(2,1)} %get-tuple-element.41) | copy-start | bytes 7077892
  339.6 14.3 %slice-start.9 = ((s8[4718592]{0:T(1024)(128)(4,1)}), s8[524288]{0:T(1024)(128)(4,1)S(1)}, s32[]{:S(2)}) async-start(s8[4718592]{0:T(1024)(128)(4,1)} %bitcast.205), calls=%async_computation.9 | async-start | bytes 1048576
  568.7 6.1 %copy-start.12 = (bf16[4,64,1152]{2,1,0:T(8,128)(2,1)S(1)}, bf16[4,64,1152]{2,1,0:T(8,128)(2,1)}, u32[]{:S(2)}) copy-start(bf16[4,64,1152]{2,1,0:T(8,128)(2,1)} %get-tuple-element.29) | copy-start | bytes 1769476
  568.7 6.1 %copy-start.13 = (bf16[4,64,1152]{2,1,0:T(8,128)(2,1)S(1)}, bf16[4,64,1152]{2,1,0:T(8,128)(2,1)}, u32[]{:S(2)}) copy-start(bf16[4,64,1152]{2,1,0:T(8,128)(2,1)} %get-tuple-element.30) | copy-start | bytes 1769476
  574.9 2.4 copy-start.17
  574.9 2.6 copy-start.16
  575.1 3.9 copy-start.20

commit v3 on v2

--- a/solution.py
+++ b/solution.py
@@ -97,11 +97,14 @@
         self.ssem, self.rsem, self.chunks = ssem, rsem, chunks
         self.rows = own.shape[0] // chunks
 
+    def span(self, i):
+        return pl.ds(pl.multiple_of(i * self.rows, self.rows), self.rows)
+
     def part(self, shard, i):
-        return self.whole.at[shard, pl.ds(i * self.rows, self.rows), :]
+        return self.whole.at[shard, self.span(i), :]
 
     def mine(self, i):
-        return self.own.at[pl.ds(i * self.rows, self.rows), :]
+        return self.own.at[self.span(i), :]
 
     def copy(self, kind, i, src, shard, w):
         k = kind * self.chunks + i
@@ -123,19 +126,20 @@
     def middle(self):
         return (self.w == 1) | (self.w == 2)
 
+    def start_chunk(self, i):
+        self.far(i).start()
+
+        @pl.when(self.w > 0)
+        def _():
+            self.left(i).start()
+
+        @pl.when(self.w < 3)
+        def _():
+            self.right(i).start()
+
     def start(self):
         for i in range(self.chunks):
-            self.far(i).start()
-
-        @pl.when(self.w > 0)
-        def _():
-            for i in range(self.chunks):
-                self.left(i).start()
-
-        @pl.when(self.w < 3)
-        def _():
-            for i in range(self.chunks):
-                self.right(i).start()
+            self.start_chunk(i)
 
     def forward(self, i):
         self.far(i).wait_recv()
@@ -144,31 +148,42 @@
         def _():
             self.onward(i).start()
 
+    def ready(self, i):
+        @pl.when(self.w > 0)
+        def _():
+            self.right(i).wait_recv()
+
+        @pl.when(self.w < 3)
+        def _():
+            self.left(i).wait_recv()
+
+        @pl.when((self.w == 0) | (self.w == 3))
+        def _():
+            self.onward(i).wait_recv()
+
+    def finish_sends(self):
+        for i in range(self.chunks):
+            self.far(i).wait_send()
+
+        @pl.when(self.w > 0)
+        def _():
+            for i in range(self.chunks):
+                self.left(i).wait_send()
+
+        @pl.when(self.w < 3)
+        def _():
+            for i in range(self.chunks):
+                self.right(i).wait_send()
+
+        @pl.when(self.middle())
+        def _():
+            for i in range(self.chunks):
+                self.onward(i).wait_send()
+
     def finish(self):
         for i in range(self.chunks):
-            self.far(i).wait_send()
-
-        @pl.when(self.w > 0)
-        def _():
-            for i in range(self.chunks):
-                self.left(i).wait_send()
-                self.right(i).wait_recv()
-
-        @pl.when(self.w < 3)
-        def _():
-            for i in range(self.chunks):
-                self.right(i).wait_send()
-                self.left(i).wait_recv()
-
-        @pl.when(self.middle())
-        def _():
-            for i in range(self.chunks):
-                self.onward(i).wait_send()
-
-        @pl.when((self.w == 0) | (self.w == 3))
-        def _():
-            for i in range(self.chunks):
-                self.onward(i).wait_recv()
+            self.ready(i)
+        self.finish_sends()
 
 
 def first_kernel(
@@ -354,41 +369,6 @@
     )(query, key, value, project, gains, cotangent)
 
 
-def line_gather_kernel(x_ref, whole, buf, in_sem, out_sem, ssem, rsem):
-    n, w = lax.axis_index("narrow"), lax.axis_index("wide")
-    cp = pltpu.make_async_copy(x_ref, buf, in_sem)
-    cp.start()
-    greet([], n, w, True)
-    line = LineGather(n, w, x_ref, whole, ssem, rsem, 4)
-    line.start()
-    cp.wait()
-    cp = pltpu.make_async_copy(buf, whole.at[w], out_sem)
-    cp.start()
-    for i in range(4):
-        line.forward(i)
-    line.finish()
-    cp.wait()
-
-
-def line_gather(rows):
-    spec = pl.BlockSpec(memory_space=pl.ANY)
-    return pl.pallas_call(
-        line_gather_kernel,
-        name="line_gather",
-        out_shape=jax.ShapeDtypeStruct((4,) + rows.shape, BF),
-        in_specs=[spec],
-        out_specs=spec,
-        scratch_shapes=[
-            pltpu.VMEM(rows.shape, BF),
-            pltpu.SemaphoreType.DMA,
-            pltpu.SemaphoreType.DMA,
-            pltpu.SemaphoreType.DMA((16,)),
-            pltpu.SemaphoreType.DMA((16,)),
-        ],
-        compiler_params=pltpu.CompilerParams(collective_id=2, has_side_effects=True),
-    )(rows)
-
-
 class LineScatter:
     def __init__(self, n, w, terms, bufs, ssem, rsem, chunks):
         self.n, self.w, self.terms = n, w, terms
@@ -396,11 +376,14 @@
         self.ssem, self.rsem, self.chunks = ssem, rsem, chunks
         self.rows = terms.shape[1] // chunks
 
+    def span(self, i):
+        return pl.ds(pl.multiple_of(i * self.rows, self.rows), self.rows)
+
     def cut(self, ref, i):
-        return ref.at[pl.ds(i * self.rows, self.rows), :]
+        return ref.at[self.span(i), :]
 
     def term(self, d, i):
-        return self.terms.at[d, pl.ds(i * self.rows, self.rows), :]
+        return self.terms.at[d, self.span(i), :]
 
     def copy(self, kind, i, src, dst, w):
         k = kind * self.chunks + i
@@ -431,36 +414,35 @@
     def end(self):
         return (self.w == 0) | (self.w == 3)
 
+    def start_chunk(self, i):
+        @pl.when(self.end())
+        def _():
+            self.relay(i).start()
+            self.far(i).start()
+
+        @pl.when(self.w > 0)
+        def _():
+            self.left(i).start()
+
+        @pl.when(self.w < 3)
+        def _():
+            self.right(i).start()
+
     def start(self):
-        @pl.when(self.end())
-        def _():
-            for i in range(self.chunks):
-                self.relay(i).start()
-            for i in range(self.chunks):
-                self.far(i).start()
-
-        @pl.when(self.w > 0)
-        def _():
-            for i in range(self.chunks):
-                self.left(i).start()
-
-        @pl.when(self.w < 3)
-        def _():
-            for i in range(self.chunks):
-                self.right(i).start()
+        for i in range(self.chunks):
+            self.start_chunk(i)
 
     def pass_on(self, i, mine):
         @pl.when(self.middle())
         def _():
             self.relay(i).wait_recv()
-            rows = pl.ds(i * self.rows, self.rows)
-            self.total[rows, :] = (
-                mine[rows, :].astype(F32) + self.relayed[rows, :].astype(F32)
-            ).astype(BF)
+            rows = self.span(i)
+            own = self.terms[flip(self.w, 2), rows, :] if mine is None else mine[rows, :]
+            self.total[rows, :] = (own.astype(F32) + self.relayed[rows, :].astype(F32)).astype(BF)
             self.far_sum(i).start()
 
     def finish(self, i, mine, out):
-        rows = pl.ds(i * self.rows, self.rows)
+        rows = self.span(i)
         self.far(i).wait_recv()
 
         @pl.when(self.w > 0)
@@ -471,30 +453,24 @@
         def _():
             self.left(i).wait_recv()
 
+        def put(*bufs):
+            own = self.terms[self.w, rows, :] if mine is None else mine[rows, :]
+            total = own.astype(F32)
+            for buf in bufs:
+                total = total + buf[rows, :].astype(F32)
+            out[rows, :] = total.astype(out.dtype)
+
         @pl.when(self.w == 0)
         def _():
-            out[rows, :] = (
-                mine[rows, :].astype(F32)
-                + self.from_far[rows, :].astype(F32)
-                + self.from_right[rows, :].astype(F32)
-            ).astype(out.dtype)
+            put(self.from_far, self.from_right)
 
         @pl.when(self.w == 3)
         def _():
-            out[rows, :] = (
-                mine[rows, :].astype(F32)
-                + self.from_far[rows, :].astype(F32)
-                + self.from_left[rows, :].astype(F32)
-            ).astype(out.dtype)
+            put(self.from_far, self.from_left)
 
         @pl.when(self.middle())
         def _():
-            out[rows, :] = (
-                mine[rows, :].astype(F32)
-                + self.from_far[rows, :].astype(F32)
-                + self.from_left[rows, :].astype(F32)
-                + self.from_right[rows, :].astype(F32)
-            ).astype(out.dtype)
+            put(self.from_far, self.from_left, self.from_right)
 
     def drain(self):
         for i in range(self.chunks):
@@ -516,42 +492,313 @@
                 self.right(i).wait_send()
 
 
-def line_scatter_kernel(terms, out, mine, away, fl, fr, ff, rl, tot, in_sem, ssem, rsem):
+def middle_kernel(
+    mixed,
+    cot,
+    wg,
+    wu,
+    wd,
+    live,
+    back_out,
+    partial_out,
+    gate_go,
+    gate_stay,
+    up_go,
+    up_stay,
+    low_go,
+    low_stay,
+    high_go,
+    high_stay,
+    x_all,
+    cot_v,
+    wg_v,
+    wu_v,
+    wd_v,
+    gate_f,
+    up_f,
+    back_f,
+    hid,
+    gb,
+    ub,
+    terms,
+    from_left,
+    from_right,
+    from_far,
+    relayed,
+    total,
+    part_buf,
+    gate_k,
+    up_k,
+    down_k,
+    in_sem,
+    ag_s,
+    ag_r,
+    rs_s,
+    rs_r,
+    part_sem,
+    sw_s,
+    sw_r,
+    out_sem,
+    ready,
+):
     n, w = lax.axis_index("narrow"), lax.axis_index("wide")
-    cps = [
-        pltpu.make_async_copy(terms.at[w], mine, in_sem.at[0]),
-        pltpu.make_async_copy(terms.at[flip(w, 2)], away, in_sem.at[1]),
+    y, x, core = n // 4, lax.rem(n // 2, 2), lax.rem(n, 2)
+    mate = flip(n, 1)
+    chunks = 4
+    rows = mixed.shape[0] // chunks
+    tokens, model = 4 * mixed.shape[0], mixed.shape[1]
+    width = wg.shape[1]
+    batch = 4 * rows
+    loads = [
+        pltpu.make_async_copy(src, dst, in_sem.at[k])
+        for k, (src, dst) in enumerate(
+            ((mixed, x_all.at[w]), (wg, wg_v), (wu, wu_v), (cot, cot_v), (wd, wd_v))
+        )
     ]
-    for cp in cps:
+    for cp in loads:
         cp.start()
-    greet([], n, w, True)
-    line = LineScatter(n, w, terms, (fl, fr, ff, rl, tot), ssem, rsem, 4)
-    line.start()
-    for cp in cps:
+    greet([mate], n, w, True)
+
+    gather = LineGather(n, w, mixed, x_all, ag_s, ag_r, chunks)
+    scatter = LineScatter(
+        n, w, terms, (from_left, from_right, from_far, relayed, total), rs_s, rs_r, chunks
+    )
+    for i in range(chunks):
+        gather.start_chunk(i)
+    gather.forward(0)
+    for cp in loads:
         cp.wait()
-    for i in range(4):
-        line.pass_on(i, away)
-    for i in range(4):
-        line.finish(i, mine, out)
-    line.drain()
-
-
-def line_scatter(terms):
-    shape = terms.shape[1:]
+
+    def rows_of(ref, i):
+        r = pl.ds(pl.multiple_of(i * rows, rows), rows)
+        return ref[:, r, :].reshape(batch, ref.shape[2])
+
+    def store(i):
+        return pltpu.make_async_copy(
+            part_buf.at[lax.rem(i, 2)],
+            partial_out.at[:, pl.ds(pl.multiple_of(i * rows, rows), rows), :],
+            part_sem.at[lax.rem(i, 2)],
+        )
+
+    @pl.loop(0, chunks)
+    def _(i):
+        r = pl.ds(pl.multiple_of(i * rows, rows), rows)
+        gather.ready(i)
+        xs = rows_of(x_all, i)
+        gate_f[...] = jnp.dot(xs, wg_v[...], preferred_element_type=F32)
+        up_f[...] = jnp.dot(xs, wu_v[...], preferred_element_type=F32)
+
+        @pl.when(i < chunks - 1)
+        def _():
+            gather.forward(i + 1)
+
+        back_f[...] = contract_cols(rows_of(cot_v, i), wd_v[...])
+        step = 16
+
+        @pl.loop(0, batch // step)
+        def _(t):
+            s = pl.ds(pl.multiple_of(t * step, step), step)
+            d = t // (rows // step)
+            into = pl.ds(
+                pl.multiple_of(i * rows + lax.rem(t, rows // step) * step, step), step
+            )
+            gate, up = gate_f[s, :], up_f[s, :] * live[...]
+            sigma = jax.nn.sigmoid(gate)
+            silu = gate * sigma
+            hid[d, into, :] = (silu * up).astype(BF)
+            back = back_f[s, :]
+            gb[d, into, :] = (back * up * sigma * (1.0 + gate * (1.0 - sigma))).astype(BF)
+            ub[d, into, :] = (back * silu * live[...]).astype(BF)
+
+        @pl.when(i > 0)
+        def _():
+            scatter.pass_on(i - 1, None)
+
+        terms[:, r, :] = (
+            (contract_cols(rows_of(gb, i), wg_v[...]) + contract_cols(rows_of(ub, i), wu_v[...]))
+            .astype(BF)
+            .reshape(4, rows, model)
+        )
+        scatter.start_chunk(i)
+
+        @pl.when(i > 1)
+        def _():
+            store(i - 2).wait()
+
+        part_buf[lax.rem(i, 2)] = (
+            jnp.dot(rows_of(hid, i), wd_v[...], preferred_element_type=F32)
+            .astype(BF)
+            .reshape(4, rows, model)
+        )
+        store(i).start()
+
+    pl.semaphore_signal(
+        ready, inc=1, device_id=at(mate, w), device_id_type=pl.DeviceIdType.MESH
+    )
+    scatter.pass_on(chunks - 1, None)
+
+    def row_grad(back, block):
+        cols = pl.ds(pl.multiple_of(block * (model // 8), model // 8), model // 8)
+        return contract_rows(
+            x_all[:, :, cols].reshape(tokens, model // 8), back[...].reshape(tokens, width)
+        )
+
+    def col_grad(block):
+        cols = pl.ds(pl.multiple_of(block * (model // 8), model // 8), model // 8)
+        return contract_rows(
+            hid[...].reshape(tokens, width), cot_v[:, :, cols].reshape(tokens, model // 8)
+        )
+
+    eighth, half = model // 8, model // 2
+
+    def place(j, base):
+        return pl.ds(pl.multiple_of(base + j * eighth, eighth), eighth)
+
+    swaps = [
+        send(buf.at[pl.ds(half, half), :], buf.at[pl.ds(0, half), :], sw_s.at[k], sw_r.at[k], mate, w)
+        for k, buf in enumerate((wg_v, wu_v))
+    ]
+    swaps.append(
+        send(
+            wd_v.at[:, pl.ds(half, half)], wd_v.at[:, pl.ds(0, half)], sw_s.at[2], sw_r.at[2], mate, w
+        )
+    )
+
+    @pl.loop(0, 4)
+    def _(j):
+        wg_v[place(j, half), :] = row_grad(gb, 2 * j + 1 - core).astype(BF)
+
+    pl.semaphore_wait(ready, 1)
+    swaps[0].start()
+
+    @pl.loop(0, 4)
+    def _(j):
+        wu_v[place(j, half), :] = row_grad(ub, 2 * j + 1 - core).astype(BF)
+
+    swaps[1].start()
+
+    @pl.loop(0, 4)
+    def _(j):
+        wd_v[:, place(j, half)] = col_grad(2 * j + 1 - core).astype(BF)
+
+    swaps[2].start()
+
+    swaps[0].wait_recv()
+
+    @pl.loop(0, 4)
+    def _(j):
+        gate_k[j // 2, lax.rem(j, 2)] = (
+            row_grad(gb, 2 * j + core) + wg_v[place(j, 0), :].astype(F32)
+        ).astype(BF)
+
+    cut = width // 2
+    pieces = (
+        (gate_k.at[:, 1 - x], gate_go),
+        (gate_k.at[:, x], gate_stay),
+        (up_k.at[1 - y], up_go),
+        (up_k.at[y], up_stay),
+        (down_k.at[:, 1 - x, pl.ds(0, cut), :], low_go),
+        (down_k.at[:, x, pl.ds(0, cut), :], low_stay),
+        (down_k.at[1 - y, :, pl.ds(cut, cut), :], high_go),
+        (down_k.at[y, :, pl.ds(cut, cut), :], high_stay),
+    )
+    puts = [
+        pltpu.make_async_copy(src, dst, out_sem.at[k]) for k, (src, dst) in enumerate(pieces)
+    ]
+    for k in (0, 1):
+        puts[k].start()
+    swaps[1].wait_recv()
+
+    @pl.loop(0, 4)
+    def _(j):
+        up_k[j // 2, lax.rem(j, 2)] = (
+            row_grad(ub, 2 * j + core) + wu_v[place(j, 0), :].astype(F32)
+        ).astype(BF)
+
+    for k in (2, 3):
+        puts[k].start()
+    swaps[2].wait_recv()
+
+    @pl.loop(0, 4)
+    def _(j):
+        down_k[j // 2, lax.rem(j, 2)] = (
+            col_grad(2 * j + core) + wd_v[:, place(j, 0)].astype(F32)
+        ).astype(BF)
+
+    for k in (4, 5, 6, 7):
+        puts[k].start()
+    for i in range(chunks):
+        scatter.finish(i, None, back_out)
+    scatter.drain()
+    gather.finish_sends()
+    for k in range(3):
+        swaps[k].wait_send()
+    store(chunks - 2).wait()
+    store(chunks - 1).wait()
+    for cp in puts:
+        cp.wait()
+
+
+def feed_forward(mixed, cot, gate_weight, up_weight, down_weight, live):
+    tokens_here, model = mixed.shape
+    width = gate_weight.shape[1]
+    rows, eighth, cut = tokens_here // 4, model // 8, width // 2
+    hbm, vmem = pl.BlockSpec(memory_space=pl.ANY), pl.BlockSpec(memory_space=pltpu.VMEM)
+    row_piece = jax.ShapeDtypeStruct((2, eighth, width), BF)
+    col_piece = jax.ShapeDtypeStruct((2, cut, eighth), BF)
+    dma = pltpu.SemaphoreType.DMA
+    acc = pltpu.VMEM((4 * rows, width), F32)
+    act = pltpu.VMEM((4, tokens_here, width), BF)
+    tok = pltpu.VMEM((4, tokens_here, model), BF)
+    own = pltpu.VMEM((tokens_here, model), BF)
     return pl.pallas_call(
-        line_scatter_kernel,
-        name="line_scatter",
-        out_shape=jax.ShapeDtypeStruct(shape, F32),
-        in_specs=[pl.BlockSpec(memory_space=pl.ANY)],
-        out_specs=pl.BlockSpec(memory_space=pltpu.VMEM),
-        scratch_shapes=[pltpu.VMEM(shape, BF)] * 7
-        + [
-            pltpu.SemaphoreType.DMA((2,)),
-            pltpu.SemaphoreType.DMA((16,)),
-            pltpu.SemaphoreType.DMA((16,)),
+        middle_kernel,
+        name="feed_forward",
+        out_shape=(
+            jax.ShapeDtypeStruct(mixed.shape, F32),
+            jax.ShapeDtypeStruct((4,) + mixed.shape, BF),
+        )
+        + (row_piece,) * 4
+        + (col_piece,) * 4,
+        in_specs=[hbm] * 5 + [vmem],
+        out_specs=[vmem] + [hbm] * 9,
+        scratch_shapes=[
+            tok,
+            tok,
+            pltpu.VMEM(gate_weight.shape, BF),
+            pltpu.VMEM(up_weight.shape, BF),
+            pltpu.VMEM(down_weight.shape, BF),
+            acc,
+            acc,
+            acc,
+            act,
+            act,
+            act,
+            tok,
+            own,
+            own,
+            own,
+            own,
+            own,
+            pltpu.VMEM((2, 4, rows, model), BF),
+            pltpu.VMEM((2, 2, eighth, width), BF),
+            pltpu.VMEM((2, 2, eighth, width), BF),
+            pltpu.VMEM((2, 2, width, eighth), BF),
+            dma((5,)),
+            dma((16,)),
+            dma((16,)),
+            dma((16,)),
+            dma((16,)),
+            dma((2,)),
+            dma((3,)),
+            dma((3,)),
+            dma((8,)),
+            pltpu.SemaphoreType.REGULAR,
         ],
-        compiler_params=pltpu.CompilerParams(collective_id=3, has_side_effects=True),
-    )(terms)
+        compiler_params=pltpu.CompilerParams(
+            collective_id=5, has_side_effects=True, vmem_limit_bytes=64 * 1024 * 1024 - 65536
+        ),
+    )(mixed, cot, gate_weight, up_weight, down_weight, live)
 
 
 class Reduce:
@@ -614,6 +861,8 @@
             for second in (1 - b, b):
                 block = self.block(first, second)
                 self.add(block, self.pair.at[block])
+            if first is not a:
+                self.stage(1).start()
 
     def after_one(self):
         a, b = self.axes()
@@ -631,14 +880,58 @@
         return self.sum.at[self.y, self.x]
 
 
+class Half:
+    def __init__(self, me, kept, came, x_first, bufs, sems, k):
+        self.n, self.w, self.y, self.x, self.core = me
+        self.kept, self.came, self.x_first = kept, came, x_first
+        self.sum, self.one, self.two = bufs
+        self.sems, self.k = sems, k
+        self.rows = kept.shape[1]
+        self.next = flip(self.n, 4) if x_first else flip(self.n, 2)
+        self.here = self.y if x_first else self.x
+
+    def loads(self):
+        return [
+            pltpu.make_async_copy(self.kept, self.sum, self.sems[0].at[2 * self.k]),
+            pltpu.make_async_copy(self.came, self.one, self.sems[0].at[2 * self.k + 1]),
+        ]
+
+    def stage(self):
+        return send(
+            self.sum.at[1 - self.here],
+            self.two,
+            self.sems[1].at[self.k],
+            self.sems[2].at[self.k],
+            self.next,
+            self.w,
+        )
+
+    def add(self, block, other):
+        @pl.loop(0, self.rows // 64)
+        def _(i):
+            r = pl.ds(pl.multiple_of(i * 64, 64), 64)
+            self.sum[block, r, :] = self.sum[block, r, :] + other[r, :]
+
+    def after_one(self):
+        for cp in self.loads():
+            cp.wait()
+        self.add(1 - self.here, self.one.at[1 - self.here])
+        self.stage().start()
+        self.add(self.here, self.one.at[self.here])
+
+    def after_two(self):
+        self.stage().wait()
+        self.add(self.here, self.two)
+
+    def result(self):
+        return self.sum.at[self.here]
+
+
 class Spread:
-    def __init__(self, item, full, sems, k):
-        self.item, self.full, self.sems, self.k = item, full, sems, k
+    def __init__(self, item, region, sems, k):
+        self.item, self.region, self.sems, self.k = item, region, sems, k
         n = item.n
         self.blocks = (n, flip(n, 2), flip(n, 4), flip(flip(n, 2), 4))
-
-    def region(self, block):
-        return self.full.at[block, :, self.item.cols]
 
     def copy(self, kind, src, block, peer):
         k = 7 * self.k + kind
@@ -707,7 +1000,7 @@
         return self.ref.at[pl.ds(d * self.shape[1] + r.start, r.size), :]
 
 
-def last_kernel(items, n_attn, *refs):
+def last_kernel(items, *refs):
     refs = list(refs)
 
     def take(count):
@@ -715,33 +1008,51 @@
         del refs[:count]
         return out
 
-    parts = take(5)
+    parts = take(2)
+    stays, comes = take(4), take(4)
     feed_terms, gain_parts = take(2)
-    outs = take(n_attn)
-    full = take(3)
+    outs = take(4)
+    gate_full, up_full, down_full = take(3)
     feed_out, gain_out = take(2)
-    bufs = [take(4) for _ in items]
-    line_bufs = [take(6) for _ in range(n_attn)]
+    attn_bufs = [take(4) for _ in range(4)]
+    ffn_bufs = [take(3) for _ in range(4)]
+    line_bufs = [take(6) for _ in range(4)]
     feed_bufs = take(7)
     gain_in, gain_sum, gain_line = take(3)
     load_sem, swap_s, swap_r, st_s, st_r = take(5)
-    sp_s, sp_r, sp_l = take(3)
+    half_sems = take(3)
+    sp_sems = take(3)
     lr_s, lr_r, lg_s, lg_r, lg_l = take(5)
     fd_s, fd_r, fd_l = take(3)
     gn_s, gn_r, gz_s, gz_r = take(4)
 
     n, w = lax.axis_index("narrow"), lax.axis_index("wide")
     me = (n, w, n // 4, lax.rem(n // 2, 2), lax.rem(n, 2))
-    red = [
-        Reduce(me, parts[p], cols, xf, bufs[k], (load_sem, swap_s, swap_r, st_s, st_r), k)
+    attn = [
+        Reduce(me, parts[p], cols, xf, attn_bufs[k], (load_sem, swap_s, swap_r, st_s, st_r), k)
         for k, (p, cols, xf) in enumerate(items)
     ]
-    attn, ffn = red[:n_attn], red[n_attn:]
-    spread = [
-        Spread(item, full[items[n_attn + k][0] - 2], (sp_s, sp_r, sp_l), k)
-        for k, item in enumerate(ffn)
+    ffn = [
+        Half(me, stays[k], comes[k], k % 2 == 0, ffn_bufs[k], half_sems, k) for k in range(4)
     ]
-    for item in red:
+    cut, eighth = stays[2].shape[1], stays[2].shape[2]
+
+    def down_region(k):
+        return lambda block: down_full.at[
+            pl.ds(k * cut, cut), pl.ds(pl.multiple_of(block * eighth, eighth), eighth)
+        ]
+
+    regions = (
+        lambda block: gate_full.at[block],
+        lambda block: up_full.at[block],
+        down_region(0),
+        down_region(1),
+    )
+    spread = [Spread(ffn[k], regions[k], sp_sems, k) for k in range(4)]
+    for item in ffn:
+        for cp in item.loads():
+            cp.start()
+    for item in attn:
         item.load().start()
     mine, away = feed_bufs[0], feed_bufs[1]
     feed_loads = [
@@ -764,7 +1075,7 @@
         )
     pl.semaphore_wait(barrier, 10)
 
-    for item in red:
+    for item in attn:
         item.swap().start()
     feed = LineScatter(n, w, feed_terms, feed_bufs[2:], fd_s, fd_r, 4)
     feed.start()
@@ -779,28 +1090,14 @@
     for i in range(7):
         gain_narrow(i).start()
 
-    for item in attn:
-        item.after_swap()
-        item.stage(1).start()
+    for item in ffn:
+        item.after_one()
     for cp in feed_loads:
         cp.wait()
     feed.pass_on(0, away)
-    for item in ffn[:2]:
+    for item in attn:
         item.after_swap()
     feed.pass_on(1, away)
-    for item in attn[:2]:
-        item.after_one()
-    for item in ffn[:2]:
-        item.stage(1).start()
-    feed.pass_on(2, away)
-    for item in ffn[2:]:
-        item.after_swap()
-    feed.pass_on(3, away)
-    for item in attn[2:]:
-        item.after_one()
-    for item in ffn[2:]:
-        item.stage(1).start()
-
     for i in range(7):
         gain_narrow(i).wait()
     total = gain_parts[n]
@@ -809,6 +1106,15 @@
     gain_sum[...] = total
     for i in range(3):
         gain_wide(i).start()
+    feed.pass_on(2, away)
+    for item in attn[:2]:
+        item.after_one()
+    feed.pass_on(3, away)
+    for item in attn[2:]:
+        item.after_one()
+    for k in range(4):
+        ffn[k].after_two()
+        spread[k].start()
 
     scatters, gathers = [], []
     for k, item in enumerate(attn):
@@ -840,75 +1146,60 @@
     for k in (2, 3):
         attn[k].after_two()
         scatters[k].start()
-    for k in (0, 1):
+    for k in (0, 1, 2, 3):
         line_pass(k)
-    for item in ffn[:2]:
-        item.after_one()
-    for k in (2, 3):
-        line_pass(k)
-    for k in (0, 1):
+    for k in (0, 1, 2, 3):
         line_turn(k)
-    for item in ffn[2:]:
-        item.after_one()
-    for k in (2, 3):
-        line_turn(k)
-    for k in (0, 1):
+    for s in spread[:2]:
+        s.relay()
+    for k in (0, 1, 2, 3):
         gathers[k].forward(0)
-    for k in (0, 1):
-        ffn[k].after_two()
-        spread[k].start()
-    for k in (2, 3):
-        gathers[k].forward(0)
-    for k in (2, 3):
-        ffn[k].after_two()
-        spread[k].start()
+    for s in spread[2:]:
+        s.relay()
     for i in range(3):
         gain_wide(i).wait()
-    gain_out[...] = ((gain_sum[...] + gain_line[0]) + (gain_line[1] + gain_line[2]))
-    for s in spread:
-        s.relay()
+    gain_out[...] = (gain_sum[...] + gain_line[0]) + (gain_line[1] + gain_line[2])
     for s in spread:
         s.last()
     for s in spread:
         s.finish()
-    for item in red:
+    for item in attn:
         item.swap().wait_send()
-    for k in range(n_attn):
+    for k in range(4):
         scatters[k].drain()
         gathers[k].finish()
         keep(k).wait()
     feed.drain()
 
 
-def reduce_last(qkv_part, project_part, gate_part, up_part, down_part, feed_terms, gain_parts):
-    whole = [qkv_part, project_part, gate_part, up_part, down_part]
-    parts = [p.reshape(2, 2, 2, p.shape[0] // 8, p.shape[1]) for p in whole]
+def reduce_last(qkv_part, project_part, stays, comes, feed_terms, gain_parts):
+    parts = [p.reshape(2, 2, 2, p.shape[0] // 8, p.shape[1]) for p in (qkv_part, project_part)]
+    rows = parts[0].shape[3]
     items = []
     for p, xf in ((0, True), (0, False), (1, True), (1, False)):
         half = parts[p].shape[4] // 2
         items.append((p, (0 if xf else half, half), xf))
-    n_attn = len(items)
-    items.append((2, (0, gate_part.shape[1]), True))
-    items.append((3, (0, up_part.shape[1]), False))
-    half = down_part.shape[1] // 2
-    items.append((4, (0, half), True))
-    items.append((4, (half, half), False))
     scratch = []
-    for p, (_, cols), _ in items:
-        rows = parts[p].shape[3]
+    for _, (_, cols), _ in items:
         scratch += [
             pltpu.VMEM((2, 2, rows, cols), BF),
             pltpu.VMEM((2, 2, rows, cols), BF),
             pltpu.VMEM((2, rows, cols), BF),
             pltpu.VMEM((rows, cols), BF),
         ]
+    for stay in stays:
+        scratch += [
+            pltpu.VMEM(stay.shape, BF),
+            pltpu.VMEM(stay.shape, BF),
+            pltpu.VMEM(stay.shape[1:], BF),
+        ]
     outs = []
-    for p, (_, cols), _ in items[:n_attn]:
-        quarter = (parts[p].shape[3] // 4, cols)
-        scratch += [pltpu.VMEM(quarter, BF)] * 6
-        outs.append(jax.ShapeDtypeStruct((4,) + quarter, BF))
-    for part in parts[2:]:
-        outs.append(jax.ShapeDtypeStruct((8,) + part.shape[3:], BF))
+    for _, (_, cols), _ in items:
+        scratch += [pltpu.VMEM((rows // 4, cols), BF)] * 6
+        outs.append(jax.ShapeDtypeStruct((4, rows // 4, cols), BF))
+    outs.append(jax.ShapeDtypeStruct((8,) + stays[0].shape[1:], BF))
+    outs.append(jax.ShapeDtypeStruct((8,) + stays[1].shape[1:], BF))
+    outs.append(jax.ShapeDtypeStruct((2 * stays[2].shape[1], 8 * stays[2].shape[2]), BF))
     outs.append(jax.ShapeDtypeStruct(feed_terms.shape[1:], F32))
     outs.append(jax.ShapeDtypeStruct(gain_parts.shape[1:], F32))
     scratch += [pltpu.VMEM(feed_terms.shape[1:], BF)] * 7
@@ -918,29 +1209,29 @@
         pltpu.VMEM((3,) + gain_parts.shape[1:], F32),
     ]
     dma = pltpu.SemaphoreType.DMA
-    k, f = len(items), len(items) - n_attn
-    scratch += [dma((k,)), dma((k,)), dma((k,)), dma((2 * k,)), dma((2 * k,))]
-    scratch += [dma((7 * f,)), dma((7 * f,)), dma((f,))]
-    scratch += [dma((n_attn, 4))] * 4 + [dma((n_attn,))]
+    scratch += [dma((4,)), dma((4,)), dma((4,)), dma((8,)), dma((8,))]
+    scratch += [dma((8,)), dma((4,)), dma((4,))]
+    scratch += [dma((28,)), dma((28,)), dma((4,))]
+    scratch += [dma((4, 4))] * 4 + [dma((4,))]
     scratch += [dma((16,)), dma((16,)), dma((2,))]
     scratch += [dma((7,)), dma((7,)), dma((3,)), dma((3,))]
     hbm, vmem = pl.BlockSpec(memory_space=pl.ANY), pl.BlockSpec(memory_space=pltpu.VMEM)
     out = pl.pallas_call(
-        functools.partial(last_kernel, items, n_attn),
+        functools.partial(last_kernel, items),
         name="reduce_last",
         out_shape=tuple(outs),
-        in_specs=[hbm] * 6 + [vmem],
-        out_specs=[hbm] * (n_attn + 3) + [vmem] * 2,
+        in_specs=[hbm] * 11 + [vmem],
+        out_specs=[hbm] * 7 + [vmem] * 2,
         scratch_shapes=scratch,
         compiler_params=pltpu.CompilerParams(
             collective_id=4, has_side_effects=True, vmem_limit_bytes=64 * 1024 * 1024 - 65536
         ),
-    )(*parts, feed_terms, gain_parts)
-    rows = parts[0].shape[3]
+    )(*parts, *stays, *comes, feed_terms, gain_parts)
     qkv = jnp.concatenate([out[0].reshape(rows, -1), out[1].reshape(rows, -1)], axis=1)
     project = jnp.concatenate([out[2].reshape(rows, -1), out[3].reshape(rows, -1)], axis=1)
-    ffn = [o.reshape(-1, o.shape[2]) for o in out[n_attn : n_attn + 3]]
-    return qkv, project, ffn, out[n_attn + 3], out[n_attn + 4]
+    width = out[4].shape[2]
+    ffn = [out[4].reshape(-1, width), out[5].reshape(-1, width), out[6]]
+    return qkv, project, ffn, out[7], out[8]
 
 
 def per_device(
@@ -965,7 +1256,6 @@
         qkv_full, project_full, gains_full, grad_rows = gather_first(
             query_weight, key_weight, value_weight, project_weight, gains, cotangent
         )
-        grad_rows = grad_rows.reshape(-1, model)
         gains_full = gains_full.reshape(8, 2, -1)
         first_gain = gains_full[:, 0].reshape(-1)
         second_gain = gains_full[:, 1].reshape(-1)
@@ -1013,39 +1303,43 @@
     branch = jnp.dot(attended, project_full, preferred_element_type=jnp.float32)
     middle = inputs_f + branch
     mixed_in = rms_scale(middle, second_gain).astype(jnp.bfloat16)
-    if fast:
-        gathered = line_gather(mixed_in).reshape(-1, model)
-    else:
-        gathered = lax.all_gather(mixed_in, "wide", axis=0, tiled=True)
     width = gate_weight.shape[1]
     wide_index = lax.axis_index("wide")
     my_count = jnp.sum(
         jnp.where(jnp.arange(tile_counts.shape[0], dtype=jnp.int32) == wide_index, tile_counts, 0)
     )
     live = (jnp.arange(width, dtype=jnp.int32) // TILE < my_count).astype(jnp.float32)
-    gate_pre = jnp.dot(gathered, gate_weight, preferred_element_type=jnp.float32)
-    up_pre = jnp.dot(gathered, up_weight, preferred_element_type=jnp.float32)
-    hidden_back = contract_cols(grad_rows, down_weight)
-    sigma = jax.nn.sigmoid(gate_pre)
-    hidden = (gate_pre * sigma * up_pre * live).astype(jnp.bfloat16)
-    gate_back = (hidden_back * up_pre * live * sigma * (1.0 + gate_pre * (1.0 - sigma))).astype(
-        jnp.bfloat16
-    )
-    up_back = (hidden_back * gate_pre * sigma * live).astype(jnp.bfloat16)
-    mixed_terms = (
-        contract_cols(gate_back, gate_weight) + contract_cols(up_back, up_weight)
-    ).astype(jnp.bfloat16)
     if fast:
-        mixed_back = line_scatter(mixed_terms.reshape(4, tokens_here, model))
+        mixed_back, feed_terms, *pieces = feed_forward(
+            mixed_in, grad_rows, gate_weight, up_weight, down_weight, live.reshape(1, -1)
+        )
+        stays = pieces[1::2]
+        comes = [
+            lax.ppermute(piece, "narrow", [(i, i ^ bit) for i in range(8)])
+            for piece, bit in zip(pieces[0::2], (2, 4, 2, 4))
+        ]
     else:
+        gathered = lax.all_gather(mixed_in, "wide", axis=0, tiled=True)
+        gate_pre = jnp.dot(gathered, gate_weight, preferred_element_type=jnp.float32)
+        up_pre = jnp.dot(gathered, up_weight, preferred_element_type=jnp.float32)
+        hidden_back = contract_cols(grad_rows, down_weight)
+        sigma = jax.nn.sigmoid(gate_pre)
+        hidden = (gate_pre * sigma * up_pre * live).astype(BF)
+        gate_back = (
+            hidden_back * up_pre * live * sigma * (1.0 + gate_pre * (1.0 - sigma))
+        ).astype(BF)
+        up_back = (hidden_back * gate_pre * sigma * live).astype(BF)
+        mixed_terms = (
+            contract_cols(gate_back, gate_weight) + contract_cols(up_back, up_weight)
+        ).astype(BF)
         mixed_back = lax.psum_scatter(
             mixed_terms, "wide", scatter_dimension=0, tiled=True
         ).astype(F32)
-    partial_rows = jnp.dot(hidden, down_weight, preferred_element_type=jnp.float32)
+        partial_rows = jnp.dot(hidden, down_weight, preferred_element_type=jnp.float32)
+        down_part = contract_rows(hidden, grad_rows)
+        gate_part = contract_rows(gathered, gate_back)
+        up_part = contract_rows(gathered, up_back)
     out_grad = cotangent.astype(jnp.float32)
-    down_part = contract_rows(hidden, grad_rows)
-    gate_part = contract_rows(gathered, gate_back)
-    up_part = contract_rows(gathered, up_back)
     unused_second, second_backward = jax.vjp(rms_scale, middle, second_gain)
     middle_norm_back, second_gain_part = second_backward(mixed_back)
     middle_back = out_grad + middle_norm_back
@@ -1107,10 +1401,9 @@
         qkv_total, project_total, ffn_totals, feed, gain_total = reduce_last(
             qkv_part.astype(BF),
             project_part.astype(BF),
-            gate_part.astype(BF),
-            up_part.astype(BF),
-            down_part.astype(BF),
-            partial_rows.astype(BF).reshape(4, tokens_here, model),
+            stays,
+            comes,
+            feed_terms,
             gain_parts,
         )
         gain_total = gain_total.reshape(2, -1)

time: 606 us -> 488 us (0.81)
  matrix products: 120 us -> 49.4 us
  Pallas kernels: 427 us -> 371 us
    pallas_call x3 -> x2, Pallas kernels: 351 us -> 295 us  [the longest x1 153 us: reduce_last(): pl.pallas_call(functools.partial(last_kernel, items), name='reduce_last',...]
    dot_general x3 -> x0, matrix products: 29.1 us -> none  [the longest x1 11.6 us: per_device(): up_pre = jnp.dot(gathered, up_weight, preferred_element_type=jnp.float32)]
    dot_general x5 -> x2, matrix products: 36.1 us -> 13.8 us  [contract_cols(): lax.dot_general(left, right, (((1,), (1,)), ((), ())), preferred_element_...]
    dot_general x5 -> x2, matrix products: 31.9 us -> 11.2 us  [contract_rows(): lax.dot_general(left, right, (((0,), (0,)), ((), ())), preferred_element_...]
  transfers between devices with their start and end apart: 0 -> 4, of which waited for: 0 -> 0; matrix products, arithmetic and copies ran while one was open for 0% -> 11% of each run, Pallas kernels for 0% -> 0%
where the time goes in v3:
time: 488 us; the launch traced here: 480 us
  Pallas kernels  371 us (76%)
  matrix products  49.4 us (10%)
  other arithmetic  42.1 us (9%)
  local copies, waits for them, and re-layouts  12.2 us (2%)
    pallas_call x1, Pallas kernels, reduce_last(): pl.pallas_call(functools.partial(last_kernel, items), name='reduce_last',...  153 us
    pallas_call x1, Pallas kernels, feed_forward(): pl.pallas_call(middle_kernel, name='feed_forward', out_shape=(jax.ShapeDt...  142 us
    pallas_call x1, Pallas kernels, gather_first(): pl.pallas_call(first_kernel, name='gather_first', out_shape=(jax.ShapeDty...  75.6 us
    convert_element_type x2, other arithmetic, per_device(): gate_total, up_total, down_total = [t.astype(F32) for t in ffn_totals]  19.1 us
    dot_general x2, matrix products, contract_cols(): lax.dot_general(left, right, (((1,), (1,)), ((), ())), preferred_element_...  13.8 us
    dot_general x2, matrix products, contract_rows(): lax.dot_general(left, right, (((0,), (0,)), ((), ())), preferred_element_...  11.2 us
  transfers between devices with their start and end apart: 4, of which 0 were waited for; matrix products, arithmetic and copies ran while one was open for 11% of the time, Pallas kernels for 0%

profile of v3, /device:TPU:0, one launch (start us, length us, event | category | flops | bytes accessed | tf_op | source)
XLA Modules:
  0.0 480.0 jit_solution(18232376962404645858)
XLA Ops:
  0.6 0.0 copy-start.4
  0.7 1.6 fusion.19
  2.3 0.7 stack.12
  2.9 0.7 stack.13
  3.6 0.6 copy.66
  4.2 75.6 %gather_first.1 = (bf16[2048,2304]{1,0:T(8,128)(2,1)}, bf16[1536,2048]{1,0:T(8,128)(2,1)}, f32[8,1,512]{2,1,0:T(1,128)}, bf16[4,256,2048]{2,1,0:T(8,128)(2,1)}) custom-call(bf16[256,1536]{1,0:T(8,128)(2,1)} %q_ref.1, bf16[256,384]{1,0:T(8,128)(2,1)} %k_ref.1, bf16[256,384]{1,0:T(8,128)(2,1)} %v_ref.1, bf16[1536,256]{1,0:T(8,128)(2,1)} %p_ref.1, ...), custom_call_target="tpu_custom_call" | custom-call | tf_op jit(solution)/shard_map/gather_first/pallas_call | solution.py:341
  79.8 0.8 reduce
  80.7 6.3 %convolution_convert_fusion.2 = bf16[256,2304]{1,0:T(8,128)(2,1)S(1)} fusion(bf16[2048,2304]{1,0:T(8,128)(2,1)} %get-tuple-element.35, bf16[256,2048]{1,0:T(8,128)(2,1)S(1)} %copy-done.4, f32[2048]{0:T(1024)S(1)} %bitcast.149, f32[256]{0:T(256)S(1)} %fusion.36), kind=kOutput, calls=%fused_computation.22 | convolution fusion | flops 2418606080 | bytes 11674624 | tf_op jit(solution)/shard_map/dot_general | solution.py:1280
  87.0 0.0 copy-start.39
  87.1 0.1 slice.45
  87.2 0.5 copy-done.39
  87.7 0.2 reduce-window.8
  87.9 0.1 convert_reduce_fusion
  88.0 0.6 fusion.38
  88.6 1.2 compare_convert_fusion.live
  89.8 0.1 fusion.35
  90.0 0.3 copy.50
  90.2 0.0 copy-start.7
  90.3 0.1 copy.49
  90.4 0.1 copy.48
  90.6 0.0 copy-start.18
  90.6 1.1 fusion.5
  91.7 0.0 copy-start
  91.7 1.3 fusion.6
  93.1 1.3 copy-done
  94.4 1.8 fusion.21
  96.2 0.7 slice-done.3
  96.8 1.9 multiply_reduce_fusion.2
  98.8 0.0 copy-start.1
  98.8 1.3 copy-done.1
  100.1 1.2 multiply_convert_fusion.mixed
  101.3 142.4 %feed_forward.1 = (f32[256,2048]{1,0:T(8,128)}, bf16[4,256,2048]{2,1,0:T(8,128)(2,1)}, bf16[2,256,1152]{2,1,0:T(8,128)(2,1)}, bf16[2,256,1152]{2,1,0:T(8,128)(2,...) custom-call(bf16[256,2048]{1,0:T(8,128)(2,1)} %multiply_convert_fusi, ...), custom_call_target="tpu_custom_call" | custom-call | tf_op jit(solution)/shard_map/feed_forward/pallas_call | solution.py:754
  243.8 0.7 collective-permute-start.2
  244.5 1.0 collective-permute-start.3
  245.5 1.1 collective-permute-start
  246.6 1.4 collective-permute-start.1
  247.9 2.7 multiply_reduce_fusion
  250.7 1.9 fusion.16
  252.7 5.5 %convolution_convert_fusion.3 = bf16[256,1536]{1,0:T(8,128)(2,1)} fusion(bf16[1536,2048]{1,0:T(8,128)(2,1)} %get-tuple-element.36, f32[256,2048]{1,0:T(8,128)S(1)} %fusion.16), kind=kOutput, calls=%fused_computation.29 | convolution fusion | flops 1611530240 | bytes 9175040 | tf_op jit(solution)/shard_map/dot_general | solution.py:34
  258.2 1.4 copy.52
  259.7 4.2 fusion.27
  263.9 0.0 slice-start.1
  263.9 7.4 %fusion = (f32[6,4,256]{2,1,0:T(4,128)S(1)}, f32[6,256,256,4]{2,1,3,0:T(8,128)}) fusion(f32[6,256,256,4]{2,1,3,0:T(8,128)} %copy-done, f32[6,4,256]{2,1,0:T(4,128)S(1)} %bitcast.147, pred[256,256]{0,1:T(8,128)(4,1)S(1)} %copy-done.17, bf16[256,6,64,1]{0,2,3,1:T(8,128)(2,1)S(1)} %bitcast.142, bf16[256,6,4,64]{0,3,2,1:T(8,128)(2,1)S(1)} %bitcast.130), kind=kOutput, calls=%fused_computation.4 | convolution fusion | flops 209184768 | bytes 13680640 | tf_op jit(solution)/shard_map/qcgd,kcd->cgqk/dot_general | solution.py:1366
  271.3 4.7 fusion.2
  276.1 1.1 fusion.26
  277.2 0.7 multiply_convert_fusion.1
  277.8 0.5 copy-done.5
  278.4 8.2 %fusion.20 = (f32[256]{0:T(256)S(1)}, f32[2048]{0:T(1024)S(1)}, f32[256,2048]{1,0:T(8,128)}) fusion(bf16[256,2048]{1,0:T(8,128)(2,1)S(1)} %copy-done.5, f32[2048]{0:T(1024)S(1)} %bitcast.150, f32[256]{0:T(256)S(1)} %copy-done.31, bf16[2048,2304]{1,0:T(8,128)(2,1)} %get-tuple-element.35, bf16[256,384]{0,1:T(8,128)(2,1)S(1)} %bitcast.153, ...), kind=kOutput, calls=%fused_computation.38 | convolution fusion | flops 2423125760 | bytes 13780992 | tf_op jit(solution)/shard_map/dot_general | solution.py:34
  286.6 5.4 %convolution_convert_fusion = bf16[2048,2304]{1,0:T(8,128)(2,1)} fusion(bf16[256,384]{0,1:T(8,128)(2,1)S(1)} %bitcast.154, bf16[256,384]{0,1:T(8,128)(2,1)S(1)} %bitcast.140, bf16[256,1536]{0,1:T(8,128)(2,1)S(1)} %bitcast.132, bf16[256,2048]{1,0:T(8,128)(2,1)S(1)} %copy-done.5, f32[2048]{0:T(1024)S(1)} %bitcast.151, f32[256]{0:T(256)S(1)} %copy-done.31), kind=kOutput, calls=%fused_computation | convolution fusion | flops 2426273792 | bytes 11674624 | tf_op jit(solution)/shard_map/dot_general | solution.py:28
  292.0 0.6 reshape.227.refs_11_
  292.7 5.8 %convolution_convert_fusion.1 = bf16[2048,1536]{1,0:T(8,128)(2,1)} fusion(bf16[256,1536]{0,1:T(8,128)(2,1)} %bitcast.128, f32[256,2048]{1,0:T(8,128)S(1)} %fusion.16), kind=kOutput, calls=%fused_computation.1 | convolution fusion | flops 1614282752 | bytes 9175040 | tf_op jit(solution)/shard_map/dot_general | solution.py:28
  298.5 1.6 fusion.18
  300.2 152.7 %reduce_last.1 = (bf16[4,64,1152]{2,1,0:T(8,128)(2,1)}, bf16[4,64,1152]{2,1,0:T(8,128)(2,1)}, bf16[4,64,768]{2,1,0:T(8,128)(2,1)}, bf16[4,64,768]{2,1,0:T(8,128)...) custom-call(bf16[2,2,2,256,2304]{4,3,2,1,0:T(8,128)(2,1)} %bitcast.1, ...), custom_call_target="tpu_custom_call" | custom-call | tf_op jit(solution)/shard_map/reduce_last/pallas_call | solution.py:1219
  452.9 2.1 maximum_convert_fusion.1
  455.0 0.2 maximum_convert_fusion
  455.2 0.8 copy-done.13
  455.9 1.2 add_convert_fusion
  457.2 0.6 fusion.47
  457.7 0.2 copy.56
  457.9 0.2 copy.57
  458.1 1.4 slice.47
  459.4 7.3 %convert_element_type.149 = f32[1152,2048]{1,0:T(8,128)} convert(bf16[1152,2048]{1,0:T(8,128)(2,1)} %get-tuple-element.56) | non-fusion elementwise | flops 2359296 | bytes 14155776 | tf_op jit(solution)/shard_map/convert_element_type | solution.py:1413
  466.7 1.3 convert_bitcast_fusion
  468.0 11.8 %bitcast_convert_fusion = (f32[2048,1152]{1,0:T(8,128)}, f32[2048,1152]{1,0:T(8,128)}) fusion(bf16[8,256,1152]{2,1,0:T(8,128)(2,1)} %get-tuple-element.55, bf16[8,256,1152]{2,1,0:T(8,128)(2,1)} %get-tuple-element.54), kind=kLoop, calls=%fused_computation.15 | loop fusion | flops 4718592 | bytes 28311552 | tf_op jit(solution)/shard_map/convert_element_type | solution.py:1413
  (93 shorter events, 0.4 us)
Async XLA Ops:
  0.6 80.0 %copy-start.4 = (bf16[256,2048]{1,0:T(8,128)(2,1)S(1)}, bf16[256,2048]{1,0:T(8,128)(2,1)}, u32[]{:S(2)}) copy-start(bf16[256,2048]{1,0:T(8,128)(2,1)} %param.13) | copy-start | bytes 3145732
  2.3 77.6 %copy-start.34 = (f32[256]{0:T(256)}, f32[256]{0:T(256)S(1)}, u32[]{:S(2)}) copy-start(f32[256]{0:T(256)S(1)} %fusion.19) | copy-start | bytes 3076
  2.3 84.7 %copy-start.30 = (f32[256]{0:T(256)}, f32[256]{0:T(256)S(1)}, u32[]{:S(2)}) copy-start(f32[256]{0:T(256)S(1)} %fusion.36) | copy-start | bytes 3076
  80.6 6.4 %copy-start.24 = (f32[8,1,256]{2,1,0:T(1,128)}, f32[8,1,256]{2,1,0:T(1,128)S(1)}, u32[]{:S(2)}) copy-start(f32[8,1,256]{2,1,0:T(1,128)S(1)} %get-tuple-element.66) | copy-start | bytes 24580
  80.7 18.2 %copy-start.26 = (f32[8,1,256]{2,1,0:T(1,128)}, f32[8,1,256]{2,1,0:T(1,128)S(1)}, u32[]{:S(2)}) copy-start(f32[8,1,256]{2,1,0:T(1,128)S(1)} %get-tuple-element.65) | copy-start | bytes 24580
  87.0 0.7 copy-start.39
  87.1 0.9 copy-start.40
  90.0 3.1 copy-start.16
  90.2 1.4 copy-start.7
  90.4 1.2 copy-start.14
  90.6 2.5 copy-start.18
  91.7 2.7 copy-start
  91.7 2.7 copy-start.22
  93.0 3.1 copy-start.28
  93.0 3.1 slice-start.2
  94.4 2.5 slice-start.3
  96.1 2.6 copy-start.9
  98.8 1.3 copy-start.1
  98.8 2.5 copy-start.36
  98.8 2.5 copy-start.32
  243.8 6.9 %copy-start.37 = (f32[256]{0:T(256)S(1)}, f32[256]{0:T(256)}, u32[]{:S(2)}) copy-start(f32[256]{0:T(256)} %copy-done.36) | copy-start | bytes 3076
  243.8 6.9 %copy-start.2 = (f32[256,2048]{1,0:T(8,128)S(1)}, f32[256,2048]{1,0:T(8,128)}, u32[]{:S(2)}) copy-start(f32[256,2048]{1,0:T(8,128)} %copy-done.1) | copy-start | bytes 6291460
  243.8 6.9 %copy-start.6 = (f32[256,2048]{1,0:T(8,128)S(1)}, f32[256,2048]{1,0:T(8,128)}, u32[]{:S(2)}) copy-start(f32[256,2048]{1,0:T(8,128)} %get-tuple-element.38) | copy-start | bytes 6291460
  243.8 6.9 %copy-start.27 = (f32[8,1,256]{2,1,0:T(1,128)S(1)}, f32[8,1,256]{2,1,0:T(1,128)}, u32[]{:S(2)}) copy-start(f32[8,1,256]{2,1,0:T(1,128)} %copy-done.26) | copy-start | bytes 24580
  243.8 6.9 %copy-start.33 = (f32[256]{0:T(256)S(1)}, f32[256]{0:T(256)}, u32[]{:S(2)}) copy-start(f32[256]{0:T(256)} %copy-done.32) | copy-start | bytes 3076
  243.8 56.3 %collective-permute-start.2 = (bf16[2,576,256]{2,1,0:T(8,128)(2,1)}, bf16[2,576,256]{2,1,0:T(8,128)(2,1)}, u32[]{:S(2)}, u32[]{:S(2)}) collective-permute-start(bf16[2,576,256]{2,1,0:T(8,128)(2,1)} %get-tuple-element.45), channel_id=1, source_target_pairs={{0,8},{4,12},{8,0},{12,4},{16,24},{20,28},{24,16},{28,20},{1,9},{5... | collective-permute-start | bytes 1769480 | tf_op jit(solution)/shard_map/ppermute | solution.py:1318
  244.5 55.6 %collective-permute-start.3 = (bf16[2,576,256]{2,1,0:T(8,128)(2,1)}, bf16[2,576,256]{2,1,0:T(8,128)(2,1)}, u32[]{:S(2)}, u32[]{:S(2)}) collective-permute-start(bf16[2,576,256]{2,1,0:T(8,128)(2,1)} %get-tuple-element.46), channel_id=1, source_target_pairs={{0,16},{4,20},{8,24},{12,28},{16,0},{20,4},{24,8},{28,12},{1,17},{... | collective-permute-start | bytes 1769480 | tf_op jit(solution)/shard_map/ppermute | solution.py:1318
  245.5 54.6 %collective-permute-start = (bf16[2,256,1152]{2,1,0:T(8,128)(2,1)}, bf16[2,256,1152]{2,1,0:T(8,128)(2,1)}, u32[]{:S(2)}, u32[]{:S(2)}) collective-permute-start(bf16[2,256,1152]{2,1,0:T(8,128)(2,1)} %get-tuple-element.43), channel_id=1, source_target_pairs={{0,8},{4,12},{8,0},{12,4},{16,24},{20,28},{24,16},{28,20},{1,9},{5... | collective-permute-start | bytes 3538952 | tf_op jit(solution)/shard_map/ppermute | solution.py:1318
  246.6 53.6 %collective-permute-start.1 = (bf16[2,256,1152]{2,1,0:T(8,128)(2,1)}, bf16[2,256,1152]{2,1,0:T(8,128)(2,1)}, u32[]{:S(2)}, u32[]{:S(2)}) collective-permute-start(bf16[2,256,1152]{2,1,0:T(8,128)(2,1)} %get-tuple-element.44), channel_id=1, source_target_pairs={{0,16},{4,20},{8,24},{12,28},{16,0},{20,4},{24,8},{28,12},{1,17},{... | collective-permute-start | bytes 3538952 | tf_op jit(solution)/shard_map/ppermute | solution.py:1318
  252.6 7.0 %copy-start.23 = (f32[6,4,256]{2,1,0:T(4,128)S(1)}, f32[6,4,256]{2,1,0:T(4,128)}, u32[]{:S(2)}) copy-start(f32[6,4,256]{2,1,0:T(4,128)} %copy-done.22) | copy-start | bytes 73732
  252.6 7.0 %copy-start.29 = (f32[6,4,256]{2,1,0:T(4,128)S(1)}, f32[6,4,256]{2,1,0:T(4,128)}, u32[]{:S(2)}) copy-start(f32[6,4,256]{2,1,0:T(4,128)} %copy-done.28) | copy-start | bytes 73732
  252.6 7.0 %copy-start.17 = (pred[256,256]{0,1:T(8,128)(4,1)S(1)}, pred[256,256]{0,1:T(8,128)(4,1)}, u32[]{:S(2)}) copy-start(pred[256,256]{0,1:T(8,128)(4,1)} %copy-done.16) | copy-start | bytes 196612
  259.6 4.2 copy-start.19
  259.7 11.6 %slice-start = ((s8[6291456]{0:T(1024)(128)(4,1)}), s8[4194304]{0:T(1024)(128)(4,1)S(1)}, s32[]{:S(2)}) async-start(s8[6291456]{0:T(1024)(128)(4,1)} %bitcast.119), calls=%async_computation | async-start | bytes 8388608
  263.9 7.4 %slice-start.1 = ((s8[6291456]{0:T(1024)(128)(4,1)}), s8[2097152]{0:T(1024)(128)(4,1)S(1)}, s32[]{:S(2)}) async-start(s8[6291456]{0:T(1024)(128)(4,1)} %bitcast.119), calls=%async_computation.1 | async-start | bytes 4194304
  271.3 4.8 copy-start.8
  276.1 1.1 copy-start.15
  277.1 1.2 copy-start.5
  277.2 1.2 copy-start.25
  277.2 1.2 copy-start.31
  286.6 6.1 %copy-start.35 = (f32[256]{0:T(256)S(1)}, f32[256]{0:T(256)}, u32[]{:S(2)}) copy-start(f32[256]{0:T(256)} %copy-done.34) | copy-start | bytes 3076
  292.7 5.9 %copy-start.12 = (f32[256,2048]{1,0:T(8,128)S(1)}, f32[256,2048]{1,0:T(8,128)}, u32[]{:S(2)}) copy-start(f32[256,2048]{1,0:T(8,128)} %get-tuple-element.75) | copy-start | bytes 6291460
  452.8 2.1 copy-start.10
  452.9 2.1 copy-start.11
  452.9 2.3 copy-start.3
  452.9 3.0 copy-start.13
  455.9 1.2 copy-start.38
  455.9 1.8 copy-start.21
  455.9 2.0 copy-start.20

commit v4 on v3

--- a/solution.py
+++ b/solution.py
@@ -64,9 +64,6 @@
     if not line:
         pl.semaphore_wait(barrier, len(narrow_peers))
     if line:
-        pl.semaphore_signal(
-            barrier, inc=1, device_id=at(n, flip(w, 2)), device_id_type=pl.DeviceIdType.MESH
-        )
 
         @pl.when(w > 0)
         def _():
@@ -82,16 +79,14 @@
 
         @pl.when((w == 0) | (w == 3))
         def _():
+            pl.semaphore_wait(barrier, len(narrow_peers) + 1)
+
+        @pl.when((w == 1) | (w == 2))
+        def _():
             pl.semaphore_wait(barrier, len(narrow_peers) + 2)
 
-        @pl.when((w == 1) | (w == 2))
-        def _():
-            pl.semaphore_wait(barrier, len(narrow_peers) + 3)
-
 
 class LineGather:
-    KINDS = 4
-
     def __init__(self, n, w, own, whole, ssem, rsem, chunks):
         self.n, self.w, self.own, self.whole = n, w, own, whole
         self.ssem, self.rsem, self.chunks = ssem, rsem, chunks
@@ -103,82 +98,78 @@
     def part(self, shard, i):
         return self.whole.at[shard, self.span(i), :]
 
-    def mine(self, i):
-        return self.own.at[self.span(i), :]
-
-    def copy(self, kind, i, src, shard, w):
-        k = kind * self.chunks + i
-        return send(src, self.part(shard, i), self.ssem.at[k], self.rsem.at[k], self.n, w)
-
-    def far(self, i):
-        return self.copy(0, i, self.mine(i), self.w, flip(self.w, 2))
-
-    def left(self, i):
-        return self.copy(1, i, self.mine(i), self.w, jnp.maximum(self.w - 1, 0))
-
-    def right(self, i):
-        return self.copy(2, i, self.mine(i), self.w, jnp.minimum(self.w + 1, 3))
-
-    def onward(self, i):
-        shard = flip(self.w, 2)
-        return self.copy(3, i, self.part(shard, i), shard, 3 * (self.w // 2))
-
-    def middle(self):
-        return (self.w == 1) | (self.w == 2)
+    def put(self, way, here, shard, i):
+        src = self.own.at[self.span(i), :] if shard is here else self.part(shard, i)
+        to = here + 1 - 2 * way
+        s = (way * 4 + shard) * self.chunks + i
+        r = shard * self.chunks + i
+        return send(src, self.part(shard, i), self.ssem.at[s], self.rsem.at[r], self.n, to)
+
+    def came(self, shard, i):
+        self.put(0, 0, shard, i).wait_recv()
 
     def start_chunk(self, i):
-        self.far(i).start()
+        @pl.when(self.w < 3)
+        def _():
+            self.put(0, self.w, self.w, i).start()
 
         @pl.when(self.w > 0)
         def _():
-            self.left(i).start()
-
-        @pl.when(self.w < 3)
-        def _():
-            self.right(i).start()
+            self.put(1, self.w, self.w, i).start()
 
     def start(self):
         for i in range(self.chunks):
             self.start_chunk(i)
 
-    def forward(self, i):
-        self.far(i).wait_recv()
-
-        @pl.when(self.middle())
-        def _():
-            self.onward(i).start()
+    def near(self, i):
+        @pl.when(self.w == 1)
+        def _():
+            self.came(0, i)
+            self.put(0, 1, 0, i).start()
+            self.came(2, i)
+            self.put(1, 1, 2, i).start()
+
+        @pl.when(self.w == 2)
+        def _():
+            self.came(3, i)
+            self.put(1, 2, 3, i).start()
+            self.came(1, i)
+            self.put(0, 2, 1, i).start()
+
+    def far(self, i):
+        @pl.when(self.w == 1)
+        def _():
+            self.came(3, i)
+            self.put(1, 1, 3, i).start()
+
+        @pl.when(self.w == 2)
+        def _():
+            self.came(0, i)
+            self.put(0, 2, 0, i).start()
 
     def ready(self, i):
-        @pl.when(self.w > 0)
-        def _():
-            self.right(i).wait_recv()
-
-        @pl.when(self.w < 3)
-        def _():
-            self.left(i).wait_recv()
-
-        @pl.when((self.w == 0) | (self.w == 3))
-        def _():
-            self.onward(i).wait_recv()
+        @pl.when(self.w == 0)
+        def _():
+            for shard in (1, 2, 3):
+                self.came(shard, i)
+
+        @pl.when(self.w == 3)
+        def _():
+            for shard in (2, 1, 0):
+                self.came(shard, i)
 
     def finish_sends(self):
-        for i in range(self.chunks):
-            self.far(i).wait_send()
-
-        @pl.when(self.w > 0)
-        def _():
-            for i in range(self.chunks):
-                self.left(i).wait_send()
-
-        @pl.when(self.w < 3)
-        def _():
-            for i in range(self.chunks):
-                self.right(i).wait_send()
-
-        @pl.when(self.middle())
-        def _():
-            for i in range(self.chunks):
-                self.onward(i).wait_send()
+        for here in range(4):
+
+            @pl.when(self.w == here)
+            def _():
+                for i in range(self.chunks):
+                    if here < 3:
+                        for shard in range(here + 1):
+                            self.put(0, here, shard, i).wait_send()
+                    if here > 0:
+                        for shard in range(here, 4):
+                            self.put(1, here, shard, i).wait_send()
 
     def finish(self):
         for i in range(self.chunks):
@@ -309,14 +300,16 @@
         on_y(t).wait_recv()
         to_c(t, 3).start()
 
-    line.forward(0)
+    for i in range(3):
+        line.near(i)
     relay(0)
-    line.forward(1)
+    line.near(3)
     relay(1)
     relay(2)
-    line.forward(2)
+    for i in range(3):
+        line.far(i)
     relay(3)
-    line.forward(3)
+    line.far(3)
     for t in range(4):
         corner(t)
     for t in range(4):
@@ -362,7 +355,7 @@
             pltpu.SemaphoreType.DMA((40,)),
             pltpu.SemaphoreType.DMA((7,)),
             pltpu.SemaphoreType.DMA((7,)),
-            pltpu.SemaphoreType.DMA((16,)),
+            pltpu.SemaphoreType.DMA((32,)),
             pltpu.SemaphoreType.DMA((16,)),
         ],
         compiler_params=pltpu.CompilerParams(collective_id=1, has_side_effects=True),
@@ -371,125 +364,91 @@
 
 class LineScatter:
     def __init__(self, n, w, terms, bufs, ssem, rsem, chunks):
-        self.n, self.w, self.terms = n, w, terms
-        self.from_left, self.from_right, self.from_far, self.relayed, self.total = bufs
+        self.n, self.w, self.terms, self.bufs = n, w, terms, bufs
         self.ssem, self.rsem, self.chunks = ssem, rsem, chunks
         self.rows = terms.shape[1] // chunks
 
     def span(self, i):
         return pl.ds(pl.multiple_of(i * self.rows, self.rows), self.rows)
 
-    def cut(self, ref, i):
-        return ref.at[self.span(i), :]
-
     def term(self, d, i):
         return self.terms.at[d, self.span(i), :]
 
-    def copy(self, kind, i, src, dst, w):
-        k = kind * self.chunks + i
-        return send(src, self.cut(dst, i), self.ssem.at[k], self.rsem.at[k], self.n, w)
-
-    def relay(self, i):
-        end = 3 - 3 * (self.w // 2)
-        return self.copy(0, i, self.term(end, i), self.relayed, 1 + self.w // 3)
-
-    def far(self, i):
-        d = flip(self.w, 2)
-        return self.copy(1, i, self.term(d, i), self.from_far, d)
-
-    def far_sum(self, i):
-        return self.copy(1, i, self.cut(self.total, i), self.from_far, flip(self.w, 2))
-
-    def left(self, i):
-        d = jnp.maximum(self.w - 1, 0)
-        return self.copy(2, i, self.term(d, i), self.from_right, d)
-
-    def right(self, i):
-        d = jnp.minimum(self.w + 1, 3)
-        return self.copy(3, i, self.term(d, i), self.from_left, d)
-
-    def middle(self):
-        return (self.w == 1) | (self.w == 2)
-
-    def end(self):
-        return (self.w == 0) | (self.w == 3)
-
-    def start_chunk(self, i):
-        @pl.when(self.end())
-        def _():
-            self.relay(i).start()
-            self.far(i).start()
-
-        @pl.when(self.w > 0)
-        def _():
-            self.left(i).start()
-
-        @pl.when(self.w < 3)
-        def _():
-            self.right(i).start()
-
-    def start(self):
-        for i in range(self.chunks):
-            self.start_chunk(i)
-
-    def pass_on(self, i, mine):
-        @pl.when(self.middle())
-        def _():
-            self.relay(i).wait_recv()
-            rows = self.span(i)
-            own = self.terms[flip(self.w, 2), rows, :] if mine is None else mine[rows, :]
-            self.total[rows, :] = (own.astype(F32) + self.relayed[rows, :].astype(F32)).astype(BF)
-            self.far_sum(i).start()
-
-    def finish(self, i, mine, out):
-        rows = self.span(i)
-        self.far(i).wait_recv()
-
-        @pl.when(self.w > 0)
-        def _():
-            self.right(i).wait_recv()
-
-        @pl.when(self.w < 3)
-        def _():
-            self.left(i).wait_recv()
-
-        def put(*bufs):
-            own = self.terms[self.w, rows, :] if mine is None else mine[rows, :]
-            total = own.astype(F32)
-            for buf in bufs:
-                total = total + buf[rows, :].astype(F32)
-            out[rows, :] = total.astype(out.dtype)
-
-        @pl.when(self.w == 0)
-        def _():
-            put(self.from_far, self.from_right)
-
-        @pl.when(self.w == 3)
-        def _():
-            put(self.from_far, self.from_left)
-
-        @pl.when(self.middle())
-        def _():
-            put(self.from_far, self.from_left, self.from_right)
+    def slot(self, way, slot, i):
+        return self.bufs[way].at[slot, self.span(i), :]
+
+    def put(self, way, here, d, i, src):
+        slot = d - here - 1 if way == 0 else here - 1 - d
+        k = (way * 3 + slot) * self.chunks + i
+        to = here + 1 - 2 * way
+        return send(src, self.slot(way, slot, i), self.ssem.at[k], self.rsem.at[k], self.n, to)
+
+    def came(self, way, slot, i):
+        k = (way * 3 + slot) * self.chunks + i
+        ref = self.slot(way, slot, i)
+        send(ref, ref, self.ssem.at[k], self.rsem.at[k], self.n, 1).wait_recv()
+
+    def begin(self, i):
+        for here, way in ((0, 0), (3, 1)):
+
+            @pl.when(self.w == here)
+            def _():
+                for d in (3, 2, 1) if way == 0 else (0, 1, 2):
+                    self.put(way, here, d, i, self.term(d, i)).start()
+
+    def join(self, way, here, d, i):
+        slot = d - here if way == 0 else here - d
+        self.came(way, slot, i)
+        mine, sum_ = self.term(d, i), self.slot(way, slot, i)
+        sum_[...] = (mine[...].astype(F32) + sum_[...].astype(F32)).astype(BF)
+        self.put(way, here, d, i, sum_).start()
+
+    def pass_on(self, i):
+        @pl.when(self.w == 1)
+        def _():
+            self.join(0, 1, 3, i)
+            self.join(0, 1, 2, i)
+
+        @pl.when(self.w == 2)
+        def _():
+            self.join(1, 2, 0, i)
+            self.join(1, 2, 1, i)
+
+    def pass_end(self, i):
+        @pl.when(self.w == 1)
+        def _():
+            self.join(1, 1, 0, i)
+
+        @pl.when(self.w == 2)
+        def _():
+            self.join(0, 2, 3, i)
+
+    def finish(self, i, out):
+        for here, ways in ((0, (1,)), (1, (0, 1)), (2, (0, 1)), (3, (0,))):
+
+            @pl.when(self.w == here)
+            def _():
+                for way in ways:
+                    self.came(way, 0, i)
+                total = self.term(here, i)[...].astype(F32)
+                for way in ways:
+                    total = total + self.slot(way, 0, i)[...].astype(F32)
+                out[self.span(i), :] = total.astype(out.dtype)
 
     def drain(self):
-        for i in range(self.chunks):
-            self.far(i).wait_send()
-
-        @pl.when(self.end())
-        def _():
-            for i in range(self.chunks):
-                self.relay(i).wait_send()
-
-        @pl.when(self.w > 0)
-        def _():
-            for i in range(self.chunks):
-                self.left(i).wait_send()
-
-        @pl.when(self.w < 3)
-        def _():
-            for i in range(self.chunks):
-                self.right(i).wait_send()
+        sent = {
+            0: ((0, 3), (0, 2), (0, 1)),
+            1: ((0, 3), (0, 2), (1, 0)),
+            2: ((1, 0), (1, 1), (0, 3)),
+            3: ((1, 0), (1, 1), (1, 2)),
+        }
+        for here in range(4):
+
+            @pl.when(self.w == here)
+            def _():
+                for i in range(self.chunks):
+                    for way, d in sent[here]:
+                        self.put(way, here, d, i, self.term(d, i)).wait_send()
 
 
 def middle_kernel(
@@ -523,9 +482,6 @@
     terms,
     from_left,
     from_right,
-    from_far,
-    relayed,
-    total,
     part_buf,
     gate_k,
     up_k,
@@ -560,12 +516,11 @@
     greet([mate], n, w, True)
 
     gather = LineGather(n, w, mixed, x_all, ag_s, ag_r, chunks)
-    scatter = LineScatter(
-        n, w, terms, (from_left, from_right, from_far, relayed, total), rs_s, rs_r, chunks
-    )
-    for i in range(chunks):
-        gather.start_chunk(i)
-    gather.forward(0)
+    scatter = LineScatter(n, w, terms, (from_left, from_right), rs_s, rs_r, chunks)
+    gather.start_chunk(0)
+    gather.start_chunk(1)
+    gather.near(0)
+    gather.far(0)
     for cp in loads:
         cp.wait()
 
@@ -590,7 +545,11 @@
 
         @pl.when(i < chunks - 1)
         def _():
-            gather.forward(i + 1)
+            gather.near(i + 1)
+
+        @pl.when(i < chunks - 2)
+        def _():
+            gather.start_chunk(i + 2)
 
         back_f[...] = contract_cols(rows_of(cot_v, i), wd_v[...])
         step = 16
@@ -612,14 +571,18 @@
 
         @pl.when(i > 0)
         def _():
-            scatter.pass_on(i - 1, None)
+            scatter.pass_on(i - 1)
+
+        @pl.when(i < chunks - 1)
+        def _():
+            gather.far(i + 1)
 
         terms[:, r, :] = (
             (contract_cols(rows_of(gb, i), wg_v[...]) + contract_cols(rows_of(ub, i), wu_v[...]))
             .astype(BF)
             .reshape(4, rows, model)
         )
-        scatter.start_chunk(i)
+        scatter.begin(i)
 
         @pl.when(i > 1)
         def _():
@@ -632,10 +595,13 @@
         )
         store(i).start()
 
+        @pl.when(i > 0)
+        def _():
+            scatter.pass_end(i - 1)
+
     pl.semaphore_signal(
         ready, inc=1, device_id=at(mate, w), device_id_type=pl.DeviceIdType.MESH
     )
-    scatter.pass_on(chunks - 1, None)
 
     def row_grad(back, block):
         cols = pl.ds(pl.multiple_of(block * (model // 8), model // 8), model // 8)
@@ -668,6 +634,7 @@
     def _(j):
         wg_v[place(j, half), :] = row_grad(gb, 2 * j + 1 - core).astype(BF)
 
+    scatter.pass_on(chunks - 1)
     pl.semaphore_wait(ready, 1)
     swaps[0].start()
 
@@ -682,7 +649,6 @@
         wd_v[:, place(j, half)] = col_grad(2 * j + 1 - core).astype(BF)
 
     swaps[2].start()
-
     swaps[0].wait_recv()
 
     @pl.loop(0, 4)
@@ -707,6 +673,7 @@
     ]
     for k in (0, 1):
         puts[k].start()
+    scatter.pass_end(chunks - 1)
     swaps[1].wait_recv()
 
     @pl.loop(0, 4)
@@ -728,7 +695,7 @@
     for k in (4, 5, 6, 7):
         puts[k].start()
     for i in range(chunks):
-        scatter.finish(i, None, back_out)
+        scatter.finish(i, back_out)
     scatter.drain()
     gather.finish_sends()
     for k in range(3):
@@ -750,7 +717,7 @@
     acc = pltpu.VMEM((4 * rows, width), F32)
     act = pltpu.VMEM((4, tokens_here, width), BF)
     tok = pltpu.VMEM((4, tokens_here, model), BF)
-    own = pltpu.VMEM((tokens_here, model), BF)
+    three = pltpu.VMEM((3, tokens_here, model), BF)
     return pl.pallas_call(
         middle_kernel,
         name="feed_forward",
@@ -775,20 +742,17 @@
             act,
             act,
             tok,
-            own,
-            own,
-            own,
-            own,
-            own,
+            three,
+            three,
             pltpu.VMEM((2, 4, rows, model), BF),
             pltpu.VMEM((2, 2, eighth, width), BF),
             pltpu.VMEM((2, 2, eighth, width), BF),
             pltpu.VMEM((2, 2, width, eighth), BF),
             dma((5,)),
+            dma((32,)),
             dma((16,)),
-            dma((16,)),
-            dma((16,)),
-            dma((16,)),
+            dma((24,)),
+            dma((24,)),
             dma((2,)),
             dma((3,)),
             dma((3,)),
@@ -997,7 +961,8 @@
 
     def __getitem__(self, index):
         d, r, _ = index
-        return self.ref.at[pl.ds(d * self.shape[1] + r.start, r.size), :]
+        start = pl.multiple_of(d * self.shape[1] + r.start, r.size)
+        return self.ref.at[pl.ds(start, r.size), :]
 
 
 def last_kernel(items, *refs):
@@ -1016,8 +981,8 @@
     feed_out, gain_out = take(2)
     attn_bufs = [take(4) for _ in range(4)]
     ffn_bufs = [take(3) for _ in range(4)]
-    line_bufs = [take(6) for _ in range(4)]
-    feed_bufs = take(7)
+    line_bufs = [take(3) for _ in range(4)]
+    feed_v, feed_left, feed_right = take(3)
     gain_in, gain_sum, gain_line = take(3)
     load_sem, swap_s, swap_r, st_s, st_r = take(5)
     half_sems = take(3)
@@ -1054,13 +1019,8 @@
             cp.start()
     for item in attn:
         item.load().start()
-    mine, away = feed_bufs[0], feed_bufs[1]
-    feed_loads = [
-        pltpu.make_async_copy(feed_terms.at[w], mine, fd_l.at[0]),
-        pltpu.make_async_copy(feed_terms.at[flip(w, 2)], away, fd_l.at[1]),
-    ]
-    for cp in feed_loads:
-        cp.start()
+    feed_load = pltpu.make_async_copy(feed_terms, feed_v, fd_l)
+    feed_load.start()
 
     barrier = pltpu.get_barrier_semaphore()
     narrow_peers = [lax.rem(n + i, 8) for i in range(1, 8)]
@@ -1077,8 +1037,10 @@
 
     for item in attn:
         item.swap().start()
-    feed = LineScatter(n, w, feed_terms, feed_bufs[2:], fd_s, fd_r, 4)
-    feed.start()
+    feed_load.wait()
+    feed = LineScatter(n, w, feed_v, (feed_left, feed_right), fd_s, fd_r, 4)
+    for i in range(4):
+        feed.begin(i)
 
     def gain_narrow(i):
         peer = narrow_peers[i]
@@ -1092,12 +1054,11 @@
 
     for item in ffn:
         item.after_one()
-    for cp in feed_loads:
-        cp.wait()
-    feed.pass_on(0, away)
+    feed.pass_on(0)
     for item in attn:
         item.after_swap()
-    feed.pass_on(1, away)
+    feed.pass_on(1)
+    feed.pass_end(0)
     for i in range(7):
         gain_narrow(i).wait()
     total = gain_parts[n]
@@ -1106,54 +1067,55 @@
     gain_sum[...] = total
     for i in range(3):
         gain_wide(i).start()
-    feed.pass_on(2, away)
+    feed.pass_on(2)
+    feed.pass_end(1)
     for item in attn[:2]:
         item.after_one()
-    feed.pass_on(3, away)
+    feed.pass_on(3)
+    feed.pass_end(2)
     for item in attn[2:]:
         item.after_one()
+    feed.pass_end(3)
     for k in range(4):
         ffn[k].after_two()
         spread[k].start()
 
     scatters, gathers = [], []
     for k, item in enumerate(attn):
-        own = line_bufs[k][5]
+        left, right, own = line_bufs[k]
         scatters.append(
-            LineScatter(n, w, Rows(item.result()), line_bufs[k][:5], lr_s.at[k], lr_r.at[k], 1)
+            LineScatter(n, w, Rows(item.result()), (left, right), lr_s.at[k], lr_r.at[k], 1)
         )
         gathers.append(LineGather(n, w, own, outs[k], lg_s.at[k], lg_r.at[k], 1))
 
-    def quarter(item, d):
-        return item.result().at[pl.ds(d * (item.rows // 4), item.rows // 4), :]
-
-    def line_pass(k):
-        scatters[k].pass_on(0, quarter(attn[k], flip(w, 2)))
-
     def keep(k):
-        return pltpu.make_async_copy(line_bufs[k][5], outs[k].at[w], lg_l.at[k])
+        return pltpu.make_async_copy(line_bufs[k][2], outs[k].at[w], lg_l.at[k])
 
     def line_turn(k):
-        scatters[k].finish(0, quarter(attn[k], w), line_bufs[k][5])
+        scatters[k].finish(0, line_bufs[k][2])
         gathers[k].start()
         keep(k).start()
 
     for k in (0, 1):
         attn[k].after_two()
-        scatters[k].start()
+        scatters[k].begin(0)
     for i in range(4):
-        feed.finish(i, mine, feed_out)
+        feed.finish(i, feed_out)
     for k in (2, 3):
         attn[k].after_two()
-        scatters[k].start()
+        scatters[k].begin(0)
     for k in (0, 1, 2, 3):
-        line_pass(k)
+        scatters[k].pass_on(0)
+    for k in (0, 1, 2, 3):
+        scatters[k].pass_end(0)
     for k in (0, 1, 2, 3):
         line_turn(k)
     for s in spread[:2]:
         s.relay()
     for k in (0, 1, 2, 3):
-        gathers[k].forward(0)
+        gathers[k].near(0)
+    for k in (0, 1, 2, 3):
+        gathers[k].far(0)
     for s in spread[2:]:
         s.relay()
     for i in range(3):
@@ -1195,14 +1157,15 @@
         ]
     outs = []
     for _, (_, cols), _ in items:
-        scratch += [pltpu.VMEM((rows // 4, cols), BF)] * 6
+        scratch += [pltpu.VMEM((3, rows // 4, cols), BF)] * 2 + [pltpu.VMEM((rows // 4, cols), BF)]
         outs.append(jax.ShapeDtypeStruct((4, rows // 4, cols), BF))
     outs.append(jax.ShapeDtypeStruct((8,) + stays[0].shape[1:], BF))
     outs.append(jax.ShapeDtypeStruct((8,) + stays[1].shape[1:], BF))
     outs.append(jax.ShapeDtypeStruct((2 * stays[2].shape[1], 8 * stays[2].shape[2]), BF))
     outs.append(jax.ShapeDtypeStruct(feed_terms.shape[1:], F32))
     outs.append(jax.ShapeDtypeStruct(gain_parts.shape[1:], F32))
-    scratch += [pltpu.VMEM(feed_terms.shape[1:], BF)] * 7
+    scratch += [pltpu.VMEM(feed_terms.shape, BF)]
+    scratch += [pltpu.VMEM((3,) + feed_terms.shape[1:], BF)] * 2
     scratch += [
         pltpu.VMEM((7,) + gain_parts.shape[1:], F32),
         pltpu.VMEM(gain_parts.shape[1:], F32),
@@ -1212,8 +1175,8 @@
     scratch += [dma((4,)), dma((4,)), dma((4,)), dma((8,)), dma((8,))]
     scratch += [dma((8,)), dma((4,)), dma((4,))]
     scratch += [dma((28,)), dma((28,)), dma((4,))]
-    scratch += [dma((4, 4))] * 4 + [dma((4,))]
-    scratch += [dma((16,)), dma((16,)), dma((2,))]
+    scratch += [dma((4, 6)), dma((4, 6)), dma((4, 8)), dma((4, 4)), dma((4,))]
+    scratch += [dma((24,)), dma((24,)), dma]
     scratch += [dma((7,)), dma((7,)), dma((3,)), dma((3,))]
     hbm, vmem = pl.BlockSpec(memory_space=pl.ANY), pl.BlockSpec(memory_space=pltpu.VMEM)
     out = pl.pallas_call(

time: 488 us -> 471 us (0.965)
  the two profiles are of different devices: /device:TPU:0 before, /device:TPU:9 now
where the time goes in v4:
time: 471 us; the launch traced here: 464 us
  Pallas kernels  355 us (75%)
  matrix products  49.2 us (10%)
  other arithmetic  42.1 us (9%)
  local copies, waits for them, and re-layouts  12.2 us (3%)
    pallas_call x1, Pallas kernels, reduce_last(): pl.pallas_call(functools.partial(last_kernel, items), name='reduce_last',...  155 us
    pallas_call x1, Pallas kernels, feed_forward(): pl.pallas_call(middle_kernel, name='feed_forward', out_shape=(jax.ShapeDt...  129 us
    pallas_call x1, Pallas kernels, gather_first(): pl.pallas_call(first_kernel, name='gather_first', out_shape=(jax.ShapeDty...  71.9 us
    convert_element_type x2, other arithmetic, per_device(): gate_total, up_total, down_total = [t.astype(F32) for t in ffn_totals]  19.1 us
    dot_general x2, matrix products, contract_cols(): lax.dot_general(left, right, (((1,), (1,)), ((), ())), preferred_element_...  13.6 us
    dot_general x2, matrix products, contract_rows(): lax.dot_general(left, right, (((0,), (0,)), ((), ())), preferred_element_...  11.2 us
  transfers between devices with their start and end apart: 4, of which 0 were waited for; matrix products, arithmetic and copies ran while one was open for 11% of the time, Pallas kernels for 0%

profile of v4, /device:TPU:9, one launch (start us, length us, event | category | flops | bytes accessed | tf_op | source)
XLA Modules:
  0.0 463.6 jit_solution(5170533389500720168)
XLA Ops:
  0.6 0.0 copy-start.4
  0.7 1.6 fusion.19
  2.3 0.7 stack.12
  2.9 0.7 stack.13
  3.6 0.6 copy.66
  4.2 71.9 %gather_first.1 = (bf16[2048,2304]{1,0:T(8,128)(2,1)}, bf16[1536,2048]{1,0:T(8,128)(2,1)}, f32[8,1,512]{2,1,0:T(1,128)}, bf16[4,256,2048]{2,1,0:T(8,128)(2,1)}) custom-call(bf16[256,1536]{1,0:T(8,128)(2,1)} %q_ref.1, bf16[256,384]{1,0:T(8,128)(2,1)} %k_ref.1, bf16[256,384]{1,0:T(8,128)(2,1)} %v_ref.1, bf16[1536,256]{1,0:T(8,128)(2,1)} %p_ref.1, ...), custom_call_target="tpu_custom_call" | custom-call | tf_op jit(solution)/shard_map/gather_first/pallas_call | solution.py:334
  76.2 0.8 reduce
  77.0 6.3 %convolution_convert_fusion.2 = bf16[256,2304]{1,0:T(8,128)(2,1)S(1)} fusion(bf16[2048,2304]{1,0:T(8,128)(2,1)} %get-tuple-element.35, bf16[256,2048]{1,0:T(8,128)(2,1)S(1)} %copy-done.4, f32[2048]{0:T(1024)S(1)} %bitcast.149, f32[256]{0:T(256)S(1)} %fusion.36), kind=kOutput, calls=%fused_computation.22 | convolution fusion | flops 2418606080 | bytes 11674624 | tf_op jit(solution)/shard_map/dot_general | solution.py:1243
  83.4 0.0 copy-start.40
  83.4 0.1 slice.45
  83.5 0.5 copy-done.39
  84.0 0.2 reduce-window.8
  84.2 0.1 convert_reduce_fusion
  84.3 0.6 fusion.38
  84.9 1.2 compare_convert_fusion.live
  86.2 0.1 fusion.35
  86.3 0.0 copy-start.16
  86.3 0.3 copy.50
  86.6 0.1 copy.49
  86.7 0.0 copy-start.14
  86.7 0.1 copy.48
  86.9 1.1 fusion.5
  88.0 0.0 copy-start.22
  88.0 1.3 fusion.6
  89.4 1.3 copy-done
  90.7 1.8 fusion.21
  92.5 0.0 copy-start.9
  92.5 0.7 slice-done.3
  93.2 1.9 multiply_reduce_fusion.2
  95.1 1.3 copy-done.1
  96.4 1.2 multiply_convert_fusion.mixed
  97.6 128.7 %feed_forward.1 = (f32[256,2048]{1,0:T(8,128)}, bf16[4,256,2048]{2,1,0:T(8,128)(2,1)}, bf16[2,256,1152]{2,1,0:T(8,128)(2,1)}, bf16[2,256,1152]{2,1,0:T(8,128)(2,...) custom-call(bf16[256,2048]{1,0:T(8,128)(2,1)} %multiply_convert_fusi, ...), custom_call_target="tpu_custom_call" | custom-call | tf_op jit(solution)/shard_map/feed_forward/pallas_call | solution.py:721
  226.4 0.5 collective-permute-start.2
  226.9 0.3 collective-permute-start.3
  227.2 1.2 collective-permute-start
  228.3 1.0 collective-permute-start.1
  229.4 2.7 multiply_reduce_fusion
  232.2 1.9 fusion.16
  234.1 5.5 %convolution_convert_fusion.3 = bf16[256,1536]{1,0:T(8,128)(2,1)} fusion(bf16[1536,2048]{1,0:T(8,128)(2,1)} %get-tuple-element.36, f32[256,2048]{1,0:T(8,128)S(1)} %fusion.16), kind=kOutput, calls=%fused_computation.29 | convolution fusion | flops 1611530240 | bytes 9175040 | tf_op jit(solution)/shard_map/dot_general | solution.py:34
  239.6 1.4 copy.52
  241.1 4.2 fusion.27
  245.3 0.0 slice-start.1
  245.3 7.4 %fusion = (f32[6,4,256]{2,1,0:T(4,128)S(1)}, f32[6,256,256,4]{2,1,3,0:T(8,128)}) fusion(f32[6,256,256,4]{2,1,3,0:T(8,128)} %copy-done, f32[6,4,256]{2,1,0:T(4,128)S(1)} %bitcast.147, pred[256,256]{0,1:T(8,128)(4,1)S(1)} %copy-done.17, bf16[256,6,64,1]{0,2,3,1:T(8,128)(2,1)S(1)} %bitcast.142, bf16[256,6,4,64]{0,3,2,1:T(8,128)(2,1)S(1)} %bitcast.130), kind=kOutput, calls=%fused_computation.4 | convolution fusion | flops 209184768 | bytes 13680640 | tf_op jit(solution)/shard_map/qcgd,kcd->cgqk/dot_general | solution.py:1329
  252.8 4.7 %fusion.2 = bf16[6,4,256,256]{2,3,1,0:T(8,128)(2,1)S(1)} fusion(f32[6,256,256,4]{2,1,3,0:T(8,128)} %get-tuple-element.74, f32[6,256,256,4]{2,1,3,0:T(8,128)S(1)} %bitcast.120, f32[6,4,256]{2,1,0:T(4,128)S(1)} %get-tuple-element.73, f32[6,4,256]{2,1,0:T(4,128)S(1)} %bitcast.148, pred[256,256]{0,1:T(8,128)(4,1)S(1)} %copy-done.17), kind=kLoop, calls=%fused_computation.6 | loop fusion | flops 9437184 | bytes 15843328 | tf_op jit(solution)/shard_map/convert_element_type | solution.py:1334
  257.5 1.1 fusion.26
  258.6 0.7 multiply_convert_fusion.1
  259.3 0.5 copy-done.5
  259.8 8.0 %fusion.20 = (f32[256]{0:T(256)S(1)}, f32[2048]{0:T(1024)S(1)}, f32[256,2048]{1,0:T(8,128)}) fusion(bf16[256,2048]{1,0:T(8,128)(2,1)S(1)} %copy-done.5, f32[2048]{0:T(1024)S(1)} %bitcast.150, f32[256]{0:T(256)S(1)} %copy-done.31, bf16[2048,2304]{1,0:T(8,128)(2,1)} %get-tuple-element.35, bf16[256,384]{0,1:T(8,128)(2,1)S(1)} %bitcast.153, ...), kind=kOutput, calls=%fused_computation.38 | convolution fusion | flops 2423125760 | bytes 13780992 | tf_op jit(solution)/shard_map/dot_general | solution.py:34
  267.9 5.4 %convolution_convert_fusion = bf16[2048,2304]{1,0:T(8,128)(2,1)} fusion(bf16[256,384]{0,1:T(8,128)(2,1)S(1)} %bitcast.154, bf16[256,384]{0,1:T(8,128)(2,1)S(1)} %bitcast.140, bf16[256,1536]{0,1:T(8,128)(2,1)S(1)} %bitcast.132, bf16[256,2048]{1,0:T(8,128)(2,1)S(1)} %copy-done.5, f32[2048]{0:T(1024)S(1)} %bitcast.151, f32[256]{0:T(256)S(1)} %copy-done.31), kind=kOutput, calls=%fused_computation | convolution fusion | flops 2426273792 | bytes 11674624 | tf_op jit(solution)/shard_map/dot_general | solution.py:28
  273.3 0.6 reshape.227.refs_11_
  273.9 5.8 %convolution_convert_fusion.1 = bf16[2048,1536]{1,0:T(8,128)(2,1)} fusion(bf16[256,1536]{0,1:T(8,128)(2,1)} %bitcast.128, f32[256,2048]{1,0:T(8,128)S(1)} %fusion.16), kind=kOutput, calls=%fused_computation.1 | convolution fusion | flops 1614282752 | bytes 9175040 | tf_op jit(solution)/shard_map/dot_general | solution.py:28
  279.8 1.6 fusion.18
  281.4 154.7 %reduce_last.1 = (bf16[4,64,1152]{2,1,0:T(8,128)(2,1)}, bf16[4,64,1152]{2,1,0:T(8,128)(2,1)}, bf16[4,64,768]{2,1,0:T(8,128)(2,1)}, bf16[4,64,768]{2,1,0:T(8,128)...) custom-call(bf16[2,2,2,256,2304]{4,3,2,1,0:T(8,128)(2,1)} %bitcast.1, ...), custom_call_target="tpu_custom_call" | custom-call | tf_op jit(solution)/shard_map/reduce_last/pallas_call | solution.py:1182
  436.2 2.1 maximum_convert_fusion.1
  438.3 0.2 maximum_convert_fusion
  438.5 0.8 copy-done.13
  439.2 1.2 add_convert_fusion
  440.5 0.6 fusion.47
  441.0 0.2 copy.56
  441.2 0.2 copy.57
  441.4 1.4 slice.47
  442.7 7.3 %convert_element_type.149 = f32[1152,2048]{1,0:T(8,128)} convert(bf16[1152,2048]{1,0:T(8,128)(2,1)} %get-tuple-element.56) | non-fusion elementwise | flops 2359296 | bytes 14155776 | tf_op jit(solution)/shard_map/convert_element_type | solution.py:1376
  450.1 1.3 convert_bitcast_fusion
  451.3 11.8 %bitcast_convert_fusion = (f32[2048,1152]{1,0:T(8,128)}, f32[2048,1152]{1,0:T(8,128)}) fusion(bf16[8,256,1152]{2,1,0:T(8,128)(2,1)} %get-tuple-element.55, bf16[8,256,1152]{2,1,0:T(8,128)(2,1)} %get-tuple-element.54), kind=kLoop, calls=%fused_computation.15 | loop fusion | flops 4718592 | bytes 28311552 | tf_op jit(solution)/shard_map/convert_element_type | solution.py:1376
  (93 shorter events, 0.4 us)
Async XLA Ops:
  0.6 76.3 %copy-start.4 = (bf16[256,2048]{1,0:T(8,128)(2,1)S(1)}, bf16[256,2048]{1,0:T(8,128)(2,1)}, u32[]{:S(2)}) copy-start(bf16[256,2048]{1,0:T(8,128)(2,1)} %param.13) | copy-start | bytes 3145732
  2.3 73.9 %copy-start.34 = (f32[256]{0:T(256)}, f32[256]{0:T(256)S(1)}, u32[]{:S(2)}) copy-start(f32[256]{0:T(256)S(1)} %fusion.19) | copy-start | bytes 3076
  2.3 81.1 %copy-start.30 = (f32[256]{0:T(256)}, f32[256]{0:T(256)S(1)}, u32[]{:S(2)}) copy-start(f32[256]{0:T(256)S(1)} %fusion.36) | copy-start | bytes 3076
  77.0 6.4 %copy-start.24 = (f32[8,1,256]{2,1,0:T(1,128)}, f32[8,1,256]{2,1,0:T(1,128)S(1)}, u32[]{:S(2)}) copy-start(f32[8,1,256]{2,1,0:T(1,128)S(1)} %get-tuple-element.66) | copy-start | bytes 24580
  77.0 18.2 %copy-start.26 = (f32[8,1,256]{2,1,0:T(1,128)}, f32[8,1,256]{2,1,0:T(1,128)S(1)}, u32[]{:S(2)}) copy-start(f32[8,1,256]{2,1,0:T(1,128)S(1)} %get-tuple-element.65) | copy-start | bytes 24580
  83.3 0.7 copy-start.39
  83.4 0.9 copy-start.40
  86.3 3.1 copy-start.16
  86.5 1.4 copy-start.7
  86.7 1.2 copy-start.14
  86.9 2.5 copy-start.18
  88.0 2.7 copy-start
  88.0 2.7 copy-start.22
  89.3 3.1 copy-start.28
  89.3 3.1 slice-start.2
  90.7 2.5 slice-start.3
  92.5 2.6 copy-start.9
  95.1 1.3 copy-start.1
  95.1 2.5 copy-start.36
  95.1 2.5 copy-start.32
  226.3 5.8 %copy-start.37 = (f32[256]{0:T(256)S(1)}, f32[256]{0:T(256)}, u32[]{:S(2)}) copy-start(f32[256]{0:T(256)} %copy-done.36) | copy-start | bytes 3076
  226.3 5.8 %copy-start.2 = (f32[256,2048]{1,0:T(8,128)S(1)}, f32[256,2048]{1,0:T(8,128)}, u32[]{:S(2)}) copy-start(f32[256,2048]{1,0:T(8,128)} %copy-done.1) | copy-start | bytes 6291460
  226.4 5.8 %copy-start.6 = (f32[256,2048]{1,0:T(8,128)S(1)}, f32[256,2048]{1,0:T(8,128)}, u32[]{:S(2)}) copy-start(f32[256,2048]{1,0:T(8,128)} %get-tuple-element.38) | copy-start | bytes 6291460
  226.4 5.8 %copy-start.27 = (f32[8,1,256]{2,1,0:T(1,128)S(1)}, f32[8,1,256]{2,1,0:T(1,128)}, u32[]{:S(2)}) copy-start(f32[8,1,256]{2,1,0:T(1,128)} %copy-done.26) | copy-start | bytes 24580
  226.4 5.8 %copy-start.33 = (f32[256]{0:T(256)S(1)}, f32[256]{0:T(256)}, u32[]{:S(2)}) copy-start(f32[256]{0:T(256)} %copy-done.32) | copy-start | bytes 3076
  226.4 55.0 %collective-permute-start.2 = (bf16[2,576,256]{2,1,0:T(8,128)(2,1)}, bf16[2,576,256]{2,1,0:T(8,128)(2,1)}, u32[]{:S(2)}, u32[]{:S(2)}) collective-permute-start(bf16[2,576,256]{2,1,0:T(8,128)(2,1)} %get-tuple-element.45), channel_id=1, source_target_pairs={{0,8},{4,12},{8,0},{12,4},{16,24},{20,28},{24,16},{28,20},{1,9},{5... | collective-permute-start | bytes 1769480 | tf_op jit(solution)/shard_map/ppermute | solution.py:1281
  226.9 54.5 %collective-permute-start.3 = (bf16[2,576,256]{2,1,0:T(8,128)(2,1)}, bf16[2,576,256]{2,1,0:T(8,128)(2,1)}, u32[]{:S(2)}, u32[]{:S(2)}) collective-permute-start(bf16[2,576,256]{2,1,0:T(8,128)(2,1)} %get-tuple-element.46), channel_id=1, source_target_pairs={{0,16},{4,20},{8,24},{12,28},{16,0},{20,4},{24,8},{28,12},{1,17},{... | collective-permute-start | bytes 1769480 | tf_op jit(solution)/shard_map/ppermute | solution.py:1281
  227.2 54.2 %collective-permute-start = (bf16[2,256,1152]{2,1,0:T(8,128)(2,1)}, bf16[2,256,1152]{2,1,0:T(8,128)(2,1)}, u32[]{:S(2)}, u32[]{:S(2)}) collective-permute-start(bf16[2,256,1152]{2,1,0:T(8,128)(2,1)} %get-tuple-element.43), channel_id=1, source_target_pairs={{0,8},{4,12},{8,0},{12,4},{16,24},{20,28},{24,16},{28,20},{1,9},{5... | collective-permute-start | bytes 3538952 | tf_op jit(solution)/shard_map/ppermute | solution.py:1281
  228.3 53.0 %collective-permute-start.1 = (bf16[2,256,1152]{2,1,0:T(8,128)(2,1)}, bf16[2,256,1152]{2,1,0:T(8,128)(2,1)}, u32[]{:S(2)}, u32[]{:S(2)}) collective-permute-start(bf16[2,256,1152]{2,1,0:T(8,128)(2,1)} %get-tuple-element.44), channel_id=1, source_target_pairs={{0,16},{4,20},{8,24},{12,28},{16,0},{20,4},{24,8},{28,12},{1,17},{... | collective-permute-start | bytes 3538952 | tf_op jit(solution)/shard_map/ppermute | solution.py:1281
  234.1 7.0 %copy-start.23 = (f32[6,4,256]{2,1,0:T(4,128)S(1)}, f32[6,4,256]{2,1,0:T(4,128)}, u32[]{:S(2)}) copy-start(f32[6,4,256]{2,1,0:T(4,128)} %copy-done.22) | copy-start | bytes 73732
  234.1 7.0 %copy-start.29 = (f32[6,4,256]{2,1,0:T(4,128)S(1)}, f32[6,4,256]{2,1,0:T(4,128)}, u32[]{:S(2)}) copy-start(f32[6,4,256]{2,1,0:T(4,128)} %copy-done.28) | copy-start | bytes 73732
  234.1 7.0 %copy-start.17 = (pred[256,256]{0,1:T(8,128)(4,1)S(1)}, pred[256,256]{0,1:T(8,128)(4,1)}, u32[]{:S(2)}) copy-start(pred[256,256]{0,1:T(8,128)(4,1)} %copy-done.16) | copy-start | bytes 196612
  241.1 4.2 copy-start.19
  241.1 11.6 %slice-start = ((s8[6291456]{0:T(1024)(128)(4,1)}), s8[4194304]{0:T(1024)(128)(4,1)S(1)}, s32[]{:S(2)}) async-start(s8[6291456]{0:T(1024)(128)(4,1)} %bitcast.119), calls=%async_computation | async-start | bytes 8388608
  245.3 7.4 %slice-start.1 = ((s8[6291456]{0:T(1024)(128)(4,1)}), s8[2097152]{0:T(1024)(128)(4,1)S(1)}, s32[]{:S(2)}) async-start(s8[6291456]{0:T(1024)(128)(4,1)} %bitcast.119), calls=%async_computation.1 | async-start | bytes 4194304
  252.7 4.8 %copy-start.8 = (bf16[256,1536]{0,1:T(8,128)(2,1)S(1)}, bf16[256,1536]{0,1:T(8,128)(2,1)}, u32[]{:S(2)}) copy-start(bf16[256,1536]{0,1:T(8,128)(2,1)} %copy-done.7) | copy-start | bytes 2359300
  257.5 1.1 copy-start.15
  258.6 1.2 copy-start.5
  258.6 1.2 copy-start.25
  258.6 1.2 copy-start.31
  267.9 6.0 %copy-start.35 = (f32[256]{0:T(256)S(1)}, f32[256]{0:T(256)}, u32[]{:S(2)}) copy-start(f32[256]{0:T(256)} %copy-done.34) | copy-start | bytes 3076
  273.9 5.9 %copy-start.12 = (f32[256,2048]{1,0:T(8,128)S(1)}, f32[256,2048]{1,0:T(8,128)}, u32[]{:S(2)}) copy-start(f32[256,2048]{1,0:T(8,128)} %get-tuple-element.75) | copy-start | bytes 6291460
  436.1 2.1 copy-start.10
  436.2 2.1 copy-start.11
  436.2 2.3 copy-start.3
  436.2 3.0 copy-start.13
  439.2 1.2 copy-start.38
  439.2 1.8 copy-start.21
  439.2 2.0 copy-start.20

commit v5 on v4

--- a/solution.py
+++ b/solution.py
@@ -766,29 +766,36 @@
 
 
 class Reduce:
-    def __init__(self, me, part, cols, x_first, bufs, sems, k):
+    def __init__(self, me, factors, cols, x_first, bufs, sems, k):
         self.n, self.w, self.y, self.x, self.core = me
-        self.part, self.cols, self.x_first = part, pl.ds(*cols), x_first
-        self.sum, self.pair, self.one, self.two = bufs
+        self.left, self.right = factors
+        self.cols, self.x_first = pl.ds(*cols), x_first
+        self.away, self.sum, self.pair, self.one, self.two = bufs
         self.sems, self.k = sems, k
-        self.rows = part.shape[3]
+        self.rows = self.sum.shape[2]
         self.near = flip(self.n, 2) if x_first else flip(self.n, 4)
         self.next = flip(self.n, 4) if x_first else flip(self.n, 2)
 
-    def load(self):
-        return pltpu.make_async_copy(
-            self.part.at[:, :, self.core, :, self.cols], self.sum, self.sems[0].at[self.k]
-        )
+    def term(self, block):
+        own = pl.ds(pl.multiple_of(block * self.rows, self.rows), self.rows)
+        return contract_rows(self.left[:, own], self.right[:, self.cols])
 
     def swap(self):
         return send(
-            self.part.at[:, :, 1 - self.core, :, self.cols],
+            self.away,
             self.pair,
+            self.sems[0].at[self.k],
             self.sems[1].at[self.k],
-            self.sems[2].at[self.k],
             flip(self.n, 1),
             self.w,
         )
+
+    def before_swap(self):
+        @pl.loop(0, 4)
+        def _(j):
+            self.away[j // 2, lax.rem(j, 2)] = self.term(2 * j + 1 - self.core).astype(BF)
+
+        self.swap().start()
 
     def block(self, first, second):
         return (second, first) if self.x_first else (first, second)
@@ -805,7 +812,7 @@
             src = self.sum.at[self.block(a, 1 - b)]
             dst, peer = self.two, self.next
         k = 2 * self.k + s - 1
-        return send(src, dst, self.sems[3].at[k], self.sems[4].at[k], peer, self.w)
+        return send(src, dst, self.sems[2].at[k], self.sems[3].at[k], peer, self.w)
 
     def add(self, block, other):
         step = 64 if self.rows % 64 == 0 else 48
@@ -818,15 +825,17 @@
             )
 
     def after_swap(self):
-        a, b = self.axes()
+        a, _ = self.axes()
         self.swap().wait_recv()
-        self.load().wait()
-        for first in (1 - a, a):
-            for second in (1 - b, b):
-                block = self.block(first, second)
-                self.add(block, self.pair.at[block])
-            if first is not a:
-                self.stage(1).start()
+
+        @pl.loop(0, 4)
+        def _(j):
+            first = lax.rem(1 - a + j // 2, 2)
+            y, x = self.block(first, lax.rem(j, 2))
+            total = self.term(4 * y + 2 * x + self.core) + self.pair[y, x].astype(F32)
+            self.sum[y, x] = total.astype(BF)
+
+        self.stage(1).start()
 
     def after_one(self):
         a, b = self.axes()
@@ -973,17 +982,18 @@
         del refs[:count]
         return out
 
-    parts = take(2)
+    factors = take(4)
     stays, comes = take(4), take(4)
     feed_terms, gain_parts = take(2)
     outs = take(4)
     gate_full, up_full, down_full = take(3)
     feed_out, gain_out = take(2)
-    attn_bufs = [take(4) for _ in range(4)]
+    attn_bufs = [take(5) for _ in range(4)]
     ffn_bufs = [take(3) for _ in range(4)]
     line_bufs = [take(3) for _ in range(4)]
     feed_v, feed_left, feed_right = take(3)
     gain_in, gain_sum, gain_line = take(3)
+    factor_bufs = take(4)
     load_sem, swap_s, swap_r, st_s, st_r = take(5)
     half_sems = take(3)
     sp_sems = take(3)
@@ -994,7 +1004,15 @@
     n, w = lax.axis_index("narrow"), lax.axis_index("wide")
     me = (n, w, n // 4, lax.rem(n // 2, 2), lax.rem(n, 2))
     attn = [
-        Reduce(me, parts[p], cols, xf, attn_bufs[k], (load_sem, swap_s, swap_r, st_s, st_r), k)
+        Reduce(
+            me,
+            factor_bufs[2 * p : 2 * p + 2],
+            cols,
+            xf,
+            attn_bufs[k],
+            (swap_s, swap_r, st_s, st_r),
+            k,
+        )
         for k, (p, cols, xf) in enumerate(items)
     ]
     ffn = [
@@ -1017,8 +1035,12 @@
     for item in ffn:
         for cp in item.loads():
             cp.start()
-    for item in attn:
-        item.load().start()
+    factor_loads = [
+        pltpu.make_async_copy(src, dst, load_sem.at[k])
+        for k, (src, dst) in enumerate(zip(factors, factor_bufs))
+    ]
+    for cp in factor_loads:
+        cp.start()
     feed_load = pltpu.make_async_copy(feed_terms, feed_v, fd_l)
     feed_load.start()
 
@@ -1035,8 +1057,6 @@
         )
     pl.semaphore_wait(barrier, 10)
 
-    for item in attn:
-        item.swap().start()
     feed_load.wait()
     feed = LineScatter(n, w, feed_v, (feed_left, feed_right), fd_s, fd_r, 4)
     for i in range(4):
@@ -1054,6 +1074,10 @@
 
     for item in ffn:
         item.after_one()
+    for cp in factor_loads:
+        cp.wait()
+    for item in attn:
+        item.before_swap()
     feed.pass_on(0)
     for item in attn:
         item.after_swap()
@@ -1134,16 +1158,16 @@
     feed.drain()
 
 
-def reduce_last(qkv_part, project_part, stays, comes, feed_terms, gain_parts):
-    parts = [p.reshape(2, 2, 2, p.shape[0] // 8, p.shape[1]) for p in (qkv_part, project_part)]
-    rows = parts[0].shape[3]
+def reduce_last(factors, stays, comes, feed_terms, gain_parts):
+    rows = factors[0].shape[1] // 8
     items = []
     for p, xf in ((0, True), (0, False), (1, True), (1, False)):
-        half = parts[p].shape[4] // 2
+        half = factors[2 * p + 1].shape[1] // 2
         items.append((p, (0 if xf else half, half), xf))
     scratch = []
     for _, (_, cols), _ in items:
         scratch += [
+            pltpu.VMEM((2, 2, rows, cols), BF),
             pltpu.VMEM((2, 2, rows, cols), BF),
             pltpu.VMEM((2, 2, rows, cols), BF),
             pltpu.VMEM((2, rows, cols), BF),
@@ -1171,6 +1195,7 @@
         pltpu.VMEM(gain_parts.shape[1:], F32),
         pltpu.VMEM((3,) + gain_parts.shape[1:], F32),
     ]
+    scratch += [pltpu.VMEM(f.shape, BF) for f in factors]
     dma = pltpu.SemaphoreType.DMA
     scratch += [dma((4,)), dma((4,)), dma((4,)), dma((8,)), dma((8,))]
     scratch += [dma((8,)), dma((4,)), dma((4,))]
@@ -1183,13 +1208,13 @@
         functools.partial(last_kernel, items),
         name="reduce_last",
         out_shape=tuple(outs),
-        in_specs=[hbm] * 11 + [vmem],
+        in_specs=[hbm] * 13 + [vmem],
         out_specs=[hbm] * 7 + [vmem] * 2,
         scratch_shapes=scratch,
         compiler_params=pltpu.CompilerParams(
             collective_id=4, has_side_effects=True, vmem_limit_bytes=64 * 1024 * 1024 - 65536
         ),
-    )(*parts, *stays, *comes, feed_terms, gain_parts)
+    )(*factors, *stays, *comes, feed_terms, gain_parts)
     qkv = jnp.concatenate([out[0].reshape(rows, -1), out[1].reshape(rows, -1)], axis=1)
     project = jnp.concatenate([out[2].reshape(rows, -1), out[3].reshape(rows, -1)], axis=1)
     width = out[4].shape[2]
@@ -1307,7 +1332,6 @@
     middle_norm_back, second_gain_part = second_backward(mixed_back)
     middle_back = out_grad + middle_norm_back
     branch_back = middle_back.astype(jnp.bfloat16)
-    project_part = contract_rows(branch_back, attended)
     attended_back = (
         contract_cols(branch_back, project_full)
         .astype(jnp.bfloat16)
@@ -1351,7 +1375,6 @@
         .reshape(tokens_here, KV_HEADS * HEAD_DIM)
     )
     qkv_back = jnp.concatenate([query_back, key_back, value_back], axis=1)
-    qkv_part = contract_rows(normed, qkv_back)
     normed_back = contract_cols(qkv_back, qkv_full)
     unused_first, first_backward = jax.vjp(rms_scale, inputs_f, first_gain)
     input_norm_back, first_gain_part = first_backward(normed_back)
@@ -1362,8 +1385,7 @@
             [first_gain_part.reshape(8, -1), second_gain_part.reshape(8, -1)], axis=1
         ).reshape(8, 1, -1)
         qkv_total, project_total, ffn_totals, feed, gain_total = reduce_last(
-            qkv_part.astype(BF),
-            project_part.astype(BF),
+            (normed, qkv_back, branch_back, attended),
             stays,
             comes,
             feed_terms,
@@ -1380,8 +1402,8 @@
             share = lax.psum_scatter(part.astype(BF), "narrow", scatter_dimension=0, tiled=True)
             return lax.psum(share, "wide").astype(F32)
 
-        qkv_total = owned(qkv_part)
-        project_total = owned(project_part).T
+        qkv_total = owned(contract_rows(normed, qkv_back))
+        project_total = owned(contract_rows(branch_back, attended)).T
         first_total = owned(first_gain_part)
         second_total = owned(second_gain_part)
         gate_total, up_total, down_total = (

time: 471 us -> 469 us (level)
  the two profiles are of different devices: /device:TPU:9 before, /device:TPU:0 now
where the time goes in v5:
time: 469 us; the launch traced here: 460 us
  Pallas kernels  360 us (77%)
  other arithmetic  43 us (9%)
  matrix products  35.6 us (8%)
  local copies, waits for them, and re-layouts  15.3 us (3%)
    pallas_call x1, Pallas kernels, reduce_last(): pl.pallas_call(functools.partial(last_kernel, items), name='reduce_last',...  149 us
    pallas_call x1, Pallas kernels, feed_forward(): pl.pallas_call(middle_kernel, name='feed_forward', out_shape=(jax.ShapeDt...  135 us
    pallas_call x1, Pallas kernels, gather_first(): pl.pallas_call(first_kernel, name='gather_first', out_shape=(jax.ShapeDty...  75.6 us
    convert_element_type x2, other arithmetic, per_device(): gate_total, up_total, down_total = [t.astype(F32) for t in ffn_totals]  19.3 us
    dot_general x2, matrix products, contract_cols(): lax.dot_general(left, right, (((1,), (1,)), ((), ())), preferred_element_...  12.7 us
  transfers between devices with their start and end apart: 4, of which 0 were waited for; matrix products, arithmetic and copies ran while one was open for 8% of the time, Pallas kernels for 0%

profile of v5, /device:TPU:0, one launch (start us, length us, event | category | flops | bytes accessed | tf_op | source)
XLA Modules:
  0.0 459.9 jit_solution(7083418484534498189)
XLA Ops:
  0.6 0.0 copy-start.5
  0.7 1.6 fusion.19
  2.3 0.7 stack.12
  2.9 0.7 stack.13
  3.6 0.6 copy.78
  4.2 75.6 %gather_first.1 = (bf16[2048,2304]{1,0:T(8,128)(2,1)}, bf16[1536,2048]{1,0:T(8,128)(2,1)}, f32[8,1,512]{2,1,0:T(1,128)}, bf16[4,256,2048]{2,1,0:T(8,128)(2,1)}) custom-call(bf16[256,1536]{1,0:T(8,128)(2,1)} %q_ref.1, bf16[256,384]{1,0:T(8,128)(2,1)} %k_ref.1, bf16[256,384]{1,0:T(8,128)(2,1)} %v_ref.1, bf16[1536,256]{1,0:T(8,128)(2,1)} %p_ref.1, ...), custom_call_target="tpu_custom_call" | custom-call | tf_op jit(solution)/shard_map/gather_first/pallas_call | solution.py:334
  79.8 0.8 reduce
  80.7 0.3 fusion.14.refs_0_
  81.0 0.0 copy-start.12
  81.0 6.7 %convolution_convert_fusion = bf16[256,2304]{1,0:T(8,128)(2,1)S(1)} fusion(bf16[256,2048]{1,0:T(8,128)(2,1)S(1)} %fusion.14.refs_0_, bf16[2048,2304]{1,0:T(8,128)(2,1)} %get-tuple-element.35), kind=kOutput, calls=%fused_computation.20 | convolution fusion | flops 2416508928 | bytes 11665408 | tf_op jit(solution)/shard_map/dot_general | solution.py:1268
  87.8 0.1 slice.45
  87.8 0.5 copy-done.48
  88.4 0.2 reduce-window.8
  88.5 0.1 convert_reduce_fusion
  88.6 0.6 fusion.33
  89.3 1.2 compare_convert_fusion.live
  90.5 0.1 fusion.30
  90.6 0.3 copy.58
  90.9 0.1 copy.57
  91.1 0.1 copy.56
  91.2 1.1 fusion.5
  92.3 1.3 fusion.6
  93.7 1.3 copy-done
  95.0 1.8 fusion.21
  96.8 0.7 slice-done.3
  97.5 1.9 multiply_reduce_fusion.2
  99.5 1.3 copy-done.1
  100.8 1.2 multiply_convert_fusion.mixed
  102.0 134.9 %feed_forward.1 = (f32[256,2048]{1,0:T(8,128)}, bf16[4,256,2048]{2,1,0:T(8,128)(2,1)}, bf16[2,256,1152]{2,1,0:T(8,128)(2,1)}, bf16[2,256,1152]{2,1,0:T(8,128)(2,...) custom-call(bf16[256,2048]{1,0:T(8,128)(2,1)} %multiply_convert_fusi, ...), custom_call_target="tpu_custom_call" | custom-call | tf_op jit(solution)/shard_map/feed_forward/pallas_call | solution.py:721
  237.0 0.8 collective-permute-start.2
  237.8 0.6 collective-permute-start.3
  238.3 1.5 collective-permute-start
  239.8 1.3 collective-permute-start.1
  241.1 2.4 copy.67.refs_3_
  243.5 2.9 multiply_reduce_fusion
  246.4 0.6 copy-done.37
  247.0 0.7 fusion.39.refs_2_
  247.7 1.0 copy-done.13
  248.7 4.6 %convolution_convert_fusion.1 = bf16[256,1536]{1,0:T(8,128)(2,1)S(1)} fusion(bf16[256,2048]{1,0:T(8,128)(2,1)S(1)} %fusion.39.refs_2_, bf16[1536,2048]{1,0:T(8,128)(2,1)} %get-tuple-element.36), kind=kOutput, calls=%fused_computation.27 | convolution fusion | flops 1611005952 | bytes 8126464 | tf_op jit(solution)/shard_map/dot_general | solution.py:34
  253.3 0.3 copy.60
  253.7 4.9 %fusion.27 = bf16[6,64,256]{2,1,0:T(8,128)(2,1)} fusion(bf16[256,6,4,64]{0,3,2,1:T(8,128)(2,1)S(1)} %bitcast.127, f32[6,256,256,4]{2,1,3,0:T(8,128)} %copy-done, f32[6,4,256]{2,1,0:T(4,128)S(1)} %bitcast.141, pred[256,256]{0,1:T(8,128)(4,1)S(1)} %copy-done.19), kind=kOutput, calls=%fused_computation.51 | convolution fusion | flops 207716352 | bytes 7364608 | tf_op jit(solution)/shard_map/cgqk,qcgd->kcd/dot_general | solution.py:1347
  258.5 4.9 %fusion = (f32[6,4,256]{2,1,0:T(4,128)S(1)}, f32[6,256,256,4]{2,1,3,0:T(8,128)S(1)}) fusion(f32[6,256,256,4]{2,1,3,0:T(8,128)} %copy-done, f32[6,4,256]{2,1,0:T(4,128)S(1)} %bitcast.142, pred[256,256]{0,1:T(8,128)(4,1)S(1)} %copy-done.19, bf16[256,6,64,1]{0,2,3,1:T(8,128)(2,1)S(1)} %bitcast.137, bf16[256,6,4,64]{0,3,2,1:T(8,128)(2,1)S(1)} %bitcast.128), kind=kOutput, calls=%fused_computation.2 | convolution fusion | flops 209184768 | bytes 13680640 | tf_op jit(solution)/shard_map/qcgd,kcd->cgqk/dot_general | solution.py:1353
  263.5 1.9 fusion.2
  265.4 1.1 fusion.26
  266.5 0.7 multiply_convert_fusion.1
  267.2 1.1 copy.66
  268.3 0.3 copy.64
  268.6 0.2 copy.65
  268.8 8.0 %fusion.20 = (f32[256]{0:T(256)S(1)}, f32[2048]{0:T(1024)S(1)}, f32[256,2048]{1,0:T(8,128)}) fusion(bf16[256,2048]{1,0:T(8,128)(2,1)S(1)} %copy-done.6, f32[2048]{0:T(1024)S(1)} %bitcast.151, f32[256]{0:T(256)S(1)} %copy-done.40, bf16[2048,2304]{1,0:T(8,128)(2,1)} %get-tuple-element.35, bf16[256,384]{1,0:T(8,128)(2,1)S(1)} %copy.66, ...), kind=kOutput, calls=%fused_computation.36 | convolution fusion | flops 2423125760 | bytes 13780992 | tf_op jit(solution)/shard_map/dot_general | solution.py:34
  276.9 0.6 reshape.219.refs_13_
  277.5 0.6 multiply_multiply_fusion
  278.1 1.1 pad_maximum_fusion.refs_1_
  279.2 149.4 %reduce_last.1 = (bf16[4,64,1152]{2,1,0:T(8,128)(2,1)}, bf16[4,64,1152]{2,1,0:T(8,128)(2,1)}, bf16[4,64,768]{2,1,0:T(8,128)(2,1)}, bf16[4,64,768]{2,1,0:T(8,128)...) custom-call(bf16[256,2048]{1,0:T(8,128)(2,1)} %copy-done.12, ...), custom_call_target="tpu_custom_call" | custom-call | tf_op jit(solution)/shard_map/reduce_last/pallas_call | solution.py:1207
  428.6 2.1 maximum_convert_fusion.1
  430.7 0.2 maximum_convert_fusion
  430.9 0.6 fusion.42
  431.4 0.2 copy.68
  431.6 0.1 copy-done.22
  431.7 0.2 copy.69
  431.9 1.4 slice.47
  433.2 7.3 %convert_element_type.141 = f32[1152,2048]{1,0:T(8,128)} convert(bf16[1152,2048]{1,0:T(8,128)(2,1)} %get-tuple-element.56) | non-fusion elementwise | flops 2359296 | bytes 14155776 | tf_op jit(solution)/shard_map/convert_element_type | solution.py:1398
  440.5 1.3 convert_bitcast_fusion
  441.8 12.0 %bitcast_convert_fusion = (f32[2048,1152]{1,0:T(8,128)}, f32[2048,1152]{1,0:T(8,128)}) fusion(bf16[8,256,1152]{2,1,0:T(8,128)(2,1)} %get-tuple-element.55, bf16[8,256,1152]{2,1,0:T(8,128)(2,1)} %get-tuple-element.54), kind=kLoop, calls=%fused_computation.13 | loop fusion | flops 4718592 | bytes 28311552 | tf_op jit(solution)/shard_map/convert_element_type | solution.py:1398
  453.8 5.6 %fusion.18 = (bf16[256,2048]{1,0:T(8,128)(2,1)}, bf16[256,2048]{1,0:T(8,128)(2,1)}) fusion(bf16[256,2048]{1,0:T(8,128)(2,1)S(1)} %copy-done.7, f32[256,2048]{1,0:T(8,128)} %get-tuple-element.77, f32[256]{0:T(256)S(1)} %copy-done.46, f32[2048]{0:T(1024)S(1)} %bitcast.152, f32[256]{0:T(256)S(1)} %copy-done.41, f32[256,2048]{1,0:T(8,128)S(1)} %copy-done.3, ...), kind=kLoop, calls=%fused_computation.34 | loop fusion | flops 8912896 | bytes 12603392 | tf_op jit(solution)/shard_map/convert_element_type | solution.py:1381
  (114 shorter events, 0.4 us)
Async XLA Ops:
  0.6 80.0 %copy-start.5 = (bf16[256,2048]{1,0:T(8,128)(2,1)S(1)}, bf16[256,2048]{1,0:T(8,128)(2,1)}, u32[]{:S(2)}) copy-start(bf16[256,2048]{1,0:T(8,128)(2,1)} %param.13) | copy-start | bytes 3145732
  2.3 78.3 %copy-start.42 = (f32[256]{0:T(256)}, f32[256]{0:T(256)S(1)}, u32[]{:S(2)}) copy-start(f32[256]{0:T(256)S(1)} %fusion.19) | copy-start | bytes 3076
  2.3 78.7 %copy-start.39 = (f32[256]{0:T(256)}, f32[256]{0:T(256)S(1)}, u32[]{:S(2)}) copy-start(f32[256]{0:T(256)S(1)} %fusion.31) | copy-start | bytes 3076
  80.6 7.0 %copy-start.31 = (f32[8,1,256]{2,1,0:T(1,128)}, f32[8,1,256]{2,1,0:T(1,128)S(1)}, u32[]{:S(2)}) copy-start(f32[8,1,256]{2,1,0:T(1,128)S(1)} %get-tuple-element.68) | copy-start | bytes 24580
  80.7 18.8 %copy-start.26 = (f32[8,1,256]{2,1,0:T(1,128)}, f32[8,1,256]{2,1,0:T(1,128)S(1)}, u32[]{:S(2)}) copy-start(f32[8,1,256]{2,1,0:T(1,128)S(1)} %get-tuple-element.67) | copy-start | bytes 24580
  81.0 6.7 %copy-start.12 = (bf16[256,2048]{1,0:T(8,128)(2,1)}, bf16[256,2048]{1,0:T(8,128)(2,1)S(1)}, u32[]{:S(2)}) copy-start(bf16[256,2048]{1,0:T(8,128)(2,1)S(1)} %fusion.14.refs_0_) | copy-start | bytes 3145732
  87.7 0.7 copy-start.48
  87.7 0.9 copy-start.49
  90.6 3.1 copy-start.18
  90.9 1.4 copy-start.9
  91.1 1.2 copy-start.16
  91.2 2.5 copy-start.20
  92.3 2.7 copy-start
  92.3 2.7 copy-start.24
  93.7 3.1 copy-start.29
  93.7 3.1 slice-start.2
  95.0 2.5 slice-start.3
  96.8 2.6 copy-start.11
  99.4 1.4 copy-start.1
  99.4 2.6 copy-start.44
  99.5 2.6 copy-start.34
  237.0 42.2 %collective-permute-start.2 = (bf16[2,576,256]{2,1,0:T(8,128)(2,1)}, bf16[2,576,256]{2,1,0:T(8,128)(2,1)}, u32[]{:S(2)}, u32[]{:S(2)}) collective-permute-start(bf16[2,576,256]{2,1,0:T(8,128)(2,1)} %get-tuple-element.45), channel_id=1, source_target_pairs={{0,8},{4,12},{8,0},{12,4},{16,24},{20,28},{24,16},{28,20},{1,9},{5... | collective-permute-start | bytes 1769480 | tf_op jit(solution)/shard_map/ppermute | solution.py:1306
  237.8 41.4 %collective-permute-start.3 = (bf16[2,576,256]{2,1,0:T(8,128)(2,1)}, bf16[2,576,256]{2,1,0:T(8,128)(2,1)}, u32[]{:S(2)}, u32[]{:S(2)}) collective-permute-start(bf16[2,576,256]{2,1,0:T(8,128)(2,1)} %get-tuple-element.46), channel_id=1, source_target_pairs={{0,16},{4,20},{8,24},{12,28},{16,0},{20,4},{24,8},{28,12},{1,17},{... | collective-permute-start | bytes 1769480 | tf_op jit(solution)/shard_map/ppermute | solution.py:1306
  238.3 40.9 %collective-permute-start = (bf16[2,256,1152]{2,1,0:T(8,128)(2,1)}, bf16[2,256,1152]{2,1,0:T(8,128)(2,1)}, u32[]{:S(2)}, u32[]{:S(2)}) collective-permute-start(bf16[2,256,1152]{2,1,0:T(8,128)(2,1)} %get-tuple-element.43), channel_id=1, source_target_pairs={{0,8},{4,12},{8,0},{12,4},{16,24},{20,28},{24,16},{28,20},{1,9},{5... | collective-permute-start | bytes 3538952 | tf_op jit(solution)/shard_map/ppermute | solution.py:1306
  239.8 39.4 %collective-permute-start.1 = (bf16[2,256,1152]{2,1,0:T(8,128)(2,1)}, bf16[2,256,1152]{2,1,0:T(8,128)(2,1)}, u32[]{:S(2)}, u32[]{:S(2)}) collective-permute-start(bf16[2,256,1152]{2,1,0:T(8,128)(2,1)} %get-tuple-element.44), channel_id=1, source_target_pairs={{0,16},{4,20},{8,24},{12,28},{16,0},{20,4},{24,8},{28,12},{1,17},{... | collective-permute-start | bytes 3538952 | tf_op jit(solution)/shard_map/ppermute | solution.py:1306
  241.1 5.9 %copy-start.8 = (bf16[256,2048]{1,0:T(8,128)(2,1)S(1)}, bf16[256,2048]{1,0:T(8,128)(2,1)}, u32[]{:S(2)}) copy-start(bf16[256,2048]{1,0:T(8,128)(2,1)} %c_ref.1) | copy-start | bytes 3145732
  243.5 2.9 copy-start.45
  243.5 3.5 copy-start.2
  243.5 3.5 copy-start.4
  243.5 3.5 copy-start.27
  243.5 3.5 copy-start.35
  246.4 0.6 copy-start.37
  247.7 1.0 copy-start.13
  248.7 4.9 %copy-start.25 = (f32[6,4,256]{2,1,0:T(4,128)S(1)}, f32[6,4,256]{2,1,0:T(4,128)}, u32[]{:S(2)}) copy-start(f32[6,4,256]{2,1,0:T(4,128)} %copy-done.24) | copy-start | bytes 73732
  248.7 4.9 %copy-start.30 = (f32[6,4,256]{2,1,0:T(4,128)S(1)}, f32[6,4,256]{2,1,0:T(4,128)}, u32[]{:S(2)}) copy-start(f32[6,4,256]{2,1,0:T(4,128)} %copy-done.29) | copy-start | bytes 73732
  248.7 5.0 %copy-start.19 = (pred[256,256]{0,1:T(8,128)(4,1)S(1)}, pred[256,256]{0,1:T(8,128)(4,1)}, u32[]{:S(2)}) copy-start(pred[256,256]{0,1:T(8,128)(4,1)} %copy-done.18) | copy-start | bytes 196612
  253.6 4.9 %copy-start.21 = (bf16[256,384]{0,1:T(8,128)(2,1)S(1)}, bf16[256,384]{0,1:T(8,128)(2,1)}, u32[]{:S(2)}) copy-start(bf16[256,384]{0,1:T(8,128)(2,1)} %copy-done.20) | copy-start | bytes 589828
  253.7 9.8 %slice-start = ((s8[6291456]{0:T(1024)(128)(4,1)}), s8[4194304]{0:T(1024)(128)(4,1)S(1)}, s32[]{:S(2)}) async-start(s8[6291456]{0:T(1024)(128)(4,1)} %bitcast.118), calls=%async_computation | async-start | bytes 8388608
  258.5 4.9 %slice-start.1 = ((s8[6291456]{0:T(1024)(128)(4,1)}), s8[2097152]{0:T(1024)(128)(4,1)S(1)}, s32[]{:S(2)}) async-start(s8[6291456]{0:T(1024)(128)(4,1)} %bitcast.118), calls=%async_computation.1 | async-start | bytes 4194304
  263.5 1.9 copy-start.10
  265.4 1.1 copy-start.17
  266.5 2.3 copy-start.6
  266.5 2.3 copy-start.32
  266.5 2.3 copy-start.40
  268.8 8.7 %copy-start.43 = (f32[256]{0:T(256)S(1)}, f32[256]{0:T(256)}, u32[]{:S(2)}) copy-start(f32[256]{0:T(256)} %copy-done.42) | copy-start | bytes 3076
  428.6 2.1 copy-start.14
  428.6 2.1 copy-start.15
  428.6 2.3 copy-start.47
  428.6 2.8 copy-start.23
  430.7 1.0 copy-start.22
  441.8 12.0 %copy-start.3 = (f32[256,2048]{1,0:T(8,128)S(1)}, f32[256,2048]{1,0:T(8,128)}, u32[]{:S(2)}) copy-start(f32[256,2048]{1,0:T(8,128)} %copy-done.1) | copy-start | bytes 6291460
  441.8 12.0 %copy-start.7 = (bf16[256,2048]{1,0:T(8,128)(2,1)S(1)}, bf16[256,2048]{1,0:T(8,128)(2,1)}, u32[]{:S(2)}) copy-start(bf16[256,2048]{1,0:T(8,128)(2,1)} %param.13) | copy-start | bytes 3145732
  441.8 12.0 %copy-start.28 = (f32[8,1,256]{2,1,0:T(1,128)S(1)}, f32[8,1,256]{2,1,0:T(1,128)}, u32[]{:S(2)}) copy-start(f32[8,1,256]{2,1,0:T(1,128)} %copy-done.26) | copy-start | bytes 24580
  441.8 12.0 %copy-start.33 = (f32[8,1,256]{2,1,0:T(1,128)S(1)}, f32[8,1,256]{2,1,0:T(1,128)}, u32[]{:S(2)}) copy-start(f32[8,1,256]{2,1,0:T(1,128)} %copy-done.31) | copy-start | bytes 24580
  441.8 12.0 %copy-start.36 = (f32[256]{0:T(256)S(1)}, f32[256]{0:T(256)}, u32[]{:S(2)}) copy-start(f32[256]{0:T(256)} %copy-done.34) | copy-start | bytes 3076
  441.8 12.0 %copy-start.38 = (f32[256]{0:T(256)S(1)}, f32[256]{0:T(256)}, u32[]{:S(2)}) copy-start(f32[256]{0:T(256)} %copy-done.37) | copy-start | bytes 3076
  441.8 12.0 %copy-start.41 = (f32[256]{0:T(256)S(1)}, f32[256]{0:T(256)}, u32[]{:S(2)}) copy-start(f32[256]{0:T(256)} %copy-done.39) | copy-start | bytes 3076
  441.8 12.0 %copy-start.46 = (f32[256]{0:T(256)S(1)}, f32[256]{0:T(256)}, u32[]{:S(2)}) copy-start(f32[256]{0:T(256)} %multiply_multiply_fusion) | copy-start | bytes 3076

commit v6 on v5

--- a/solution.py
+++ b/solution.py
@@ -178,22 +178,30 @@
 
 
 def first_kernel(
+    x_ref,
     q_ref,
     k_ref,
     v_ref,
     p_ref,
     g_ref,
     c_ref,
+    bias_ref,
+    qkv_out,
+    p_full,
+    c_full,
+    normed_out,
+    rows_out,
+    att_out,
+    g_full,
+    log_out,
     qkv_full,
-    p_full,
-    g_full,
-    c_full,
-    q_buf,
-    k_buf,
-    v_buf,
     p_buf,
-    g_buf,
     c_buf,
+    x_buf,
+    gain_row,
+    normed,
+    qkv,
+    att,
     in_sem,
     out_sem,
     ssem,
@@ -212,22 +220,31 @@
     qc, kc = q_ref.shape[1], k_ref.shape[1]
     cols = ((0, qc), (qc, kc), (qc + kc, kc))
 
+    def region(t, block, h):
+        if t == 3:
+            r = pl.ds(0, depth) if h == 2 else pl.ds(h * (depth // 2), depth // 2)
+            return p_full.at[r, pl.ds(pl.multiple_of(block * rows, rows), rows)]
+        start = pl.multiple_of(block * rows, rows)
+        r = pl.ds(start, rows) if h == 2 else pl.ds(start + h * half, half)
+        return qkv_full.at[r, pl.ds(cols[t][0], cols[t][1])]
+
     locals_in = []
     for i, (src, dst) in enumerate(
-        ((q_ref, q_buf), (k_ref, k_buf), (v_ref, v_buf), (p_ref, p_buf), (g_ref, g_buf), (c_ref, c_buf))
+        (
+            (g_ref, g_full.at[n]),
+            (x_ref, x_buf),
+            (p_ref, p_buf),
+            (c_ref, c_buf),
+            (q_ref, region(0, n, 2)),
+            (k_ref, region(1, n, 2)),
+            (v_ref, region(2, n, 2)),
+        )
     ):
         cp = pltpu.make_async_copy(src, dst, in_sem.at[i])
         cp.start()
         locals_in.append(cp)
 
     greet(others, n, w, True)
-
-    def region(t, block, h):
-        if t == 3:
-            r = pl.ds(0, depth) if h == 2 else pl.ds(h * (depth // 2), depth // 2)
-            return p_full.at[r, pl.ds(pl.multiple_of(block * rows, rows), rows)]
-        r = pl.ds(block * rows, rows) if h == 2 else pl.ds(block * rows + h * half, half)
-        return qkv_full.at[r, pl.ds(cols[t][0], cols[t][1])]
 
     def own(t, h):
         ref = (q_ref, k_ref, v_ref, p_ref)[t]
@@ -257,33 +274,48 @@
         src = own(t, 2) if which == 0 else region(t, block, 2)
         return msg(t, 6 + which, src, block, 2, c)
 
-    line = LineGather(n, w, c_ref, c_full, zs_sem, zr_sem, 4)
-    for t in range(4):
+    def start_own(t):
         to_x(t, 1).start()
         to_y(t, 0).start()
         to_x(t, 0).start()
         to_y(t, 1).start()
-        if t == 0:
-            line.start()
-    for t in range(4):
+
+    def gain(i):
+        return send(g_ref, g_full.at[n], gs_sem.at[i], gr_sem.at[i], others[i], w)
+
+    line = LineGather(n, w, c_ref, c_full, zs_sem, zr_sem, 4)
+    for i in range(7):
+        gain(i).start()
+    start_own(0)
+    line.start()
+    for t in (1, 2):
+        start_own(t)
+    for t in range(3):
         to_c(t, 0).start()
-    for i, peer in enumerate(others):
-        send(g_ref, g_full.at[n], gs_sem.at[i], gr_sem.at[i], peer, w).start()
-
-    outs = (
-        (q_buf, region(0, n, 2)),
-        (k_buf, region(1, n, 2)),
-        (v_buf, region(2, n, 2)),
-        (p_buf, region(3, n, 2)),
-        (g_buf, g_full.at[n]),
-        (c_buf, c_full.at[w]),
-    )
+
     locals_out = []
-    for i, (src, dst) in enumerate(outs):
-        locals_in[i].wait()
-        cp = pltpu.make_async_copy(src, dst, out_sem.at[i])
+
+    def put(src, dst):
+        cp = pltpu.make_async_copy(src, dst, out_sem.at[len(locals_out)])
         cp.start()
         locals_out.append(cp)
+
+    for i in range(7):
+        gain(i).wait()
+    for cp in locals_in:
+        cp.wait()
+    put(p_buf, region(3, n, 2))
+    put(c_buf, c_full.at[w])
+    for k in range(8):
+        gain_row[:, pl.ds(k * rows, rows)] = g_full[k, :, :rows]
+    strip = 16
+
+    @pl.loop(0, x_buf.shape[0] // strip)
+    def _(i):
+        s = pl.ds(pl.multiple_of(i * strip, strip), strip)
+        normed[s, :] = rms_scale(x_buf[s, :].astype(F32), gain_row[...]).astype(BF)
+
+    put(normed, normed_out)
 
     def relay(t):
         to_y(t, 0).wait_recv()
@@ -300,18 +332,66 @@
         on_y(t).wait_recv()
         to_c(t, 3).start()
 
-    for i in range(3):
-        line.near(i)
+    line.near(0)
     relay(0)
+    line.near(1)
+    relay(1)
+    line.near(2)
+    relay(2)
+    start_own(3)
+    to_c(3, 0).start()
     line.near(3)
-    relay(1)
-    relay(2)
-    for i in range(3):
-        line.far(i)
+    line.far(0)
+    line.far(1)
+    for t in range(3):
+        corner(t)
+    line.far(2)
+    for t in range(3):
+        for which in range(4):
+            to_c(t, which).wait_recv()
+    put(qkv_full, qkv_out)
+    tile = 256
+
+    @pl.loop(0, qkv.shape[1] // tile)
+    def _(i):
+        s = pl.ds(pl.multiple_of(i * tile, tile), tile)
+        qkv[:, s] = jnp.dot(normed[...], qkv_full[:, s], preferred_element_type=F32).astype(BF)
+
+    put(qkv, rows_out)
+    line.far(3)
+
+    log_out[...] = jnp.zeros(log_out.shape, F32)
+    pair = 2 * HEAD_DIM
+    group = HEADS // KV_HEADS
+
+    @pl.loop(0, KV_HEADS // 2)
+    def _(i):
+        keys = qkv[:, pl.ds(pl.multiple_of(qc + i * pair, pair), pair)]
+        values = qkv[:, pl.ds(pl.multiple_of(qc + kc + i * pair, pair), pair)]
+        lane = lax.broadcasted_iota(jnp.int32, log_out.shape, 1)
+        for b in range(group):
+            at_cols = pl.ds(pl.multiple_of((i * group + b) * pair, pair), pair)
+            queries = qkv[:, at_cols]
+            side = (2 * b) // group
+            key = keys[:, side * HEAD_DIM : (side + 1) * HEAD_DIM]
+            value = values[:, side * HEAD_DIM : (side + 1) * HEAD_DIM]
+            heads = []
+            for e in range(2):
+                query = queries[:, e * HEAD_DIM : (e + 1) * HEAD_DIM]
+                masked = contract_cols(query, key) * (HEAD_DIM**-0.5) + bias_ref[...]
+                peak = jnp.max(masked, axis=-1, keepdims=True)
+                expo = jnp.exp(masked - peak)
+                total = jnp.sum(expo, axis=-1, keepdims=True)
+                probs = (expo * (1.0 / total)).astype(BF)
+                heads.append(jnp.dot(probs, value, preferred_element_type=F32))
+                log_out[...] = jnp.where(
+                    lane == 2 * (i * group + b) + e, peak + jnp.log(total), log_out[...]
+                )
+            att[:, at_cols] = jnp.concatenate(heads, axis=1).astype(BF)
+
+    put(att, att_out)
     relay(3)
-    line.far(3)
-    for t in range(4):
-        corner(t)
+    corner(3)
     for t in range(4):
         for h in range(2):
             to_x(t, h).wait_send()
@@ -319,37 +399,44 @@
         on_x(t).wait_send()
         on_y(t).wait_send()
         for which in range(4):
-            to_c(t, which).wait()
-    for i, peer in enumerate(others):
-        send(g_ref, g_full.at[n], gs_sem.at[i], gr_sem.at[i], peer, w).wait()
+            if t == 3:
+                to_c(t, which).wait_recv()
+            to_c(t, which).wait_send()
     line.finish()
     for cp in locals_out:
         cp.wait()
 
 
-def gather_first(query, key, value, project, gains, cotangent):
+def gather_first(rows_in, query, key, value, project, gains, cotangent, bias):
     rows = query.shape[0]
     width = query.shape[1] + 2 * key.shape[1]
-    spec = pl.BlockSpec(memory_space=pl.ANY)
+    tokens_here, model = rows_in.shape
+    hbm, vmem = pl.BlockSpec(memory_space=pl.ANY), pl.BlockSpec(memory_space=pltpu.VMEM)
     return pl.pallas_call(
         first_kernel,
         name="gather_first",
         out_shape=(
             jax.ShapeDtypeStruct((8 * rows, width), BF),
             jax.ShapeDtypeStruct((project.shape[0], 8 * rows), BF),
+            jax.ShapeDtypeStruct((4,) + cotangent.shape, BF),
+            jax.ShapeDtypeStruct((tokens_here, model), BF),
+            jax.ShapeDtypeStruct((tokens_here, width), BF),
+            jax.ShapeDtypeStruct((tokens_here, query.shape[1]), BF),
             jax.ShapeDtypeStruct((8,) + gains.shape, gains.dtype),
-            jax.ShapeDtypeStruct((4,) + cotangent.shape, BF),
+            jax.ShapeDtypeStruct((tokens_here, 128), F32),
         ),
-        in_specs=[spec] * 6,
-        out_specs=[spec] * 4,
+        in_specs=[hbm] * 7 + [vmem],
+        out_specs=[hbm] * 6 + [vmem] * 2,
         scratch_shapes=[
-            pltpu.VMEM(query.shape, BF),
-            pltpu.VMEM(key.shape, BF),
-            pltpu.VMEM(value.shape, BF),
+            pltpu.VMEM((8 * rows, width), BF),
             pltpu.VMEM(project.shape, BF),
-            pltpu.VMEM(gains.shape, gains.dtype),
             pltpu.VMEM(cotangent.shape, BF),
-            pltpu.SemaphoreType.DMA((6,)),
+            pltpu.VMEM((tokens_here, model), BF),
+            pltpu.VMEM((1, model), F32),
+            pltpu.VMEM((tokens_here, model), BF),
+            pltpu.VMEM((tokens_here, width), BF),
+            pltpu.VMEM((tokens_here, query.shape[1]), BF),
+            pltpu.SemaphoreType.DMA((7,)),
             pltpu.SemaphoreType.DMA((6,)),
             pltpu.SemaphoreType.DMA((40,)),
             pltpu.SemaphoreType.DMA((40,)),
@@ -359,7 +446,7 @@
             pltpu.SemaphoreType.DMA((16,)),
         ],
         compiler_params=pltpu.CompilerParams(collective_id=1, has_side_effects=True),
-    )(query, key, value, project, gains, cotangent)
+    )(rows_in, query, key, value, project, gains, cotangent, bias)
 
 
 class LineScatter:
@@ -1239,14 +1326,31 @@
     tile_counts,
 ):
     tokens_here, model = block_input.shape
+    group = HEADS // KV_HEADS
+    scale = HEAD_DIM ** (-0.5)
+    q_cols, k_cols = HEADS * HEAD_DIM, KV_HEADS * HEAD_DIM
+    inputs_f = block_input.astype(jnp.float32)
+    ends = jnp.cumsum(doc_lengths[0])
+    position = jnp.arange(tokens_here, dtype=jnp.int32)
+    segment = jnp.sum((position[:, None] >= ends[None, :]).astype(jnp.int32), axis=1)
+    allowed = (segment[:, None] == segment[None, :]) & (position[None, :] <= position[:, None])
     if fast:
         gains = jnp.stack([prenorm_gain, midnorm_gain]).astype(F32).reshape(1, -1)
-        qkv_full, project_full, gains_full, grad_rows = gather_first(
-            query_weight, key_weight, value_weight, project_weight, gains, cotangent
+        bias = jnp.where(allowed, 0.0, -1e30).astype(F32)
+        qkv_full, project_full, grad_rows, normed, qkv, attended, gains_full, logs = gather_first(
+            block_input,
+            query_weight,
+            key_weight,
+            value_weight,
+            project_weight,
+            gains,
+            cotangent,
+            bias,
         )
         gains_full = gains_full.reshape(8, 2, -1)
         first_gain = gains_full[:, 0].reshape(-1)
         second_gain = gains_full[:, 1].reshape(-1)
+        logsum = logs[:, :HEADS].T.reshape(KV_HEADS, group, tokens_here, 1)
     else:
         qkv_full = jnp.concatenate(
             [
@@ -1260,34 +1364,27 @@
         first_gain = lax.all_gather(prenorm_gain, "narrow", axis=0, tiled=True).astype(F32)
         second_gain = lax.all_gather(midnorm_gain, "narrow", axis=0, tiled=True).astype(F32)
         grad_rows = lax.all_gather(cotangent, "wide", axis=0, tiled=True)
-    group = HEADS // KV_HEADS
-    scale = HEAD_DIM ** (-0.5)
-    q_cols, k_cols = HEADS * HEAD_DIM, KV_HEADS * HEAD_DIM
-    inputs_f = block_input.astype(jnp.float32)
-    normed = rms_scale(inputs_f, first_gain).astype(jnp.bfloat16)
-    qkv = jnp.dot(normed, qkv_full, preferred_element_type=jnp.float32).astype(jnp.bfloat16)
+        normed = rms_scale(inputs_f, first_gain).astype(jnp.bfloat16)
+        qkv = jnp.dot(normed, qkv_full, preferred_element_type=jnp.float32).astype(jnp.bfloat16)
     query_rows = qkv[:, :q_cols].reshape(tokens_here, KV_HEADS, group, HEAD_DIM)
     key_rows = qkv[:, q_cols : q_cols + k_cols].reshape(tokens_here, KV_HEADS, HEAD_DIM)
     value_rows = qkv[:, q_cols + k_cols :].reshape(tokens_here, KV_HEADS, HEAD_DIM)
-    ends = jnp.cumsum(doc_lengths[0])
-    position = jnp.arange(tokens_here, dtype=jnp.int32)
-    segment = jnp.sum((position[:, None] >= ends[None, :]).astype(jnp.int32), axis=1)
-    allowed = (segment[:, None] == segment[None, :]) & (position[None, :] <= position[:, None])
-    scores = (
-        jnp.einsum("qcgd,kcd->cgqk", query_rows, key_rows, preferred_element_type=jnp.float32)
-        * scale
-    )
-    masked = jnp.where(allowed, scores, -1e30)
-    peak = jnp.max(masked, axis=-1, keepdims=True)
-    expo = jnp.exp(masked - peak)
-    total = jnp.sum(expo, axis=-1, keepdims=True)
-    probs_low = (expo / total).astype(jnp.bfloat16)
-    logsum = peak + jnp.log(total)
-    attended = (
-        jnp.einsum("cgqk,kcd->qcgd", probs_low, value_rows, preferred_element_type=jnp.float32)
-        .astype(jnp.bfloat16)
-        .reshape(tokens_here, HEADS * HEAD_DIM)
-    )
+    if not fast:
+        scores = (
+            jnp.einsum("qcgd,kcd->cgqk", query_rows, key_rows, preferred_element_type=jnp.float32)
+            * scale
+        )
+        masked = jnp.where(allowed, scores, -1e30)
+        peak = jnp.max(masked, axis=-1, keepdims=True)
+        expo = jnp.exp(masked - peak)
+        total = jnp.sum(expo, axis=-1, keepdims=True)
+        probs_low = (expo / total).astype(jnp.bfloat16)
+        logsum = peak + jnp.log(total)
+        attended = (
+            jnp.einsum("cgqk,kcd->qcgd", probs_low, value_rows, preferred_element_type=jnp.float32)
+            .astype(jnp.bfloat16)
+            .reshape(tokens_here, HEADS * HEAD_DIM)
+        )
     branch = jnp.dot(attended, project_full, preferred_element_type=jnp.float32)
     middle = inputs_f + branch
     mixed_in = rms_scale(middle, second_gain).astype(jnp.bfloat16)
@@ -1384,6 +1481,7 @@
         gain_parts = jnp.stack(
             [first_gain_part.reshape(8, -1), second_gain_part.reshape(8, -1)], axis=1
         ).reshape(8, 1, -1)
+        input_grad, qkv_back = lax.optimization_barrier((input_grad, qkv_back))
         qkv_total, project_total, ffn_totals, feed, gain_total = reduce_last(
             (normed, qkv_back, branch_back, attended),
             stays,

time: 469 us -> 455 us (0.970)
  matrix products: 35.6 us -> 26.9 us
  Pallas kernels: 360 us -> 353 us
  local copies, waits for them, and re-layouts: 15.3 us -> 21.6 us
    dot_general x2 -> x0, matrix products: 8.42 us -> none  [the longest x1 6.65 us: per_device(): jnp.dot(normed, qkv_full, preferred_element_type=jnp.float32)]
    pallas_call x1, Pallas kernels: 135 us -> 127 us  [feed_forward(): pl.pallas_call(middle_kernel, name='feed_forward', out_shape=(jax.ShapeDt...]
    convert_element_type x2 -> x3, other arithmetic: 19.3 us -> 16.8 us  [per_device(): gate_total, up_total, down_total = [t.astype(F32) for t in ffn_totals]]
  transfers between devices with their start and end apart: 4 -> 4, of which waited for: 0 -> 0; matrix products, arithmetic and copies ran while one was open for 8% -> 10% of each run, Pallas kernels for 0% -> 0%
where the time goes in v6:
time: 455 us; the launch traced here: 449 us
  Pallas kernels  353 us (78%)
  other arithmetic  41.2 us (9%)
  matrix products  26.9 us (6%)
  local copies, waits for them, and re-layouts  21.6 us (5%)
    pallas_call x1, Pallas kernels, reduce_last(): pl.pallas_call(functools.partial(last_kernel, items), name='reduce_last',...  149 us
    pallas_call x1, Pallas kernels, feed_forward(): pl.pallas_call(middle_kernel, name='feed_forward', out_shape=(jax.ShapeDt...  127 us
    pallas_call x1, Pallas kernels, gather_first(): pl.pallas_call(first_kernel, name='gather_first', out_shape=(jax.ShapeDty...  77.4 us
    convert_element_type x3, other arithmetic, per_device(): gate_total, up_total, down_total = [t.astype(F32) for t in ffn_totals]  16.8 us
    dot_general x2, matrix products, contract_cols(): lax.dot_general(left, right, (((1,), (1,)), ((), ())), preferred_element_...  11.8 us
  transfers between devices with their start and end apart: 4, of which 0 were waited for; matrix products, arithmetic and copies ran while one was open for 10% of the time, Pallas kernels for 0%

profile of v6, /device:TPU:0, one launch (start us, length us, event | category | flops | bytes accessed | tf_op | source)
XLA Modules:
  0.0 448.6 jit_solution(5789540194673982286)
XLA Ops:
  0.6 0.7 stack.13
  1.3 0.7 stack.12
  2.0 0.6 copy.76
  2.6 0.8 reduce-window.8
  3.4 0.1 convert_reduce_fusion
  3.5 0.6 copy-done.25
  4.0 0.8 broadcast_select_fusion.bias_ref
  4.8 1.5 fusion.12
  6.4 77.4 %gather_first.1 = (bf16[2048,2304]{1,0:T(8,128)(2,1)}, bf16[1536,2048]{1,0:T(8,128)(2,1)}, bf16[4,256,2048]{2,1,0:T(8,128)(2,1)}, bf16[256,2048]{1,0:T(8,128)(2,...) custom-call(bf16[256,2048]{1,0:T(8,128)(2,1)} %x_ref.1, ...), custom_call_target="tpu_custom_call" | custom-call | tf_op jit(solution)/shard_map/gather_first/pallas_call | solution.py:415
  83.8 0.8 reduce
  84.5 0.6 fusion.33
  85.2 0.6 fusion.27
  85.8 1.2 compare_convert_fusion.live
  87.0 5.0 %multiply_reduce_fusion.2 = (f32[256]{0:T(256)S(1)}, f32[256,2048]{1,0:T(8,128)S(1)}) fusion(bf16[256,1536]{1,0:T(8,128)(2,1)} %get-tuple-element.40.refs_3_, bf16[1536,2048]{1,0:T(8,128)(2,1)} %get-tuple-element.41, bf16[256,2048]{1,0:T(8,128)(2,1)S(1)} %copy-done.5), kind=kOutput, calls=%fused_computation.32 | convolution fusion | flops 1612709632 | bytes 10224640 | tf_op jit(solution)/shard_map/dot_general | solution.py:1388
  92.0 0.6 fusion.25
  92.7 0.7 copy-done
  93.3 1.2 multiply_convert_fusion.mixed
  94.6 126.6 %feed_forward.1 = (f32[256,2048]{1,0:T(8,128)}, bf16[4,256,2048]{2,1,0:T(8,128)(2,1)}, bf16[2,256,1152]{2,1,0:T(8,128)(2,1)}, bf16[2,256,1152]{2,1,0:T(8,128)(2,...) custom-call(bf16[256,2048]{1,0:T(8,128)(2,1)} %multiply_convert_fusi, ...), custom_call_target="tpu_custom_call" | custom-call | tf_op jit(solution)/shard_map/feed_forward/pallas_call | solution.py:808
  221.2 0.9 collective-permute-start
  222.1 0.6 collective-permute-start.1
  222.6 1.4 collective-permute-start.2
  224.0 1.3 collective-permute-start.3
  225.3 1.1 fusion.32
  226.4 2.1 slice.37
  228.5 0.7 fusion.24
  229.2 2.3 multiply_reduce_fusion
  231.5 0.2 copy-done.7
  231.7 0.7 fusion.31.refs_2_
  232.4 1.0 copy-done.9
  233.4 4.6 %convolution_convert_fusion = bf16[256,1536]{1,0:T(8,128)(2,1)S(1)} fusion(bf16[256,2048]{1,0:T(8,128)(2,1)S(1)} %fusion.31.refs_2_, bf16[1536,2048]{1,0:T(8,128)(2,1)} %get-tuple-element.41), kind=kOutput, calls=%fused_computation.20 | convolution fusion | flops 1611005952 | bytes 8126464 | tf_op jit(solution)/shard_map/dot_general | solution.py:34
  238.0 1.2 copy.60
  239.1 0.1 copy.55
  239.3 1.4 copy.57
  240.7 0.9 slice_bitcast_fusion
  241.7 0.6 sub.25
  242.3 1.0 copy.56
  243.3 0.1 copy.59
  243.5 1.0 fusion.35
  244.5 0.1 copy-done.11
  244.6 1.9 fusion.21
  246.5 4.6 %fusion = (f32[6,4,256]{2,1,0:T(4,128)S(1)}, f32[6,256,256,4]{2,1,3,0:T(8,128)}) fusion(f32[6,256,256,4]{2,1,3,0:T(8,128)S(1)} %fusion.35, f32[6,4,256]{2,1,0:T(4,128)S(1)} %copy-done.18, pred[256,256]{0,1:T(8,128)(4,1)S(1)} %copy.56, bf16[256,6,64,1]{0,2,3,1:T(8,128)(2,1)S(1)} %bitcast.115, bf16[256,6,4,64]{0,3,2,1:T(8,128)(2,1)S(1)} %bitcast.107), kind=kOutput, calls=%fused_computation.2 | convolution fusion | flops 209184768 | bytes 13680640 | tf_op jit(solution)/shard_map/qcgd,kcd->cgqk/dot_general | solution.py:1450
  251.1 4.6 %fusion.2 = bf16[6,4,256,256]{2,3,1,0:T(8,128)(2,1)S(1)} fusion(f32[6,256,256,4]{2,1,3,0:T(8,128)} %get-tuple-element.84, f32[6,256,256,4]{2,1,3,0:T(8,128)S(1)} %fusion.35, f32[6,4,256]{2,1,0:T(4,128)S(1)} %get-tuple-element.83, f32[6,4,256]{2,1,0:T(4,128)S(1)} %copy-done.18, pred[256,256]{0,1:T(8,128)(4,1)S(1)} %copy.56), kind=kLoop, calls=%fused_computation.4 | loop fusion | flops 9437184 | bytes 15843328 | tf_op jit(solution)/shard_map/convert_element_type | solution.py:1455
  255.7 1.1 fusion.20
  256.8 1.6 multiply_convert_fusion.1
  258.4 1.2 copy.66
  259.5 0.8 copy.65
  260.4 2.3 copy.64
  262.7 7.2 %fusion.15 = (f32[2048]{0:T(1024)S(1)}, f32[256]{0:T(256)S(1)}, f32[256,2048]{1,0:T(8,128)S(1)}) fusion(bf16[256,2048]{1,0:T(8,128)(2,1)S(1)} %copy-done.6, f32[256]{0:T(256)} %get-tuple-element.87, f32[2048]{0:T(1024)} %bitcast.124, bf16[2048,2304]{1,0:T(8,128)(2,1)} %get-tuple-element.48, bf16[256,384]{1,0:T(8,128)(2,1)S(1)} %copy.66, ...), kind=kOutput, calls=%fused_computation.27 | convolution fusion | flops 2423125760 | bytes 13780992 | tf_op jit(solution)/shard_map/dot_general | solution.py:34
  270.0 2.2 fusion.11
  272.2 1.1 pad_maximum_fusion.refs_1_
  273.4 0.6 reshape.207.refs_13_
  274.0 149.4 %reduce_last.1 = (bf16[4,64,1152]{2,1,0:T(8,128)(2,1)}, bf16[4,64,1152]{2,1,0:T(8,128)(2,1)}, bf16[4,64,768]{2,1,0:T(8,128)(2,1)}, bf16[4,64,768]{2,1,0:T(8,128)...) custom-call(bf16[256,2048]{1,0:T(8,128)(2,1)} %get-tuple-element.42., ...), custom_call_target="tpu_custom_call" | custom-call | tf_op jit(solution)/shard_map/reduce_last/pallas_call | solution.py:1294
  423.5 1.5 maximum_convert_fusion
  425.1 0.9 maximum_convert_fusion.1
  426.0 0.7 copy-done.14
  426.7 1.2 add_convert_fusion
  427.9 1.4 slice.48
  429.3 0.2 copy.68
  429.5 0.2 copy.67
  429.7 0.6 fusion.34
  430.2 7.1 %bitcast_convert_fusion.1 = f32[2048,1152]{1,0:T(8,128)} fusion(bf16[8,256,1152]{2,1,0:T(8,128)(2,1)} %get-tuple-element.66), kind=kLoop, calls=%fused_computation.9 | loop fusion | flops 2359296 | bytes 14155776 | tf_op jit(solution)/shard_map/convert_element_type | solution.py:1496
  437.4 4.7 %bitcast_convert_fusion = f32[2048,1152]{1,0:T(8,128)} fusion(bf16[8,256,1152]{2,1,0:T(8,128)(2,1)S(1)} %bitcast.104), kind=kLoop, calls=%fused_computation.8 | loop fusion | flops 2359296 | bytes 14155776 | tf_op jit(solution)/shard_map/convert_element_type | solution.py:1496
  442.1 4.9 %convert_element_type.121 = f32[1152,2048]{1,0:T(8,128)} convert(bf16[1152,2048]{1,0:T(8,128)(2,1)S(1)} %bitcast.102) | non-fusion elementwise | flops 2359296 | bytes 14155776 | tf_op jit(solution)/shard_map/convert_element_type | solution.py:1496
  447.1 1.3 convert_bitcast_fusion
  (86 shorter events, 0.3 us)
Async XLA Ops:
  3.5 0.6 copy-start.25
  6.3 85.7 %copy-start.29 = (f32[256]{0:T(256)}, f32[256]{0:T(256)S(1)}, u32[]{:S(2)}) copy-start(f32[256]{0:T(256)S(1)} %fusion.12) | copy-start | bytes 3076
  6.4 78.8 %copy-start.35 = (s32[4]{0:T(128)S(1)}, s32[4]{0:T(128)}, u32[]{:S(2)}) copy-start(s32[4]{0:T(128)} %param.25) | copy-start | bytes 52
  6.4 80.7 %copy-start.5 = (bf16[256,2048]{1,0:T(8,128)(2,1)S(1)}, bf16[256,2048]{1,0:T(8,128)(2,1)}, u32[]{:S(2)}) copy-start(bf16[256,2048]{1,0:T(8,128)(2,1)} %x_ref.1) | copy-start | bytes 3145732
  85.2 7.5 %copy-start.19 = (f32[8,1,256]{2,1,0:T(1,128)}, f32[8,1,256]{2,1,0:T(1,128)S(1)}, u32[]{:S(2)}) copy-start(f32[8,1,256]{2,1,0:T(1,128)S(1)} %get-tuple-element.78) | copy-start | bytes 24580
  92.0 1.3 copy-start
  92.0 2.5 copy-start.32
  92.7 1.9 copy-start.22
  221.2 7.3 %copy-start.26 = (s32[256]{0:T(256)S(1)}, s32[256]{0:T(256)}, u32[]{:S(2)}) copy-start(s32[256]{0:T(256)} %copy-done.25) | copy-start | bytes 3076
  221.2 8.0 %copy-start.1 = (f32[256,2048]{1,0:T(8,128)S(1)}, f32[256,2048]{1,0:T(8,128)}, u32[]{:S(2)}) copy-start(f32[256,2048]{1,0:T(8,128)} %copy-done) | copy-start | bytes 6291460
  221.2 8.0 %copy-start.20 = (f32[8,1,256]{2,1,0:T(1,128)S(1)}, f32[8,1,256]{2,1,0:T(1,128)}, u32[]{:S(2)}) copy-start(f32[8,1,256]{2,1,0:T(1,128)} %copy-done.19) | copy-start | bytes 24580
  221.2 8.0 %copy-start.23 = (f32[256]{0:T(256)S(1)}, f32[256]{0:T(256)}, u32[]{:S(2)}) copy-start(f32[256]{0:T(256)} %copy-done.22) | copy-start | bytes 3076
  221.2 52.8 %collective-permute-start = (bf16[2,256,1152]{2,1,0:T(8,128)(2,1)}, bf16[2,256,1152]{2,1,0:T(8,128)(2,1)}, u32[]{:S(2)}, u32[]{:S(2)}) collective-permute-start(bf16[2,256,1152]{2,1,0:T(8,128)(2,1)} %get-tuple-element.54), channel_id=1, source_target_pairs={{0,8},{4,12},{8,0},{12,4},{16,24},{20,28},{24,16},{28,20},{1,9},{5... | collective-permute-start | bytes 3538952 | tf_op jit(solution)/shard_map/ppermute | solution.py:1403
  222.1 51.9 %collective-permute-start.1 = (bf16[2,256,1152]{2,1,0:T(8,128)(2,1)}, bf16[2,256,1152]{2,1,0:T(8,128)(2,1)}, u32[]{:S(2)}, u32[]{:S(2)}) collective-permute-start(bf16[2,256,1152]{2,1,0:T(8,128)(2,1)} %get-tuple-element.55), channel_id=1, source_target_pairs={{0,16},{4,20},{8,24},{12,28},{16,0},{20,4},{24,8},{28,12},{1,17},{... | collective-permute-start | bytes 3538952 | tf_op jit(solution)/shard_map/ppermute | solution.py:1403
  222.6 51.4 %collective-permute-start.2 = (bf16[2,576,256]{2,1,0:T(8,128)(2,1)}, bf16[2,576,256]{2,1,0:T(8,128)(2,1)}, u32[]{:S(2)}, u32[]{:S(2)}) collective-permute-start(bf16[2,576,256]{2,1,0:T(8,128)(2,1)} %get-tuple-element.56), channel_id=1, source_target_pairs={{0,8},{4,12},{8,0},{12,4},{16,24},{20,28},{24,16},{28,20},{1,9},{5... | collective-permute-start | bytes 1769480 | tf_op jit(solution)/shard_map/ppermute | solution.py:1403
  224.0 50.0 %collective-permute-start.3 = (bf16[2,576,256]{2,1,0:T(8,128)(2,1)}, bf16[2,576,256]{2,1,0:T(8,128)(2,1)}, u32[]{:S(2)}, u32[]{:S(2)}) collective-permute-start(bf16[2,576,256]{2,1,0:T(8,128)(2,1)} %get-tuple-element.57), channel_id=1, source_target_pairs={{0,16},{4,20},{8,24},{12,28},{16,0},{20,4},{24,8},{28,12},{1,17},{... | collective-permute-start | bytes 1769480 | tf_op jit(solution)/shard_map/ppermute | solution.py:1403
  229.2 2.3 copy-start.33
  229.2 2.3 copy-start.3
  229.2 2.5 copy-start.7
  231.7 0.7 copy-start.27
  232.4 1.0 copy-start.9
  243.5 1.1 copy-start.11
  243.5 1.1 copy-start.18
  258.4 4.3 copy-start.6
  262.6 7.2 %copy-start.30 = (f32[256]{0:T(256)S(1)}, f32[256]{0:T(256)}, u32[]{:S(2)}) copy-start(f32[256]{0:T(256)} %copy-done.29) | copy-start | bytes 3076
  262.7 7.3 %copy-start.4 = (f32[256,2048]{1,0:T(8,128)S(1)}, f32[256,2048]{1,0:T(8,128)}, u32[]{:S(2)}) copy-start(f32[256,2048]{1,0:T(8,128)} %get-tuple-element.45) | copy-start | bytes 6291460
  262.7 7.3 %copy-start.8 = (bf16[256,2048]{1,0:T(8,128)(2,1)S(1)}, bf16[256,2048]{1,0:T(8,128)(2,1)}, u32[]{:S(2)}) copy-start(bf16[256,2048]{1,0:T(8,128)(2,1)} %c_ref.1) | copy-start | bytes 3145732
  262.7 7.3 %copy-start.21 = (f32[8,1,256]{2,1,0:T(1,128)S(1)}, f32[8,1,256]{2,1,0:T(1,128)}, u32[]{:S(2)}) copy-start(f32[8,1,256]{2,1,0:T(1,128)} %get-tuple-element.77) | copy-start | bytes 24580
  262.7 7.3 %copy-start.24 = (f32[256]{0:T(256)S(1)}, f32[256]{0:T(256)}, u32[]{:S(2)}) copy-start(f32[256]{0:T(256)} %copy-done.22) | copy-start | bytes 3076
  262.7 7.3 %copy-start.28 = (f32[256]{0:T(256)S(1)}, f32[256]{0:T(256)}, u32[]{:S(2)}) copy-start(f32[256]{0:T(256)} %copy-done.27) | copy-start | bytes 3076
  262.7 7.3 %copy-start.31 = (f32[256]{0:T(256)S(1)}, f32[256]{0:T(256)}, u32[]{:S(2)}) copy-start(f32[256]{0:T(256)} %get-tuple-element.87) | copy-start | bytes 3076
  270.0 2.3 copy-start.10
  270.0 2.2 copy-start.15
  423.5 1.6 copy-start.12
  423.5 1.6 copy-start.13
  423.5 2.5 copy-start.2
  423.5 3.2 copy-start.14
  427.9 1.4 copy-start.17
  427.9 1.5 copy-start.16
  427.9 1.7 copy-start.34
  429.5 7.9 %slice-start.2 = ((s8[4718592]{0:T(1024)(128)(4,1)}), s8[524288]{0:T(1024)(128)(4,1)S(1)}, s32[]{:S(2)}) async-start(s8[4718592]{0:T(1024)(128)(4,1)} %bitcast.103), calls=%async_computation.2 | async-start | bytes 1048576
  430.2 7.2 %slice-start.3 = ((s8[4718592]{0:T(1024)(128)(4,1)}), s8[4194304]{0:T(1024)(128)(4,1)S(1)}, s32[]{:S(2)}) async-start(s8[4718592]{0:T(1024)(128)(4,1)} %bitcast.103), calls=%async_computation.3 | async-start | bytes 8388608
  430.2 11.9 %slice-start = ((s8[4718592]{0:T(1024)(128)(4,1)}), s8[4194304]{0:T(1024)(128)(4,1)S(1)}, s32[]{:S(2)}) async-start(s8[4718592]{0:T(1024)(128)(4,1)} %bitcast.101), calls=%async_computation | async-start | bytes 8388608
  437.4 4.7 %slice-start.1 = ((s8[4718592]{0:T(1024)(128)(4,1)}), s8[524288]{0:T(1024)(128)(4,1)S(1)}, s32[]{:S(2)}) async-start(s8[4718592]{0:T(1024)(128)(4,1)} %bitcast.101), calls=%async_computation.1 | async-start | bytes 1048576

commit v7 on v6

--- a/solution.py
+++ b/solution.py
@@ -447,6 +447,65 @@
         ],
         compiler_params=pltpu.CompilerParams(collective_id=1, has_side_effects=True),
     )(rows_in, query, key, value, project, gains, cotangent, bias)
+
+
+def attention_back_kernel(qkv, back, logs, bias, out):
+    q_cols, k_cols = HEADS * HEAD_DIM, KV_HEADS * HEAD_DIM
+    pair = 2 * HEAD_DIM
+    group = HEADS // KV_HEADS
+    scale = HEAD_DIM**-0.5
+
+    @pl.loop(0, KV_HEADS // 2)
+    def _(i):
+        key_at = pl.ds(pl.multiple_of(q_cols + i * pair, pair), pair)
+        value_at = pl.ds(pl.multiple_of(q_cols + k_cols + i * pair, pair), pair)
+        keys, values = qkv[:, key_at], qkv[:, value_at]
+        lane = lax.broadcasted_iota(jnp.int32, logs.shape, 1)
+        key_backs, value_backs = [], []
+        for side in range(2):
+            key = keys[:, side * HEAD_DIM : (side + 1) * HEAD_DIM]
+            value = values[:, side * HEAD_DIM : (side + 1) * HEAD_DIM]
+            key_back = jnp.zeros(key.shape, F32)
+            value_back = jnp.zeros(key.shape, F32)
+            for b in range(side * group // 2, (side + 1) * group // 2):
+                at_cols = pl.ds(pl.multiple_of((i * group + b) * pair, pair), pair)
+                queries, backs = qkv[:, at_cols], back[:, at_cols]
+                heads = []
+                for e in range(2):
+                    query = queries[:, e * HEAD_DIM : (e + 1) * HEAD_DIM]
+                    given = backs[:, e * HEAD_DIM : (e + 1) * HEAD_DIM]
+                    logsum = jnp.sum(
+                        jnp.where(lane == 2 * (i * group + b) + e, logs[...], 0.0),
+                        axis=-1,
+                        keepdims=True,
+                    )
+                    probs = jnp.exp(contract_cols(query, key) * scale + bias[...] - logsum)
+                    value_back = value_back + contract_rows(probs.astype(BF), given)
+                    probs_back = contract_cols(given, value)
+                    inner = jnp.sum(probs * probs_back, axis=-1, keepdims=True)
+                    scores_back = (probs * (probs_back - inner)).astype(BF)
+                    heads.append(jnp.dot(scores_back, key, preferred_element_type=F32) * scale)
+                    key_back = key_back + contract_rows(scores_back, query)
+                out[:, at_cols] = jnp.concatenate(heads, axis=1).astype(BF)
+            key_backs.append(key_back * scale)
+            value_backs.append(value_back)
+        out[:, key_at] = jnp.concatenate(key_backs, axis=1).astype(BF)
+        out[:, value_at] = jnp.concatenate(value_backs, axis=1).astype(BF)
+
+
+def attention_back(qkv, back, logs, bias):
+    vmem = pl.BlockSpec(memory_space=pltpu.VMEM)
+    heads = HEADS * qkv.shape[0] * qkv.shape[0]
+    return pl.pallas_call(
+        attention_back_kernel,
+        name="attention_back",
+        out_shape=jax.ShapeDtypeStruct(qkv.shape, BF),
+        in_specs=[vmem] * 4,
+        out_specs=vmem,
+        cost_estimate=pl.CostEstimate(
+            flops=10 * heads * HEAD_DIM, bytes_accessed=8 * qkv.size, transcendentals=heads
+        ),
+    )(qkv, back, logs, bias)
 
 
 class LineScatter:
@@ -1350,7 +1409,6 @@
         gains_full = gains_full.reshape(8, 2, -1)
         first_gain = gains_full[:, 0].reshape(-1)
         second_gain = gains_full[:, 1].reshape(-1)
-        logsum = logs[:, :HEADS].T.reshape(KV_HEADS, group, tokens_here, 1)
     else:
         qkv_full = jnp.concatenate(
             [
@@ -1366,10 +1424,10 @@
         grad_rows = lax.all_gather(cotangent, "wide", axis=0, tiled=True)
         normed = rms_scale(inputs_f, first_gain).astype(jnp.bfloat16)
         qkv = jnp.dot(normed, qkv_full, preferred_element_type=jnp.float32).astype(jnp.bfloat16)
-    query_rows = qkv[:, :q_cols].reshape(tokens_here, KV_HEADS, group, HEAD_DIM)
-    key_rows = qkv[:, q_cols : q_cols + k_cols].reshape(tokens_here, KV_HEADS, HEAD_DIM)
-    value_rows = qkv[:, q_cols + k_cols :].reshape(tokens_here, KV_HEADS, HEAD_DIM)
     if not fast:
+        query_rows = qkv[:, :q_cols].reshape(tokens_here, KV_HEADS, group, HEAD_DIM)
+        key_rows = qkv[:, q_cols : q_cols + k_cols].reshape(tokens_here, KV_HEADS, HEAD_DIM)
+        value_rows = qkv[:, q_cols + k_cols :].reshape(tokens_here, KV_HEADS, HEAD_DIM)
         scores = (
             jnp.einsum("qcgd,kcd->cgqk", query_rows, key_rows, preferred_element_type=jnp.float32)
             * scale
@@ -1429,49 +1487,49 @@
     middle_norm_back, second_gain_part = second_backward(mixed_back)
     middle_back = out_grad + middle_norm_back
     branch_back = middle_back.astype(jnp.bfloat16)
-    attended_back = (
-        contract_cols(branch_back, project_full)
-        .astype(jnp.bfloat16)
-        .reshape(tokens_here, KV_HEADS, group, HEAD_DIM)
-    )
-    scores_again = (
-        jnp.einsum("qcgd,kcd->cgqk", query_rows, key_rows, preferred_element_type=jnp.float32)
-        * scale
-    )
-    probs_again = jnp.where(allowed, jnp.exp(scores_again - logsum), 0.0)
-    probs_again_low = probs_again.astype(jnp.bfloat16)
-    value_back = (
-        jnp.einsum(
-            "cgqk,qcgd->kcd", probs_again_low, attended_back, preferred_element_type=jnp.float32
-        )
-        .astype(jnp.bfloat16)
-        .reshape(tokens_here, KV_HEADS * HEAD_DIM)
-    )
-    probs_back = jnp.einsum(
-        "qcgd,kcd->cgqk", attended_back, value_rows, preferred_element_type=jnp.float32
-    )
-    scores_back = (
-        probs_again * (probs_back - jnp.sum(probs_again * probs_back, axis=-1, keepdims=True))
-    ).astype(jnp.bfloat16)
-    query_back = (
-        (
-            jnp.einsum("cgqk,kcd->qcgd", scores_back, key_rows, preferred_element_type=jnp.float32)
+    attended_back = contract_cols(branch_back, project_full).astype(jnp.bfloat16)
+    if fast:
+        qkv_back = attention_back(qkv, attended_back, logs, bias)
+    else:
+        attended_back = attended_back.reshape(tokens_here, KV_HEADS, group, HEAD_DIM)
+        scores_again = (
+            jnp.einsum("qcgd,kcd->cgqk", query_rows, key_rows, preferred_element_type=jnp.float32)
             * scale
         )
-        .astype(jnp.bfloat16)
-        .reshape(tokens_here, HEADS * HEAD_DIM)
-    )
-    key_back = (
-        (
+        probs_again = jnp.where(allowed, jnp.exp(scores_again - logsum), 0.0)
+        probs_again_low = probs_again.astype(jnp.bfloat16)
+        value_back = (
             jnp.einsum(
-                "cgqk,qcgd->kcd", scores_back, query_rows, preferred_element_type=jnp.float32
+                "cgqk,qcgd->kcd", probs_again_low, attended_back, preferred_element_type=jnp.float32
             )
-            * scale
-        )
-        .astype(jnp.bfloat16)
-        .reshape(tokens_here, KV_HEADS * HEAD_DIM)
-    )
-    qkv_back = jnp.concatenate([query_back, key_back, value_back], axis=1)
+            .astype(jnp.bfloat16)
+            .reshape(tokens_here, KV_HEADS * HEAD_DIM)
+        )
+        probs_back = jnp.einsum(
+            "qcgd,kcd->cgqk", attended_back, value_rows, preferred_element_type=jnp.float32
+        )
+        scores_back = (
+            probs_again * (probs_back - jnp.sum(probs_again * probs_back, axis=-1, keepdims=True))
+        ).astype(jnp.bfloat16)
+        query_back = (
+            (
+                jnp.einsum("cgqk,kcd->qcgd", scores_back, key_rows, preferred_element_type=jnp.float32)
+                * scale
+            )
+            .astype(jnp.bfloat16)
+            .reshape(tokens_here, HEADS * HEAD_DIM)
+        )
+        key_back = (
+            (
+                jnp.einsum(
+                    "cgqk,qcgd->kcd", scores_back, query_rows, preferred_element_type=jnp.float32
+                )
+                * scale
+            )
+            .astype(jnp.bfloat16)
+            .reshape(tokens_here, KV_HEADS * HEAD_DIM)
+        )
+        qkv_back = jnp.concatenate([query_back, key_back, value_back], axis=1)
     normed_back = contract_cols(qkv_back, qkv_full)
     unused_first, first_backward = jax.vjp(rms_scale, inputs_f, first_gain)
     input_norm_back, first_gain_part = first_backward(normed_back)

time: 455 us -> 445 us (0.978)
  local copies, waits for them, and re-layouts: 21.6 us -> 8.19 us
  Pallas kernels: 353 us -> 366 us
  matrix products: 26.9 us -> 19 us
    pallas_call x0 -> x1, Pallas kernels: none -> 13.2 us  [attention_back(): pl.pallas_call(attention_back_kernel, name='attention_back', out_shape=ja...]
    dot_general x5 -> x0, matrix products: 10.1 us -> none  [the longest x1 4.55 us: per_device(): jnp.einsum('qcgd,kcd->cgqk', attended_back, value_rows, preferred_element...]
    slice x5 -> x0, local copies, waits for them, and re-layouts: 4.82 us -> none  [the longest x2 3.47 us: per_device(): query_rows = qkv[:, :q_cols].reshape(tokens_here, KV_HEADS, group, HEAD_DIM)]
    convert_element_type x1 -> x0, other arithmetic: 4.64 us -> none  [per_device(): scores_back = (probs_again * (probs_back - jnp.sum(probs_again * probs_ba...]
  transfers between devices with their start and end apart: 4 -> 4, of which waited for: 0 -> 0; matrix products, arithmetic and copies ran while one was open for 10% -> 6% of each run, Pallas kernels for 0% -> 3%
where the time goes in v7:
time: 445 us; the launch traced here: 438 us
  Pallas kernels  366 us (82%)
  other arithmetic  39.4 us (9%)
  matrix products  19 us (4%)
  local copies, waits for them, and re-layouts  8.19 us (2%)
    pallas_call x1, Pallas kernels, reduce_last(): pl.pallas_call(functools.partial(last_kernel, items), name='reduce_last',...  149 us
    pallas_call x1, Pallas kernels, feed_forward(): pl.pallas_call(middle_kernel, name='feed_forward', out_shape=(jax.ShapeDt...  126 us
    pallas_call x1, Pallas kernels, gather_first(): pl.pallas_call(first_kernel, name='gather_first', out_shape=(jax.ShapeDty...  77.3 us
    convert_element_type x3, other arithmetic, per_device(): gate_total, up_total, down_total = [t.astype(F32) for t in ffn_totals]  16.8 us
    dot_general x2, matrix products, contract_cols(): lax.dot_general(left, right, (((1,), (1,)), ((), ())), preferred_element_...  14 us
    pallas_call x1, Pallas kernels, attention_back(): pl.pallas_call(attention_back_kernel, name='attention_back', out_shape=ja...  13.2 us
  transfers between devices with their start and end apart: 4, of which 0 were waited for; matrix products, arithmetic and copies ran while one was open for 6% of the time, Pallas kernels for 3%

profile of v7, /device:TPU:0, one launch (start us, length us, event | category | flops | bytes accessed | tf_op | source)
XLA Modules:
  0.0 438.4 jit_solution(8961671667524444015)
XLA Ops:
  0.6 0.8 reduce-window.8
  1.5 0.1 convert_reduce_fusion
  1.6 1.5 fusion.3
  3.1 0.7 stack.12
  3.7 0.7 stack.13
  4.4 0.6 copy.28
  5.0 1.3 fusion.11
  6.3 1.2 compare_convert_fusion.live
  7.5 0.8 fusion.8.bias_ref.bias
  8.3 77.3 %gather_first.1 = (bf16[2048,2304]{1,0:T(8,128)(2,1)}, bf16[1536,2048]{1,0:T(8,128)(2,1)}, bf16[4,256,2048]{2,1,0:T(8,128)(2,1)}, bf16[256,2048]{1,0:T(8,128)(2,...) custom-call(bf16[256,2048]{1,0:T(8,128)(2,1)} %x_ref.1, ...), custom_call_target="tpu_custom_call" | custom-call | tf_op jit(solution)/shard_map/gather_first/pallas_call | solution.py:415
  85.7 0.8 reduce
  86.5 0.6 fusion.13
  87.1 0.0 copy-done.4
  87.1 5.0 %multiply_reduce_fusion.2 = (f32[256]{0:T(256)S(1)}, f32[256,2048]{1,0:T(8,128)S(1)}) fusion(bf16[256,1536]{1,0:T(8,128)(2,1)} %get-tuple-element.40.refs_3_, bf16[1536,2048]{1,0:T(8,128)(2,1)} %get-tuple-element.41, bf16[256,2048]{1,0:T(8,128)(2,1)S(1)} %copy-done.4), kind=kOutput, calls=%fused_computation.21 | convolution fusion | flops 1612709632 | bytes 10224640 | tf_op jit(solution)/shard_map/dot_general | solution.py:1446
  92.1 0.0 copy-start
  92.1 0.0 copy-start.20
  92.1 0.0 copy-done.17
  92.1 0.6 fusion.9
  92.7 0.0 copy-done.12
  92.7 0.7 copy-done
  93.4 1.2 multiply_convert_fusion.mixed
  94.6 0.0 copy-done.20
  94.6 0.0 copy-done.15
  94.6 126.4 %feed_forward.1 = (f32[256,2048]{1,0:T(8,128)}, bf16[4,256,2048]{2,1,0:T(8,128)(2,1)}, bf16[2,256,1152]{2,1,0:T(8,128)(2,1)}, bf16[2,256,1152]{2,1,0:T(8,128)(2,...) custom-call(bf16[256,2048]{1,0:T(8,128)(2,1)} %multiply_convert_fusi, ...), custom_call_target="tpu_custom_call" | custom-call | tf_op jit(solution)/shard_map/feed_forward/pallas_call | solution.py:867
  221.0 0.9 collective-permute-start.2
  221.9 0.6 collective-permute-start.3
  222.4 1.4 collective-permute-start
  223.8 1.3 collective-permute-start.1
  225.1 0.0 copy-start.16
  225.1 2.9 multiply_reduce_fusion
  228.0 0.0 copy-done.21
  228.0 0.6 copy-done.3
  228.6 0.0 copy-done.16
  228.6 2.0 fusion.12.refs_2_
  230.6 0.0 copy-start.6
  230.6 5.9 %convolution_convert_fusion.back = bf16[256,1536]{1,0:T(8,128)(2,1)} fusion(bf16[256,2048]{1,0:T(8,128)(2,1)S(1)} %fusion.12.refs_2_, bf16[1536,2048]{1,0:T(8,128)(2,1)} %get-tuple-element.41), kind=kOutput, calls=%fused_computation.9 | convolution fusion | flops 1611005952 | bytes 8126464 | tf_op jit(solution)/shard_map/dot_general | solution.py:34
  236.5 13.2 %attention_back.1.refs_1_ = bf16[256,2304]{1,0:T(8,128)(2,1)} custom-call(bf16[256,2304]{1,0:T(8,128)(2,1)} %get-tuple-element.46.qkv, bf16[256,1536]{1,0:T(8,128)(2,1)} %convolution_convert_fusion.back, f32[256,128]{1,0:T(8,128)} %get-tuple-element.47.logs, f32[256,256]{1,0:T(8,128)} %fusion.8.bias_ref.bias), custom_call_target="tpu_custom_call" | custom-call | flops 1006632960 | bytes 4718592 | tf_op jit(solution)/shard_map/attention_back/pallas_call | solution.py:499
  249.7 0.0 copy-done.14
  249.7 0.0 copy-start.18
  249.7 8.1 %fusion.6 = (f32[2048]{0:T(1024)S(1)}, f32[256]{0:T(256)S(1)}, f32[256,2048]{1,0:T(8,128)}) fusion(bf16[256,2048]{1,0:T(8,128)(2,1)S(1)} %copy-done.5, f32[256]{0:T(256)S(1)} %copy-done.19, f32[2048]{0:T(1024)S(1)} %bitcast.45, bf16[256,2304]{1,0:T(8,128)(2,1)} %attention_back.1.refs_1_, bf16[2048,2304]{1,0:T(8,128)(2,1)} %get-tuple-element.48), kind=kOutput, calls=%fused_computation.16 | convolution fusion | flops 2419586816 | bytes 13780992 | tf_op jit(solution)/shard_map/dot_general | solution.py:34
  257.8 0.6 reshape.176.refs_13_
  258.5 4.6 %fusion.2 = bf16[256,2048]{1,0:T(8,128)(2,1)} fusion(bf16[256,2048]{1,0:T(8,128)(2,1)S(1)} %copy-done.5, f32[256,2048]{1,0:T(8,128)} %get-tuple-element.81, f32[256]{0:T(256)S(1)} %multiply_multiply_fusion, f32[256]{0:T(256)S(1)} %copy-done.19, f32[2048]{0:T(1024)S(1)} %bitcast.46, f32[256,2048]{1,0:T(8,128)S(1)} %copy-done.1, ...), kind=kLoop, calls=%fused_computation.12 | loop fusion | flops 7864320 | bytes 9457664 | tf_op jit(solution)/shard_map/convert_element_type | solution.py:1536
  263.1 0.0 collective-permute-done.2.refs_10_
  263.1 0.0 collective-permute-done.3.refs_11_
  263.1 0.0 collective-permute-done.refs_8_
  263.1 0.0 collective-permute-done.1.refs_9_
  263.1 149.4 %reduce_last.1 = (bf16[4,64,1152]{2,1,0:T(8,128)(2,1)}, bf16[4,64,1152]{2,1,0:T(8,128)(2,1)}, bf16[4,64,768]{2,1,0:T(8,128)(2,1)}, bf16[4,64,768]{2,1,0:T(8,128)...) custom-call(bf16[256,2048]{1,0:T(8,128)(2,1)} %get-tuple-element.42., ...), custom_call_target="tpu_custom_call" | custom-call | tf_op jit(solution)/shard_map/reduce_last/pallas_call | solution.py:1353
  412.6 2.1 maximum_convert_fusion.1
  414.7 0.0 copy-done.7
  414.7 0.2 maximum_convert_fusion
  414.9 1.4 copy-done.2
  416.3 1.2 add_convert_fusion
  417.6 0.0 copy-done.22
  417.6 0.6 fusion.14
  418.1 0.0 copy-done.11
  418.1 0.2 copy.26
  418.3 0.2 copy.27
  418.5 0.0 slice-start.2
  418.5 1.4 slice.32
  419.9 7.2 %bitcast_convert_fusion.1 = f32[2048,1152]{1,0:T(8,128)} fusion(bf16[8,256,1152]{2,1,0:T(8,128)(2,1)} %get-tuple-element.66), kind=kLoop, calls=%fused_computation.1 | loop fusion | flops 2359296 | bytes 14155776 | tf_op jit(solution)/shard_map/convert_element_type | solution.py:1554
  427.0 4.7 %bitcast_convert_fusion = f32[2048,1152]{1,0:T(8,128)} fusion(bf16[8,256,1152]{2,1,0:T(8,128)(2,1)S(1)} %bitcast.33), kind=kLoop, calls=%fused_computation | loop fusion | flops 2359296 | bytes 14155776 | tf_op jit(solution)/shard_map/convert_element_type | solution.py:1554
  431.7 0.0 slice-done.1
  431.7 4.9 %convert_element_type.89 = f32[1152,2048]{1,0:T(8,128)} convert(bf16[1152,2048]{1,0:T(8,128)(2,1)S(1)} %bitcast.31) | non-fusion elementwise | flops 2359296 | bytes 14155776 | tf_op jit(solution)/shard_map/convert_element_type | solution.py:1554
  436.7 1.3 convert_bitcast_fusion
  (40 shorter events, 0.1 us)
Async XLA Ops:
  3.1 89.0 %copy-start.17 = (f32[256]{0:T(256)}, f32[256]{0:T(256)S(1)}, u32[]{:S(2)}) copy-start(f32[256]{0:T(256)S(1)} %fusion.3) | copy-start | bytes 3076
  8.3 78.7 %copy-start.4 = (bf16[256,2048]{1,0:T(8,128)(2,1)S(1)}, bf16[256,2048]{1,0:T(8,128)(2,1)}, u32[]{:S(2)}) copy-start(bf16[256,2048]{1,0:T(8,128)(2,1)} %x_ref.1) | copy-start | bytes 3145732
  87.1 5.7 %copy-start.12 = (f32[8,1,256]{2,1,0:T(1,128)}, f32[8,1,256]{2,1,0:T(1,128)S(1)}, u32[]{:S(2)}) copy-start(f32[8,1,256]{2,1,0:T(1,128)S(1)} %get-tuple-element.76) | copy-start | bytes 24580
  92.1 1.3 copy-start
  92.1 2.5 copy-start.20
  92.7 1.9 copy-start.15
  221.0 42.1 %collective-permute-start.2 = (bf16[2,576,256]{2,1,0:T(8,128)(2,1)}, bf16[2,576,256]{2,1,0:T(8,128)(2,1)}, u32[]{:S(2)}, u32[]{:S(2)}) collective-permute-start(bf16[2,576,256]{2,1,0:T(8,128)(2,1)} %get-tuple-element.56), channel_id=1, source_target_pairs={{0,8},{4,12},{8,0},{12,4},{16,24},{20,28},{24,16},{28,20},{1,9},{5... | collective-permute-start | bytes 1769480 | tf_op jit(solution)/shard_map/ppermute | solution.py:1461
  221.9 41.2 %collective-permute-start.3 = (bf16[2,576,256]{2,1,0:T(8,128)(2,1)}, bf16[2,576,256]{2,1,0:T(8,128)(2,1)}, u32[]{:S(2)}, u32[]{:S(2)}) collective-permute-start(bf16[2,576,256]{2,1,0:T(8,128)(2,1)} %get-tuple-element.57), channel_id=1, source_target_pairs={{0,16},{4,20},{8,24},{12,28},{16,0},{20,4},{24,8},{28,12},{1,17},{... | collective-permute-start | bytes 1769480 | tf_op jit(solution)/shard_map/ppermute | solution.py:1461
  222.4 40.7 %collective-permute-start = (bf16[2,256,1152]{2,1,0:T(8,128)(2,1)}, bf16[2,256,1152]{2,1,0:T(8,128)(2,1)}, u32[]{:S(2)}, u32[]{:S(2)}) collective-permute-start(bf16[2,256,1152]{2,1,0:T(8,128)(2,1)} %get-tuple-element.54), channel_id=1, source_target_pairs={{0,8},{4,12},{8,0},{12,4},{16,24},{20,28},{24,16},{28,20},{1,9},{5... | collective-permute-start | bytes 3538952 | tf_op jit(solution)/shard_map/ppermute | solution.py:1461
  223.8 39.3 %collective-permute-start.1 = (bf16[2,256,1152]{2,1,0:T(8,128)(2,1)}, bf16[2,256,1152]{2,1,0:T(8,128)(2,1)}, u32[]{:S(2)}, u32[]{:S(2)}) collective-permute-start(bf16[2,256,1152]{2,1,0:T(8,128)(2,1)} %get-tuple-element.55), channel_id=1, source_target_pairs={{0,16},{4,20},{8,24},{12,28},{16,0},{20,4},{24,8},{28,12},{1,17},{... | collective-permute-start | bytes 3538952 | tf_op jit(solution)/shard_map/ppermute | solution.py:1461
  225.1 2.9 copy-start.21
  225.1 2.9 copy-start.1
  225.1 3.5 copy-start.3
  225.1 3.5 copy-start.13
  225.1 3.5 copy-start.16
  230.6 5.9 %copy-start.6 = (bf16[256,2048]{1,0:T(8,128)(2,1)}, bf16[256,2048]{1,0:T(8,128)(2,1)S(1)}, u32[]{:S(2)}) copy-start(bf16[256,2048]{1,0:T(8,128)(2,1)S(1)} %fusion.12.refs_2_) | copy-start | bytes 3145732
  236.5 13.2 %copy-start.5 = (bf16[256,2048]{1,0:T(8,128)(2,1)S(1)}, bf16[256,2048]{1,0:T(8,128)(2,1)}, u32[]{:S(2)}) copy-start(bf16[256,2048]{1,0:T(8,128)(2,1)} %x_ref.1) | copy-start | bytes 3145732
  236.5 13.2 %copy-start.14 = (f32[8,1,256]{2,1,0:T(1,128)S(1)}, f32[8,1,256]{2,1,0:T(1,128)}, u32[]{:S(2)}) copy-start(f32[8,1,256]{2,1,0:T(1,128)} %get-tuple-element.75) | copy-start | bytes 24580
  236.5 13.2 %copy-start.19 = (f32[256]{0:T(256)S(1)}, f32[256]{0:T(256)}, u32[]{:S(2)}) copy-start(f32[256]{0:T(256)} %get-tuple-element.83) | copy-start | bytes 3076
  249.7 8.8 %copy-start.18 = (f32[256]{0:T(256)S(1)}, f32[256]{0:T(256)}, u32[]{:S(2)}) copy-start(f32[256]{0:T(256)} %copy-done.17) | copy-start | bytes 3076
  412.6 2.1 copy-start.7
  412.6 2.1 copy-start.8
  412.6 2.3 copy-start.9
  414.7 1.6 copy-start.2
  416.3 1.2 copy-start.22
  416.3 1.8 copy-start.11
  416.3 2.0 copy-start.10
  418.5 8.5 %slice-start.2 = ((s8[4718592]{0:T(1024)(128)(4,1)}), s8[4194304]{0:T(1024)(128)(4,1)S(1)}, s32[]{:S(2)}) async-start(s8[4718592]{0:T(1024)(128)(4,1)} %bitcast.32), calls=%async_computation.2 | async-start | bytes 8388608
  419.8 7.2 %slice-start.3 = ((s8[4718592]{0:T(1024)(128)(4,1)}), s8[524288]{0:T(1024)(128)(4,1)S(1)}, s32[]{:S(2)}) async-start(s8[4718592]{0:T(1024)(128)(4,1)} %bitcast.32), calls=%async_computation.3 | async-start | bytes 1048576
  419.9 11.9 %slice-start = ((s8[4718592]{0:T(1024)(128)(4,1)}), s8[4194304]{0:T(1024)(128)(4,1)S(1)}, s32[]{:S(2)}) async-start(s8[4718592]{0:T(1024)(128)(4,1)} %bitcast.30), calls=%async_computation | async-start | bytes 8388608
  427.0 4.7 %slice-start.1 = ((s8[4718592]{0:T(1024)(128)(4,1)}), s8[524288]{0:T(1024)(128)(4,1)S(1)}, s32[]{:S(2)}) async-start(s8[4718592]{0:T(1024)(128)(4,1)} %bitcast.30), calls=%async_computation.1 | async-start | bytes 1048576

commit v8 on v7

--- a/solution.py
+++ b/solution.py
@@ -641,16 +641,20 @@
     sw_s,
     sw_r,
     out_sem,
+    st_s,
+    st_r,
     ready,
+    ready_x,
+    ready_y,
 ):
     n, w = lax.axis_index("narrow"), lax.axis_index("wide")
     y, x, core = n // 4, lax.rem(n // 2, 2), lax.rem(n, 2)
-    mate = flip(n, 1)
+    mate, peer_x, peer_y = flip(n, 1), flip(n, 2), flip(n, 4)
     chunks = 4
     rows = mixed.shape[0] // chunks
     tokens, model = 4 * mixed.shape[0], mixed.shape[1]
     width = wg.shape[1]
-    batch = 4 * rows
+    batch, block = 4 * rows, 512
     loads = [
         pltpu.make_async_copy(src, dst, in_sem.at[k])
         for k, (src, dst) in enumerate(
@@ -659,7 +663,7 @@
     ]
     for cp in loads:
         cp.start()
-    greet([mate], n, w, True)
+    greet([mate, peer_x, peer_y], n, w, True)
 
     gather = LineGather(n, w, mixed, x_all, ag_s, ag_r, chunks)
     scatter = LineScatter(n, w, terms, (from_left, from_right), rs_s, rs_r, chunks)
@@ -723,22 +727,33 @@
         def _():
             gather.far(i + 1)
 
-        terms[:, r, :] = (
-            (contract_cols(rows_of(gb, i), wg_v[...]) + contract_cols(rows_of(ub, i), wu_v[...]))
-            .astype(BF)
-            .reshape(4, rows, model)
-        )
+        @pl.loop(0, model // block)
+        def _(j):
+            b = pl.ds(pl.multiple_of(j * block, block), block)
+            terms[:, r, b] = (
+                (
+                    contract_cols(rows_of(gb, i), wg_v[b, :])
+                    + contract_cols(rows_of(ub, i), wu_v[b, :])
+                )
+                .astype(BF)
+                .reshape(4, rows, block)
+            )
+
         scatter.begin(i)
 
         @pl.when(i > 1)
         def _():
             store(i - 2).wait()
 
-        part_buf[lax.rem(i, 2)] = (
-            jnp.dot(rows_of(hid, i), wd_v[...], preferred_element_type=F32)
-            .astype(BF)
-            .reshape(4, rows, model)
-        )
+        @pl.loop(0, model // block)
+        def _(j):
+            b = pl.ds(pl.multiple_of(j * block, block), block)
+            part_buf[lax.rem(i, 2), :, :, b] = (
+                jnp.dot(rows_of(hid, i), wd_v[:, b], preferred_element_type=F32)
+                .astype(BF)
+                .reshape(4, rows, block)
+            )
+
         store(i).start()
 
         @pl.when(i > 0)
@@ -780,7 +795,6 @@
     def _(j):
         wg_v[place(j, half), :] = row_grad(gb, 2 * j + 1 - core).astype(BF)
 
-    scatter.pass_on(chunks - 1)
     pl.semaphore_wait(ready, 1)
     swaps[0].start()
 
@@ -789,6 +803,7 @@
         wu_v[place(j, half), :] = row_grad(ub, 2 * j + 1 - core).astype(BF)
 
     swaps[1].start()
+    scatter.pass_on(chunks - 1)
 
     @pl.loop(0, 4)
     def _(j):
@@ -803,12 +818,50 @@
             row_grad(gb, 2 * j + core) + wg_v[place(j, 0), :].astype(F32)
         ).astype(BF)
 
+    def gate_send(b, k):
+        src, dst = gate_k.at[b, 1 - x], wg_v.at[place(b, 0), :]
+        return send(src, dst, st_s.at[k], st_r.at[k], peer_x, w)
+
+    def up_send(b, k):
+        src, dst = up_k.at[1 - y, b], wu_v.at[place(b, 0), :]
+        return send(src, dst, st_s.at[2 + k], st_r.at[2 + k], peer_y, w)
+
+    pl.semaphore_signal(
+        ready_x, inc=1, device_id=at(peer_x, w), device_id_type=pl.DeviceIdType.MESH
+    )
+    swaps[0].wait_send()
+    pl.semaphore_wait(ready_x, 1)
+    gate_send(1 - y, 0).start()
+    gate_send(y, 1).start()
+    swaps[1].wait_recv()
+
+    @pl.loop(0, 4)
+    def _(j):
+        up_k[j // 2, lax.rem(j, 2)] = (
+            row_grad(ub, 2 * j + core) + wu_v[place(j, 0), :].astype(F32)
+        ).astype(BF)
+
+    pl.semaphore_signal(
+        ready_y, inc=1, device_id=at(peer_y, w), device_id_type=pl.DeviceIdType.MESH
+    )
+    swaps[1].wait_send()
+    pl.semaphore_wait(ready_y, 1)
+    up_send(1 - x, 0).start()
+    up_send(x, 1).start()
+    swaps[2].wait_recv()
+
+    @pl.loop(0, 4)
+    def _(j):
+        down_k[j // 2, lax.rem(j, 2)] = (
+            col_grad(2 * j + core) + wd_v[:, place(j, 0)].astype(F32)
+        ).astype(BF)
+
     cut = width // 2
     pieces = (
-        (gate_k.at[:, 1 - x], gate_go),
-        (gate_k.at[:, x], gate_stay),
-        (up_k.at[1 - y], up_go),
-        (up_k.at[y], up_stay),
+        (gate_k.at[1 - y, x], gate_go),
+        (gate_k.at[y, x], gate_stay),
+        (up_k.at[y, 1 - x], up_go),
+        (up_k.at[y, x], up_stay),
         (down_k.at[:, 1 - x, pl.ds(0, cut), :], low_go),
         (down_k.at[:, x, pl.ds(0, cut), :], low_stay),
         (down_k.at[1 - y, :, pl.ds(cut, cut), :], high_go),
@@ -817,35 +870,34 @@
     puts = [
         pltpu.make_async_copy(src, dst, out_sem.at[k]) for k, (src, dst) in enumerate(pieces)
     ]
-    for k in (0, 1):
+    for k in (4, 5, 6, 7):
         puts[k].start()
     scatter.pass_end(chunks - 1)
-    swaps[1].wait_recv()
-
-    @pl.loop(0, 4)
-    def _(j):
-        up_k[j // 2, lax.rem(j, 2)] = (
-            row_grad(ub, 2 * j + core) + wu_v[place(j, 0), :].astype(F32)
-        ).astype(BF)
-
-    for k in (2, 3):
-        puts[k].start()
-    swaps[2].wait_recv()
-
-    @pl.loop(0, 4)
-    def _(j):
-        down_k[j // 2, lax.rem(j, 2)] = (
-            col_grad(2 * j + core) + wd_v[:, place(j, 0)].astype(F32)
-        ).astype(BF)
-
-    for k in (4, 5, 6, 7):
-        puts[k].start()
     for i in range(chunks):
         scatter.finish(i, back_out)
+    step = 64
+
+    def join(sums, b0, b1, came, b):
+        @pl.loop(0, eighth // step)
+        def _(t):
+            s = pl.ds(pl.multiple_of(t * step, step), step)
+            o = pl.ds(pl.multiple_of(b * eighth + t * step, step), step)
+            sums[b0, b1, s, :] = sums[b0, b1, s, :] + came[o, :]
+
+    for k, b in enumerate((1 - y, y)):
+        gate_send(b, k).wait_recv()
+        join(gate_k, b, x, wg_v, b)
+        puts[k].start()
+    for k, b in enumerate((1 - x, x)):
+        up_send(b, k).wait_recv()
+        join(up_k, y, b, wu_v, b)
+        puts[2 + k].start()
     scatter.drain()
     gather.finish_sends()
-    for k in range(3):
-        swaps[k].wait_send()
+    swaps[2].wait_send()
+    for k in range(2):
+        gate_send(0, k).wait_send()
+        up_send(0, k).wait_send()
     store(chunks - 2).wait()
     store(chunks - 1).wait()
     for cp in puts:
@@ -857,7 +909,7 @@
     width = gate_weight.shape[1]
     rows, eighth, cut = tokens_here // 4, model // 8, width // 2
     hbm, vmem = pl.BlockSpec(memory_space=pl.ANY), pl.BlockSpec(memory_space=pltpu.VMEM)
-    row_piece = jax.ShapeDtypeStruct((2, eighth, width), BF)
+    row_piece = jax.ShapeDtypeStruct((eighth, width), BF)
     col_piece = jax.ShapeDtypeStruct((2, cut, eighth), BF)
     dma = pltpu.SemaphoreType.DMA
     acc = pltpu.VMEM((4 * rows, width), F32)
@@ -903,6 +955,10 @@
             dma((3,)),
             dma((3,)),
             dma((8,)),
+            dma((4,)),
+            dma((4,)),
+            pltpu.SemaphoreType.REGULAR,
+            pltpu.SemaphoreType.REGULAR,
             pltpu.SemaphoreType.REGULAR,
         ],
         compiler_params=pltpu.CompilerParams(
@@ -1046,6 +1102,32 @@
         return self.sum.at[self.here]
 
 
+class Whole:
+    def __init__(self, me, kept, came, x_first, bufs, sems, k):
+        self.n, self.w = me[:2]
+        self.kept, self.came, self.x_first = kept, came, x_first
+        self.sum, self.one = bufs
+        self.sems, self.k = sems, k
+
+    def loads(self):
+        return [
+            pltpu.make_async_copy(self.kept, self.sum, self.sems[0].at[2 * self.k]),
+            pltpu.make_async_copy(self.came, self.one, self.sems[0].at[2 * self.k + 1]),
+        ]
+
+    def join(self):
+        for cp in self.loads():
+            cp.wait()
+
+        @pl.loop(0, self.sum.shape[0] // 64)
+        def _(i):
+            r = pl.ds(pl.multiple_of(i * 64, 64), 64)
+            self.sum[r, :] = self.sum[r, :] + self.one[r, :]
+
+    def result(self):
+        return self.sum
+
+
 class Spread:
     def __init__(self, item, region, sems, k):
         self.item, self.region, self.sems, self.k = item, region, sems, k
@@ -1135,7 +1217,7 @@
     gate_full, up_full, down_full = take(3)
     feed_out, gain_out = take(2)
     attn_bufs = [take(5) for _ in range(4)]
-    ffn_bufs = [take(3) for _ in range(4)]
+    ffn_bufs = [take(count) for count in (2, 2, 3, 3)]
     line_bufs = [take(3) for _ in range(4)]
     feed_v, feed_left, feed_right = take(3)
     gain_in, gain_sum, gain_line = take(3)
@@ -1162,7 +1244,8 @@
         for k, (p, cols, xf) in enumerate(items)
     ]
     ffn = [
-        Half(me, stays[k], comes[k], k % 2 == 0, ffn_bufs[k], half_sems, k) for k in range(4)
+        (Whole, Half)[k // 2](me, stays[k], comes[k], k % 2 == 0, ffn_bufs[k], half_sems, k)
+        for k in range(4)
     ]
     cut, eighth = stays[2].shape[1], stays[2].shape[2]
 
@@ -1218,8 +1301,10 @@
     for i in range(7):
         gain_narrow(i).start()
 
-    for item in ffn:
+    for item in ffn[2:]:
         item.after_one()
+    ffn[0].join()
+    spread[0].start()
     for cp in factor_loads:
         cp.wait()
     for item in attn:
@@ -1246,7 +1331,10 @@
     for item in attn[2:]:
         item.after_one()
     feed.pass_end(3)
-    for k in range(4):
+    spread[0].relay()
+    ffn[1].join()
+    spread[1].start()
+    for k in (2, 3):
         ffn[k].after_two()
         spread[k].start()
 
@@ -1280,8 +1368,7 @@
         scatters[k].pass_end(0)
     for k in (0, 1, 2, 3):
         line_turn(k)
-    for s in spread[:2]:
-        s.relay()
+    spread[1].relay()
     for k in (0, 1, 2, 3):
         gathers[k].near(0)
     for k in (0, 1, 2, 3):
@@ -1319,18 +1406,16 @@
             pltpu.VMEM((2, rows, cols), BF),
             pltpu.VMEM((rows, cols), BF),
         ]
-    for stay in stays:
-        scratch += [
-            pltpu.VMEM(stay.shape, BF),
-            pltpu.VMEM(stay.shape, BF),
-            pltpu.VMEM(stay.shape[1:], BF),
-        ]
+    for k, stay in enumerate(stays):
+        scratch += [pltpu.VMEM(stay.shape, BF), pltpu.VMEM(stay.shape, BF)]
+        if k > 1:
+            scratch += [pltpu.VMEM(stay.shape[1:], BF)]
     outs = []
     for _, (_, cols), _ in items:
         scratch += [pltpu.VMEM((3, rows // 4, cols), BF)] * 2 + [pltpu.VMEM((rows // 4, cols), BF)]
         outs.append(jax.ShapeDtypeStruct((4, rows // 4, cols), BF))
-    outs.append(jax.ShapeDtypeStruct((8,) + stays[0].shape[1:], BF))
-    outs.append(jax.ShapeDtypeStruct((8,) + stays[1].shape[1:], BF))
+    outs.append(jax.ShapeDtypeStruct((8,) + stays[0].shape, BF))
+    outs.append(jax.ShapeDtypeStruct((8,) + stays[1].shape, BF))
     outs.append(jax.ShapeDtypeStruct((2 * stays[2].shape[1], 8 * stays[2].shape[2]), BF))
     outs.append(jax.ShapeDtypeStruct(feed_terms.shape[1:], F32))
     outs.append(jax.ShapeDtypeStruct(gain_parts.shape[1:], F32))
@@ -1459,7 +1544,7 @@
         stays = pieces[1::2]
         comes = [
             lax.ppermute(piece, "narrow", [(i, i ^ bit) for i in range(8)])
-            for piece, bit in zip(pieces[0::2], (2, 4, 2, 4))
+            for piece, bit in zip(pieces[0::2], (4, 2, 2, 4))
         ]
     else:
         gathered = lax.all_gather(mixed_in, "wide", axis=0, tiled=True)

time: 445 us -> 456 us (1.025)
  Pallas kernels: 366 us -> 380 us
    pallas_call x1, Pallas kernels: 126 us -> 140 us  [feed_forward(): pl.pallas_call(middle_kernel, name='feed_forward', out_shape=(jax.ShapeDt...]
  transfers between devices with their start and end apart: 4 -> 4, of which waited for: 0 -> 0; matrix products, arithmetic and copies ran while one was open for 6% -> 5% of each run, Pallas kernels for 3% -> 3%
where the time goes in v8:
time: 456 us; the launch traced here: 452 us
  Pallas kernels  380 us (83%)
  other arithmetic  39.4 us (9%)
  matrix products  19 us (4%)
  local copies, waits for them, and re-layouts  8.19 us (2%)
    pallas_call x1, Pallas kernels, reduce_last(): pl.pallas_call(functools.partial(last_kernel, items), name='reduce_last',...  149 us
    pallas_call x1, Pallas kernels, feed_forward(): pl.pallas_call(middle_kernel, name='feed_forward', out_shape=(jax.ShapeDt...  140 us
    pallas_call x1, Pallas kernels, gather_first(): pl.pallas_call(first_kernel, name='gather_first', out_shape=(jax.ShapeDty...  77.3 us
    convert_element_type x3, other arithmetic, per_device(): gate_total, up_total, down_total = [t.astype(F32) for t in ffn_totals]  16.8 us
    dot_general x2, matrix products, contract_cols(): lax.dot_general(left, right, (((1,), (1,)), ((), ())), preferred_element_...  14 us
    pallas_call x1, Pallas kernels, attention_back(): pl.pallas_call(attention_back_kernel, name='attention_back', out_shape=ja...  13.2 us
  transfers between devices with their start and end apart: 4, of which 0 were waited for; matrix products, arithmetic and copies ran while one was open for 5% of the time, Pallas kernels for 3%

profile of v8, /device:TPU:0, one launch (start us, length us, event | category | flops | bytes accessed | tf_op | source)
XLA Modules:
  0.0 451.6 jit_solution(4023385102645500094)
XLA Ops:
  0.6 0.8 reduce-window.8
  1.5 0.1 convert_reduce_fusion
  1.6 1.5 fusion.3
  3.1 0.7 stack.12
  3.7 0.7 stack.13
  4.4 0.6 copy.28
  5.0 1.3 fusion.11
  6.3 1.2 compare_convert_fusion.live
  7.5 0.8 fusion.8.bias_ref.bias
  8.3 77.3 %gather_first.1 = (bf16[2048,2304]{1,0:T(8,128)(2,1)}, bf16[1536,2048]{1,0:T(8,128)(2,1)}, bf16[4,256,2048]{2,1,0:T(8,128)(2,1)}, bf16[256,2048]{1,0:T(8,128)(2,...) custom-call(bf16[256,2048]{1,0:T(8,128)(2,1)} %x_ref.1, ...), custom_call_target="tpu_custom_call" | custom-call | tf_op jit(solution)/shard_map/gather_first/pallas_call | solution.py:415
  85.7 0.8 reduce
  86.5 0.6 fusion.13
  87.1 0.0 copy-done.4
  87.1 5.0 %multiply_reduce_fusion.2 = (f32[256]{0:T(256)S(1)}, f32[256,2048]{1,0:T(8,128)S(1)}) fusion(bf16[256,1536]{1,0:T(8,128)(2,1)} %get-tuple-element.40.refs_3_, bf16[1536,2048]{1,0:T(8,128)(2,1)} %get-tuple-element.41, bf16[256,2048]{1,0:T(8,128)(2,1)S(1)} %copy-done.4), kind=kOutput, calls=%fused_computation.21 | convolution fusion | flops 1612709632 | bytes 10224640 | tf_op jit(solution)/shard_map/dot_general | solution.py:1531
  92.0 0.0 copy-start
  92.1 0.0 copy-start.20
  92.1 0.0 copy-done.17
  92.1 0.6 fusion.9
  92.7 0.0 copy-done.12
  92.7 0.7 copy-done
  93.4 1.2 multiply_convert_fusion.mixed
  94.6 0.0 copy-done.20
  94.6 0.0 copy-done.15
  94.6 140.1 %feed_forward.1 = (f32[256,2048]{1,0:T(8,128)}, bf16[4,256,2048]{2,1,0:T(8,128)(2,1)}, bf16[256,1152]{1,0:T(8,128)(2,1)}, bf16[256,1152]{1,0:T(8,128)(2,1)}, bf1...) custom-call(bf16[256,2048]{1,0:T(8,128)(2,1)} %multiply_convert_fusi, ...), custom_call_target="tpu_custom_call" | custom-call | tf_op jit(solution)/shard_map/feed_forward/pallas_call | solution.py:919
  234.7 0.6 collective-permute-start
  235.3 1.4 collective-permute-start.1
  236.7 0.6 collective-permute-start.2
  237.3 1.5 collective-permute-start.3
  238.8 0.0 copy-start.16
  238.8 2.9 multiply_reduce_fusion
  241.7 0.0 copy-done.21
  241.7 0.0 copy-done.1
  241.7 0.6 copy-done.3
  242.3 0.0 copy-done.13
  242.3 0.0 copy-done.16
  242.3 2.0 fusion.12.refs_2_
  244.3 0.0 copy-start.6
  244.3 5.9 %convolution_convert_fusion.back = bf16[256,1536]{1,0:T(8,128)(2,1)} fusion(bf16[256,2048]{1,0:T(8,128)(2,1)S(1)} %fusion.12.refs_2_, bf16[1536,2048]{1,0:T(8,128)(2,1)} %get-tuple-element.41), kind=kOutput, calls=%fused_computation.9 | convolution fusion | flops 1611005952 | bytes 8126464 | tf_op jit(solution)/shard_map/dot_general | solution.py:34
  250.2 0.0 copy-done.6
  250.2 13.2 %attention_back.1.refs_1_ = bf16[256,2304]{1,0:T(8,128)(2,1)} custom-call(bf16[256,2304]{1,0:T(8,128)(2,1)} %get-tuple-element.46.qkv, bf16[256,1536]{1,0:T(8,128)(2,1)} %convolution_convert_fusion.back, f32[256,128]{1,0:T(8,128)} %get-tuple-element.47.logs, f32[256,256]{1,0:T(8,128)} %fusion.8.bias_ref.bias), custom_call_target="tpu_custom_call" | custom-call | flops 1006632960 | bytes 4718592 | tf_op jit(solution)/shard_map/attention_back/pallas_call | solution.py:499
  263.4 0.0 copy-done.5
  263.4 0.0 copy-done.14
  263.4 0.0 copy-start.18
  263.4 8.1 %fusion.6 = (f32[2048]{0:T(1024)S(1)}, f32[256]{0:T(256)S(1)}, f32[256,2048]{1,0:T(8,128)}) fusion(bf16[256,2048]{1,0:T(8,128)(2,1)S(1)} %copy-done.5, f32[256]{0:T(256)S(1)} %copy-done.19, f32[2048]{0:T(1024)S(1)} %bitcast.45, bf16[256,2304]{1,0:T(8,128)(2,1)} %attention_back.1.refs_1_, bf16[2048,2304]{1,0:T(8,128)(2,1)} %get-tuple-element.48), kind=kOutput, calls=%fused_computation.16 | convolution fusion | flops 2419586816 | bytes 13780992 | tf_op jit(solution)/shard_map/dot_general | solution.py:34
  271.5 0.6 reshape.176.refs_13_
  272.2 4.6 %fusion.2 = bf16[256,2048]{1,0:T(8,128)(2,1)} fusion(bf16[256,2048]{1,0:T(8,128)(2,1)S(1)} %copy-done.5, f32[256,2048]{1,0:T(8,128)} %get-tuple-element.81, f32[256]{0:T(256)S(1)} %multiply_multiply_fusion, f32[256]{0:T(256)S(1)} %copy-done.19, f32[2048]{0:T(1024)S(1)} %bitcast.46, f32[256,2048]{1,0:T(8,128)S(1)} %copy-done.1, ...), kind=kLoop, calls=%fused_computation.12 | loop fusion | flops 7864320 | bytes 9457664 | tf_op jit(solution)/shard_map/convert_element_type | solution.py:1621
  276.8 0.0 collective-permute-done.refs_8_
  276.8 0.0 collective-permute-done.1.refs_9_
  276.8 0.0 collective-permute-done.2.refs_10_
  276.8 0.0 collective-permute-done.3.refs_11_
  276.8 148.9 %reduce_last.1 = (bf16[4,64,1152]{2,1,0:T(8,128)(2,1)}, bf16[4,64,1152]{2,1,0:T(8,128)(2,1)}, bf16[4,64,768]{2,1,0:T(8,128)(2,1)}, bf16[4,64,768]{2,1,0:T(8,128)...) custom-call(bf16[256,2048]{1,0:T(8,128)(2,1)} %get-tuple-element.42., ...), custom_call_target="tpu_custom_call" | custom-call | tf_op jit(solution)/shard_map/reduce_last/pallas_call | solution.py:1438
  425.8 2.1 maximum_convert_fusion.1
  427.9 0.2 maximum_convert_fusion
  428.1 1.4 copy-done.2
  429.5 1.2 add_convert_fusion
  430.7 0.6 fusion.14
  431.3 0.2 copy.26
  431.5 0.2 copy.27
  431.7 0.0 slice-start.2
  431.7 1.4 slice.32
  433.0 7.2 %bitcast_convert_fusion.1 = f32[2048,1152]{1,0:T(8,128)} fusion(bf16[8,256,1152]{2,1,0:T(8,128)(2,1)} %get-tuple-element.66), kind=kLoop, calls=%fused_computation.1 | loop fusion | flops 2359296 | bytes 14155776 | tf_op jit(solution)/shard_map/convert_element_type | solution.py:1639
  440.2 4.7 %bitcast_convert_fusion = f32[2048,1152]{1,0:T(8,128)} fusion(bf16[8,256,1152]{2,1,0:T(8,128)(2,1)S(1)} %bitcast.33), kind=kLoop, calls=%fused_computation | loop fusion | flops 2359296 | bytes 14155776 | tf_op jit(solution)/shard_map/convert_element_type | solution.py:1639
  444.9 4.9 %convert_element_type.89 = f32[1152,2048]{1,0:T(8,128)} convert(bf16[1152,2048]{1,0:T(8,128)(2,1)S(1)} %bitcast.31) | non-fusion elementwise | flops 2359296 | bytes 14155776 | tf_op jit(solution)/shard_map/convert_element_type | solution.py:1639
  449.9 1.3 convert_bitcast_fusion
  (40 shorter events, 0.1 us)
Async XLA Ops:
  3.1 89.0 %copy-start.17 = (f32[256]{0:T(256)}, f32[256]{0:T(256)S(1)}, u32[]{:S(2)}) copy-start(f32[256]{0:T(256)S(1)} %fusion.3) | copy-start | bytes 3076
  8.3 78.7 %copy-start.4 = (bf16[256,2048]{1,0:T(8,128)(2,1)S(1)}, bf16[256,2048]{1,0:T(8,128)(2,1)}, u32[]{:S(2)}) copy-start(bf16[256,2048]{1,0:T(8,128)(2,1)} %x_ref.1) | copy-start | bytes 3145732
  87.1 5.7 %copy-start.12 = (f32[8,1,256]{2,1,0:T(1,128)}, f32[8,1,256]{2,1,0:T(1,128)S(1)}, u32[]{:S(2)}) copy-start(f32[8,1,256]{2,1,0:T(1,128)S(1)} %get-tuple-element.76) | copy-start | bytes 24580
  92.0 1.3 copy-start
  92.1 2.5 copy-start.20
  92.7 1.9 copy-start.15
  234.7 42.1 %collective-permute-start = (bf16[256,1152]{1,0:T(8,128)(2,1)}, bf16[256,1152]{1,0:T(8,128)(2,1)}, u32[]{:S(2)}, u32[]{:S(2)}) collective-permute-start(bf16[256,1152]{1,0:T(8,128)(2,1)} %get-tuple-element.54), channel_id=1, source_target_pairs={{0,16},{4,20},{8,24},{12,28},{16,0},{20,4},{24,8},{28,12},{1,17},{... | collective-permute-start | bytes 1769480 | tf_op jit(solution)/shard_map/ppermute | solution.py:1546
  235.3 41.5 %collective-permute-start.1 = (bf16[256,1152]{1,0:T(8,128)(2,1)}, bf16[256,1152]{1,0:T(8,128)(2,1)}, u32[]{:S(2)}, u32[]{:S(2)}) collective-permute-start(bf16[256,1152]{1,0:T(8,128)(2,1)} %get-tuple-element.55), channel_id=1, source_target_pairs={{0,8},{4,12},{8,0},{12,4},{16,24},{20,28},{24,16},{28,20},{1,9},{5... | collective-permute-start | bytes 1769480 | tf_op jit(solution)/shard_map/ppermute | solution.py:1546
  236.7 40.1 %collective-permute-start.2 = (bf16[2,576,256]{2,1,0:T(8,128)(2,1)}, bf16[2,576,256]{2,1,0:T(8,128)(2,1)}, u32[]{:S(2)}, u32[]{:S(2)}) collective-permute-start(bf16[2,576,256]{2,1,0:T(8,128)(2,1)} %get-tuple-element.56), channel_id=1, source_target_pairs={{0,8},{4,12},{8,0},{12,4},{16,24},{20,28},{24,16},{28,20},{1,9},{5... | collective-permute-start | bytes 1769480 | tf_op jit(solution)/shard_map/ppermute | solution.py:1546
  237.3 39.5 %collective-permute-start.3 = (bf16[2,576,256]{2,1,0:T(8,128)(2,1)}, bf16[2,576,256]{2,1,0:T(8,128)(2,1)}, u32[]{:S(2)}, u32[]{:S(2)}) collective-permute-start(bf16[2,576,256]{2,1,0:T(8,128)(2,1)} %get-tuple-element.57), channel_id=1, source_target_pairs={{0,16},{4,20},{8,24},{12,28},{16,0},{20,4},{24,8},{28,12},{1,17},{... | collective-permute-start | bytes 1769480 | tf_op jit(solution)/shard_map/ppermute | solution.py:1546
  238.8 2.9 copy-start.21
  238.8 2.9 copy-start.1
  238.8 3.5 copy-start.3
  238.8 3.5 copy-start.13
  238.8 3.5 copy-start.16
  244.3 5.9 %copy-start.6 = (bf16[256,2048]{1,0:T(8,128)(2,1)}, bf16[256,2048]{1,0:T(8,128)(2,1)S(1)}, u32[]{:S(2)}) copy-start(bf16[256,2048]{1,0:T(8,128)(2,1)S(1)} %fusion.12.refs_2_) | copy-start | bytes 3145732
  250.2 13.2 %copy-start.5 = (bf16[256,2048]{1,0:T(8,128)(2,1)S(1)}, bf16[256,2048]{1,0:T(8,128)(2,1)}, u32[]{:S(2)}) copy-start(bf16[256,2048]{1,0:T(8,128)(2,1)} %x_ref.1) | copy-start | bytes 3145732
  250.2 13.2 %copy-start.14 = (f32[8,1,256]{2,1,0:T(1,128)S(1)}, f32[8,1,256]{2,1,0:T(1,128)}, u32[]{:S(2)}) copy-start(f32[8,1,256]{2,1,0:T(1,128)} %get-tuple-element.75) | copy-start | bytes 24580
  250.2 13.2 %copy-start.19 = (f32[256]{0:T(256)S(1)}, f32[256]{0:T(256)}, u32[]{:S(2)}) copy-start(f32[256]{0:T(256)} %get-tuple-element.83) | copy-start | bytes 3076
  263.4 8.8 %copy-start.18 = (f32[256]{0:T(256)S(1)}, f32[256]{0:T(256)}, u32[]{:S(2)}) copy-start(f32[256]{0:T(256)} %copy-done.17) | copy-start | bytes 3076
  425.8 2.1 copy-start.7
  425.8 2.1 copy-start.8
  425.8 2.3 copy-start.9
  427.9 1.6 copy-start.2
  429.5 1.2 copy-start.22
  429.5 1.8 copy-start.11
  429.5 2.0 copy-start.10
  431.7 8.5 %slice-start.2 = ((s8[4718592]{0:T(1024)(128)(4,1)}), s8[4194304]{0:T(1024)(128)(4,1)S(1)}, s32[]{:S(2)}) async-start(s8[4718592]{0:T(1024)(128)(4,1)} %bitcast.32), calls=%async_computation.2 | async-start | bytes 8388608
  433.0 7.2 %slice-start.3 = ((s8[4718592]{0:T(1024)(128)(4,1)}), s8[524288]{0:T(1024)(128)(4,1)S(1)}, s32[]{:S(2)}) async-start(s8[4718592]{0:T(1024)(128)(4,1)} %bitcast.32), calls=%async_computation.3 | async-start | bytes 1048576
  433.0 11.9 %slice-start = ((s8[4718592]{0:T(1024)(128)(4,1)}), s8[4194304]{0:T(1024)(128)(4,1)S(1)}, s32[]{:S(2)}) async-start(s8[4718592]{0:T(1024)(128)(4,1)} %bitcast.30), calls=%async_computation | async-start | bytes 8388608
  440.2 4.7 %slice-start.1 = ((s8[4718592]{0:T(1024)(128)(4,1)}), s8[524288]{0:T(1024)(128)(4,1)S(1)}, s32[]{:S(2)}) async-start(s8[4718592]{0:T(1024)(128)(4,1)} %bitcast.30), calls=%async_computation.1 | async-start | bytes 1048576

commit v9 on v7

--- a/solution.py
+++ b/solution.py
@@ -185,20 +185,22 @@
     p_ref,
     g_ref,
     c_ref,
-    bias_ref,
+    docs_ref,
     qkv_out,
     p_full,
     c_full,
     normed_out,
     rows_out,
     att_out,
+    gain_row,
+    gain_late,
+    bias_ref,
+    log_out,
     g_full,
-    log_out,
     qkv_full,
     p_buf,
     c_buf,
     x_buf,
-    gain_row,
     normed,
     qkv,
     att,
@@ -308,6 +310,7 @@
     put(c_buf, c_full.at[w])
     for k in range(8):
         gain_row[:, pl.ds(k * rows, rows)] = g_full[k, :, :rows]
+        gain_late[:, pl.ds(k * rows, rows)] = g_full[k, :, rows:]
     strip = 16
 
     @pl.loop(0, x_buf.shape[0] // strip)
@@ -316,6 +319,19 @@
         normed[s, :] = rms_scale(x_buf[s, :].astype(F32), gain_row[...]).astype(BF)
 
     put(normed, normed_out)
+
+    docs = docs_ref[...]
+    late = lax.broadcasted_iota(jnp.int32, bias_ref.shape, 0)
+    early = lax.broadcasted_iota(jnp.int32, bias_ref.shape, 1)
+    end = docs[:, :1]
+    late_doc = jnp.where(late >= end, 1, 0)
+    early_doc = jnp.where(early >= end, 1, 0)
+    for k in range(1, docs.shape[1]):
+        end = end + docs[:, k : k + 1]
+        late_doc = late_doc + jnp.where(late >= end, 1, 0)
+        early_doc = early_doc + jnp.where(early >= end, 1, 0)
+    allowed = (late_doc == early_doc) & (early <= late)
+    bias_ref[...] = jnp.where(allowed, 0.0, -1e30)
 
     def relay(t):
         to_y(t, 0).wait_recv()
@@ -407,7 +423,7 @@
         cp.wait()
 
 
-def gather_first(rows_in, query, key, value, project, gains, cotangent, bias):
+def gather_first(rows_in, query, key, value, project, gains, cotangent, docs):
     rows = query.shape[0]
     width = query.shape[1] + 2 * key.shape[1]
     tokens_here, model = rows_in.shape
@@ -422,17 +438,19 @@
             jax.ShapeDtypeStruct((tokens_here, model), BF),
             jax.ShapeDtypeStruct((tokens_here, width), BF),
             jax.ShapeDtypeStruct((tokens_here, query.shape[1]), BF),
-            jax.ShapeDtypeStruct((8,) + gains.shape, gains.dtype),
+            jax.ShapeDtypeStruct((1, model), F32),
+            jax.ShapeDtypeStruct((1, model), F32),
+            jax.ShapeDtypeStruct((tokens_here, tokens_here), F32),
             jax.ShapeDtypeStruct((tokens_here, 128), F32),
         ),
         in_specs=[hbm] * 7 + [vmem],
-        out_specs=[hbm] * 6 + [vmem] * 2,
+        out_specs=[hbm] * 6 + [vmem] * 4,
         scratch_shapes=[
+            pltpu.VMEM((8,) + gains.shape, gains.dtype),
             pltpu.VMEM((8 * rows, width), BF),
             pltpu.VMEM(project.shape, BF),
             pltpu.VMEM(cotangent.shape, BF),
             pltpu.VMEM((tokens_here, model), BF),
-            pltpu.VMEM((1, model), F32),
             pltpu.VMEM((tokens_here, model), BF),
             pltpu.VMEM((tokens_here, width), BF),
             pltpu.VMEM((tokens_here, query.shape[1]), BF),
@@ -446,7 +464,7 @@
             pltpu.SemaphoreType.DMA((16,)),
         ],
         compiler_params=pltpu.CompilerParams(collective_id=1, has_side_effects=True),
-    )(rows_in, query, key, value, project, gains, cotangent, bias)
+    )(rows_in, query, key, value, project, gains, cotangent, docs)
 
 
 def attention_back_kernel(qkv, back, logs, bias, out):
@@ -603,7 +621,7 @@
     wg,
     wu,
     wd,
-    live,
+    counts,
     back_out,
     partial_out,
     gate_go,
@@ -642,6 +660,7 @@
     sw_r,
     out_sem,
     ready,
+    live,
 ):
     n, w = lax.axis_index("narrow"), lax.axis_index("wide")
     y, x, core = n // 4, lax.rem(n // 2, 2), lax.rem(n, 2)
@@ -665,6 +684,10 @@
     scatter = LineScatter(n, w, terms, (from_left, from_right), rs_s, rs_r, chunks)
     gather.start_chunk(0)
     gather.start_chunk(1)
+    here = lax.broadcasted_iota(jnp.int32, counts.shape, 1) == w
+    count = jnp.sum(jnp.where(here, counts[...].astype(F32), 0.0), axis=-1, keepdims=True)
+    slot = lax.broadcasted_iota(jnp.int32, live.shape, 1) // TILE
+    live[...] = jnp.where(slot.astype(F32) < count, 1.0, 0.0)
     gather.near(0)
     gather.far(0)
     for cp in loads:
@@ -852,7 +875,7 @@
         cp.wait()
 
 
-def feed_forward(mixed, cot, gate_weight, up_weight, down_weight, live):
+def feed_forward(mixed, cot, gate_weight, up_weight, down_weight, counts):
     tokens_here, model = mixed.shape
     width = gate_weight.shape[1]
     rows, eighth, cut = tokens_here // 4, model // 8, width // 2
@@ -904,11 +927,12 @@
             dma((3,)),
             dma((8,)),
             pltpu.SemaphoreType.REGULAR,
+            pltpu.VMEM((1, width), F32),
         ],
         compiler_params=pltpu.CompilerParams(
             collective_id=5, has_side_effects=True, vmem_limit_bytes=64 * 1024 * 1024 - 65536
         ),
-    )(mixed, cot, gate_weight, up_weight, down_weight, live)
+    )(mixed, cot, gate_weight, up_weight, down_weight, counts)
 
 
 class Reduce:
@@ -1306,10 +1330,13 @@
 
 def reduce_last(factors, stays, comes, feed_terms, gain_parts):
     rows = factors[0].shape[1] // 8
-    items = []
-    for p, xf in ((0, True), (0, False), (1, True), (1, False)):
-        half = factors[2 * p + 1].shape[1] // 2
-        items.append((p, (0 if xf else half, half), xf))
+    q_cols, k_cols = HEADS * HEAD_DIM, KV_HEADS * HEAD_DIM
+    items = [
+        (0, (0, q_cols), True),
+        (0, (q_cols, 2 * k_cols), False),
+        (1, (0, k_cols), True),
+        (1, (k_cols, q_cols - k_cols), False),
+    ]
     scratch = []
     for _, (_, cols), _ in items:
         scratch += [
@@ -1361,7 +1388,7 @@
             collective_id=4, has_side_effects=True, vmem_limit_bytes=64 * 1024 * 1024 - 65536
         ),
     )(*factors, *stays, *comes, feed_terms, gain_parts)
-    qkv = jnp.concatenate([out[0].reshape(rows, -1), out[1].reshape(rows, -1)], axis=1)
+    qkv = out[0].reshape(rows, -1), out[1].reshape(rows, -1)
     project = jnp.concatenate([out[2].reshape(rows, -1), out[3].reshape(rows, -1)], axis=1)
     width = out[4].shape[2]
     ffn = [out[4].reshape(-1, width), out[5].reshape(-1, width), out[6]]
@@ -1395,8 +1422,7 @@
     allowed = (segment[:, None] == segment[None, :]) & (position[None, :] <= position[:, None])
     if fast:
         gains = jnp.stack([prenorm_gain, midnorm_gain]).astype(F32).reshape(1, -1)
-        bias = jnp.where(allowed, 0.0, -1e30).astype(F32)
-        qkv_full, project_full, grad_rows, normed, qkv, attended, gains_full, logs = gather_first(
+        qkv_full, project_full, grad_rows, normed, qkv, attended, *small = gather_first(
             block_input,
             query_weight,
             key_weight,
@@ -1404,11 +1430,10 @@
             project_weight,
             gains,
             cotangent,
-            bias,
-        )
-        gains_full = gains_full.reshape(8, 2, -1)
-        first_gain = gains_full[:, 0].reshape(-1)
-        second_gain = gains_full[:, 1].reshape(-1)
+            doc_lengths,
+        )
+        first_gain, second_gain, bias, logs = small
+        first_gain, second_gain = first_gain.reshape(-1), second_gain.reshape(-1)
     else:
         qkv_full = jnp.concatenate(
             [
@@ -1454,7 +1479,7 @@
     live = (jnp.arange(width, dtype=jnp.int32) // TILE < my_count).astype(jnp.float32)
     if fast:
         mixed_back, feed_terms, *pieces = feed_forward(
-            mixed_in, grad_rows, gate_weight, up_weight, down_weight, live.reshape(1, -1)
+            mixed_in, grad_rows, gate_weight, up_weight, down_weight, tile_counts.reshape(1, -1)
         )
         stays = pieces[1::2]
         comes = [
@@ -1549,7 +1574,9 @@
         )
         gain_total = gain_total.reshape(2, -1)
         first_total, second_total = gain_total[0], gain_total[1]
-        qkv_total = qkv_total.astype(F32)
+        query_total = qkv_total[0].astype(F32)
+        key_total = qkv_total[1][:, :k_cols].astype(F32)
+        value_total = qkv_total[1][:, k_cols:].astype(F32)
         project_total = project_total.T.astype(F32)
         gate_total, up_total, down_total = [t.astype(F32) for t in ffn_totals]
     else:
@@ -1559,6 +1586,9 @@
             return lax.psum(share, "wide").astype(F32)
 
         qkv_total = owned(contract_rows(normed, qkv_back))
+        query_total = qkv_total[:, :q_cols]
+        key_total = qkv_total[:, q_cols : q_cols + k_cols]
+        value_total = qkv_total[:, q_cols + k_cols :]
         project_total = owned(contract_rows(branch_back, attended)).T
         first_total = owned(first_gain_part)
         second_total = owned(second_gain_part)
@@ -1574,9 +1604,9 @@
     return (
         block_output,
         input_grad,
-        qkv_total[:, :q_cols],
-        qkv_total[:, q_cols : q_cols + k_cols],
-        qkv_total[:, q_cols + k_cols :],
+        query_total,
+        key_total,
+        value_total,
         project_total,
         first_total,
         second_total,

time: 445 us -> 438 us (0.984)
  no operation moved by 1% of the time
where the time goes in v9:
time: 438 us; the launch traced here: 432 us
  Pallas kernels  366 us (84%)
  other arithmetic  36.8 us (8%)
  matrix products  19 us (4%)
  local copies, waits for them, and re-layouts  4.93 us (1%)
    pallas_call x1, Pallas kernels, reduce_last(): pl.pallas_call(functools.partial(last_kernel, items), name='reduce_last',...  149 us
    pallas_call x1, Pallas kernels, feed_forward(): pl.pallas_call(middle_kernel, name='feed_forward', out_shape=(jax.ShapeDt...  126 us
    pallas_call x1, Pallas kernels, gather_first(): pl.pallas_call(first_kernel, name='gather_first', out_shape=(jax.ShapeDty...  77.1 us
    convert_element_type x3, other arithmetic, per_device(): gate_total, up_total, down_total = [t.astype(F32) for t in ffn_totals]  16.8 us
    dot_general x2, matrix products, contract_cols(): lax.dot_general(left, right, (((1,), (1,)), ((), ())), preferred_element_...  14 us
    pallas_call x1, Pallas kernels, attention_back(): pl.pallas_call(attention_back_kernel, name='attention_back', out_shape=ja...  13.2 us
  transfers between devices with their start and end apart: 4, of which 0 were waited for; matrix products, arithmetic and copies ran while one was open for 6% of the time, Pallas kernels for 3%

profile of v9, /device:TPU:0, one launch (start us, length us, event | category | flops | bytes accessed | tf_op | source)
XLA Modules:
  0.0 432.2 jit_solution(8606770913307803635)
XLA Ops:
  0.6 1.5 fusion.3
  2.2 0.0 copy-start.3
  2.2 0.7 stack.12
  2.9 0.7 stack.13
  3.6 0.6 copy.26
  4.2 77.1 %gather_first.1 = (bf16[2048,2304]{1,0:T(8,128)(2,1)}, bf16[1536,2048]{1,0:T(8,128)(2,1)}, bf16[4,256,2048]{2,1,0:T(8,128)(2,1)}, bf16[256,2048]{1,0:T(8,128)(2,...) custom-call(bf16[256,2048]{1,0:T(8,128)(2,1)} %x_ref.1, ...), custom_call_target="tpu_custom_call" | custom-call | tf_op jit(solution)/shard_map/gather_first/pallas_call | solution.py:431
  81.2 0.0 copy-done.3
  81.3 0.0 copy-start.10
  81.3 5.0 %multiply_reduce_fusion.2 = (f32[256]{0:T(256)S(1)}, f32[256,2048]{1,0:T(8,128)S(1)}) fusion(bf16[256,1536]{1,0:T(8,128)(2,1)} %get-tuple-element.42.refs_3_, bf16[1536,2048]{1,0:T(8,128)(2,1)} %get-tuple-element.43, bf16[256,2048]{1,0:T(8,128)(2,1)S(1)} %copy-done.3), kind=kOutput, calls=%fused_computation.21 | convolution fusion | flops 1612709632 | bytes 10224640 | tf_op jit(solution)/shard_map/dot_general | solution.py:1471
  86.2 0.0 copy-start
  86.3 0.0 copy-start.18
  86.3 0.0 copy-done.14
  86.3 0.6 fusion.7
  86.9 0.7 copy-done
  87.6 0.0 copy-done.10
  87.6 1.2 multiply_convert_fusion.mixed
  88.8 0.0 copy-done.12
  88.8 0.0 copy-done.18
  88.8 126.3 %feed_forward.1 = (f32[256,2048]{1,0:T(8,128)}, bf16[4,256,2048]{2,1,0:T(8,128)(2,1)}, bf16[2,256,1152]{2,1,0:T(8,128)(2,1)}, bf16[2,256,1152]{2,1,0:T(8,128)(2,...) custom-call(bf16[256,2048]{1,0:T(8,128)(2,1)} %multiply_convert_fusi, ...), custom_call_target="tpu_custom_call" | custom-call | tf_op jit(solution)/shard_map/feed_forward/pallas_call | solution.py:890
  215.1 0.9 collective-permute-start.2
  216.0 0.6 collective-permute-start.3
  216.6 1.4 collective-permute-start
  218.0 1.3 collective-permute-start.1
  219.3 0.0 copy-start.13
  219.3 2.9 multiply_reduce_fusion
  222.2 0.0 copy-done.19
  222.2 0.0 copy-done.1
  222.2 0.6 copy-done.2
  222.8 0.0 copy-done.11
  222.8 0.0 copy-done.13
  222.8 2.0 fusion.9.refs_2_
  224.8 0.0 copy-start.5
  224.8 5.9 %convolution_convert_fusion.back = bf16[256,1536]{1,0:T(8,128)(2,1)} fusion(bf16[256,2048]{1,0:T(8,128)(2,1)S(1)} %fusion.9.refs_2_, bf16[1536,2048]{1,0:T(8,128)(2,1)} %get-tuple-element.43), kind=kOutput, calls=%fused_computation.9 | convolution fusion | flops 1611005952 | bytes 8126464 | tf_op jit(solution)/shard_map/dot_general | solution.py:34
  230.7 0.0 copy-done.5
  230.7 13.2 %attention_back.1.refs_1_ = bf16[256,2304]{1,0:T(8,128)(2,1)} custom-call(bf16[256,2304]{1,0:T(8,128)(2,1)} %get-tuple-element.48.qkv, bf16[256,1536]{1,0:T(8,128)(2,1)} %convolution_convert_fusion.back, f32[256,128]{1,0:T(8,128)} %get-tuple-element.49.logs, f32[256,256]{1,0:T(8,128)} %get-tuple-element.50.bias), custom_call_target="tpu_custom_call" | custom-call | flops 1006632960 | bytes 4718592 | tf_op jit(solution)/shard_map/attention_back/pallas_call | solution.py:517
  243.9 0.0 copy-done.4
  243.9 0.0 copy-done.16
  243.9 0.0 copy-done.17
  243.9 0.0 copy-start.15
  243.9 8.1 %fusion.6 = (f32[2048]{0:T(1024)S(1)}, f32[256]{0:T(256)S(1)}, f32[256,2048]{1,0:T(8,128)}) fusion(bf16[256,2048]{1,0:T(8,128)(2,1)S(1)} %copy-done.4, f32[256]{0:T(256)S(1)} %copy-done.17, f32[2048]{0:T(1024)S(1)} %bitcast.45, bf16[256,2304]{1,0:T(8,128)(2,1)} %attention_back.1.refs_1_, bf16[2048,2304]{1,0:T(8,128)(2,1)} %get-tuple-element.51), kind=kOutput, calls=%fused_computation.16 | convolution fusion | flops 2419586816 | bytes 13780992 | tf_op jit(solution)/shard_map/dot_general | solution.py:34
  252.0 0.6 reshape.105.refs_13_
  252.6 0.0 copy-done.15
  252.7 4.6 %fusion.2 = bf16[256,2048]{1,0:T(8,128)(2,1)} fusion(bf16[256,2048]{1,0:T(8,128)(2,1)S(1)} %copy-done.4, f32[256,2048]{1,0:T(8,128)} %get-tuple-element.83, f32[256]{0:T(256)S(1)} %multiply_multiply_fusion, f32[256]{0:T(256)S(1)} %copy-done.17, f32[2048]{0:T(1024)S(1)} %bitcast.46, f32[256,2048]{1,0:T(8,128)S(1)} %copy-done.1, ...), kind=kLoop, calls=%fused_computation.12 | loop fusion | flops 7864320 | bytes 9457664 | tf_op jit(solution)/shard_map/convert_element_type | solution.py:1561
  257.3 0.0 collective-permute-done.2.refs_10_
  257.3 0.0 collective-permute-done.3.refs_11_
  257.3 0.0 collective-permute-done.refs_8_
  257.3 0.0 collective-permute-done.1.refs_9_
  257.3 149.5 %reduce_last.1 = (bf16[4,64,1536]{2,1,0:T(8,128)(2,1)}, bf16[4,64,768]{2,1,0:T(8,128)(2,1)}, bf16[4,64,384]{2,1,0:T(8,128)(2,1)}, bf16[4,64,1152]{2,1,0:T(8,128)...) custom-call(bf16[256,2048]{1,0:T(8,128)(2,1)} %get-tuple-element.44., ...), custom_call_target="tpu_custom_call" | custom-call | tf_op jit(solution)/shard_map/reduce_last/pallas_call | solution.py:1380
  406.8 0.0 copy-start.20
  406.8 0.0 copy-start.9
  406.8 3.6 add_convert_fusion
  410.4 0.0 copy-done.20
  410.4 0.6 fusion.10
  410.9 0.0 copy-done.9
  410.9 0.1 copy.24
  411.1 0.2 copy.25
  411.4 0.9 slice_convert_fusion
  412.3 0.0 copy-done.6
  412.3 1.4 bitcast_convert_fusion.2
  413.7 7.1 %bitcast_convert_fusion.1 = f32[2048,1152]{1,0:T(8,128)} fusion(bf16[8,256,1152]{2,1,0:T(8,128)(2,1)} %get-tuple-element.70), kind=kLoop, calls=%fused_computation.1 | loop fusion | flops 2359296 | bytes 14155776 | tf_op jit(solution)/shard_map/convert_element_type | solution.py:1581
  420.8 4.7 %bitcast_convert_fusion = f32[2048,1152]{1,0:T(8,128)} fusion(bf16[8,256,1152]{2,1,0:T(8,128)(2,1)S(1)} %bitcast.34), kind=kLoop, calls=%fused_computation | loop fusion | flops 2359296 | bytes 14155776 | tf_op jit(solution)/shard_map/convert_element_type | solution.py:1581
  425.5 0.0 slice-done.1
  425.5 4.9 %convert_element_type.86 = f32[1152,2048]{1,0:T(8,128)} convert(bf16[1152,2048]{1,0:T(8,128)(2,1)S(1)} %bitcast.32) | non-fusion elementwise | flops 2359296 | bytes 14155776 | tf_op jit(solution)/shard_map/convert_element_type | solution.py:1581
  430.5 1.3 convert_bitcast_fusion
  (27 shorter events, 0.1 us)
Async XLA Ops:
  2.2 84.1 %copy-start.14 = (f32[256]{0:T(256)}, f32[256]{0:T(256)S(1)}, u32[]{:S(2)}) copy-start(f32[256]{0:T(256)S(1)} %fusion.3) | copy-start | bytes 3076
  2.2 79.1 %copy-start.3 = (bf16[256,2048]{1,0:T(8,128)(2,1)S(1)}, bf16[256,2048]{1,0:T(8,128)(2,1)}, u32[]{:S(2)}) copy-start(bf16[256,2048]{1,0:T(8,128)(2,1)} %x_ref.1) | copy-start | bytes 3145732
  81.3 6.3 %copy-start.10 = (f32[1,2048]{1,0:T(1,128)S(1)}, f32[1,2048]{1,0:T(1,128)}, u32[]{:S(2)}) copy-start(f32[1,2048]{1,0:T(1,128)} %get-tuple-element.45) | copy-start | bytes 24580
  86.2 1.3 copy-start
  86.3 2.5 copy-start.18
  86.9 1.9 copy-start.12
  215.1 42.1 %collective-permute-start.2 = (bf16[2,576,256]{2,1,0:T(8,128)(2,1)}, bf16[2,576,256]{2,1,0:T(8,128)(2,1)}, u32[]{:S(2)}, u32[]{:S(2)}) collective-permute-start(bf16[2,576,256]{2,1,0:T(8,128)(2,1)} %get-tuple-element.60), channel_id=1, source_target_pairs={{0,8},{4,12},{8,0},{12,4},{16,24},{20,28},{24,16},{28,20},{1,9},{5... | collective-permute-start | bytes 1769480 | tf_op jit(solution)/shard_map/ppermute | solution.py:1486
  216.0 41.3 %collective-permute-start.3 = (bf16[2,576,256]{2,1,0:T(8,128)(2,1)}, bf16[2,576,256]{2,1,0:T(8,128)(2,1)}, u32[]{:S(2)}, u32[]{:S(2)}) collective-permute-start(bf16[2,576,256]{2,1,0:T(8,128)(2,1)} %get-tuple-element.61), channel_id=1, source_target_pairs={{0,16},{4,20},{8,24},{12,28},{16,0},{20,4},{24,8},{28,12},{1,17},{... | collective-permute-start | bytes 1769480 | tf_op jit(solution)/shard_map/ppermute | solution.py:1486
  216.6 40.7 %collective-permute-start = (bf16[2,256,1152]{2,1,0:T(8,128)(2,1)}, bf16[2,256,1152]{2,1,0:T(8,128)(2,1)}, u32[]{:S(2)}, u32[]{:S(2)}) collective-permute-start(bf16[2,256,1152]{2,1,0:T(8,128)(2,1)} %get-tuple-element.58), channel_id=1, source_target_pairs={{0,8},{4,12},{8,0},{12,4},{16,24},{20,28},{24,16},{28,20},{1,9},{5... | collective-permute-start | bytes 3538952 | tf_op jit(solution)/shard_map/ppermute | solution.py:1486
  218.0 39.3 %collective-permute-start.1 = (bf16[2,256,1152]{2,1,0:T(8,128)(2,1)}, bf16[2,256,1152]{2,1,0:T(8,128)(2,1)}, u32[]{:S(2)}, u32[]{:S(2)}) collective-permute-start(bf16[2,256,1152]{2,1,0:T(8,128)(2,1)} %get-tuple-element.59), channel_id=1, source_target_pairs={{0,16},{4,20},{8,24},{12,28},{16,0},{20,4},{24,8},{28,12},{1,17},{... | collective-permute-start | bytes 3538952 | tf_op jit(solution)/shard_map/ppermute | solution.py:1486
  219.3 2.9 copy-start.19
  219.3 2.9 copy-start.1
  219.3 3.5 copy-start.2
  219.3 3.5 copy-start.11
  219.3 3.5 copy-start.13
  224.8 5.9 %copy-start.5 = (bf16[256,2048]{1,0:T(8,128)(2,1)}, bf16[256,2048]{1,0:T(8,128)(2,1)S(1)}, u32[]{:S(2)}) copy-start(bf16[256,2048]{1,0:T(8,128)(2,1)S(1)} %fusion.9.refs_2_) | copy-start | bytes 3145732
  230.7 13.2 %copy-start.4 = (bf16[256,2048]{1,0:T(8,128)(2,1)S(1)}, bf16[256,2048]{1,0:T(8,128)(2,1)}, u32[]{:S(2)}) copy-start(bf16[256,2048]{1,0:T(8,128)(2,1)} %x_ref.1) | copy-start | bytes 3145732
  230.7 13.2 %copy-start.16 = (f32[1,2048]{1,0:T(1,128)S(1)}, f32[1,2048]{1,0:T(1,128)}, u32[]{:S(2)}) copy-start(f32[1,2048]{1,0:T(1,128)} %get-tuple-element.52) | copy-start | bytes 24580
  230.7 13.2 %copy-start.17 = (f32[256]{0:T(256)S(1)}, f32[256]{0:T(256)}, u32[]{:S(2)}) copy-start(f32[256]{0:T(256)} %get-tuple-element.85) | copy-start | bytes 3076
  243.9 8.8 %copy-start.15 = (f32[256]{0:T(256)S(1)}, f32[256]{0:T(256)}, u32[]{:S(2)}) copy-start(f32[256]{0:T(256)} %copy-done.14) | copy-start | bytes 3076
  406.8 3.6 copy-start.20
  406.8 4.2 copy-start.9
  406.8 4.3 copy-start.7
  406.8 4.6 %copy-start.8 = (bf16[4,64,768]{2,1,0:T(8,128)(2,1)S(1)}, bf16[4,64,768]{2,1,0:T(8,128)(2,1)}, u32[]{:S(2)}) copy-start(bf16[4,64,768]{2,1,0:T(8,128)(2,1)} %get-tuple-element.66) | copy-start | bytes 1179652
  410.4 1.9 copy-start.6
  412.3 8.5 %slice-start.2 = ((s8[4718592]{0:T(1024)(128)(4,1)}), s8[4194304]{0:T(1024)(128)(4,1)S(1)}, s32[]{:S(2)}) async-start(s8[4718592]{0:T(1024)(128)(4,1)} %bitcast.33), calls=%async_computation.2 | async-start | bytes 8388608
  413.7 7.1 %slice-start.3 = ((s8[4718592]{0:T(1024)(128)(4,1)}), s8[524288]{0:T(1024)(128)(4,1)S(1)}, s32[]{:S(2)}) async-start(s8[4718592]{0:T(1024)(128)(4,1)} %bitcast.33), calls=%async_computation.3 | async-start | bytes 1048576
  413.7 11.9 %slice-start = ((s8[4718592]{0:T(1024)(128)(4,1)}), s8[4194304]{0:T(1024)(128)(4,1)S(1)}, s32[]{:S(2)}) async-start(s8[4718592]{0:T(1024)(128)(4,1)} %bitcast.31), calls=%async_computation | async-start | bytes 8388608
  420.8 4.7 %slice-start.1 = ((s8[4718592]{0:T(1024)(128)(4,1)}), s8[524288]{0:T(1024)(128)(4,1)S(1)}, s32[]{:S(2)}) async-start(s8[4718592]{0:T(1024)(128)(4,1)} %bitcast.31), calls=%async_computation.1 | async-start | bytes 1048576

commit v10 on v9

--- a/solution.py
+++ b/solution.py
@@ -22,6 +22,12 @@
 def rms_scale(rows, gain):
     factor = lax.rsqrt(jnp.mean(rows * rows, axis=-1, keepdims=True) + EPSILON)
     return rows * factor * gain
+
+
+def scale_back(back, rows, gain, factor):
+    scaled = back * gain
+    inner = jnp.mean(scaled * rows, axis=-1, keepdims=True)
+    return factor * scaled - rows * (factor**3 * inner), jnp.sum(back * rows * factor, axis=0)
 
 
 def contract_rows(left, right):
@@ -187,21 +193,25 @@
     c_ref,
     docs_ref,
     qkv_out,
-    p_full,
+    p_out,
     c_full,
     normed_out,
     rows_out,
     att_out,
+    middle_out,
+    mixed_out,
     gain_row,
     gain_late,
     bias_ref,
     log_out,
     g_full,
     qkv_full,
-    p_buf,
+    p_full,
     c_buf,
     x_buf,
     normed,
+    middle,
+    mixed,
     qkv,
     att,
     in_sem,
@@ -235,7 +245,7 @@
         (
             (g_ref, g_full.at[n]),
             (x_ref, x_buf),
-            (p_ref, p_buf),
+            (p_ref, region(3, n, 2)),
             (c_ref, c_buf),
             (q_ref, region(0, n, 2)),
             (k_ref, region(1, n, 2)),
@@ -306,17 +316,22 @@
         gain(i).wait()
     for cp in locals_in:
         cp.wait()
-    put(p_buf, region(3, n, 2))
     put(c_buf, c_full.at[w])
     for k in range(8):
         gain_row[:, pl.ds(k * rows, rows)] = g_full[k, :, :rows]
         gain_late[:, pl.ds(k * rows, rows)] = g_full[k, :, rows:]
     strip = 16
 
+    def scaled(rows_f, gain_ref, s, kept, others_f):
+        factor = lax.rsqrt(jnp.mean(rows_f * rows_f, axis=-1, keepdims=True) + EPSILON)
+        lane = lax.broadcasted_iota(jnp.int32, (strip, log_out.shape[1]), 1)
+        log_out[s, :] = jnp.where(lane == kept, factor, others_f)
+        return (rows_f * factor * gain_ref[...]).astype(BF)
+
     @pl.loop(0, x_buf.shape[0] // strip)
     def _(i):
         s = pl.ds(pl.multiple_of(i * strip, strip), strip)
-        normed[s, :] = rms_scale(x_buf[s, :].astype(F32), gain_row[...]).astype(BF)
+        normed[s, :] = scaled(x_buf[s, :].astype(F32), gain_row, s, 127, 0.0)
 
     put(normed, normed_out)
 
@@ -376,7 +391,6 @@
     put(qkv, rows_out)
     line.far(3)
 
-    log_out[...] = jnp.zeros(log_out.shape, F32)
     pair = 2 * HEAD_DIM
     group = HEADS // KV_HEADS
 
@@ -408,6 +422,25 @@
     put(att, att_out)
     relay(3)
     corner(3)
+    for which in range(4):
+        to_c(3, which).wait_recv()
+    put(p_full, p_out)
+
+    @pl.loop(0, x_buf.shape[1] // tile)
+    def _(i):
+        s = pl.ds(pl.multiple_of(i * tile, tile), tile)
+        middle[:, s] = x_buf[:, s].astype(F32) + jnp.dot(
+            att[...], p_full[:, s], preferred_element_type=F32
+        )
+
+    put(middle, middle_out)
+
+    @pl.loop(0, x_buf.shape[0] // strip)
+    def _(i):
+        s = pl.ds(pl.multiple_of(i * strip, strip), strip)
+        mixed[s, :] = scaled(middle[s, :], gain_late, s, 126, log_out[s, :])
+
+    put(mixed, mixed_out)
     for t in range(4):
         for h in range(2):
             to_x(t, h).wait_send()
@@ -415,8 +448,6 @@
         on_x(t).wait_send()
         on_y(t).wait_send()
         for which in range(4):
-            if t == 3:
-                to_c(t, which).wait_recv()
             to_c(t, which).wait_send()
     line.finish()
     for cp in locals_out:
@@ -438,24 +469,28 @@
             jax.ShapeDtypeStruct((tokens_here, model), BF),
             jax.ShapeDtypeStruct((tokens_here, width), BF),
             jax.ShapeDtypeStruct((tokens_here, query.shape[1]), BF),
+            jax.ShapeDtypeStruct((tokens_here, model), F32),
+            jax.ShapeDtypeStruct((tokens_here, model), BF),
             jax.ShapeDtypeStruct((1, model), F32),
             jax.ShapeDtypeStruct((1, model), F32),
             jax.ShapeDtypeStruct((tokens_here, tokens_here), F32),
             jax.ShapeDtypeStruct((tokens_here, 128), F32),
         ),
         in_specs=[hbm] * 7 + [vmem],
-        out_specs=[hbm] * 6 + [vmem] * 4,
+        out_specs=[hbm] * 8 + [vmem] * 4,
         scratch_shapes=[
             pltpu.VMEM((8,) + gains.shape, gains.dtype),
             pltpu.VMEM((8 * rows, width), BF),
-            pltpu.VMEM(project.shape, BF),
+            pltpu.VMEM((project.shape[0], 8 * rows), BF),
             pltpu.VMEM(cotangent.shape, BF),
             pltpu.VMEM((tokens_here, model), BF),
+            pltpu.VMEM((tokens_here, model), BF),
+            pltpu.VMEM((tokens_here, model), F32),
             pltpu.VMEM((tokens_here, model), BF),
             pltpu.VMEM((tokens_here, width), BF),
             pltpu.VMEM((tokens_here, query.shape[1]), BF),
             pltpu.SemaphoreType.DMA((7,)),
-            pltpu.SemaphoreType.DMA((6,)),
+            pltpu.SemaphoreType.DMA((8,)),
             pltpu.SemaphoreType.DMA((40,)),
             pltpu.SemaphoreType.DMA((40,)),
             pltpu.SemaphoreType.DMA((7,)),
@@ -1422,7 +1457,7 @@
     allowed = (segment[:, None] == segment[None, :]) & (position[None, :] <= position[:, None])
     if fast:
         gains = jnp.stack([prenorm_gain, midnorm_gain]).astype(F32).reshape(1, -1)
-        qkv_full, project_full, grad_rows, normed, qkv, attended, *small = gather_first(
+        qkv_full, project_full, grad_rows, normed, qkv, attended, *rest = gather_first(
             block_input,
             query_weight,
             key_weight,
@@ -1432,7 +1467,7 @@
             cotangent,
             doc_lengths,
         )
-        first_gain, second_gain, bias, logs = small
+        middle, mixed_in, first_gain, second_gain, bias, logs = rest
         first_gain, second_gain = first_gain.reshape(-1), second_gain.reshape(-1)
     else:
         qkv_full = jnp.concatenate(
@@ -1468,9 +1503,9 @@
             .astype(jnp.bfloat16)
             .reshape(tokens_here, HEADS * HEAD_DIM)
         )
-    branch = jnp.dot(attended, project_full, preferred_element_type=jnp.float32)
-    middle = inputs_f + branch
-    mixed_in = rms_scale(middle, second_gain).astype(jnp.bfloat16)
+        branch = jnp.dot(attended, project_full, preferred_element_type=jnp.float32)
+        middle = inputs_f + branch
+        mixed_in = rms_scale(middle, second_gain).astype(jnp.bfloat16)
     width = gate_weight.shape[1]
     wide_index = lax.axis_index("wide")
     my_count = jnp.sum(
@@ -1508,8 +1543,13 @@
         gate_part = contract_rows(gathered, gate_back)
         up_part = contract_rows(gathered, up_back)
     out_grad = cotangent.astype(jnp.float32)
-    unused_second, second_backward = jax.vjp(rms_scale, middle, second_gain)
-    middle_norm_back, second_gain_part = second_backward(mixed_back)
+    if fast:
+        middle_norm_back, second_gain_part = scale_back(
+            mixed_back, middle, second_gain, logs[:, 126:127]
+        )
+    else:
+        unused_second, second_backward = jax.vjp(rms_scale, middle, second_gain)
+        middle_norm_back, second_gain_part = second_backward(mixed_back)
     middle_back = out_grad + middle_norm_back
     branch_back = middle_back.astype(jnp.bfloat16)
     attended_back = contract_cols(branch_back, project_full).astype(jnp.bfloat16)
@@ -1556,8 +1596,13 @@
         )
         qkv_back = jnp.concatenate([query_back, key_back, value_back], axis=1)
     normed_back = contract_cols(qkv_back, qkv_full)
-    unused_first, first_backward = jax.vjp(rms_scale, inputs_f, first_gain)
-    input_norm_back, first_gain_part = first_backward(normed_back)
+    if fast:
+        input_norm_back, first_gain_part = scale_back(
+            normed_back, inputs_f, first_gain, logs[:, 127:128]
+        )
+    else:
+        unused_first, first_backward = jax.vjp(rms_scale, inputs_f, first_gain)
+        input_norm_back, first_gain_part = first_backward(normed_back)
     input_grad = (middle_back + input_norm_back).astype(jnp.bfloat16)
 
     if fast:

time: 438 us -> 436 us (level)
  matrix products: 19 us -> 11 us
  Pallas kernels: 366 us -> 372 us
    dot_general x1 -> x0, matrix products: 4.98 us -> none  [per_device(): branch = jnp.dot(attended, project_full, preferred_element_type=jnp.float32)]
    convert_element_type x3 -> x2, other arithmetic: 16.8 us -> 19.1 us  [per_device(): gate_total, up_total, down_total = [t.astype(F32) for t in ffn_totals]]
  transfers between devices with their start and end apart: 4 -> 4, of which waited for: 0 -> 0; matrix products, arithmetic and copies ran while one was open for 6% -> 5% of each run, Pallas kernels for 3% -> 3%
where the time goes in v10:
time: 436 us; the launch traced here: 431 us
  Pallas kernels  372 us (85%)
  other arithmetic  36.4 us (8%)
  matrix products  11 us (3%)
  local copies, waits for them, and re-layouts  6.27 us (1%)
    pallas_call x1, Pallas kernels, reduce_last(): pl.pallas_call(functools.partial(last_kernel, items), name='reduce_last',...  150 us
    pallas_call x1, Pallas kernels, feed_forward(): pl.pallas_call(middle_kernel, name='feed_forward', out_shape=(jax.ShapeDt...  129 us
    pallas_call x1, Pallas kernels, gather_first(): pl.pallas_call(first_kernel, name='gather_first', out_shape=(jax.ShapeDty...  79.3 us
    convert_element_type x2, other arithmetic, per_device(): gate_total, up_total, down_total = [t.astype(F32) for t in ffn_totals]  19.1 us
    pallas_call x1, Pallas kernels, attention_back(): pl.pallas_call(attention_back_kernel, name='attention_back', out_shape=ja...  13.1 us
    dot_general x2, matrix products, contract_cols(): lax.dot_general(left, right, (((1,), (1,)), ((), ())), preferred_element_...  11 us
  transfers between devices with their start and end apart: 4, of which 0 were waited for; matrix products, arithmetic and copies ran while one was open for 5% of the time, Pallas kernels for 3%

profile of v10, /device:TPU:0, one launch (start us, length us, event | category | flops | bytes accessed | tf_op | source)
XLA Modules:
  0.0 430.9 jit_solution(109847794116227400)
XLA Ops:
  0.6 0.7 stack.13
  1.3 0.7 stack.12
  2.0 0.6 copy.34
  2.6 79.3 %gather_first.1 = (bf16[2048,2304]{1,0:T(8,128)(2,1)}, bf16[1536,2048]{1,0:T(8,128)(2,1)}, bf16[4,256,2048]{2,1,0:T(8,128)(2,1)}, bf16[256,2048]{1,0:T(8,128)(2,...) custom-call(bf16[256,2048]{1,0:T(8,128)(2,1)} %x_ref.1, ...), custom_call_target="tpu_custom_call" | custom-call | tf_op jit(solution)/shard_map/gather_first/pallas_call | solution.py:462
  81.9 129.2 %feed_forward.1 = (f32[256,2048]{1,0:T(8,128)}, bf16[4,256,2048]{2,1,0:T(8,128)(2,1)}, bf16[2,256,1152]{2,1,0:T(8,128)(2,1)}, bf16[2,256,1152]{2,1,0:T(8,128)(2,...) custom-call(bf16[256,2048]{1,0:T(8,128)(2,1)} %get-tuple-element.47., ...), custom_call_target="tpu_custom_call" | custom-call | tf_op jit(solution)/shard_map/feed_forward/pallas_call | solution.py:925
  211.1 1.5 collective-permute-start
  212.6 0.6 collective-permute-start.1
  213.2 1.4 collective-permute-start.2
  214.6 0.6 collective-permute-start.3
  215.2 1.1 slice_reduce_fusion.1
  216.3 0.0 copy-start.3
  216.3 0.0 copy-start
  216.3 0.0 copy-start.1
  216.3 0.0 copy-start.9
  216.3 2.9 multiply_reduce_fusion
  219.3 0.1 copy.30
  219.4 0.0 copy-done.3
  219.4 0.3 slice_reduce_fusion
  219.7 0.0 copy-done
  219.7 0.0 copy-done.1
  219.7 0.0 copy-done.9
  219.7 0.0 copy-start.12
  219.7 2.3 fusion.10.refs_2_
  222.0 0.0 copy-start.2
  222.0 1.4 copy-done.12
  223.4 2.7 convolution_convert_fusion.back
  226.1 0.0 copy-done.2
  226.1 0.0 copy-start.10
  226.1 13.1 %attention_back.1.refs_1_ = bf16[256,2304]{1,0:T(8,128)(2,1)} custom-call(bf16[256,2304]{1,0:T(8,128)(2,1)} %get-tuple-element.51.qkv, bf16[256,1536]{1,0:T(8,128)(2,1)} %convolution_convert_fusion.back, f32[256,128]{1,0:T(8,128)} %get-tuple-element.46.logs, f32[256,256]{1,0:T(8,128)} %get-tuple-element.53.bias), custom_call_target="tpu_custom_call" | custom-call | flops 1006632960 | bytes 4718592 | tf_op jit(solution)/shard_map/attention_back/pallas_call | solution.py:552
  239.2 0.0 copy-done.10
  239.2 0.0 copy-start.4
  239.3 8.3 %fusion.5 = (f32[2048]{0:T(1024)S(1)}, f32[256]{0:T(256)S(1)}, f32[256,2048]{1,0:T(8,128)}) fusion(bf16[256,2048]{1,0:T(8,128)(2,1)} %x_ref.1, f32[256]{0:T(256)S(1)} %get-tuple-element.81, f32[2048]{0:T(1024)S(1)} %bitcast.40, bf16[256,2304]{1,0:T(8,128)(2,1)} %attention_back.1.refs_1_, bf16[2048,2304]{1,0:T(8,128)(2,1)} %get-tuple-element.54), kind=kOutput, calls=%fused_computation.11 | convolution fusion | flops 2419586816 | bytes 13780992 | tf_op jit(solution)/shard_map/dot_general | solution.py:40
  247.6 0.1 copy.31
  247.7 0.0 copy-done.4
  247.7 0.2 fusion.9
  247.9 4.5 %fusion.3 = bf16[256,2048]{1,0:T(8,128)(2,1)} fusion(bf16[256,2048]{1,0:T(8,128)(2,1)} %x_ref.1, f32[256,2048]{1,0:T(8,128)} %get-tuple-element.87, f32[256]{0:T(256)S(1)} %fusion.9, f32[2048]{0:T(1024)S(1)} %bitcast.41, f32[256]{0:T(256)S(1)} %get-tuple-element.81, f32[256,2048]{1,0:T(8,128)S(1)} %copy-done, f32[256]{0:T(256)S(1)} %get-tuple-element.82, ...), kind=kLoop, calls=%fused_computation.9 | loop fusion | flops 6815744 | bytes 9457664 | tf_op jit(solution)/shard_map/convert_element_type | solution.py:1606
  252.5 0.6 reshape.85.refs_13_
  253.1 0.0 collective-permute-done.2.refs_10_
  253.1 0.0 collective-permute-done.3.refs_11_
  253.1 0.0 collective-permute-done.refs_8_
  253.1 0.0 collective-permute-done.1.refs_9_
  253.1 150.1 %reduce_last.1 = (bf16[4,64,1536]{2,1,0:T(8,128)(2,1)}, bf16[4,64,768]{2,1,0:T(8,128)(2,1)}, bf16[4,64,384]{2,1,0:T(8,128)(2,1)}, bf16[4,64,1152]{2,1,0:T(8,128)...) custom-call(bf16[256,2048]{1,0:T(8,128)(2,1)} %get-tuple-element.45., ...), custom_call_target="tpu_custom_call" | custom-call | tf_op jit(solution)/shard_map/reduce_last/pallas_call | solution.py:1415
  403.2 0.0 copy-start.5
  403.2 3.5 add_convert_fusion
  406.7 0.0 copy-start.7
  406.8 0.0 copy-start.6
  406.8 0.0 copy-done.5
  406.8 0.0 copy-start.8
  406.8 0.0 copy-start.11
  406.8 1.4 bitcast_convert_fusion.2
  408.1 0.0 copy-done.7
  408.2 0.9 slice_convert_fusion
  409.1 0.0 copy-done.6
  409.1 0.2 copy.33
  409.3 0.0 copy-done.8
  409.3 0.1 copy.32
  409.5 0.0 copy-done.11
  409.5 0.6 fusion.11
  410.1 7.3 %convert_element_type.82 = f32[1152,2048]{1,0:T(8,128)} convert(bf16[1152,2048]{1,0:T(8,128)(2,1)} %get-tuple-element.76) | non-fusion elementwise | flops 2359296 | bytes 14155776 | tf_op jit(solution)/shard_map/convert_element_type | solution.py:1626
  417.4 1.3 convert_bitcast_fusion
  418.6 11.8 %bitcast_convert_fusion = (f32[2048,1152]{1,0:T(8,128)}, f32[2048,1152]{1,0:T(8,128)}) fusion(bf16[8,256,1152]{2,1,0:T(8,128)(2,1)} %get-tuple-element.75, bf16[8,256,1152]{2,1,0:T(8,128)(2,1)} %get-tuple-element.74), kind=kLoop, calls=%fused_computation | loop fusion | flops 4718592 | bytes 28311552 | tf_op jit(solution)/shard_map/convert_element_type | solution.py:1626
  (4 shorter events, 0.0 us)
Async XLA Ops:
  211.1 42.0 %collective-permute-start = (bf16[2,256,1152]{2,1,0:T(8,128)(2,1)}, bf16[2,256,1152]{2,1,0:T(8,128)(2,1)}, u32[]{:S(2)}, u32[]{:S(2)}) collective-permute-start(bf16[2,256,1152]{2,1,0:T(8,128)(2,1)} %get-tuple-element.62), channel_id=1, source_target_pairs={{0,8},{4,12},{8,0},{12,4},{16,24},{20,28},{24,16},{28,20},{1,9},{5... | collective-permute-start | bytes 3538952 | tf_op jit(solution)/shard_map/ppermute | solution.py:1521
  212.6 40.5 %collective-permute-start.1 = (bf16[2,256,1152]{2,1,0:T(8,128)(2,1)}, bf16[2,256,1152]{2,1,0:T(8,128)(2,1)}, u32[]{:S(2)}, u32[]{:S(2)}) collective-permute-start(bf16[2,256,1152]{2,1,0:T(8,128)(2,1)} %get-tuple-element.63), channel_id=1, source_target_pairs={{0,16},{4,20},{8,24},{12,28},{16,0},{20,4},{24,8},{28,12},{1,17},{... | collective-permute-start | bytes 3538952 | tf_op jit(solution)/shard_map/ppermute | solution.py:1521
  213.2 39.9 %collective-permute-start.2 = (bf16[2,576,256]{2,1,0:T(8,128)(2,1)}, bf16[2,576,256]{2,1,0:T(8,128)(2,1)}, u32[]{:S(2)}, u32[]{:S(2)}) collective-permute-start(bf16[2,576,256]{2,1,0:T(8,128)(2,1)} %get-tuple-element.64), channel_id=1, source_target_pairs={{0,8},{4,12},{8,0},{12,4},{16,24},{20,28},{24,16},{28,20},{1,9},{5... | collective-permute-start | bytes 1769480 | tf_op jit(solution)/shard_map/ppermute | solution.py:1521
  214.6 38.5 %collective-permute-start.3 = (bf16[2,576,256]{2,1,0:T(8,128)(2,1)}, bf16[2,576,256]{2,1,0:T(8,128)(2,1)}, u32[]{:S(2)}, u32[]{:S(2)}) collective-permute-start(bf16[2,576,256]{2,1,0:T(8,128)(2,1)} %get-tuple-element.65), channel_id=1, source_target_pairs={{0,16},{4,20},{8,24},{12,28},{16,0},{20,4},{24,8},{28,12},{1,17},{... | collective-permute-start | bytes 1769480 | tf_op jit(solution)/shard_map/ppermute | solution.py:1521
  216.3 3.1 copy-start.3
  216.3 3.4 copy-start
  216.3 3.4 copy-start.1
  216.3 3.4 copy-start.9
  219.7 3.7 copy-start.12
  222.0 4.1 copy-start.2
  226.1 13.1 %copy-start.10 = (f32[1,2048]{1,0:T(1,128)S(1)}, f32[1,2048]{1,0:T(1,128)}, u32[]{:S(2)}) copy-start(f32[1,2048]{1,0:T(1,128)} %get-tuple-element.55) | copy-start | bytes 24580
  239.2 8.5 %copy-start.4 = (f32[256,128]{1,0:T(8,128)S(1)}, f32[256,128]{1,0:T(8,128)}, u32[]{:S(2)}) copy-start(f32[256,128]{1,0:T(8,128)} %get-tuple-element.46.logs) | copy-start | bytes 393220
  403.2 3.5 copy-start.5
  406.7 1.4 copy-start.7
  406.8 2.3 copy-start.6
  406.8 2.6 copy-start.8
  406.8 2.7 copy-start.11

commit v11 on v10

--- a/solution.py
+++ b/solution.py
@@ -838,7 +838,6 @@
     def _(j):
         wg_v[place(j, half), :] = row_grad(gb, 2 * j + 1 - core).astype(BF)
 
-    scatter.pass_on(chunks - 1)
     pl.semaphore_wait(ready, 1)
     swaps[0].start()
 
@@ -847,6 +846,7 @@
         wu_v[place(j, half), :] = row_grad(ub, 2 * j + 1 - core).astype(BF)
 
     swaps[1].start()
+    scatter.pass_on(chunks - 1)
 
     @pl.loop(0, 4)
     def _(j):

time: 436 us -> 432 us (level)
  no operation moved by 1% of the time
where the time goes in v11:
time: 432 us; the launch traced here: 427 us
  Pallas kernels  368 us (85%)
  other arithmetic  36.4 us (8%)
  matrix products  11.1 us (3%)
  local copies, waits for them, and re-layouts  6.27 us (1%)
    pallas_call x1, Pallas kernels, reduce_last(): pl.pallas_call(functools.partial(last_kernel, items), name='reduce_last',...  150 us
    pallas_call x1, Pallas kernels, feed_forward(): pl.pallas_call(middle_kernel, name='feed_forward', out_shape=(jax.ShapeDt...  126 us
    pallas_call x1, Pallas kernels, gather_first(): pl.pallas_call(first_kernel, name='gather_first', out_shape=(jax.ShapeDty...  79.3 us
    convert_element_type x2, other arithmetic, per_device(): gate_total, up_total, down_total = [t.astype(F32) for t in ffn_totals]  19.1 us
    pallas_call x1, Pallas kernels, attention_back(): pl.pallas_call(attention_back_kernel, name='attention_back', out_shape=ja...  13.1 us
    dot_general x2, matrix products, contract_cols(): lax.dot_general(left, right, (((1,), (1,)), ((), ())), preferred_element_...  11.1 us
  transfers between devices with their start and end apart: 4, of which 0 were waited for; matrix products, arithmetic and copies ran while one was open for 5% of the time, Pallas kernels for 3%

profile of v11, /device:TPU:0, one launch (start us, length us, event | category | flops | bytes accessed | tf_op | source)
XLA Modules:
  0.0 427.3 jit_solution(3132059742336824252)
XLA Ops:
  0.6 0.7 stack.13
  1.3 0.7 stack.12
  2.0 0.6 copy.34
  2.6 79.3 %gather_first.1 = (bf16[2048,2304]{1,0:T(8,128)(2,1)}, bf16[1536,2048]{1,0:T(8,128)(2,1)}, bf16[4,256,2048]{2,1,0:T(8,128)(2,1)}, bf16[256,2048]{1,0:T(8,128)(2,...) custom-call(bf16[256,2048]{1,0:T(8,128)(2,1)} %x_ref.1, ...), custom_call_target="tpu_custom_call" | custom-call | tf_op jit(solution)/shard_map/gather_first/pallas_call | solution.py:462
  81.9 125.6 %feed_forward.1 = (f32[256,2048]{1,0:T(8,128)}, bf16[4,256,2048]{2,1,0:T(8,128)(2,1)}, bf16[2,256,1152]{2,1,0:T(8,128)(2,1)}, bf16[2,256,1152]{2,1,0:T(8,128)(2,...) custom-call(bf16[256,2048]{1,0:T(8,128)(2,1)} %get-tuple-element.47., ...), custom_call_target="tpu_custom_call" | custom-call | tf_op jit(solution)/shard_map/feed_forward/pallas_call | solution.py:925
  207.5 1.5 collective-permute-start
  209.0 0.6 collective-permute-start.1
  209.6 1.4 collective-permute-start.2
  211.0 0.6 collective-permute-start.3
  211.6 1.1 slice_reduce_fusion.1
  212.7 0.0 copy-start.3
  212.7 0.0 copy-start
  212.7 0.0 copy-start.1
  212.7 0.0 copy-start.9
  212.7 2.9 multiply_reduce_fusion
  215.7 0.1 copy.30
  215.8 0.0 copy-done.3
  215.8 0.3 slice_reduce_fusion
  216.1 0.0 copy-done
  216.1 0.0 copy-done.1
  216.1 0.0 copy-done.9
  216.1 0.0 copy-start.12
  216.1 2.3 fusion.10.refs_2_
  218.4 0.0 copy-start.2
  218.4 1.4 copy-done.12
  219.8 2.7 convolution_convert_fusion.back
  222.5 0.0 copy-done.2
  222.5 0.0 copy-start.10
  222.5 13.1 %attention_back.1.refs_1_ = bf16[256,2304]{1,0:T(8,128)(2,1)} custom-call(bf16[256,2304]{1,0:T(8,128)(2,1)} %get-tuple-element.51.qkv, bf16[256,1536]{1,0:T(8,128)(2,1)} %convolution_convert_fusion.back, f32[256,128]{1,0:T(8,128)} %get-tuple-element.46.logs, f32[256,256]{1,0:T(8,128)} %get-tuple-element.53.bias), custom_call_target="tpu_custom_call" | custom-call | flops 1006632960 | bytes 4718592 | tf_op jit(solution)/shard_map/attention_back/pallas_call | solution.py:552
  235.7 0.0 copy-done.10
  235.7 0.0 copy-start.4
  235.7 8.3 %fusion.5 = (f32[2048]{0:T(1024)S(1)}, f32[256]{0:T(256)S(1)}, f32[256,2048]{1,0:T(8,128)}) fusion(bf16[256,2048]{1,0:T(8,128)(2,1)} %x_ref.1, f32[256]{0:T(256)S(1)} %get-tuple-element.81, f32[2048]{0:T(1024)S(1)} %bitcast.40, bf16[256,2304]{1,0:T(8,128)(2,1)} %attention_back.1.refs_1_, bf16[2048,2304]{1,0:T(8,128)(2,1)} %get-tuple-element.54), kind=kOutput, calls=%fused_computation.11 | convolution fusion | flops 2419586816 | bytes 13780992 | tf_op jit(solution)/shard_map/dot_general | solution.py:40
  244.0 0.1 copy.31
  244.1 0.0 copy-done.4
  244.2 0.2 fusion.9
  244.3 4.5 %fusion.3 = bf16[256,2048]{1,0:T(8,128)(2,1)} fusion(bf16[256,2048]{1,0:T(8,128)(2,1)} %x_ref.1, f32[256,2048]{1,0:T(8,128)} %get-tuple-element.87, f32[256]{0:T(256)S(1)} %fusion.9, f32[2048]{0:T(1024)S(1)} %bitcast.41, f32[256]{0:T(256)S(1)} %get-tuple-element.81, f32[256,2048]{1,0:T(8,128)S(1)} %copy-done, f32[256]{0:T(256)S(1)} %get-tuple-element.82, ...), kind=kLoop, calls=%fused_computation.9 | loop fusion | flops 6815744 | bytes 9457664 | tf_op jit(solution)/shard_map/convert_element_type | solution.py:1606
  248.9 0.6 reshape.85.refs_13_
  249.5 0.0 collective-permute-done.2.refs_10_
  249.5 0.0 collective-permute-done.3.refs_11_
  249.5 0.0 collective-permute-done.refs_8_
  249.5 0.0 collective-permute-done.1.refs_9_
  249.5 150.1 %reduce_last.1 = (bf16[4,64,1536]{2,1,0:T(8,128)(2,1)}, bf16[4,64,768]{2,1,0:T(8,128)(2,1)}, bf16[4,64,384]{2,1,0:T(8,128)(2,1)}, bf16[4,64,1152]{2,1,0:T(8,128)...) custom-call(bf16[256,2048]{1,0:T(8,128)(2,1)} %get-tuple-element.45., ...), custom_call_target="tpu_custom_call" | custom-call | tf_op jit(solution)/shard_map/reduce_last/pallas_call | solution.py:1415
  399.6 0.0 copy-start.5
  399.6 3.5 add_convert_fusion
  403.2 0.0 copy-start.7
  403.2 0.0 copy-start.6
  403.2 0.0 copy-done.5
  403.2 0.0 copy-start.8
  403.2 0.0 copy-start.11
  403.2 1.4 bitcast_convert_fusion.2
  404.6 0.0 copy-done.7
  404.6 0.9 slice_convert_fusion
  405.5 0.0 copy-done.6
  405.5 0.2 copy.33
  405.7 0.0 copy-done.8
  405.8 0.1 copy.32
  405.9 0.0 copy-done.11
  405.9 0.6 fusion.11
  406.5 7.3 %convert_element_type.82 = f32[1152,2048]{1,0:T(8,128)} convert(bf16[1152,2048]{1,0:T(8,128)(2,1)} %get-tuple-element.76) | non-fusion elementwise | flops 2359296 | bytes 14155776 | tf_op jit(solution)/shard_map/convert_element_type | solution.py:1626
  413.8 1.3 convert_bitcast_fusion
  415.0 11.8 %bitcast_convert_fusion = (f32[2048,1152]{1,0:T(8,128)}, f32[2048,1152]{1,0:T(8,128)}) fusion(bf16[8,256,1152]{2,1,0:T(8,128)(2,1)} %get-tuple-element.75, bf16[8,256,1152]{2,1,0:T(8,128)(2,1)} %get-tuple-element.74), kind=kLoop, calls=%fused_computation | loop fusion | flops 4718592 | bytes 28311552 | tf_op jit(solution)/shard_map/convert_element_type | solution.py:1626
  (4 shorter events, 0.0 us)
Async XLA Ops:
  207.5 42.0 %collective-permute-start = (bf16[2,256,1152]{2,1,0:T(8,128)(2,1)}, bf16[2,256,1152]{2,1,0:T(8,128)(2,1)}, u32[]{:S(2)}, u32[]{:S(2)}) collective-permute-start(bf16[2,256,1152]{2,1,0:T(8,128)(2,1)} %get-tuple-element.62), channel_id=1, source_target_pairs={{0,8},{4,12},{8,0},{12,4},{16,24},{20,28},{24,16},{28,20},{1,9},{5... | collective-permute-start | bytes 3538952 | tf_op jit(solution)/shard_map/ppermute | solution.py:1521
  209.0 40.5 %collective-permute-start.1 = (bf16[2,256,1152]{2,1,0:T(8,128)(2,1)}, bf16[2,256,1152]{2,1,0:T(8,128)(2,1)}, u32[]{:S(2)}, u32[]{:S(2)}) collective-permute-start(bf16[2,256,1152]{2,1,0:T(8,128)(2,1)} %get-tuple-element.63), channel_id=1, source_target_pairs={{0,16},{4,20},{8,24},{12,28},{16,0},{20,4},{24,8},{28,12},{1,17},{... | collective-permute-start | bytes 3538952 | tf_op jit(solution)/shard_map/ppermute | solution.py:1521
  209.6 39.9 %collective-permute-start.2 = (bf16[2,576,256]{2,1,0:T(8,128)(2,1)}, bf16[2,576,256]{2,1,0:T(8,128)(2,1)}, u32[]{:S(2)}, u32[]{:S(2)}) collective-permute-start(bf16[2,576,256]{2,1,0:T(8,128)(2,1)} %get-tuple-element.64), channel_id=1, source_target_pairs={{0,8},{4,12},{8,0},{12,4},{16,24},{20,28},{24,16},{28,20},{1,9},{5... | collective-permute-start | bytes 1769480 | tf_op jit(solution)/shard_map/ppermute | solution.py:1521
  211.0 38.5 %collective-permute-start.3 = (bf16[2,576,256]{2,1,0:T(8,128)(2,1)}, bf16[2,576,256]{2,1,0:T(8,128)(2,1)}, u32[]{:S(2)}, u32[]{:S(2)}) collective-permute-start(bf16[2,576,256]{2,1,0:T(8,128)(2,1)} %get-tuple-element.65), channel_id=1, source_target_pairs={{0,16},{4,20},{8,24},{12,28},{16,0},{20,4},{24,8},{28,12},{1,17},{... | collective-permute-start | bytes 1769480 | tf_op jit(solution)/shard_map/ppermute | solution.py:1521
  212.7 3.1 copy-start.3
  212.7 3.4 copy-start
  212.7 3.4 copy-start.1
  212.7 3.4 copy-start.9
  216.1 3.7 copy-start.12
  218.4 4.1 copy-start.2
  222.5 13.1 %copy-start.10 = (f32[1,2048]{1,0:T(1,128)S(1)}, f32[1,2048]{1,0:T(1,128)}, u32[]{:S(2)}) copy-start(f32[1,2048]{1,0:T(1,128)} %get-tuple-element.55) | copy-start | bytes 24580
  235.7 8.5 %copy-start.4 = (f32[256,128]{1,0:T(8,128)S(1)}, f32[256,128]{1,0:T(8,128)}, u32[]{:S(2)}) copy-start(f32[256,128]{1,0:T(8,128)} %get-tuple-element.46.logs) | copy-start | bytes 393220
  399.6 3.5 copy-start.5
  403.2 1.4 copy-start.7
  403.2 2.3 copy-start.6
  403.2 2.6 copy-start.8
  403.2 2.7 copy-start.11
